TPU v7x, 128 devices: a whole 4x4x4 slice. The times are simulated.
128 devices in a mesh: row: 16 (over y_lo, z, core), col: 8 (over x, y_hi).
Axes of the slice: x: 4, y: 4 (y_hi: 2, y_lo: 2; y = y_hi * 2 + y_lo), z: 4, core: 2. Of those that a mesh axis runs over, the one named last changes fastest.
Arguments:
- tokens: bfloat16 [2, 256, 256, 1024], P(None, 'row', 'col'), may hold values from -36 to 36
- norm_gain: float32 [1024], replicated, may hold values from 0.1 to 1.9
- w_query: bfloat16 [1024, 512], replicated, as said below
- w_kv: bfloat16 [1024, 1024], replicated, as said below
- w_out: bfloat16 [512, 1024], replicated, may hold values from -0.25 to 0.25
- w_pool: bfloat16 [4, 1024, 512], replicated, may hold values from -0.1875 to 0.1875
- w_join: bfloat16 [3, 3, 3072, 256], replicated, may hold values from -0.0390625 to 0.0390625
Outputs:
- joined: bfloat16 [2, 256, 256, 256], P(None, 'row', 'col')
Inputs may be any that keep to these rules, and one draw needn't show every extreme that they name: `w_query`: entries within 6 / sqrt(1024) + 10 / 1024 of zero. `w_kv`: entries within 6 / sqrt(1024) + 10 / 1024 of zero.
All inputs are finite; a program needn't handle non-finite values.
Results may differ from a plain program's by a relative error of at most 0.003.
The roundings to bfloat16 on the way count: a program that leaves them out, or rounds other values in their place, can miss the bound.
Values may be sent and summed in bfloat16 or wider, within the bound.
No kernel may reach another device: no remote copies, remote signals or barrier semaphores. Data moves between devices by JAX's collectives and lax.ppermute only.
A program may use at most 192 MiB of HBM per device.

v0:
```python
import math

import jax
import jax.numpy as jnp
from jax import lax
from jax.sharding import PartitionSpec as P

HEAD_DIM = 32
BLOCK = 8
HALO = 2


EPS = 1e-05
pool_levels = (1, 2, 3, 6)


def padded(cells, sides, width):
    for axis, dim in sides:
        count = lax.axis_size(axis)
        ends = count - 1
        head = lax.slice_in_dim(cells, 0, width, axis=dim)
        tail = lax.slice_in_dim(cells, cells.shape[dim] - width, cells.shape[dim], axis=dim)
        cells = jnp.concatenate(
            [
                lax.ppermute(tail, axis, [(i, (i + 1) % count) for i in range(ends)]),
                cells,
                lax.ppermute(head, axis, [((i + 1) % count, i) for i in range(ends)]),
            ],
            axis=dim,
        )
    return cells


def unfold(extended, axis, count):
    pad_spec = [(0, 0)] * extended.ndim
    pad_spec[axis] = (0, BLOCK - 2 * HALO)
    extended = jnp.pad(extended, pad_spec)
    nblocks = count // BLOCK
    head_part = lax.slice_in_dim(extended, 0, count, axis=axis)
    tail_part = lax.slice_in_dim(extended, BLOCK, count + BLOCK, axis=axis)
    new_shape = extended.shape[:axis] + (nblocks, BLOCK) + extended.shape[axis + 1 :]
    head_part = head_part.reshape(new_shape)
    tail_part = lax.slice_in_dim(tail_part.reshape(new_shape), 0, 2 * HALO, axis=axis + 1)
    return jnp.concatenate([head_part, tail_part], axis=axis + 1)


def attend(query_blocks, windows, row_ok, col_ok):
    sheets, nbr, _, nbc, _, inner = query_blocks.shape
    heads = inner // HEAD_DIM
    span = BLOCK + 2 * HALO
    queries = query_blocks.transpose(0, 1, 3, 2, 4, 5).reshape(
        sheets, nbr, nbc, BLOCK * BLOCK, heads, HEAD_DIM
    )
    window_kv = windows.transpose(0, 1, 3, 2, 4, 5).reshape(
        sheets, nbr, nbc, span * span, 2, heads, HEAD_DIM
    )
    keys = window_kv[:, :, :, :, 0]
    values = window_kv[:, :, :, :, 1]
    scores = jnp.einsum(
        "sabqhe,sabkhe->sabhqk", queries, keys, preferred_element_type=jnp.float32
    ) / math.sqrt(HEAD_DIM)
    allowed = row_ok[:, :, None, None] & col_ok[None, None, :, :]
    allowed = allowed.transpose(0, 2, 1, 3).reshape(nbr, nbc, 1, 1, span * span)
    scores = jnp.where(allowed[None], scores, -1e30)
    top = jnp.max(scores, axis=-1, keepdims=True)
    expon = jnp.exp(scores - top)
    weights = (expon / jnp.sum(expon, axis=-1, keepdims=True)).astype(jnp.bfloat16)
    context = jnp.einsum(
        "sabhqk,sabkhe->sabqhe", weights, values, preferred_element_type=jnp.float32
    )
    context = context.astype(jnp.bfloat16).reshape(sheets, nbr, nbc, BLOCK, BLOCK, inner)
    return context.transpose(0, 1, 3, 2, 4, 5).reshape(sheets, nbr * BLOCK, nbc * BLOCK, inner)


def pool_matrix(level, length, first, count):
    places = first + jnp.arange(count)
    cells = jnp.arange(level)
    starts = cells * length // level
    ends = ((cells + 1) * length + level - 1) // level
    member = (places[None, :] >= starts[:, None]) & (places[None, :] < ends[:, None])
    return (member, ends - starts)


def upsample_matrix(level, length, first, count):
    places = first + jnp.arange(count)
    numer = jnp.maximum((2 * places + 1) * level - length, 0)
    lower = numer // (2 * length)
    frac = (numer - lower * 2 * length).astype(jnp.float32) / (2.0 * length)
    upper = jnp.minimum(lower + 1, level - 1)
    cells = jnp.arange(level)[None, :]
    weight = (cells == lower[:, None]) * (1.0 - frac)[:, None] + (cells == upper[:, None]) * frac[
        :, None
    ]
    inside = ((places >= 0) & (places < length)).astype(jnp.float32)
    return weight * inside[:, None]


def grown_branches(branches, grid_h, grid_w, row_first, row_count, col_first, col_count):
    pieces = []
    for index, level in enumerate(pool_levels):
        row_map = upsample_matrix(level, grid_h, row_first, row_count)
        col_map = upsample_matrix(level, grid_w, col_first, col_count)
        grown = jnp.einsum(
            "ri,sijc,wj->srwc", row_map, branches[index], col_map, precision=lax.Precision.HIGHEST
        )
        pieces.append(grown.astype(jnp.bfloat16))
    return pieces


def body(tokens, norm_gain, w_query, w_kv, w_out, w_pool, w_join):
    sheets, rows_here, cols_here, width = tokens.shape
    row_index = lax.axis_index("row")
    col_index = lax.axis_index("col")
    grid_h = rows_here * lax.axis_size("row")
    grid_w = cols_here * lax.axis_size("col")
    row_first = row_index * rows_here
    col_first = col_index * cols_here
    tokens_f = tokens.astype(jnp.float32)
    center = jnp.mean(tokens_f, axis=-1, keepdims=True)
    spread = jnp.mean((tokens_f - center) ** 2, axis=-1, keepdims=True)
    normed = ((tokens_f - center) * lax.rsqrt(spread + EPS) * norm_gain).astype(jnp.bfloat16)
    queries = jnp.dot(normed, w_query, preferred_element_type=jnp.float32).astype(jnp.bfloat16)
    keyvals = jnp.dot(normed, w_kv, preferred_element_type=jnp.float32).astype(jnp.bfloat16)
    inner = queries.shape[-1]
    kv_extended = padded(keyvals, (("row", 1), ("col", 2)), HALO)
    windows = unfold(unfold(kv_extended, 1, rows_here), 3, cols_here)
    row_places = row_first - HALO + jnp.arange(rows_here + 2 * HALO)
    col_places = col_first - HALO + jnp.arange(cols_here + 2 * HALO)
    row_ok = unfold((row_places >= 0) & (row_places < grid_h), 0, rows_here)
    col_ok = unfold((col_places >= 0) & (col_places < grid_w), 0, cols_here)
    query_blocks = queries.reshape(
        sheets, rows_here // BLOCK, BLOCK, cols_here // BLOCK, BLOCK, inner
    )
    context = attend(query_blocks, windows, row_ok, col_ok)
    attended = (tokens_f + jnp.dot(context, w_out, preferred_element_type=jnp.float32)).astype(
        jnp.bfloat16
    )
    partials = []
    counts = []
    for index, level in enumerate(pool_levels):
        rows_in, rows_count = pool_matrix(level, grid_h, row_first, rows_here)
        cols_in, cols_count = pool_matrix(level, grid_w, col_first, cols_here)
        row_sums = jnp.einsum(
            "ir,srcd->sicd",
            rows_in.astype(jnp.bfloat16),
            attended,
            preferred_element_type=jnp.float32,
        )
        partials.append(
            jnp.einsum(
                "jc,sicd->sijd",
                cols_in.astype(jnp.float32),
                row_sums,
                precision=lax.Precision.HIGHEST,
            )
        )
        counts.append(
            (rows_count[:, None] * cols_count[None, :]).astype(jnp.float32)[None, :, :, None]
        )
    branches = []
    totals = lax.psum((partials[0], partials[1], partials[2], partials[3]), ("row", "col"))
    for index in range(4):
        pooled = totals[index] / counts[index]
        branch = jnp.einsum(
            "sijd,dp->sijp",
            pooled,
            w_pool[index].astype(jnp.float32),
            precision=lax.Precision.HIGHEST,
        )
        branches.append(jnp.maximum(branch, 0.0))
    pieces = grown_branches(branches, grid_h, grid_w, row_first, rows_here, col_first, cols_here)
    stacked_here = jnp.concatenate([attended] + pieces, axis=-1)
    stacked = padded(stacked_here, (("row", 1), ("col", 2)), 1)
    total = jnp.zeros((sheets, rows_here, cols_here, w_join.shape[-1]), jnp.float32)
    for shift_row in range(3):
        for shift_col in range(3):
            total = total + jnp.dot(
                stacked[:, shift_row : shift_row + rows_here, shift_col : shift_col + cols_here],
                w_join[shift_row, shift_col],
                preferred_element_type=jnp.float32,
            )
    return total.astype(jnp.bfloat16)


def solution(mesh):
    placed = (P(None, "row", "col", None), P(), P(), P(), P(), P(), P())
    return jax.shard_map(
        body, mesh=mesh, in_specs=placed, out_specs=P(None, "row", "col", None), check_vma=False
    )
```

profile of v0, /device:TPU:2, one launch (start us, length us, event | category | flops | bytes accessed | tf_op | source)
XLA Modules:
  0.0 480.4 jit_solution(9939168396102246404)
XLA Ops:
  6.5 2.1 convert_reduce_fusion
  8.6 2.3 fusion.28
  11.0 2.4 fusion.43
  13.4 1.3 copy-done.2
  14.8 1.8 collective-permute-start
  16.6 1.3 collective-permute-start.1
  18.0 0.6 add_minimum_fusion.1
  18.6 0.6 convert_multiply_fusion.1
  20.6 3.3 convolution_convert_fusion.3
  24.0 1.0 pad_maximum_fusion.8
  25.0 5.1 %collective-permute-start.2 = (bf16[2,20,2,1024]{3,2,1,0:T(2,128)(2,1)}, bf16[2,20,2,1024]{3,2,1,0:T(2,128)(2,1)}, u32[]{:S(2)}, u32[]{:S(2)}) collective-permute-start(bf16[2,20,2,1024]{3,2,1,0:T(2,128)(2,1)} %get-tuple-element.19), channel_id=1, source_target_pairs={{0,1},{1,2},{2,3},{3,4},{4,5},{5,6},{6,7},{8,9},{9,10},{10,11},{11... | collective-permute-start | bytes 491528 | tf_op jit(solution)/shard_map/ppermute | solution.py:25
  30.1 3.4 collective-permute-start.3
  33.7 3.8 reshape.611
  37.5 1.8 collective-permute-done.3
  39.3 2.9 pad_maximum_fusion.2
  42.2 0.7 fusion.301
  43.8 0.6 fusion.36
  44.4 0.8 slice.206
  45.3 1.4 maximum_bitcast_fusion
  46.6 6.8 %copy.15 = bf16[2,2,4,12,12,1024]{5,2,4,3,1,0:T(4,128)(2,1)} copy(bf16[2,2,4,12,12,1024]{5,4,2,3,1,0:T(8,128)(2,1)S(1)} %maximum_bitcast_fusion) | data formatting | bytes 9437184 | tf_op jit(solution)/shard_map/transpose | solution.py:54
  53.4 22.5 %reshape.605 = bf16[2,2,4,144,2,16,32]{6,5,4,2,3,1,0:T(8,128)(2,1)} reshape(bf16[2,2,4,12,12,1024]{5,2,4,3,1,0:T(4,128)(2,1)} %copy.15) | data formatting | bytes 9437184 | tf_op jit(solution)/shard_map/reshape | solution.py:54
  75.9 16.4 %fusion.299 = (bf16[2,2,4,144,1,16,32]{6,5,4,2,3,1,0:T(8,128)(2,1)}, bf16[2,2,4,144,1,16,32]{6,5,4,2,3,1,0:T(8,128)(2,1)}) fusion(bf16[2,2,4,144,2,16,32]{6,5,4,2,3,1,0:T(8,128)(2,1)} %reshape.605), kind=kLoop, calls=%fused_computation.368 | loop fusion | bytes 9437184 | tf_op jit(solution)/shard_map/slice | solution.py:58
  92.3 15.1 %copy.64 = bf16[2,2,4,144,1,16,32]{3,6,5,2,1,0,4:T(8,128)(2,1)} copy(bf16[2,2,4,144,1,16,32]{6,5,4,2,3,1,0:T(8,128)(2,1)} %get-tuple-element.9) | data formatting | bytes 4718592
  107.4 14.7 %copy.65 = bf16[2,2,4,144,1,16,32]{3,6,5,2,1,0,4:T(8,128)(2,1)} copy(bf16[2,2,4,144,1,16,32]{6,5,4,2,3,1,0:T(8,128)(2,1)} %get-tuple-element.10) | data formatting | bytes 4718592
  122.1 11.6 %fusion.32 = f32[2,2,4,16,64,144]{5,4,3,2,1,0:T(8,128)} fusion(bf16[2,2,4,144,1,16,32]{3,6,5,2,1,0,4:T(8,128)(2,1)} %copy.65, bf16[2,2,4,64,16,32]{5,4,3,2,1,0:T(8,128)(2,1)} %reshape.611), kind=kOutput, calls=%fused_computation.43 | convolution fusion | flops 150994944 | bytes 12845056 | tf_op jit(solution)/shard_map/sabqhe,sabkhe->sabhqk/dot_general | solution.py:59
  133.7 17.8 %fusion.305 = (f32[2,2,4,16,64]{4,3,2,1,0:T(8,128)S(1)}, f32[2,2,4,16,64,144]{5,4,3,2,1,0:T(8,128)}) fusion(f32[2,2,4,16,64,144]{5,4,3,2,1,0:T(8,128)} %fusion.32, pred[2,4,144]{2,1,0:T(4,128)(4,1)S(1)} %broadcast_and_fusion), kind=kOutput, calls=%fused_computation.374 | output fusion | flops 14155919 | bytes 18941056 | tf_op jit(solution)/shard_map/sub | solution.py:66
  151.5 8.3 %convert_bitcast_fusion = bf16[2,2,4,64,16,32]{3,5,4,2,1,0:T(8,128)(2,1)S(1)} fusion(f32[2,2,4,16,64,144]{5,4,3,2,1,0:T(8,128)} %get-tuple-element.28, f32[2,2,4,16,64]{4,3,2,1,0:T(8,128)S(1)} %get-tuple-element.27, bf16[2,2,4,144,1,16,32]{3,6,5,2,1,0,4:T(8,128)(2,1)} %copy.64), kind=kOutput, calls=%fused_computation.57 | convolution fusion | flops 156237824 | bytes 12910592 | tf_op jit(solution)/shard_map/sabhqk,sabkhe->sabqhe/dot_general | solution.py:68
  159.8 4.2 copy.20
  164.1 6.2 %reshape.612 = bf16[2,2,4,8,8,512]{5,4,3,2,1,0:T(8,128)(2,1)S(1)} reshape(bf16[2,2,4,64,16,32]{5,4,3,2,1,0:T(8,128)(2,1)} %copy.20) | data formatting | bytes 2097152 | tf_op jit(solution)/shard_map/reshape | solution.py:71
  170.4 4.4 constant_dynamic-update-slice_fusion
  174.8 1.3 fusion.75
  176.3 1.3 fusion.126
  178.1 1.3 convolution_bitcast_fusion.1
  179.3 1.5 convolution_bitcast_fusion.2
  180.8 1.3 convolution_bitcast_fusion
  182.1 2.3 fusion.129
  184.4 68.6 %all-reduce.4 = (f32[2,1,1,1024]{3,0,2,1:T(2,128)S(1)}, f32[2,2,2,1024]{3,2,1,0:T(2,128)S(1)}) all-reduce(f32[2,1,1,1024]{3,0,2,1:T(2,128)S(1)} %bitcast.274, f32[2,2,2,1024]{3,2,1,0:T(2,128)S(1)} %convolution_bitcast_fusion.3), channel_id=1, replica_groups=mesh['row'=16,'col'=8] {'row','col'}, use_global_device_ids=true, to_apply=%region_4.5 | all-reduce | flops 10240 | bytes 81920 | tf_op jit(solution)/shard_map/psum | solution.py:161
  253.0 1.7 convolution_maximum_fusion.3
  254.8 1.8 convolution_maximum_fusion.2
  256.7 1.3 fusion.133
  258.2 2.9 fusion.70
  261.1 137.8 %all-reduce.8.cloned.1.call-done = (f32[2,3,3,1024]{3,2,1,0:T(4,128)}, f32[2,6,6,1024]{3,2,1,0:T(8,128)}) async-done(((f32[2,3,3,1024]{3,2,1,0:T(4,128)}, f32[2,6,6,1024]{3,2,1,0:T(8,128)}), (f32[2,3,3,1024]{3,2,1,0:T(4,128)}, f32[2,6,6,1024]{3,2,1,0:T(8,128)})) %all-reduce.8.cloned.1.call-update) | async-done | bytes 368656 | tf_op jit(solution)/shard_map/psum | solution.py:161
  399.0 1.9 convolution_maximum_fusion.1
  400.9 2.2 convolution_maximum_fusion
  404.0 2.9 fusion.72
  406.9 2.9 fusion.68
  409.8 1.3 fusion.300
  411.1 2.4 collective-permute-start.4
  413.6 1.4 collective-permute-start.5
  415.0 5.0 %fusion.50 = f32[2,16,32,256]{3,2,1,0:T(8,128)S(1)} fusion(bf16[2,16,32,3072]{3,2,1,0:T(8,128)(2,1)} %fusion.68, bf16[3,3,3072,256]{3,2,1,0:T(8,128)(2,1)} %param.13), kind=kOutput, calls=%fused_computation.64 | convolution fusion | flops 1610612736 | bytes 8912896 | tf_op jit(solution)/shard_map/dot_general | solution.py:177
  420.1 0.9 pad_maximum_fusion.5
  420.9 4.6 collective-permute-start.6
  425.6 3.9 collective-permute-start.7
  429.5 3.2 fusion.10
  432.7 3.2 fusion.6
  435.9 8.0 %collective-permute-done.6 = bf16[2,18,1,3072]{3,2,1,0:T(2,128)(2,1)S(1)} collective-permute-done((bf16[2,18,1,3072]{3,2,1,0:T(2,128)(2,1)S(1)}, bf16[2,18,1,3072]{3,2,1,0:T(2,128)(2,1)S(1)}, u32[]{:S(2)}, u32[]{:S(2)}) %collective-permute-start.6) | collective-permute-done | bytes 221216 | tf_op jit(solution)/shard_map/ppermute | solution.py:25
  443.9 3.8 collective-permute-done.7
  447.7 5.0 %maximum_maximum_fusion = (bf16[2,18,33,3072]{3,2,1,0:T(8,128)(2,1)S(1)}, bf16[2,18,33,3072]{3,2,1,0:T(8,128)(2,1)S(1)}) fusion(bf16[2,1,32,3072]{3,2,1,0:T(8,128)(2,1)S(1)} %collective-permute-done.5, bf16[2,16,32,3072]{3,2,1,0:T(8,128)(2,1)S(1)} %bitcast.266, bf16[2,1,32,3072]{3,2,1,0:T(8,128)(2,1)S(1)} %collective-permute-done.4, ...), kind=kLoop, calls=%fused_computation.5 | loop fusion | flops 58392576 | bytes 22118400 | tf_op jit(solution)/shard_map/concatenate | solution.py:23
  452.7 3.2 fusion.16
  455.9 3.2 fusion.20
  459.1 3.2 fusion.14
  462.3 3.2 fusion.22
  465.5 3.2 fusion.104
  468.8 4.3 fusion.121
  (86 shorter events, 4.6 us)
Async XLA Ops:
  6.5 4.4 copy-start
  6.5 4.4 copy-start.9
  6.5 392.4 %all-reduce.8.cloned.1.call-start = ((), (), s32[]{:S(2)}) async-start(), calls=%async_computation | async-start | bytes 983040 | tf_op jit(solution)/shard_map/psum | solution.py:161
  6.5 4.4 copy-start.4
  13.4 1.3 copy-start.2
  14.8 9.2 %collective-permute-start = (bf16[2,2,32,1024]{3,2,1,0:T(8,128)(2,1)S(1)}, bf16[2,2,32,1024]{3,2,1,0:T(8,128)(2,1)S(1)}, u32[]{:S(2)}, u32[]{:S(2)}) collective-permute-start(bf16[2,2,32,1024]{3,2,1,0:T(8,128)(2,1)S(1)} %get-tuple-element.21), channel_id=1, source_target_pairs={{0,8},{8,16},{16,24},{24,32},{32,40},{40,48},{48,56},{56,64},{64,7... | collective-permute-start | bytes 786440 | tf_op jit(solution)/shard_map/ppermute | solution.py:25
  16.6 7.4 %collective-permute-start.1 = (bf16[2,2,32,1024]{3,2,1,0:T(8,128)(2,1)S(1)}, bf16[2,2,32,1024]{3,2,1,0:T(8,128)(2,1)S(1)}, u32[]{:S(2)}, u32[]{:S(2)}) collective-permute-start(bf16[2,2,32,1024]{3,2,1,0:T(8,128)(2,1)S(1)} %get-tuple-element.22), channel_id=1, source_target_pairs={{8,0},{16,8},{24,16},{32,24},{40,32},{48,40},{56,48},{64,56},{72,6... | collective-permute-start | bytes 786440 | tf_op jit(solution)/shard_map/ppermute | solution.py:27
  20.6 3.4 copy-start.3
  24.0 9.5 %copy-start.5 = (bf16[2,2,32,1024]{3,2,1,0:T(8,128)(2,1)}, bf16[2,2,32,1024]{3,2,1,0:T(8,128)(2,1)S(1)}, u32[]{:S(2)}) copy-start(bf16[2,2,32,1024]{3,2,1,0:T(8,128)(2,1)S(1)} %collective-permute-done.1) | copy-start | bytes 786436
  25.0 12.4 %collective-permute-start.2 = (bf16[2,20,2,1024]{3,2,1,0:T(2,128)(2,1)}, bf16[2,20,2,1024]{3,2,1,0:T(2,128)(2,1)}, u32[]{:S(2)}, u32[]{:S(2)}) collective-permute-start(bf16[2,20,2,1024]{3,2,1,0:T(2,128)(2,1)} %get-tuple-element.19), channel_id=1, source_target_pairs={{0,1},{1,2},{2,3},{3,4},{4,5},{5,6},{6,7},{8,9},{9,10},{10,11},{11... | collective-permute-start | bytes 491528 | tf_op jit(solution)/shard_map/ppermute | solution.py:25
  30.1 9.2 %collective-permute-start.3 = (bf16[2,20,2,1024]{3,2,1,0:T(2,128)(2,1)}, bf16[2,20,2,1024]{3,2,1,0:T(2,128)(2,1)}, u32[]{:S(2)}, u32[]{:S(2)}) collective-permute-start(bf16[2,20,2,1024]{3,2,1,0:T(2,128)(2,1)} %get-tuple-element.20), channel_id=1, source_target_pairs={{1,0},{2,1},{3,2},{4,3},{5,4},{6,5},{7,6},{9,8},{10,9},{11,10},{12... | collective-permute-start | bytes 491528 | tf_op jit(solution)/shard_map/ppermute | solution.py:27
  164.1 6.3 %copy-start.8 = (bf16[512,1024]{1,0:T(8,128)(2,1)S(1)}, bf16[512,1024]{1,0:T(8,128)(2,1)}, u32[]{:S(2)}) copy-start(bf16[512,1024]{1,0:T(8,128)(2,1)} %param.11) | copy-start | bytes 3145732
  254.8 148.7 %copy-start.6 = (s32[16]{0:T(128)S(1)}, s32[16]{0:T(128)}, u32[]{:S(2)}) copy-start(s32[16]{0:T(128)} %get-tuple-element.49) | copy-start | bytes 196
  254.8 148.7 %copy-start.7 = (f32[16]{0:T(128)S(1)}, f32[16]{0:T(128)}, u32[]{:S(2)}) copy-start(f32[16]{0:T(128)} %get-tuple-element.51) | copy-start | bytes 196
  409.8 10.3 %slice-start = ((s8[6291456]{0:T(1024)(128)(4,1)}), s8[4194304]{0:T(1024)(128)(4,1)S(1)}, s32[]{:S(2)}) async-start(s8[6291456]{0:T(1024)(128)(4,1)} %bitcast.265), calls=%async_computation.1 | async-start | bytes 8388608
  411.1 8.9 %collective-permute-start.4 = (bf16[2,1,32,3072]{3,2,1,0:T(8,128)(2,1)S(1)}, bf16[2,1,32,3072]{3,2,1,0:T(8,128)(2,1)S(1)}, u32[]{:S(2)}, u32[]{:S(2)}) collective-permute-start(bf16[2,1,32,3072]{3,2,1,0:T(8,128)(2,1)S(1)} %get-tuple-element.15), channel_id=1, source_target_pairs={{0,8},{8,16},{16,24},{24,32},{32,40},{40,48},{48,56},{56,64},{64,7... | collective-permute-start | bytes 1179656 | tf_op jit(solution)/shard_map/ppermute | solution.py:25
  413.6 6.5 %slice-start.1 = ((s8[6291456]{0:T(1024)(128)(4,1)}), s8[2097152]{0:T(1024)(128)(4,1)S(1)}, s32[]{:S(2)}) async-start(s8[6291456]{0:T(1024)(128)(4,1)} %bitcast.265), calls=%async_computation.2 | async-start | bytes 4194304
  413.6 6.5 %collective-permute-start.5 = (bf16[2,1,32,3072]{3,2,1,0:T(8,128)(2,1)S(1)}, bf16[2,1,32,3072]{3,2,1,0:T(8,128)(2,1)S(1)}, u32[]{:S(2)}, u32[]{:S(2)}) collective-permute-start(bf16[2,1,32,3072]{3,2,1,0:T(8,128)(2,1)S(1)} %get-tuple-element.16), channel_id=1, source_target_pairs={{8,0},{16,8},{24,16},{32,24},{40,32},{48,40},{56,48},{64,56},{72,6... | collective-permute-start | bytes 1179656 | tf_op jit(solution)/shard_map/ppermute | solution.py:27
  420.9 22.9 %collective-permute-start.6 = (bf16[2,18,1,3072]{3,2,1,0:T(2,128)(2,1)S(1)}, bf16[2,18,1,3072]{3,2,1,0:T(2,128)(2,1)S(1)}, u32[]{:S(2)}, u32[]{:S(2)}) collective-permute-start(bf16[2,18,1,3072]{3,2,1,0:T(2,128)(2,1)S(1)} %get-tuple-element.13), channel_id=1, source_target_pairs={{0,1},{1,2},{2,3},{3,4},{4,5},{5,6},{6,7},{8,9},{9,10},{10,11},{11... | collective-permute-start | bytes 663560 | tf_op jit(solution)/shard_map/ppermute | solution.py:25
  425.6 22.1 %collective-permute-start.7 = (bf16[2,18,1,3072]{3,2,1,0:T(2,128)(2,1)S(1)}, bf16[2,18,1,3072]{3,2,1,0:T(2,128)(2,1)S(1)}, u32[]{:S(2)}, u32[]{:S(2)}) collective-permute-start(bf16[2,18,1,3072]{3,2,1,0:T(2,128)(2,1)S(1)} %get-tuple-element.14), channel_id=1, source_target_pairs={{1,0},{2,1},{3,2},{4,3},{5,4},{6,5},{7,6},{9,8},{10,9},{11,10},{12... | collective-permute-start | bytes 663560 | tf_op jit(solution)/shard_map/ppermute | solution.py:27
  468.8 4.3 copy-start.1
Sparse Core Ops, SparseCore 0:
  256.8 142.1 all-reduce.7
where the time goes:
time: 489 us; the launch traced here: 480 us
  waiting for transfers between devices  151 us (31%)
  local copies, waits for them, and re-layouts  95.7 us (20%)
  matrix products  89 us (18%)
  blocking collectives  68.6 us (14%)
  other arithmetic  37.2 us (8%)
  starting transfers between devices  23.9 us (5%)
  between operations  14.5 us (3%)
    psum x1, waiting for transfers between devices, body(): lax.psum((partials[0], partials[1], partials[2], partials[3]), ('row', 'c...  138 us
    psum x1, blocking collectives, body(): lax.psum((partials[0], partials[1], partials[2], partials[3]), ('row', 'c...  68.6 us
    dot_general x9, matrix products, body(): jnp.dot(stacked[:, shift_row:shift_row + rows_here, shift_col:shift_col +...  31.8 us
    unnamed x26, local copies, waits for them, and re-layouts  31.2 us
    reshape x1, local copies, waits for them, and re-layouts, attend(): windows.transpose(0, 1, 3, 2, 4, 5)  22.5 us
    sub x1, other arithmetic, attend(): expon = jnp.exp(scores - top)  17.8 us
    slice x1, local copies, waits for them, and re-layouts, attend(): values = window_kv[:, :, :, :, 1]  16.4 us
    ppermute x4, starting transfers between devices, padded(): lax.ppermute(tail, axis, [(i, (i + 1) % count) for i in range(ends)])  13.9 us
  transfers between devices with their start and end apart: 9, of which 4 were waited for; matrix products, arithmetic and copies ran while one was open for 5% of the time, Pallas kernels for 0%

commit v1 on v0

v1 whole, which is shorter than its diff:
```python
import math

import jax
import jax.numpy as jnp
import numpy as np
from jax import lax
from jax.experimental import pallas as pl
from jax.experimental.pallas import tpu as pltpu
from jax.sharding import PartitionSpec as P

HEAD_DIM = 32
BLOCK = 8
HALO = 2
EPS = 1e-05
LEVELS = (1, 2, 3, 6)
CODED = (6, 3, 2)
UNITS = 8
STRIP_UNITS = 24
STRIP_AT = {6: 0, 3: 12, 2: 18}
SLOTS = {1: 8, 2: 8, 3: 16, 6: 40}
TAPS = 9
f32 = jnp.float32
bf16 = jnp.bfloat16


def bins_of(level, length, first, count):
    places = first + np.arange(count)
    found = []
    for cell in range(level):
        start = cell * length // level
        end = ((cell + 1) * length + level - 1) // level
        mask = (places >= start) & (places < end)
        if mask.any():
            found.append((cell, mask))
    return found


def pool_tables(rows, row_strips, cols, col_strips):
    grid_h, grid_w = rows * row_strips, cols * col_strips
    row_masks = np.zeros((row_strips, col_strips, UNITS, rows), np.float32)
    col_masks = np.zeros((row_strips, col_strips, UNITS, cols), np.float32)
    strip = np.zeros((col_strips, 2 * STRIP_UNITS, row_strips, 2 * UNITS), np.float32)
    slots = 2 * sum(SLOTS.values())
    bins = np.zeros((slots, col_strips, 2 * STRIP_UNITS), np.float32)
    scale = np.zeros((slots, 1), np.float32)
    for c in range(col_strips):
        for r in range(row_strips):
            units = []
            for level in CODED:
                for i, row_mask in bins_of(level, grid_h, r * rows, rows):
                    for g, (j, col_mask) in enumerate(bins_of(level, grid_w, c * cols, cols)):
                        key = (row_mask.tobytes(), col_mask.tobytes())
                        if key not in units:
                            units.append(key)
                            at = len(units) - 1
                            row_masks[r, c, at] = row_mask
                            col_masks[r, c, at] = col_mask
                        at = units.index(key)
                        width = 1 if level == 2 else 2
                        for s in range(2):
                            target = s * STRIP_UNITS + STRIP_AT[level] + i * width + g
                            strip[c, target, r, s * UNITS + at] = 1.0
            assert len(units) <= UNITS
        base = 0
        for level in LEVELS:
            source = 2 if level == 1 else level
            for g, (j, _) in enumerate(bins_of(source, grid_w, c * cols, cols)):
                for i in range(source):
                    for s in range(2):
                        cell = 0 if level == 1 else i * level + j
                        row = base + s * SLOTS[level] + cell
                        width = 1 if source == 2 else 2
                        bins[row, c, s * STRIP_UNITS + STRIP_AT[source] + i * width + g] = 1.0
            base += 2 * SLOTS[level]
    base = 0
    for level in LEVELS:
        row_all = bins_of(level, grid_h, 0, grid_h)
        col_all = bins_of(level, grid_w, 0, grid_w)
        for s in range(2):
            for i, row_mask in row_all:
                for j, col_mask in col_all:
                    row = base + s * SLOTS[level] + i * level + j
                    scale[row, 0] = 1.0 / (row_mask.sum() * col_mask.sum())
        base += 2 * SLOTS[level]
    return row_masks, col_masks, strip.reshape(col_strips, 2 * STRIP_UNITS, -1), bins.reshape(slots, -1), scale


def upsample_weights(level, length, first, count):
    places = first + np.arange(count)
    numer = np.maximum((2 * places + 1) * level - length, 0)
    lower = numer // (2 * length)
    frac = (numer - lower * 2 * length).astype(np.float32) / np.float32(2.0 * length)
    upper = np.minimum(lower + 1, level - 1)
    cells = np.arange(level)[None, :]
    weight = (cells == lower[:, None]) * (1.0 - frac)[:, None] + (cells == upper[:, None]) * frac[:, None]
    inside = (places >= 0) & (places < length)
    return (weight * inside[:, None]).astype(np.float32)


def upsample_tables(rows, row_strips, cols, col_strips):
    grid_h, grid_w = rows * row_strips, cols * col_strips
    width = TAPS * sum(SLOTS.values())
    by_row = np.zeros((row_strips, rows, width), np.float32)
    by_col = np.zeros((col_strips, cols, width), np.float32)
    base = 0
    for level in LEVELS:
        for a in range(3):
            for c in range(3):
                at = base + (a * 3 + c) * SLOTS[level]
                for strip in range(row_strips):
                    w = upsample_weights(level, grid_h, strip * rows + a - 1, rows)
                    by_row[strip, :, at : at + level * level] = np.repeat(w, level, axis=1)
                for strip in range(col_strips):
                    w = upsample_weights(level, grid_w, strip * cols + c - 1, cols)
                    by_col[strip, :, at : at + level * level] = np.tile(w, (1, level))
        base += TAPS * SLOTS[level]
    return by_row, by_col


def layer_norm(tokens, gain):
    x = tokens.astype(f32)
    center = jnp.mean(x, axis=-1, keepdims=True)
    x = x - center
    spread = jnp.mean(x * x, axis=-1, keepdims=True)
    return (x * lax.rsqrt(spread + EPS) * gain).astype(bf16)


def dot(a, b):
    return jnp.dot(a, b, preferred_element_type=f32)


def project_kernel(tokens_ref, gain_ref, wq_ref, wkv_ref, q_ref, kv_ref):
    normed = layer_norm(tokens_ref[...], gain_ref[...])
    q_ref[...] = dot(normed, wq_ref[...]).astype(bf16)
    kv_ref[...] = dot(normed, wkv_ref[...]).astype(bf16)


def attend_kernel(
    q_ref, kv_ref, rows_ref, sides_ref, tokens_ref, gain_ref, wkv_ref, wout_ref, bias_ref, pool_ref,
    attended_ref, sums_ref, ext, queries, context,
):
    rows, cols = queries.shape[0], queries.shape[1]
    inner = queries.shape[2]
    wide = 2 * inner
    groups = cols // BLOCK
    span = BLOCK + 2 * HALO
    gain = gain_ref[...]
    wkv = wkv_ref[...]
    halo = dot(layer_norm(rows_ref[...], gain), wkv).astype(bf16).astype(f32)
    halo = halo.reshape(2 * HALO, cols, wide)
    ext[0:HALO, BLOCK : BLOCK + cols, :] = halo[0:HALO]
    ext[rows + HALO :, BLOCK : BLOCK + cols, :] = halo[HALO:]
    sides = dot(layer_norm(sides_ref[...], gain), wkv).astype(bf16).astype(f32)
    sides = sides.reshape(rows + 2 * HALO, BLOCK, wide)
    ext[:, 0:BLOCK, :] = sides
    ext[:, BLOCK + cols :, :] = sides
    ext[HALO : rows + HALO, BLOCK : BLOCK + cols, :] = kv_ref[...].astype(f32).reshape(rows, cols, wide)
    queries[...] = q_ref[...].astype(f32).reshape(rows, cols, inner)

    half = inner // 2
    heads = half // HEAD_DIM
    count = BLOCK * BLOCK
    head_of_row = lax.broadcasted_iota(jnp.int32, (heads, count, half), 0)
    head_of_lane = lax.broadcasted_iota(jnp.int32, (heads, count, half), 2) // HEAD_DIM
    own = (head_of_row == head_of_lane).astype(f32).astype(bf16).reshape(heads * count, half)
    lane = lax.broadcasted_iota(jnp.int32, (count, 128), 1)
    place = lax.broadcasted_iota(jnp.int32, (span // 2, BLOCK, wide), 1)
    factor = math.log2(math.e) / math.sqrt(HEAD_DIM)

    def column(b, carry):
        left = pl.multiple_of(b * BLOCK, BLOCK)
        mid = pl.multiple_of(b * BLOCK + BLOCK, BLOCK)
        right = pl.multiple_of(b * BLOCK + 2 * BLOCK, BLOCK)
        for a in range(rows // BLOCK):
            at = a * BLOCK
            main = ext[at : at + span, pl.ds(mid, BLOCK), :].reshape(span * BLOCK, wide)
            west = ext[at : at + span, pl.ds(left, BLOCK), :].reshape(span // 2, 2, BLOCK, wide)
            east = ext[at : at + span, pl.ds(right, BLOCK), :].reshape(span // 2, 2, BLOCK, wide)
            even = jnp.where(place >= 6, west[:, 0], east[:, 0])
            odd = jnp.where(place >= 6, west[:, 1], east[:, 1])
            odd = pltpu.roll(odd, 4, 1)
            extra = jnp.where((place >= 6) | (place < 2), even, odd).reshape(span * 4, wide)
            window = jnp.concatenate([main, extra], axis=0).astype(bf16)
            block = queries[at : at + BLOCK, pl.ds(left, BLOCK), :].reshape(count, inner).astype(bf16)
            bias = bias_ref[a, b]
            pieces = []
            for h in range(2):
                q = block[:, h * half : (h + 1) * half]
                q = jnp.concatenate([q] * heads, axis=0) * own
                keys = window[:, h * half : (h + 1) * half]
                values = window[:, inner + h * half : inner + (h + 1) * half]
                scores = lax.dot_general(keys, q, (((1,), (1,)), ((), ())), preferred_element_type=f32)
                scores = scores + jnp.concatenate([bias] * (heads * count // 128), axis=1)
                top = jnp.max(scores, axis=0, keepdims=True)
                expon = jnp.exp2((scores - top) * factor)
                weights = (expon * (1.0 / jnp.sum(expon, axis=0, keepdims=True))).astype(bf16)
                mixed = lax.dot_general(weights, values, (((0,), (0,)), ((), ())), preferred_element_type=f32)
                mixed = mixed.reshape(heads, count, half)
                for t in range(half // 128):
                    lanes = slice(t * 128, (t + 1) * 128)
                    per = 128 // HEAD_DIM
                    piece = mixed[t * per, :, lanes]
                    for k in range(1, per):
                        piece = jnp.where(lane >= k * HEAD_DIM, mixed[t * per + k, :, lanes], piece)
                    pieces.append(piece)
            done = jnp.concatenate(pieces, axis=1).reshape(BLOCK, BLOCK, inner)
            context[at : at + BLOCK, pl.ds(left, BLOCK), :] = done
        return carry

    lax.fori_loop(0, groups, column, 0)
    mixed = context[...].reshape(rows * cols, inner).astype(bf16)
    attended = (tokens_ref[...].astype(f32) + dot(mixed, wout_ref[...])).astype(bf16)
    attended_ref[...] = attended
    sums_ref[...] = dot(pool_ref[...], attended).astype(bf16)


def combine_kernel(table_ref, parts_ref, out_ref):
    out_ref[...] = dot(table_ref[...], parts_ref[...]).astype(bf16)


def conv_kernel(attended_ref, top_ref, bottom_ref, left_ref, right_ref, w_ref, out_ref, ext):
    cols = top_ref.shape[0]
    rows = attended_ref.shape[0] // cols
    ext[0:cols] = top_ref[...]
    ext[cols : cols + rows * cols] = attended_ref[...]
    ext[cols + rows * cols :] = bottom_ref[...]

    def edge(ref, c):
        total = 0.0
        for a in range(3):
            total = total + dot(ref[...], w_ref[a, c])[a : a + rows]
        return total.reshape(rows, 1, total.shape[-1])

    def middle(c):
        total = dot(ext[0 : rows * cols], w_ref[0, c])
        for a in range(1, 3):
            total = total + dot(ext[a * cols : a * cols + rows * cols], w_ref[a, c])
        return total.reshape(rows, cols, total.shape[-1])

    place = lax.broadcasted_iota(jnp.int32, (rows, cols, w_ref.shape[-1]), 1)
    total = middle(1)
    total = total + jnp.where(place == 0, edge(left_ref, 0), pltpu.roll(middle(0), 1, 1))
    total = total + jnp.where(place == cols - 1, edge(right_ref, 2), pltpu.roll(middle(2), cols - 1, 1))
    out_ref[...] = total.reshape(rows * cols, -1)


def split(x):
    high = x.astype(bf16)
    return high, (x - high.astype(f32)).astype(bf16)


def tail_kernel(
    table_ref, scale_ref, parts_ref, wpool_ref, w1_ref, w2_ref, w3_ref, w6_ref, by_row_ref, by_col_ref, conv_ref,
    out_ref, taps,
):
    pooled = dot(table_ref[...], parts_ref[...]) * scale_ref[...]
    row = 0
    at = 0
    for index, (level, w_ref) in enumerate(zip(LEVELS, (w1_ref, w2_ref, w3_ref, w6_ref))):
        slots = SLOTS[level]
        high, low = split(pooled[row : row + 2 * slots])
        both = dot(jnp.concatenate([high, low], axis=0), wpool_ref[index])
        branch = jnp.maximum(both[: 2 * slots] + both[2 * slots :], 0.0)
        high, low = split(branch)
        both = jnp.concatenate([high, low], axis=0)
        for a in range(3):
            for c in range(3):
                tap = dot(both, w_ref[a, c])
                tap = tap[: 2 * slots] + tap[2 * slots :]
                start = at + (a * 3 + c) * slots
                for s in range(2):
                    taps[s, start : start + slots, :] = tap[s * slots : (s + 1) * slots]
        row += 2 * slots
        at += TAPS * slots
    rows, cols = by_row_ref.shape[0], by_col_ref.shape[0]
    grid = by_row_ref[...][:, None, :] * by_col_ref[...][None, :, :]
    grid_high, grid_low = split(grid.reshape(rows * cols, -1))
    for s in range(2):
        high, low = split(taps[s])
        total = conv_ref[s] + dot(grid_high, high) + dot(grid_low, high) + dot(grid_high, low)
        out_ref[s] = total.astype(bf16)


def cost(flops, nbytes, transcendentals=0):
    return pl.CostEstimate(flops=int(flops), bytes_accessed=int(nbytes), transcendentals=int(transcendentals))


def params(mib):
    return pltpu.CompilerParams(vmem_limit_bytes=mib * 2**20)


def whole(shape):
    return pl.BlockSpec(shape, lambda *_: (0,) * len(shape))


def shifts(axis):
    count = lax.axis_size(axis)
    forward = [(i, i + 1) for i in range(count - 1)]
    return forward, [(j, i) for i, j in forward]


def body(tokens, norm_gain, w_query, w_kv, w_out, w_pool, w_join):
    sheets, rows, cols, width = tokens.shape
    inner = w_query.shape[1]
    wide = w_kv.shape[1]
    out_ch = w_join.shape[-1]
    ppm = w_pool.shape[-1]
    area = rows * cols
    row_count, col_count = lax.axis_size("row"), lax.axis_size("col")
    r, c = lax.axis_index("row"), lax.axis_index("col")
    grid_h, grid_w = rows * row_count, cols * col_count
    gain = norm_gain.reshape(1, width)
    row_masks, col_masks, strip_table, bin_table, bin_scale = pool_tables(rows, row_count, cols, col_count)
    by_row, by_col = upsample_tables(rows, row_count, cols, col_count)

    def pick(table, index):
        return lax.dynamic_index_in_dim(jnp.asarray(table), index, 0, keepdims=False)

    row_fwd, row_bwd = shifts("row")
    col_fwd, col_bwd = shifts("col")
    above = lax.ppermute(tokens[:, rows - HALO :], "row", row_fwd)
    below = lax.ppermute(tokens[:, :HALO], "row", row_bwd)
    flat = tokens.reshape(sheets, area, width)
    q, kv = pl.pallas_call(
        project_kernel,
        grid=(sheets,),
        in_specs=[
            pl.BlockSpec((None, area, width), lambda s: (s, 0, 0)),
            whole((1, width)), whole((width, inner)), whole((width, wide)),
        ],
        out_specs=[
            pl.BlockSpec((None, area, inner), lambda s: (s, 0, 0)),
            pl.BlockSpec((None, area, wide), lambda s: (s, 0, 0)),
        ],
        out_shape=[
            jax.ShapeDtypeStruct((sheets, area, inner), bf16),
            jax.ShapeDtypeStruct((sheets, area, wide), bf16),
        ],
        compiler_params=params(40),
        cost_estimate=cost(2 * sheets * area * width * (inner + wide), 2 * (width * (inner + wide) + 3 * sheets * area * width)),
        name="project",
    )(flat, gain, w_query, w_kv)

    def edges(first):
        return jnp.concatenate([x[:, :, first : first + HALO] for x in (above, tokens, below)], axis=1)

    west = lax.ppermute(edges(cols - HALO), "col", col_fwd)
    east = lax.ppermute(edges(0), "col", col_bwd)
    blank = jnp.zeros((sheets, rows + 2 * HALO, BLOCK - 2 * HALO, width), bf16)
    sides = jnp.concatenate([east, blank, west], axis=2).reshape(sheets, (rows + 2 * HALO) * BLOCK, width)
    row_halo = jnp.concatenate([above, below], axis=1).reshape(sheets, 2 * HALO * cols, width)

    span = BLOCK + 2 * HALO
    k = np.arange(span * span)
    e = k - span * BLOCK
    lane8 = e % 8
    odd = (lane8 >= 2) & (lane8 < 6)
    is_west = (lane8 >= 6) | ((lane8 >= 2) & (lane8 < 4))
    key_row = np.where(e < 0, k // BLOCK, 2 * (e // 8) + odd) - HALO
    key_col = np.where(e < 0, k % BLOCK, np.where(is_west, lane8 % 2 - HALO, BLOCK + lane8 % 2))
    row_at = r * rows + jnp.arange(0, rows, BLOCK)[:, None] + jnp.asarray(key_row)[None, :]
    col_at = c * cols + jnp.arange(0, cols, BLOCK)[:, None] + jnp.asarray(key_col)[None, :]
    row_ok = (row_at >= 0) & (row_at < grid_h)
    col_ok = (col_at >= 0) & (col_at < grid_w)
    ok = row_ok[:, None, :, None] & col_ok[None, :, :, None]
    bias = jnp.broadcast_to(jnp.where(ok, 0.0, -1e30).astype(f32), ok.shape[:3] + (128,))
    row_mask = pick(row_masks.reshape(-1, UNITS, rows), r * col_count + c)
    col_mask = pick(col_masks.reshape(-1, UNITS, cols), r * col_count + c)
    pool = (row_mask[:, :, None] * col_mask[:, None, :]).reshape(UNITS, area).astype(bf16)

    blocks = (rows // BLOCK) * (cols // BLOCK)
    attended, sums = pl.pallas_call(
        attend_kernel,
        grid=(sheets,),
        in_specs=[
            pl.BlockSpec((None, area, inner), lambda s: (s, 0, 0)),
            pl.BlockSpec((None, area, wide), lambda s: (s, 0, 0)),
            pl.BlockSpec((None, 2 * HALO * cols, width), lambda s: (s, 0, 0)),
            pl.BlockSpec((None, (rows + 2 * HALO) * BLOCK, width), lambda s: (s, 0, 0)),
            pl.BlockSpec((None, area, width), lambda s: (s, 0, 0)),
            whole((1, width)), whole((width, wide)), whole((inner, width)),
            whole(bias.shape), whole((UNITS, area)),
        ],
        out_specs=[
            pl.BlockSpec((None, area, width), lambda s: (s, 0, 0)),
            pl.BlockSpec((None, UNITS, width), lambda s: (s, 0, 0)),
        ],
        out_shape=[
            jax.ShapeDtypeStruct((sheets, area, width), bf16),
            jax.ShapeDtypeStruct((sheets, UNITS, width), bf16),
        ],
        scratch_shapes=[
            pltpu.VMEM((rows + 2 * HALO, cols + 2 * BLOCK, wide), f32),
            pltpu.VMEM((rows, cols, inner), f32),
            pltpu.VMEM((rows, cols, inner), f32),
        ],
        compiler_params=params(48),
        cost_estimate=cost(2 * sheets * area * inner * width * 4, 2 * sheets * area * width * 4, sheets * blocks * 144 * 1024),
        name="attend",
    )(q, kv, row_halo, sides, flat, gain, w_kv, w_out, bias, pool)

    att = attended.reshape(sheets, rows, cols, width)
    att_above = lax.ppermute(att[:, rows - 1 :], "row", row_fwd)
    att_below = lax.ppermute(att[:, :1], "row", row_bwd)

    parts = jnp.broadcast_to(sums.reshape(1, sheets * UNITS, width), (row_count, sheets * UNITS, width))
    parts = lax.all_to_all(parts, "row", 0, 0, tiled=True).reshape(row_count * sheets * UNITS, width)
    strip_rows = sheets * STRIP_UNITS
    strips = pl.pallas_call(
        combine_kernel,
        out_shape=jax.ShapeDtypeStruct((strip_rows, width), bf16),
        compiler_params=params(8),
        name="combine",
    )(pick(strip_table, c).astype(bf16), parts)

    def att_edges(first):
        return jnp.concatenate([x[:, :, first] for x in (att_above, att, att_below)], axis=1)

    att_west = lax.ppermute(att_edges(cols - 1), "col", col_fwd)
    att_east = lax.ppermute(att_edges(0), "col", col_bwd)
    pad = ((0, 0), (0, 6), (0, 0))
    att_west, att_east = jnp.pad(att_west, pad), jnp.pad(att_east, pad)

    strips = jnp.broadcast_to(strips[None], (col_count, strip_rows, width))
    strips = lax.all_to_all(strips, "col", 0, 0, tiled=True).reshape(col_count * strip_rows, width)

    def per_sheet(*dims):
        return pl.BlockSpec((None,) + dims, lambda s: (s,) + (0,) * len(dims))

    conv = pl.pallas_call(
        conv_kernel,
        grid=(sheets,),
        in_specs=[
            per_sheet(area, width), per_sheet(cols, width), per_sheet(cols, width),
            per_sheet(rows + 8, width), per_sheet(rows + 8, width),
            pl.BlockSpec((3, 3, width, out_ch), lambda s: (0, 0, 0, 0)),
        ],
        out_specs=per_sheet(area, out_ch),
        out_shape=jax.ShapeDtypeStruct((sheets, area, out_ch), f32),
        scratch_shapes=[pltpu.VMEM((area + 2 * cols, width), bf16)],
        compiler_params=params(32),
        cost_estimate=cost(2 * sheets * area * width * 9 * out_ch, 2 * 9 * width * out_ch + 2 * sheets * area * width),
        name="conv",
    )(attended, att_above.reshape(sheets, cols, width), att_below.reshape(sheets, cols, width), att_west, att_east, w_join)

    first = width // ppm

    def level_spec(index):
        return pl.BlockSpec((3, 3, ppm, out_ch), lambda *_: (0, 0, first + index, 0), pipeline_mode=pl.Buffered(1))

    depth = TAPS * sum(SLOTS.values())
    bin_rows = 2 * sum(SLOTS.values())
    out = pl.pallas_call(
        tail_kernel,
        grid=(1,),
        in_specs=[
            whole((bin_rows, col_count * strip_rows)), whole((bin_rows, 1)), whole((col_count * strip_rows, width)),
            whole(w_pool.shape), level_spec(0), level_spec(1), level_spec(2), level_spec(3),
            whole((rows, depth)), whole((cols, depth)), whole((sheets, area, out_ch)),
        ],
        out_specs=whole((sheets, area, out_ch)),
        out_shape=jax.ShapeDtypeStruct((sheets, area, out_ch), bf16),
        scratch_shapes=[pltpu.VMEM((sheets, depth, out_ch), f32)],
        compiler_params=params(56),
        name="tail",
    )(
        jnp.asarray(bin_table).astype(bf16), jnp.asarray(bin_scale), strips,
        w_pool, w_join, w_join, w_join, w_join, pick(by_row, r), pick(by_col, c), conv,
    )
    return out.reshape(sheets, rows, cols, out_ch)


def solution(mesh):
    placed = (P(None, "row", "col", None), P(), P(), P(), P(), P(), P())
    return jax.shard_map(
        body, mesh=mesh, in_specs=placed, out_specs=P(None, "row", "col", None), check_vma=False
    )
```

time: 489 us -> 127 us (0.26); the launches traced: 480 us -> 126 us
  waiting for transfers between devices: 151 us -> 23.2 us
  matrix products: 89 us -> 0 us
  local copies, waits for them, and re-layouts: 95.7 us -> 24.5 us
  blocking collectives: 68.6 us -> 0 us
  Pallas kernels: 0 us -> 38.7 us
  other arithmetic: 37.2 us -> 2.28 us
  between operations: 14.5 us -> 0.4 us
  starting transfers between devices: 23.9 us -> 36.8 us
    psum x1 -> x0, waiting for transfers between devices: 138 us -> none  [body(): lax.psum((partials[0], partials[1], partials[2], partials[3]), ('row', 'c...]
    dot_general x32 -> x0, matrix products: 89 us -> none  [the longest x9 31.8 us: body(): jnp.dot(stacked[:, shift_row:shift_row + rows_here, shift_col:shift_col +...]
    psum x1 -> x0, blocking collectives: 68.6 us -> none  [body(): lax.psum((partials[0], partials[1], partials[2], partials[3]), ('row', 'c...]
    pallas_call x0 -> x5, Pallas kernels: none -> 38.7 us  [the longest x1 16.8 us: body(): pl.pallas_call(attend_kernel, grid=(sheets,), in_specs=[pl.BlockSpec((Non...]
    reshape x9 -> x0, local copies, waits for them, and re-layouts: 33.5 us -> none  [the longest x1 22.5 us: attend(): windows.transpose(0, 1, 3, 2, 4, 5)]
    sub x8 -> x0, other arithmetic: 17.9 us -> none  [the longest x1 17.8 us: attend(): expon = jnp.exp(scores - top)]
    unnamed x26 -> x27, local copies, waits for them, and re-layouts: 31.2 us -> 13.8 us
    slice x8 -> x9, local copies, waits for them, and re-layouts: 19.6 us -> 2.81 us  [the longest x7 1.53 us: edges(): x[:, :, first:first + HALO]]
  transfers between devices with their start and end apart: 9 -> 10, of which waited for: 4 -> 5; matrix products, arithmetic and copies ran while one was open for 5% -> 8% of each run, Pallas kernels for 0% -> 9%
where the time goes in v1:
time: 127 us; the launch traced here: 126 us
  Pallas kernels  38.7 us (30%)
  starting transfers between devices  36.8 us (29%)
  local copies, waits for them, and re-layouts  24.5 us (19%)
  waiting for transfers between devices  23.2 us (18%)
  other arithmetic  2.28 us (2%)
    pallas_call x1, Pallas kernels, body(): pl.pallas_call(attend_kernel, grid=(sheets,), in_specs=[pl.BlockSpec((Non...  16.8 us
    unnamed x27, local copies, waits for them, and re-layouts  13.8 us
    pallas_call x1, Pallas kernels, body(): pl.pallas_call(tail_kernel, grid=(1,), in_specs=[whole((bin_rows, col_cou...  10.5 us
    all_to_all x1, waiting for transfers between devices, body(): lax.all_to_all(parts, 'row', 0, 0, tiled=True)  7.34 us
    all_to_all x1, starting transfers between devices, body(): lax.all_to_all(parts, 'row', 0, 0, tiled=True)  7.29 us
    ppermute x1, waiting for transfers between devices, body(): att_east = lax.ppermute(att_edges(0), 'col', col_bwd)  7.03 us
    all_to_all x1, starting transfers between devices, body(): lax.all_to_all(strips, 'col', 0, 0, tiled=True)  6.98 us
    pallas_call x1, Pallas kernels, body(): pl.pallas_call(conv_kernel, grid=(sheets,), in_specs=[per_sheet(area, wid...  6.63 us
  transfers between devices with their start and end apart: 10, of which 5 were waited for; matrix products, arithmetic and copies ran while one was open for 8% of the time, Pallas kernels for 9%

profile of v1, /device:TPU:2, one launch (start us, length us, event | category | flops | bytes accessed | tf_op | source)
XLA Modules:
  0.0 125.9 jit_solution(9647896084438113454)
XLA Ops:
  0.0 1.1 fusion.4
  1.1 1.8 %collective-permute-start = (bf16[2,2,32,1024]{3,2,1,0:T(8,128)(2,1)S(1)}, bf16[2,2,32,1024]{3,2,1,0:T(8,128)(2,1)S(1)}, u32[]{:S(2)}, u32[]{:S(2)}) collective-permute-start(bf16[2,2,32,1024]{3,2,1,0:T(8,128)(2,1)S(1)} %get-tuple-element.19), channel_id=1, source_target_pairs={{0,8},{8,16},{16,24},{24,32},{32,40},{40,48},{48,56},{56,64},{64,7... | collective-permute-start | bytes 786440 | tf_op jit(solution)/shard_map/ppermute | solution.py:321
  2.8 1.3 %collective-permute-start.1 = (bf16[2,2,32,1024]{3,2,1,0:T(8,128)(2,1)S(1)}, bf16[2,2,32,1024]{3,2,1,0:T(8,128)(2,1)S(1)}, u32[]{:S(2)}, u32[]{:S(2)}) collective-permute-start(bf16[2,2,32,1024]{3,2,1,0:T(8,128)(2,1)S(1)} %get-tuple-element.20), channel_id=1, source_target_pairs={{8,0},{16,8},{24,16},{32,24},{40,32},{48,40},{56,48},{64,56},{72,6... | collective-permute-start | bytes 786440 | tf_op jit(solution)/shard_map/ppermute | solution.py:322
  4.1 1.4 %fusion.3 = (bf16[2,16,2,1024]{3,2,1,0:T(2,128)(2,1)S(1)}, bf16[2,16,2,1024]{3,2,1,0:T(2,128)(2,1)S(1)}) fusion(bf16[2,16,32,1024]{3,2,1,0:T(8,128)(2,1)} %param.16), kind=kLoop, calls=%fused_computation.29 | loop fusion | bytes 524288 | tf_op jit(solution)/shard_map/slice | solution.py:345
  5.6 0.7 dynamic-slice_bitcast_fusion.2
  6.3 0.7 dynamic-slice_bitcast_fusion.3
  7.0 0.1 multiply_convert_fusion
  7.1 0.8 compare_and_fusion
  7.8 0.8 fusion.1
  8.6 0.0 copy-start.2
  8.6 1.6 %copy-done.2 = bf16[2,16,32,1024]{3,2,1,0:T(8,128)(2,1)S(1)} copy-done((bf16[2,16,32,1024]{3,2,1,0:T(8,128)(2,1)S(1)}, bf16[2,16,32,1024]{3,2,1,0:T(8,128)(2,1)}, u32[]{:S(2)}) %copy-start.2) | copy-done | bytes 2097176
  10.2 0.0 copy-start.3
  10.2 1.6 %copy-done.3 = bf16[1024,1024]{1,0:T(8,128)(2,1)S(1)} copy-done((bf16[1024,1024]{1,0:T(8,128)(2,1)S(1)}, bf16[1024,1024]{1,0:T(8,128)(2,1)}, u32[]{:S(2)}) %copy-start.3) | copy-done | bytes 2097176
  11.7 1.2 copy-done.4
  13.0 0.7 copy-done.6
  13.7 4.5 %project.1 = (bf16[2,512,512]{2,1,0:T(8,128)(2,1)S(1)}, bf16[2,512,1024]{2,1,0:T(8,128)(2,1)S(1)}) custom-call(bf16[2,512,1024]{2,1,0:T(8,128)(2,1)S(1)} %bitcast.43, f32[1,1024]{1,0:T(1,128)S(1)} %bitcast.49, bf16[1024,512]{1,0:T(8,128)(2,1)S(1)} %copy-done.4, bf16[1024,1024]{1,0:T(8,128)(2,1)S(1)} %copy-done.3), custom_call_target="tpu_custom_call" | custom-call | flops 3221225472 | bytes 9437184 | tf_op jit(solution)/shard_map/project/pallas_call | solution.py:324
  18.2 0.0 copy-start.8
  18.2 1.4 %copy-done.8 = bf16[2,512,1024]{2,1,0:T(8,128)(2,1)} copy-done((bf16[2,512,1024]{2,1,0:T(8,128)(2,1)}, bf16[2,512,1024]{2,1,0:T(8,128)(2,1)S(1)}, u32[]{:S(2)}) %copy-start.8) | copy-done | bytes 2097176
  19.6 1.7 %dynamic-slice_bitcast_fusion.by_col_ref = f32[32,648]{1,0:T(8,128)} fusion(f32[8,32,648]{2,1,0:T(8,128)} %constant.78.clone, s32[]{:T(128)S(6)} %select_n.25), kind=kLoop, calls=%fused_computation.8 | loop fusion | bytes 165892 | tf_op jit(solution)/shard_map/jit(dynamic_index_in_dim)/squeeze | solution.py:317
  21.3 0.0 collective-permute-done
  21.3 0.0 collective-permute-done.1
  21.4 0.0 copy-start.7
  21.4 0.1 pad_maximum_fusion.1
  21.5 5.0 %collective-permute-start.2 = (bf16[2,20,2,1024]{3,1,2,0:T(8,128)(2,1)S(1)}, bf16[2,20,2,1024]{3,1,2,0:T(8,128)(2,1)S(1)}, u32[]{:S(2)}, u32[]{:S(2)}) collective-permute-start(bf16[2,20,2,1024]{3,1,2,0:T(8,128)(2,1)S(1)} %pad_maximum_fusion.1), channel_id=1, source_target_pairs={{1,0},{2,1},{3,2},{4,3},{5,4},{6,5},{7,6},{9,8},{10,9},{11,10},{12... | collective-permute-start | bytes 491528 | tf_op jit(solution)/shard_map/ppermute | solution.py:348
  26.6 0.1 pad_maximum_fusion.2
  26.7 0.0 copy-done.9
  26.7 2.3 %collective-permute-start.3 = (bf16[2,20,2,1024]{3,1,2,0:T(8,128)(2,1)S(1)}, bf16[2,20,2,1024]{3,1,2,0:T(8,128)(2,1)S(1)}, u32[]{:S(2)}, u32[]{:S(2)}) collective-permute-start(bf16[2,20,2,1024]{3,1,2,0:T(8,128)(2,1)S(1)} %pad_maximum_fusion.2), channel_id=1, source_target_pairs={{0,1},{1,2},{2,3},{3,4},{4,5},{5,6},{6,7},{8,9},{9,10},{10,11},{11... | collective-permute-start | bytes 491528 | tf_op jit(solution)/shard_map/ppermute | solution.py:347
  29.0 0.7 fusion.table_ref
  29.8 0.1 convert_element_type.20.pool_ref
  29.9 0.1 pad.16.clone
  30.0 0.9 collective-permute-done.2
  30.9 0.2 copy.66
  31.0 6.2 %collective-permute-done.3 = bf16[2,20,2,1024]{3,1,2,0:T(8,128)(2,1)S(1)} collective-permute-done((bf16[2,20,2,1024]{3,1,2,0:T(8,128)(2,1)S(1)}, bf16[2,20,2,1024]{3,1,2,0:T(8,128)(2,1)S(1)}, u32[]{:S(2)}, u32[]{:S(2)}) %collective-permute-start.3) | collective-permute-done | bytes 163872 | tf_op jit(solution)/shard_map/ppermute | solution.py:347
  37.2 0.2 copy.67
  37.4 0.4 maximum_bitcast_fusion.sides_ref
  37.7 0.2 broadcast_in_dim.21.bias_ref
  38.0 0.0 copy-done.7
  38.0 0.0 copy-done.10
  38.0 0.0 copy-start.5
  38.0 1.2 copy-done.5
  39.2 16.8 %attend.1 = (bf16[2,512,1024]{2,1,0:T(8,128)(2,1)S(1)}, bf16[2,8,1024]{2,1,0:T(8,128)(2,1)S(1)}) custom-call(bf16[2,512,512]{2,1,0:T(8,128)(2,1)S(1)} %copy-done.10, bf16[2,512,1024]{2,1,0:T(8,128)(2,1)} %copy-done.8, bf16[2,128,1024]{2,1,0:T(8,128)(2,1)S(1)} %bitcast.41, bf16[2,160,1024]{2,1,0:T(8,128)(2,1)S(1)} %maximum_bitcast_fusion.sides_ref, ...), custom_call_target="tpu_custom_call" | custom-call | flops 4294967296 | bytes 8388608 | tf_op jit(solution)/shard_map/attend/pallas_call | solution.py:372
  56.1 3.3 %collective-permute-start.4 = (bf16[2,1,32,1024]{3,2,0,1:T(8,128)(2,1)S(1)}, bf16[2,1,32,1024]{3,2,0,1:T(8,128)(2,1)S(1)}, u32[]{:S(2)}, u32[]{:S(2)}) collective-permute-start(bf16[2,1,32,1024]{3,2,0,1:T(8,128)(2,1)S(1)} %get-tuple-element.16), channel_id=1, source_target_pairs={{0,8},{8,16},{16,24},{24,32},{32,40},{40,48},{48,56},{56,64},{64,7... | collective-permute-start | bytes 393224 | tf_op jit(solution)/shard_map/ppermute | solution.py:403
  59.4 0.9 broadcast_in_dim.42
  60.3 7.3 %all-to-all-start = ((bf16[16,16,1024]{2,1,0:T(8,128)(2,1)}), bf16[16,16,1024]{2,1,0:T(8,128)(2,1)S(1)}, u32[]{:S(2)}, u32[]{:S(2)}) async-start(bf16[16,16,1024]{2,1,0:T(8,128)(2,1)} %broadcast_in_dim.42), calls=%async_computation | async-start | bytes 1048576 | tf_op jit(solution)/shard_map/all_to_all | solution.py:407
  67.6 0.2 fusion.2
  67.8 1.3 %collective-permute-start.5 = (bf16[2,1,32,1024]{3,2,0,1:T(8,128)(2,1)S(1)}, bf16[2,1,32,1024]{3,2,0,1:T(8,128)(2,1)S(1)}, u32[]{:S(2)}, u32[]{:S(2)}) collective-permute-start(bf16[2,1,32,1024]{3,2,0,1:T(8,128)(2,1)S(1)} %get-tuple-element.15), channel_id=1, source_target_pairs={{8,0},{16,8},{24,16},{32,24},{40,32},{48,40},{56,48},{64,56},{72,6... | collective-permute-start | bytes 393224 | tf_op jit(solution)/shard_map/ppermute | solution.py:404
  69.1 0.0 collective-permute-done.4
  69.2 1.8 %collective-permute-done.5 = bf16[2,1,32,1024]{3,2,0,1:T(8,128)(2,1)S(1)} collective-permute-done((bf16[2,1,32,1024]{3,2,0,1:T(8,128)(2,1)S(1)}, bf16[2,1,32,1024]{3,2,0,1:T(8,128)(2,1)S(1)}, u32[]{:S(2)}, u32[]{:S(2)}) %collective-permute-start.5) | collective-permute-done | bytes 131104 | tf_op jit(solution)/shard_map/ppermute | solution.py:404
  71.0 7.3 %all-to-all-done = bf16[16,16,1024]{2,1,0:T(8,128)(2,1)S(1)} async-done(((bf16[16,16,1024]{2,1,0:T(8,128)(2,1)}), bf16[16,16,1024]{2,1,0:T(8,128)(2,1)S(1)}, u32[]{:S(2)}, u32[]{:S(2)}) %all-to-all-start) | async-done | bytes 524320 | tf_op jit(solution)/shard_map/all_to_all | solution.py:407
  78.4 0.2 combine.1
  78.6 1.0 broadcast_in_dim.43
  79.6 7.0 %all-to-all-start.1 = ((bf16[8,48,1024]{2,1,0:T(8,128)(2,1)}), bf16[8,48,1024]{2,1,0:T(8,128)(2,1)}, u32[]{:S(2)}, u32[]{:S(2)}) async-start(bf16[8,48,1024]{2,1,0:T(8,128)(2,1)} %broadcast_in_dim.43), calls=%async_computation.1 | async-start | bytes 1572864 | tf_op jit(solution)/shard_map/all_to_all | solution.py:425
  86.6 4.9 %collective-permute-start.7 = (bf16[2,18,1024]{2,1,0:T(8,128)(2,1)S(1)}, bf16[2,18,1024]{2,1,0:T(8,128)(2,1)S(1)}, u32[]{:S(2)}, u32[]{:S(2)}) collective-permute-start(bf16[2,18,1024]{2,1,0:T(8,128)(2,1)S(1)} %pad_maximum_fusion.4), channel_id=1, source_target_pairs={{1,0},{2,1},{3,2},{4,3},{5,4},{6,5},{7,6},{9,8},{10,9},{11,10},{12... | collective-permute-start | bytes 221192 | tf_op jit(solution)/shard_map/ppermute | solution.py:420
  91.5 2.7 %collective-permute-start.6 = (bf16[2,18,1024]{2,1,0:T(8,128)(2,1)S(1)}, bf16[2,18,1024]{2,1,0:T(8,128)(2,1)S(1)}, u32[]{:S(2)}, u32[]{:S(2)}) collective-permute-start(bf16[2,18,1024]{2,1,0:T(8,128)(2,1)S(1)} %pad_maximum_fusion.3), channel_id=1, source_target_pairs={{0,1},{1,2},{2,3},{3,4},{4,5},{5,6},{6,7},{8,9},{9,10},{10,11},{11... | collective-permute-start | bytes 221192 | tf_op jit(solution)/shard_map/ppermute | solution.py:419
  94.2 1.4 %dynamic-slice_bitcast_fusion.1.by_row_ref = f32[16,648]{1,0:T(8,128)} fusion(f32[16,16,648]{2,1,0:T(8,128)} %constant.77.clone, s32[]{:T(128)S(6)} %select_n.28), kind=kLoop, calls=%fused_computation.12 | loop fusion | bytes 82948 | tf_op jit(solution)/shard_map/jit(dynamic_index_in_dim)/squeeze | solution.py:317
  95.6 7.0 %collective-permute-done.7 = bf16[2,18,1024]{2,1,0:T(8,128)(2,1)S(1)} collective-permute-done((bf16[2,18,1024]{2,1,0:T(8,128)(2,1)S(1)}, bf16[2,18,1024]{2,1,0:T(8,128)(2,1)S(1)}, u32[]{:S(2)}, u32[]{:S(2)}) %collective-permute-start.7) | collective-permute-done | bytes 73760 | tf_op jit(solution)/shard_map/ppermute | solution.py:420
  102.7 0.0 collective-permute-done.6
  102.7 0.0 copy-start
  102.7 5.0 %copy-done = bf16[3,3,3072,256]{3,2,1,0:T(8,128)(2,1)S(1)} copy-done((bf16[3,3,3072,256]{3,2,1,0:T(8,128)(2,1)S(1)}, bf16[3,3,3072,256]{3,2,1,0:T(8,128)(2,1)}, u32[]{:S(2)}) %copy-start) | copy-done | bytes 14155800
  107.7 6.6 %conv.1.conv_ref = f32[2,512,256]{2,1,0:T(8,128)S(1)} custom-call(bf16[2,512,1024]{2,1,0:T(8,128)(2,1)S(1)} %get-tuple-element.12.attended_ref, bf16[2,32,1024]{2,1,0:T(8,128)(2,1)S(1)} %bitcast.47, bf16[2,32,1024]{2,1,0:T(8,128)(2,1)S(1)} %bitcast.48, bf16[2,24,1024]{2,1,0:T(8,128)(2,1)S(1)} %pad.7.left_ref, bf16[2,24,1024]{2,1,0:T(8,128)(2,1)S(1)} %pad.8.right_ref, ...), custom_call_target="tpu_custom_call" | custom-call | flops 4831838208 | bytes 6815744 | tf_op jit(solution)/shard_map/conv/pallas_call | solution.py:430
  114.4 0.0 copy-start.1
  114.4 1.0 copy-done.1
  115.3 0.0 all-to-all-done.1
  115.4 10.5 %tail.1 = bf16[2,512,256]{2,1,0:T(8,128)(2,1)} custom-call(bf16[144,384]{1,0:T(8,128)(2,1)} %constant.83.table_ref, f32[144,1]{1,0:T(8,128)} %constant.76.clone.scale_ref, bf16[384,1024]{1,0:T(8,128)(2,1)} %bitcast.9.parts_ref, bf16[4,1024,512]{2,1,0:T(8,128)(2,1)} %wpool_ref.1, bf16[3,3,3072,256]{3,2,1,0:T(8,128)(2,1)} %w6_ref.1, ...), custom_call_target="tpu_custom_call" | custom-call | tf_op jit(solution)/shard_map/tail/pallas_call | solution.py:453
  (26 shorter events, 0.5 us)
Async XLA Ops:
  1.1 20.2 %collective-permute-start = (bf16[2,2,32,1024]{3,2,1,0:T(8,128)(2,1)S(1)}, bf16[2,2,32,1024]{3,2,1,0:T(8,128)(2,1)S(1)}, u32[]{:S(2)}, u32[]{:S(2)}) collective-permute-start(bf16[2,2,32,1024]{3,2,1,0:T(8,128)(2,1)S(1)} %get-tuple-element.19), channel_id=1, source_target_pairs={{0,8},{8,16},{16,24},{24,32},{32,40},{40,48},{48,56},{56,64},{64,7... | collective-permute-start | bytes 786440 | tf_op jit(solution)/shard_map/ppermute | solution.py:321
  2.8 18.5 %collective-permute-start.1 = (bf16[2,2,32,1024]{3,2,1,0:T(8,128)(2,1)S(1)}, bf16[2,2,32,1024]{3,2,1,0:T(8,128)(2,1)S(1)}, u32[]{:S(2)}, u32[]{:S(2)}) collective-permute-start(bf16[2,2,32,1024]{3,2,1,0:T(8,128)(2,1)S(1)} %get-tuple-element.20), channel_id=1, source_target_pairs={{8,0},{16,8},{24,16},{32,24},{40,32},{48,40},{56,48},{64,56},{72,6... | collective-permute-start | bytes 786440 | tf_op jit(solution)/shard_map/ppermute | solution.py:322
  8.6 1.6 %copy-start.2 = (bf16[2,16,32,1024]{3,2,1,0:T(8,128)(2,1)S(1)}, bf16[2,16,32,1024]{3,2,1,0:T(8,128)(2,1)}, u32[]{:S(2)}) copy-start(bf16[2,16,32,1024]{3,2,1,0:T(8,128)(2,1)} %param.16) | copy-start | bytes 6291460
  10.2 1.6 %copy-start.3 = (bf16[1024,1024]{1,0:T(8,128)(2,1)S(1)}, bf16[1024,1024]{1,0:T(8,128)(2,1)}, u32[]{:S(2)}) copy-start(bf16[1024,1024]{1,0:T(8,128)(2,1)} %wkv_ref.3) | copy-start | bytes 6291460
  11.7 1.2 copy-start.4
  13.0 0.7 copy-start.6
  18.2 1.4 %copy-start.8 = (bf16[2,512,1024]{2,1,0:T(8,128)(2,1)}, bf16[2,512,1024]{2,1,0:T(8,128)(2,1)S(1)}, u32[]{:S(2)}) copy-start(bf16[2,512,1024]{2,1,0:T(8,128)(2,1)S(1)} %get-tuple-element.10.kv_ref) | copy-start | bytes 6291460
  19.5 7.2 %copy-start.9 = (bf16[2,512,512]{2,1,0:T(8,128)(2,1)}, bf16[2,512,512]{2,1,0:T(8,128)(2,1)S(1)}, u32[]{:S(2)}) copy-start(bf16[2,512,512]{2,1,0:T(8,128)(2,1)S(1)} %get-tuple-element.9.q_ref) | copy-start | bytes 3145732
  21.4 16.6 %copy-start.7 = (f32[1024]{0:T(1024)S(1)}, f32[1024]{0:T(1024)}, u32[]{:S(2)}) copy-start(f32[1024]{0:T(1024)} %param.17) | copy-start | bytes 12292
  21.5 9.4 %collective-permute-start.2 = (bf16[2,20,2,1024]{3,1,2,0:T(8,128)(2,1)S(1)}, bf16[2,20,2,1024]{3,1,2,0:T(8,128)(2,1)S(1)}, u32[]{:S(2)}, u32[]{:S(2)}) collective-permute-start(bf16[2,20,2,1024]{3,1,2,0:T(8,128)(2,1)S(1)} %pad_maximum_fusion.1), channel_id=1, source_target_pairs={{1,0},{2,1},{3,2},{4,3},{5,4},{6,5},{7,6},{9,8},{10,9},{11,10},{12... | collective-permute-start | bytes 491528 | tf_op jit(solution)/shard_map/ppermute | solution.py:348
  26.7 10.5 %collective-permute-start.3 = (bf16[2,20,2,1024]{3,1,2,0:T(8,128)(2,1)S(1)}, bf16[2,20,2,1024]{3,1,2,0:T(8,128)(2,1)S(1)}, u32[]{:S(2)}, u32[]{:S(2)}) collective-permute-start(bf16[2,20,2,1024]{3,1,2,0:T(8,128)(2,1)S(1)} %pad_maximum_fusion.2), channel_id=1, source_target_pairs={{0,1},{1,2},{2,3},{3,4},{4,5},{5,6},{6,7},{8,9},{9,10},{10,11},{11... | collective-permute-start | bytes 491528 | tf_op jit(solution)/shard_map/ppermute | solution.py:347
  29.9 8.0 %copy-start.10 = (bf16[2,512,512]{2,1,0:T(8,128)(2,1)S(1)}, bf16[2,512,512]{2,1,0:T(8,128)(2,1)}, u32[]{:S(2)}) copy-start(bf16[2,512,512]{2,1,0:T(8,128)(2,1)} %copy-done.9) | copy-start | bytes 3145732
  38.0 1.2 copy-start.5
  56.1 13.1 %collective-permute-start.4 = (bf16[2,1,32,1024]{3,2,0,1:T(8,128)(2,1)S(1)}, bf16[2,1,32,1024]{3,2,0,1:T(8,128)(2,1)S(1)}, u32[]{:S(2)}, u32[]{:S(2)}) collective-permute-start(bf16[2,1,32,1024]{3,2,0,1:T(8,128)(2,1)S(1)} %get-tuple-element.16), channel_id=1, source_target_pairs={{0,8},{8,16},{16,24},{24,32},{32,40},{40,48},{48,56},{56,64},{64,7... | collective-permute-start | bytes 393224 | tf_op jit(solution)/shard_map/ppermute | solution.py:403
  60.3 18.1 %all-to-all-start = ((bf16[16,16,1024]{2,1,0:T(8,128)(2,1)}), bf16[16,16,1024]{2,1,0:T(8,128)(2,1)S(1)}, u32[]{:S(2)}, u32[]{:S(2)}) async-start(bf16[16,16,1024]{2,1,0:T(8,128)(2,1)} %broadcast_in_dim.42), calls=%async_computation | async-start | bytes 1048576 | tf_op jit(solution)/shard_map/all_to_all | solution.py:407
  67.8 3.2 %collective-permute-start.5 = (bf16[2,1,32,1024]{3,2,0,1:T(8,128)(2,1)S(1)}, bf16[2,1,32,1024]{3,2,0,1:T(8,128)(2,1)S(1)}, u32[]{:S(2)}, u32[]{:S(2)}) collective-permute-start(bf16[2,1,32,1024]{3,2,0,1:T(8,128)(2,1)S(1)} %get-tuple-element.15), channel_id=1, source_target_pairs={{8,0},{16,8},{24,16},{32,24},{40,32},{48,40},{56,48},{64,56},{72,6... | collective-permute-start | bytes 393224 | tf_op jit(solution)/shard_map/ppermute | solution.py:404
  79.6 35.8 %all-to-all-start.1 = ((bf16[8,48,1024]{2,1,0:T(8,128)(2,1)}), bf16[8,48,1024]{2,1,0:T(8,128)(2,1)}, u32[]{:S(2)}, u32[]{:S(2)}) async-start(bf16[8,48,1024]{2,1,0:T(8,128)(2,1)} %broadcast_in_dim.43), calls=%async_computation.1 | async-start | bytes 1572864 | tf_op jit(solution)/shard_map/all_to_all | solution.py:425
  86.6 16.0 %collective-permute-start.7 = (bf16[2,18,1024]{2,1,0:T(8,128)(2,1)S(1)}, bf16[2,18,1024]{2,1,0:T(8,128)(2,1)S(1)}, u32[]{:S(2)}, u32[]{:S(2)}) collective-permute-start(bf16[2,18,1024]{2,1,0:T(8,128)(2,1)S(1)} %pad_maximum_fusion.4), channel_id=1, source_target_pairs={{1,0},{2,1},{3,2},{4,3},{5,4},{6,5},{7,6},{9,8},{10,9},{11,10},{12... | collective-permute-start | bytes 221192 | tf_op jit(solution)/shard_map/ppermute | solution.py:420
  91.5 11.1 %collective-permute-start.6 = (bf16[2,18,1024]{2,1,0:T(8,128)(2,1)S(1)}, bf16[2,18,1024]{2,1,0:T(8,128)(2,1)S(1)}, u32[]{:S(2)}, u32[]{:S(2)}) collective-permute-start(bf16[2,18,1024]{2,1,0:T(8,128)(2,1)S(1)} %pad_maximum_fusion.3), channel_id=1, source_target_pairs={{0,1},{1,2},{2,3},{3,4},{4,5},{5,6},{6,7},{8,9},{9,10},{10,11},{11... | collective-permute-start | bytes 221192 | tf_op jit(solution)/shard_map/ppermute | solution.py:419
  102.7 5.0 %copy-start = (bf16[3,3,3072,256]{3,2,1,0:T(8,128)(2,1)S(1)}, bf16[3,3,3072,256]{3,2,1,0:T(8,128)(2,1)}, u32[]{:S(2)}) copy-start(bf16[3,3,3072,256]{3,2,1,0:T(8,128)(2,1)} %w6_ref.1) | copy-start | bytes 42467332
  114.4 1.0 copy-start.1

commit v2 on v1

v2 whole, which is shorter than its diff:
```python
import math

import jax
import jax.numpy as jnp
import numpy as np
from jax import lax
from jax.experimental import pallas as pl
from jax.experimental.pallas import tpu as pltpu
from jax.sharding import PartitionSpec as P

HEAD_DIM = 32
BLOCK = 8
HALO = 2
EPS = 1e-05
LEVELS = (1, 2, 3, 6)
CODED = (6, 3, 2)
UNITS = 8
STRIP_UNITS = 24
STRIP_AT = {6: 0, 3: 12, 2: 18}
SLOTS = {1: 8, 2: 8, 3: 16, 6: 40}
TAPS = 9
f32 = jnp.float32
bf16 = jnp.bfloat16


def bins_of(level, length, first, count):
    places = first + np.arange(count)
    found = []
    for cell in range(level):
        start = cell * length // level
        end = ((cell + 1) * length + level - 1) // level
        mask = (places >= start) & (places < end)
        if mask.any():
            found.append((cell, mask))
    return found


def pool_tables(rows, row_strips, cols, col_strips):
    grid_h, grid_w = rows * row_strips, cols * col_strips
    row_masks = np.zeros((row_strips, col_strips, UNITS, rows), np.float32)
    col_masks = np.zeros((row_strips, col_strips, UNITS, cols), np.float32)
    strip = np.zeros((col_strips, 2 * STRIP_UNITS, row_strips, 2 * UNITS), np.float32)
    slots = 2 * sum(SLOTS.values())
    bins = np.zeros((slots, col_strips, 2 * STRIP_UNITS), np.float32)
    scale = np.zeros((slots, 1), np.float32)
    for c in range(col_strips):
        for r in range(row_strips):
            units = []
            for level in CODED:
                for i, row_mask in bins_of(level, grid_h, r * rows, rows):
                    for g, (j, col_mask) in enumerate(bins_of(level, grid_w, c * cols, cols)):
                        key = (row_mask.tobytes(), col_mask.tobytes())
                        if key not in units:
                            units.append(key)
                            at = len(units) - 1
                            row_masks[r, c, at] = row_mask
                            col_masks[r, c, at] = col_mask
                        at = units.index(key)
                        width = 1 if level == 2 else 2
                        for s in range(2):
                            target = s * STRIP_UNITS + STRIP_AT[level] + i * width + g
                            strip[c, target, r, s * UNITS + at] = 1.0
            assert len(units) <= UNITS
        base = 0
        for level in LEVELS:
            source = 2 if level == 1 else level
            for g, (j, _) in enumerate(bins_of(source, grid_w, c * cols, cols)):
                for i in range(source):
                    for s in range(2):
                        cell = 0 if level == 1 else i * level + j
                        row = base + s * SLOTS[level] + cell
                        width = 1 if source == 2 else 2
                        bins[row, c, s * STRIP_UNITS + STRIP_AT[source] + i * width + g] = 1.0
            base += 2 * SLOTS[level]
    base = 0
    for level in LEVELS:
        row_all = bins_of(level, grid_h, 0, grid_h)
        col_all = bins_of(level, grid_w, 0, grid_w)
        for s in range(2):
            for i, row_mask in row_all:
                for j, col_mask in col_all:
                    row = base + s * SLOTS[level] + i * level + j
                    scale[row, 0] = 1.0 / (row_mask.sum() * col_mask.sum())
        base += 2 * SLOTS[level]
    return row_masks, col_masks, strip.reshape(col_strips, 2 * STRIP_UNITS, -1), bins.reshape(slots, -1), scale


def upsample_weights(level, length, first, count):
    places = first + np.arange(count)
    numer = np.maximum((2 * places + 1) * level - length, 0)
    lower = numer // (2 * length)
    frac = (numer - lower * 2 * length).astype(np.float32) / np.float32(2.0 * length)
    upper = np.minimum(lower + 1, level - 1)
    cells = np.arange(level)[None, :]
    weight = (cells == lower[:, None]) * (1.0 - frac)[:, None] + (cells == upper[:, None]) * frac[:, None]
    inside = (places >= 0) & (places < length)
    return (weight * inside[:, None]).astype(np.float32)


def upsample_tables(rows, row_strips, cols, col_strips):
    grid_h, grid_w = rows * row_strips, cols * col_strips
    width = TAPS * sum(SLOTS.values())
    cells = sum(LEVELS)
    by_row = np.zeros((row_strips, rows, 64), np.float32)
    by_col = np.zeros((col_strips, cols, 64), np.float32)
    spread = np.zeros((2, 64, width), np.float32)
    base, first = 0, 0
    for level in LEVELS:
        for a in range(3):
            for strip in range(row_strips):
                w = upsample_weights(level, grid_h, strip * rows + a - 1, rows)
                by_row[strip, :, a * cells + first : a * cells + first + level] = w
            for strip in range(col_strips):
                w = upsample_weights(level, grid_w, strip * cols + a - 1, cols)
                by_col[strip, :, a * cells + first : a * cells + first + level] = w
            for c in range(3):
                for i in range(level):
                    for j in range(level):
                        at = base + (a * 3 + c) * SLOTS[level] + i * level + j
                        spread[0, a * cells + first + i, at] = 1.0
                        spread[1, c * cells + first + j, at] = 1.0
        base += TAPS * SLOTS[level]
        first += level
    return by_row, by_col, spread


def layer_norm(tokens, gain):
    x = tokens.astype(f32)
    center = jnp.mean(x, axis=-1, keepdims=True)
    x = x - center
    spread = jnp.mean(x * x, axis=-1, keepdims=True)
    return (x * lax.rsqrt(spread + EPS) * gain).astype(bf16)


def dot(a, b):
    return jnp.dot(a, b, preferred_element_type=f32)


def project_kernel(tokens_ref, above_ref, below_ref, gain_ref, wq_ref, wkv_ref, q_ref, kv_ref):
    rows, cols, inner = q_ref.shape
    gain, wkv = gain_ref[...], wkv_ref[...]
    normed = layer_norm(tokens_ref[...], gain)
    q_ref[...] = dot(normed, wq_ref[...]).astype(bf16).astype(f32).reshape(rows, cols, inner)
    kv_ref[HALO : rows + HALO] = dot(normed, wkv).astype(bf16).astype(f32).reshape(rows, cols, -1)
    edge = layer_norm(jnp.concatenate([above_ref[...], below_ref[...]], axis=0), gain)
    edge = dot(edge, wkv).astype(bf16).astype(f32).reshape(2 * HALO, cols, -1)
    kv_ref[0:HALO] = edge[:HALO]
    kv_ref[rows + HALO :] = edge[HALO:]


def window_bias(bias, first_row, first_col, grid_h, grid_w):
    span = BLOCK + 2 * HALO
    key = lax.broadcasted_iota(jnp.int32, bias.shape[2:], 0)
    extra = key - span * BLOCK
    lane = extra & 7
    odd = ((lane >= 2) & (lane < 6)).astype(jnp.int32)
    west = (lane >= 6) | ((lane >= 2) & (lane < 4))
    main = key < span * BLOCK
    row = jnp.where(main, key >> 3, 2 * (extra >> 3) + odd) - HALO
    col = jnp.where(main, key & 7, (key & 1) + jnp.where(west, -HALO, BLOCK))
    for a in range(bias.shape[0]):
        at = row + (first_row + a * BLOCK)
        row_ok = (at >= 0) & (at < grid_h)
        for b in range(bias.shape[1]):
            at = col + (first_col + b * BLOCK)
            bias[a, b] = jnp.where(row_ok & (at >= 0) & (at < grid_w), 0.0, -1e30)


def attend_kernel(
    grid_shape, place_ref, q_ref, kv_ref, sides_ref, tokens_ref, gain_ref, wkv_ref, wout_ref, masks_ref,
    attended_ref, sums_ref, sides, context, bias, pool, scores, weights,
):
    rows, cols, inner = q_ref.shape
    groups = cols // BLOCK
    span = BLOCK + 2 * HALO

    @pl.when(pl.program_id(0) == 0)
    def _():
        window_bias(bias, place_ref[0] * rows, place_ref[1] * cols, *grid_shape)
        masks = masks_ref[...].astype(bf16)
        unit = lax.broadcasted_iota(jnp.int32, (masks.shape[1], rows * cols), 0)
        token = lax.broadcasted_iota(jnp.int32, (masks.shape[1], rows * cols), 1)
        to_row = (unit == token // cols).astype(f32).astype(bf16)
        to_col = (unit - rows == token % cols).astype(f32).astype(bf16)
        pool[...] = (dot(masks, to_row) * dot(masks, to_col)).astype(bf16)
        ends = layer_norm(sides_ref[...].reshape(-1, sides_ref.shape[-1]), gain_ref[...])
        ends = dot(ends, wkv_ref[...]).astype(bf16).astype(f32)
        sides[...] = ends.reshape(sides.shape)

    sheet = pl.program_id(0)
    count = BLOCK * BLOCK
    heads = 128 // HEAD_DIM
    head_of_row = lax.broadcasted_iota(jnp.int32, (heads, count, 128), 0)
    head_of_lane = lax.broadcasted_iota(jnp.int32, (heads, count, 128), 2) // HEAD_DIM
    own = (head_of_row == head_of_lane).astype(f32).astype(bf16).reshape(heads * count, 128)
    lane = lax.broadcasted_iota(jnp.int32, (count, 128), 1)
    place = lax.broadcasted_iota(jnp.int32, (span // 2, BLOCK, 128), 1)
    factor = math.log2(math.e) / math.sqrt(HEAD_DIM)

    def band(a, carry):
        at = pl.multiple_of(a * BLOCK, BLOCK)

        def keys_of(b, lanes):
            mid = slice(b * BLOCK, (b + 1) * BLOCK)
            main = kv_ref[pl.ds(at, span), mid, lanes].reshape(span * BLOCK, 128)

            def beside(g):
                if g < 0 or g >= groups:
                    found = sides[sheet, pl.ds(at, span), :, lanes]
                else:
                    found = kv_ref[pl.ds(at, span), g * BLOCK : (g + 1) * BLOCK, lanes]
                return found.reshape(span // 2, 2, BLOCK, 128)

            west, east = beside(b - 1), beside(b + 1)
            even = jnp.where(place >= 6, west[:, 0], east[:, 0])
            odd = pltpu.roll(jnp.where(place >= 6, west[:, 1], east[:, 1]), 4, 1)
            extra = jnp.where((place >= 6) | (place < 2), even, odd).reshape(span * 4, 128)
            return jnp.concatenate([main, extra], axis=0).astype(bf16)

        tiles = inner // 128

        def score(b, slot):
            mid = slice(b * BLOCK, (b + 1) * BLOCK)
            low = bias[a, b]
            for t in range(tiles):
                lanes = slice(t * 128, (t + 1) * 128)
                q = q_ref[pl.ds(at, BLOCK), mid, lanes].reshape(count, 128).astype(bf16)
                q = jnp.concatenate([q] * heads, axis=0) * own
                found = lax.dot_general(keys_of(b, lanes), q, (((1,), (1,)), ((), ())), preferred_element_type=f32)
                scores[slot, t] = found + jnp.concatenate([low] * (heads * count // 128), axis=1)

        def soften(slot):
            for t in range(tiles):
                for h in range(heads * count // 128):
                    lanes = slice(h * 128, (h + 1) * 128)
                    found = scores[slot, t, :, lanes]
                    top = jnp.max(found, axis=0, keepdims=True)
                    expon = jnp.exp2((found - top) * factor)
                    weights[slot, t, :, lanes] = (expon * (1.0 / jnp.sum(expon, axis=0, keepdims=True))).astype(bf16)

        def mix(b, slot):
            mid = slice(b * BLOCK, (b + 1) * BLOCK)
            for t in range(tiles):
                lanes = slice(t * 128, (t + 1) * 128)
                values = keys_of(b, slice(inner + t * 128, inner + (t + 1) * 128))
                mixed = lax.dot_general(weights[slot, t], values, (((0,), (0,)), ((), ())), preferred_element_type=f32)
                mixed = mixed.reshape(heads, count, 128)
                piece = mixed[0]
                for k in range(1, heads):
                    piece = jnp.where(lane >= k * HEAD_DIM, mixed[k], piece)
                context[pl.ds(at, BLOCK), mid, lanes] = piece.reshape(BLOCK, BLOCK, 128)

        score(0, 0)
        for b in range(groups):
            if b + 1 < groups:
                score(b + 1, (b + 1) % 2)
            soften(b % 2)
            mix(b, b % 2)
        return carry

    lax.fori_loop(0, rows // BLOCK, band, 0)
    mixed = context[...].reshape(rows * cols, inner).astype(bf16)
    attended = (tokens_ref[...].astype(f32) + dot(mixed, wout_ref[...])).astype(bf16)
    attended_ref[...] = attended
    sums = dot(pool[...], attended).astype(bf16)
    sums_ref[...] = jnp.broadcast_to(sums[None], sums_ref.shape)


def combine_kernel(place_ref, table_ref, parts_ref, out_ref):
    added = dot(table_ref[...].astype(bf16), parts_ref[...]).astype(bf16)
    out_ref[...] = jnp.broadcast_to(added[None], out_ref.shape)


def conv_kernel(attended_ref, top_ref, bottom_ref, left_ref, right_ref, w_ref, out_ref, ext):
    sheets, area, _ = attended_ref.shape
    cols = top_ref.shape[1]
    rows = area // cols
    out_ch = out_ref.shape[-1]
    step = pl.program_id(0)

    def edge(ref, s):
        total = 0.0
        for a in range(3):
            total = total + dot(ref[s], w_ref[a])[a : a + rows]
        return total.reshape(rows, 1, out_ch)

    def middle(s):
        total = dot(ext[s, 0:area], w_ref[0])
        for a in range(1, 3):
            total = total + dot(ext[s, a * cols : a * cols + area], w_ref[a])
        return total.reshape(rows, cols, out_ch)

    @pl.when(step == 0)
    def _():
        place = lax.broadcasted_iota(jnp.int32, (rows, cols, out_ch), 1)
        for s in range(sheets):
            ext[s, 0:cols] = top_ref[s]
            ext[s, cols : cols + area] = attended_ref[s]
            ext[s, cols + area :] = bottom_ref[s]
            part = jnp.where(place == 0, edge(left_ref, s), pltpu.roll(middle(s), 1, 1))
            out_ref[s] = part.reshape(area, out_ch)

    @pl.when(step == 1)
    def _():
        for s in range(sheets):
            out_ref[s] += middle(s).reshape(area, out_ch)

    @pl.when(step == 2)
    def _():
        place = lax.broadcasted_iota(jnp.int32, (rows, cols, out_ch), 1)
        for s in range(sheets):
            part = jnp.where(place == cols - 1, edge(right_ref, s), pltpu.roll(middle(s), cols - 1, 1))
            out_ref[s] += part.reshape(area, out_ch)


def split(x):
    high = x.astype(bf16)
    return high, (x - high.astype(f32)).astype(bf16)


def tail_kernel(
    place_ref, table_ref, scale_ref, parts_ref, wpool_hbm, wjoin_hbm, by_row_ref, by_col_ref, spread_ref, conv_ref,
    out_ref, taps, wpool, wjoin, sems,
):
    width, ppm = wpool.shape[1], wpool.shape[2]
    copies = []
    for index in range(len(LEVELS)):
        copies.append((
            pltpu.make_async_copy(wpool_hbm.at[index], wpool.at[index], sems.at[0, index]),
            pltpu.make_async_copy(
                wjoin_hbm.at[:, :, width + index * ppm : width + (index + 1) * ppm, :], wjoin.at[index], sems.at[1, index]
            ),
        ))
    for pair in copies:
        for copy in pair:
            copy.start()
    pooled = dot(table_ref[...], parts_ref[...]) * scale_ref[...]
    row = 0
    at = 0
    for index, level in enumerate(LEVELS):
        slots = SLOTS[level]
        high, low = split(pooled[row : row + 2 * slots])
        copies[index][0].wait()
        both = dot(jnp.concatenate([high, low], axis=0), wpool[index])
        branch = jnp.maximum(both[: 2 * slots] + both[2 * slots :], 0.0)
        high, low = split(branch)
        both = jnp.concatenate([high, low], axis=0)
        copies[index][1].wait()
        for a in range(3):
            for c in range(3):
                tap = dot(both, wjoin[index, a, c])
                tap = tap[: 2 * slots] + tap[2 * slots :]
                start = at + (a * 3 + c) * slots
                for s in range(2):
                    taps[s, start : start + slots, :] = tap[s * slots : (s + 1) * slots]
        row += 2 * slots
        at += TAPS * slots
    rows, cols = by_row_ref.shape[0], by_col_ref.shape[0]

    def along(ref, axis):
        high, low = split(ref[...])
        return dot(high, spread_ref[axis]) + dot(low, spread_ref[axis])

    grid = along(by_row_ref, 0)[:, None, :] * along(by_col_ref, 1)[None, :, :]
    grid_high, grid_low = split(grid.reshape(rows * cols, -1))
    for s in range(2):
        high, low = split(taps[s])
        total = conv_ref[s] + dot(grid_high, high) + dot(grid_low, high) + dot(grid_high, low)
        out_ref[s] = total.astype(bf16)


def cost(flops, nbytes, transcendentals=0):
    return pl.CostEstimate(flops=int(flops), bytes_accessed=int(nbytes), transcendentals=int(transcendentals))


def params(mib):
    return pltpu.CompilerParams(vmem_limit_bytes=mib * 2**20)


def whole(shape):
    return pl.BlockSpec(shape, lambda *_: (0,) * len(shape))


def shifts(axis):
    count = lax.axis_size(axis)
    forward = [(i, i + 1) for i in range(count - 1)]
    return forward, [(j, i) for i, j in forward]


def layer(tokens, norm_gain, w_query, w_kv, w_out, w_pool, w_join):
    sheets, rows, cols, width = tokens.shape
    inner = w_query.shape[1]
    wide = w_kv.shape[1]
    out_ch = w_join.shape[-1]
    ppm = w_pool.shape[-1]
    area = rows * cols
    row_count, col_count = lax.axis_size("row"), lax.axis_size("col")
    r, c = lax.axis_index("row"), lax.axis_index("col")
    grid_h, grid_w = rows * row_count, cols * col_count
    gain = norm_gain.reshape(1, width)
    row_masks, col_masks, strip_table, bin_table, bin_scale = pool_tables(rows, row_count, cols, col_count)
    by_row, by_col, spread = upsample_tables(rows, row_count, cols, col_count)
    masks = np.concatenate([row_masks, col_masks], axis=-1).reshape(row_count * col_count, UNITS, rows + cols)

    at = jnp.stack([r, c]).astype(jnp.int32)
    row_fwd, row_bwd = shifts("row")
    col_fwd, col_bwd = shifts("col")
    above = lax.ppermute(tokens[:, rows - HALO :], "row", row_fwd)
    below = lax.ppermute(tokens[:, :HALO], "row", row_bwd)

    def edges(first):
        return jnp.concatenate([x[:, :, first : first + HALO] for x in (above, tokens, below)], axis=1)

    west = lax.ppermute(edges(cols - HALO), "col", col_fwd)
    east = lax.ppermute(edges(0), "col", col_bwd)

    def per_sheet(*dims):
        return pl.BlockSpec((None,) + dims, lambda s: (s,) + (0,) * len(dims))

    flat = tokens.reshape(sheets, area, width)
    edge = HALO * cols
    q, kv = pl.pallas_call(
        project_kernel,
        grid=(sheets,),
        in_specs=[
            per_sheet(area, width), per_sheet(edge, width), per_sheet(edge, width),
            whole((1, width)), whole((width, inner)), whole((width, wide)),
        ],
        out_specs=[per_sheet(rows, cols, inner), per_sheet(rows + 2 * HALO, cols, wide)],
        out_shape=[
            jax.ShapeDtypeStruct((sheets, rows, cols, inner), f32),
            jax.ShapeDtypeStruct((sheets, rows + 2 * HALO, cols, wide), f32),
        ],
        compiler_params=params(28),
        cost_estimate=cost(2 * sheets * area * width * (inner + wide), 2 * (width * (inner + wide) + 5 * sheets * area * width)),
        name="project",
    )(flat, above.reshape(sheets, edge, width), below.reshape(sheets, edge, width), gain, w_query, w_kv)

    blank = jnp.zeros((sheets, rows + 2 * HALO, BLOCK - 2 * HALO, width), bf16)
    sides = jnp.concatenate([east, blank, west], axis=2).reshape(sheets, (rows + 2 * HALO) * BLOCK, width)
    blocks = (rows // BLOCK) * (cols // BLOCK)
    keys = (BLOCK + 2 * HALO) ** 2

    def fixed(*dims):
        return whole(dims)

    attended, sums = pl.pallas_call(
        lambda *refs: attend_kernel((grid_h, grid_w), *refs),
        grid_spec=pltpu.PrefetchScalarGridSpec(
            num_scalar_prefetch=1,
            grid=(sheets,),
            in_specs=[
                pl.BlockSpec((None, rows, cols, inner), lambda s, _: (s, 0, 0, 0)),
                pl.BlockSpec((None, rows + 2 * HALO, cols, wide), lambda s, _: (s, 0, 0, 0)),
                fixed(sheets, (rows + 2 * HALO) * BLOCK, width),
                pl.BlockSpec((None, area, width), lambda s, _: (s, 0, 0)),
                fixed(1, width), fixed(width, wide), fixed(inner, width),
                pl.BlockSpec((None, UNITS, rows + cols), lambda s, p: (p[0] * col_count + p[1], 0, 0)),
            ],
            out_specs=[
                pl.BlockSpec((None, area, width), lambda s, _: (s, 0, 0)),
                pl.BlockSpec((row_count, UNITS, width), lambda s, _: (0, s, 0)),
            ],
            scratch_shapes=[
                pltpu.VMEM((sheets, rows + 2 * HALO, BLOCK, wide), f32),
                pltpu.VMEM((rows, cols, inner), f32),
                pltpu.VMEM((rows // BLOCK, cols // BLOCK, keys, 128), f32),
                pltpu.VMEM((UNITS, area), bf16),
                pltpu.VMEM((2, inner // 128, keys, 256), f32),
                pltpu.VMEM((2, inner // 128, keys, 256), bf16),
            ],
        ),
        out_shape=[
            jax.ShapeDtypeStruct((sheets, area, width), bf16),
            jax.ShapeDtypeStruct((row_count, sheets * UNITS, width), bf16),
        ],
        compiler_params=params(32),
        cost_estimate=cost(2 * sheets * area * inner * width * 4, 2 * sheets * area * width * 4, sheets * blocks * keys * 1024),
        name="attend",
    )(at, q, kv, sides, flat, gain, w_kv, w_out, jnp.asarray(masks))

    att = attended.reshape(sheets, rows, cols, width)
    strip_rows = sheets * STRIP_UNITS
    att_above = lax.ppermute(att[:, rows - 1 :], "row", row_fwd)
    att_below = lax.ppermute(att[:, :1], "row", row_bwd)
    parts = lax.all_to_all(sums, "row", 0, 0, tiled=True).reshape(row_count * sheets * UNITS, width)

    def att_edges(first):
        return jnp.concatenate([x[:, :, first] for x in (att_above, att, att_below)], axis=1)

    att_west = lax.ppermute(att_edges(cols - 1), "col", col_fwd)
    att_east = lax.ppermute(att_edges(0), "col", col_bwd)
    pad = ((0, 0), (0, 6), (0, 0))
    att_west, att_east = jnp.pad(att_west, pad), jnp.pad(att_east, pad)

    strips = pl.pallas_call(
        combine_kernel,
        grid_spec=pltpu.PrefetchScalarGridSpec(
            num_scalar_prefetch=1,
            grid=(1,),
            in_specs=[
                pl.BlockSpec((None,) + strip_table.shape[1:], lambda k, p: (p[1], 0, 0)),
                fixed(row_count * sheets * UNITS, width),
            ],
            out_specs=fixed(col_count, strip_rows, width),
        ),
        out_shape=jax.ShapeDtypeStruct((col_count, strip_rows, width), bf16),
        compiler_params=params(8),
        name="combine",
    )(at, jnp.asarray(strip_table).astype(bf16), parts)
    strips = lax.all_to_all(strips, "col", 0, 0, tiled=True).reshape(col_count * strip_rows, width)

    conv = pl.pallas_call(
        conv_kernel,
        grid=(3,),
        in_specs=[
            whole((sheets, area, width)), whole((sheets, cols, width)), whole((sheets, cols, width)),
            whole((sheets, rows + 8, width)), whole((sheets, rows + 8, width)),
            pl.BlockSpec((3, None, width, out_ch), lambda k: (0, k, 0, 0)),
        ],
        out_specs=whole((sheets, area, out_ch)),
        out_shape=jax.ShapeDtypeStruct((sheets, area, out_ch), f32),
        scratch_shapes=[pltpu.VMEM((sheets, area + 2 * cols, width), bf16)],
        compiler_params=params(52),
        cost_estimate=cost(2 * sheets * area * width * 9 * out_ch, 2 * 9 * width * out_ch + 2 * sheets * area * width),
        name="conv",
    )(attended, att_above.reshape(sheets, cols, width), att_below.reshape(sheets, cols, width), att_west, att_east, w_join)

    depth = TAPS * sum(SLOTS.values())
    bin_rows = 2 * sum(SLOTS.values())
    out = pl.pallas_call(
        tail_kernel,
        grid_spec=pltpu.PrefetchScalarGridSpec(
            num_scalar_prefetch=1,
            grid=(1,),
            in_specs=[
                fixed(bin_rows, col_count * strip_rows), fixed(bin_rows, 1), fixed(col_count * strip_rows, width),
                pl.BlockSpec(memory_space=pl.ANY), pl.BlockSpec(memory_space=pl.ANY),
                pl.BlockSpec((None, rows, 64), lambda k, p: (p[0], 0, 0)),
                pl.BlockSpec((None, cols, 64), lambda k, p: (p[1], 0, 0)),
                fixed(2, 64, depth), fixed(sheets, area, out_ch),
            ],
            out_specs=fixed(sheets, area, out_ch),
            scratch_shapes=[
                pltpu.VMEM((sheets, depth, out_ch), f32),
                pltpu.VMEM(w_pool.shape, bf16),
                pltpu.VMEM((len(LEVELS), 3, 3, ppm, out_ch), bf16),
                pltpu.SemaphoreType.DMA((2, len(LEVELS))),
            ],
        ),
        out_shape=jax.ShapeDtypeStruct((sheets, area, out_ch), bf16),
        compiler_params=params(56),
        cost_estimate=cost(4e9, 2 * (w_pool.size + 9 * 4 * ppm * out_ch)),
        name="tail",
    )(
        at, jnp.asarray(bin_table).astype(bf16), jnp.asarray(bin_scale), strips,
        w_pool, w_join, jnp.asarray(by_row), jnp.asarray(by_col), jnp.asarray(spread).astype(bf16), conv,
    )
    return out.reshape(sheets, rows, cols, out_ch)


def solution(mesh):
    placed = (P(None, "row", "col", None), P(), P(), P(), P(), P(), P())
    return jax.shard_map(layer, mesh=mesh, in_specs=placed, out_specs=P(None, "row", "col", None), check_vma=False)
```

time: 127 us -> 108 us (0.85)
  local copies, waits for them, and re-layouts: 24.5 us -> 11.8 us
  waiting for transfers between devices: 23.2 us -> 11.7 us
  starting transfers between devices: 36.8 us -> 44.9 us
  Pallas kernels: 38.7 us -> 36.5 us
  other arithmetic: 2.28 us -> 0.7 us
    ppermute x8, waiting for transfers between devices: 15.9 us -> 8.65 us  [the longest x1 5.33 us: layer(): att_west = lax.ppermute(att_edges(cols - 1), 'col', col_fwd)]
    unnamed x27 -> x29, local copies, waits for them, and re-layouts: 13.8 us -> 7.15 us
    all_to_all x2, starting transfers between devices: 14.3 us -> 20.4 us  [the longest x1 12.1 us: layer(): lax.all_to_all(sums, 'row', 0, 0, tiled=True)]
    all_to_all x2, waiting for transfers between devices: 7.35 us -> 3.02 us  [the longest x1 3.02 us: layer(): lax.all_to_all(sums, 'row', 0, 0, tiled=True)]
    squeeze x2 -> x0, local copies, waits for them, and re-layouts: 3.08 us -> none  [pick(): lax.dynamic_index_in_dim(jnp.asarray(table), index, 0, keepdims=False)]
    pallas_call x5, Pallas kernels: 38.7 us -> 36.5 us  [the longest x1 11.1 us: layer(): pl.pallas_call(lambda *refs: attend_kernel((grid_h, grid_w), *refs), grid...]
    broadcast_in_dim x4 -> x1, local copies, waits for them, and re-layouts: 2.06 us -> 0.01 us  [layer(): blank = jnp.zeros((sheets, rows + 2 * HALO, BLOCK - 2 * HALO, width), bf16)]
    ppermute x8, starting transfers between devices: 22.5 us -> 24.4 us  [the longest x1 5.07 us: layer(): east = lax.ppermute(edges(0), 'col', col_bwd)]
  transfers between devices with their start and end apart: 10 -> 10, of which waited for: 5 -> 4; matrix products, arithmetic and copies ran while one was open for 8% -> 4% of each run, Pallas kernels for 9% -> 13%
where the time goes in v2:
time: 108 us; the launch traced here: 106 us
  starting transfers between devices  44.9 us (42%)
  Pallas kernels  36.5 us (34%)
  local copies, waits for them, and re-layouts  11.8 us (11%)
  waiting for transfers between devices  11.7 us (11%)
    all_to_all x1, starting transfers between devices, layer(): lax.all_to_all(sums, 'row', 0, 0, tiled=True)  12.1 us
    pallas_call x1, Pallas kernels, layer(): pl.pallas_call(lambda *refs: attend_kernel((grid_h, grid_w), *refs), grid...  11.1 us
    pallas_call x1, Pallas kernels, layer(): pl.pallas_call(tail_kernel, grid_spec=pltpu.PrefetchScalarGridSpec(num_sc...  10.2 us
    pallas_call x1, Pallas kernels, layer(): pl.pallas_call(conv_kernel, grid=(3,), in_specs=[whole((sheets, area, wid...  8.44 us
    all_to_all x1, starting transfers between devices, layer(): lax.all_to_all(strips, 'col', 0, 0, tiled=True)  8.36 us
    unnamed x29, local copies, waits for them, and re-layouts  7.15 us
    ppermute x1, waiting for transfers between devices, layer(): att_west = lax.ppermute(att_edges(cols - 1), 'col', col_fwd)  5.33 us
    pallas_call x1, Pallas kernels, layer(): pl.pallas_call(project_kernel, grid=(sheets,), in_specs=[per_sheet(area,...  5.15 us
  transfers between devices with their start and end apart: 10, of which 4 were waited for; matrix products, arithmetic and copies ran while one was open for 4% of the time, Pallas kernels for 13%

profile of v2, /device:TPU:2, one launch (start us, length us, event | category | flops | bytes accessed | tf_op | source)
XLA Modules:
  0.0 106.0 jit_solution(14529414558571542906)
XLA Ops:
  0.0 0.0 copy-start.1
  0.0 0.0 copy-start.9
  0.0 1.2 %fusion.2 = (bf16[2,2,32,1024]{3,2,1,0:T(8,128)(2,1)S(1)}, bf16[2,2,32,1024]{3,2,1,0:T(8,128)(2,1)S(1)}) fusion(bf16[2,16,32,1024]{3,2,1,0:T(8,128)(2,1)} %param.14), kind=kLoop, calls=%fused_computation.16 | loop fusion | bytes 1048576 | tf_op jit(solution)/shard_map/slice | solution.py:409
  1.2 1.3 %collective-permute-start.1 = (bf16[2,2,32,1024]{3,2,1,0:T(8,128)(2,1)S(1)}, bf16[2,2,32,1024]{3,2,1,0:T(8,128)(2,1)S(1)}, u32[]{:S(2)}, u32[]{:S(2)}) collective-permute-start(bf16[2,2,32,1024]{3,2,1,0:T(8,128)(2,1)S(1)} %get-tuple-element.19), channel_id=1, source_target_pairs={{8,0},{16,8},{24,16},{32,24},{40,32},{48,40},{56,48},{64,56},{72,6... | collective-permute-start | bytes 786440 | tf_op jit(solution)/shard_map/ppermute | solution.py:409
  2.5 3.0 %collective-permute-start = (bf16[2,2,32,1024]{3,2,1,0:T(8,128)(2,1)S(1)}, bf16[2,2,32,1024]{3,2,1,0:T(8,128)(2,1)S(1)}, u32[]{:S(2)}, u32[]{:S(2)}) collective-permute-start(bf16[2,2,32,1024]{3,2,1,0:T(8,128)(2,1)S(1)} %get-tuple-element.20), channel_id=1, source_target_pairs={{0,8},{8,16},{16,24},{24,32},{32,40},{40,48},{48,56},{56,64},{64,7... | collective-permute-start | bytes 786440 | tf_op jit(solution)/shard_map/ppermute | solution.py:408
  5.6 1.4 %fusion.1 = (bf16[2,16,2,1024]{3,2,1,0:T(2,128)(2,1)S(1)}, bf16[2,16,2,1024]{3,2,1,0:T(2,128)(2,1)S(1)}) fusion(bf16[2,16,32,1024]{3,2,1,0:T(8,128)(2,1)} %param.14), kind=kLoop, calls=%fused_computation.15 | loop fusion | bytes 524288 | tf_op jit(solution)/shard_map/slice | solution.py:412
  7.0 0.1 pad_add_fusion.refs_0_.place_ref
  7.1 0.0 copy-start.4
  7.2 0.1 pad.16.clone
  7.2 0.0 collective-permute-done.1
  7.3 0.0 collective-permute-done
  7.4 0.1 pad_maximum_fusion
  7.5 5.1 %collective-permute-start.2 = (bf16[2,20,2,1024]{3,1,2,0:T(8,128)(2,1)S(1)}, bf16[2,20,2,1024]{3,1,2,0:T(8,128)(2,1)S(1)}, u32[]{:S(2)}, u32[]{:S(2)}) collective-permute-start(bf16[2,20,2,1024]{3,1,2,0:T(8,128)(2,1)S(1)} %pad_maximum_fusion), channel_id=1, source_target_pairs={{1,0},{2,1},{3,2},{4,3},{5,4},{6,5},{7,6},{9,8},{10,9},{11,10},{12... | collective-permute-start | bytes 491528 | tf_op jit(solution)/shard_map/ppermute | solution.py:415
  12.6 0.1 pad_maximum_fusion.1
  12.7 2.3 %collective-permute-start.3 = (bf16[2,20,2,1024]{3,1,2,0:T(8,128)(2,1)S(1)}, bf16[2,20,2,1024]{3,1,2,0:T(8,128)(2,1)S(1)}, u32[]{:S(2)}, u32[]{:S(2)}) collective-permute-start(bf16[2,20,2,1024]{3,1,2,0:T(8,128)(2,1)S(1)} %pad_maximum_fusion.1), channel_id=1, source_target_pairs={{0,1},{1,2},{2,3},{3,4},{4,5},{5,6},{6,7},{8,9},{9,10},{10,11},{11... | collective-permute-start | bytes 491528 | tf_op jit(solution)/shard_map/ppermute | solution.py:414
  14.9 0.0 copy-done.1
  14.9 0.0 copy-done.9
  15.0 0.0 copy-start.5
  15.0 1.6 %copy-done.5 = bf16[1024,1024]{1,0:T(8,128)(2,1)S(1)} copy-done((bf16[1024,1024]{1,0:T(8,128)(2,1)S(1)}, bf16[1024,1024]{1,0:T(8,128)(2,1)}, u32[]{:S(2)}) %copy-start.5) | copy-done | bytes 2097176
  16.6 0.0 copy-start.7
  16.6 1.2 %copy-done.7 = bf16[1024,512]{1,0:T(8,128)(2,1)S(1)} copy-done((bf16[1024,512]{1,0:T(8,128)(2,1)S(1)}, bf16[1024,512]{1,0:T(8,128)(2,1)}, u32[]{:S(2)}) %copy-start.7) | copy-done | bytes 1048600
  17.8 0.0 copy-start.6
  17.8 0.0 copy-start.8
  17.8 0.0 copy-start.10
  17.8 5.1 %project.1 = (f32[2,16,32,512]{3,2,1,0:T(8,128)S(1)}, f32[2,20,32,1024]{3,2,1,0:T(8,128)S(1)}) custom-call(bf16[2,512,1024]{2,1,0:T(8,128)(2,1)S(1)} %bitcast.33, bf16[2,64,1024]{2,1,0:T(8,128)(2,1)S(1)} %bitcast.38, bf16[2,64,1024]{2,1,0:T(8,128)(2,1)S(1)} %bitcast.37, f32[1,1024]{1,0:T(1,128)S(1)} %bitcast.41, bf16[1024,512]{1,0:T(8,128)(2,1)S(1)} %copy-done.7, ...), custom_call_target="tpu_custom_call" | custom-call | flops 3221225472 | bytes 13631488 | tf_op jit(solution)/shard_map/project/pallas_call | solution.py:422
  22.9 0.0 collective-permute-done.2
  22.9 0.2 copy.65
  23.1 0.0 collective-permute-done.3
  23.1 0.2 copy.66
  23.3 0.4 maximum_bitcast_fusion.refs_3_
  23.7 0.0 copy-done.6
  23.7 0.0 copy-done.8
  23.7 0.0 copy-done.10
  23.7 11.1 %attend.1 = (bf16[2,512,1024]{2,1,0:T(8,128)(2,1)S(1)}, bf16[16,16,1024]{2,1,0:T(8,128)(2,1)}) custom-call(s32[2]{0:T(128)S(1)} %pad_add_fusion.refs_0_.place_ref, f32[2,16,32,512]{3,2,1,0:T(8,128)S(1)} %get-tuple-element.9.refs_1_, f32[2,20,32,1024]{3,2,1,0:T(8,128)S(1)} %get-tuple-element.10.refs_2_, ...), custom_call_target="tpu_custom_call" | custom-call | flops 4294967296 | bytes 8388608 | tf_op jit(solution)/shard_map/attend/pallas_call | solution.py:447
  34.8 0.0 copy-start.3
  34.8 1.4 %copy-done.3 = bf16[2,512,1024]{2,1,0:T(8,128)(2,1)} copy-done((bf16[2,512,1024]{2,1,0:T(8,128)(2,1)}, bf16[2,512,1024]{2,1,0:T(8,128)(2,1)S(1)}, u32[]{:S(2)}) %copy-start.3) | copy-done | bytes 2097176
  36.2 0.0 copy-start.2
  36.2 12.1 %all-to-all-start = ((bf16[16,16,1024]{2,1,0:T(8,128)(2,1)}), bf16[16,16,1024]{2,1,0:T(8,128)(2,1)S(1)}, u32[]{:S(2)}, u32[]{:S(2)}) async-start(bf16[16,16,1024]{2,1,0:T(8,128)(2,1)} %get-tuple-element.11), calls=%async_computation | async-start | bytes 1048576 | tf_op jit(solution)/shard_map/all_to_all | solution.py:486
  48.3 1.0 slice_bitcast_fusion
  49.3 1.3 %collective-permute-start.5 = (bf16[2,1,32,1024]{3,2,0,1:T(8,128)(2,1)S(1)}, bf16[2,1,32,1024]{3,2,0,1:T(8,128)(2,1)S(1)}, u32[]{:S(2)}, u32[]{:S(2)}) collective-permute-start(bf16[2,1,32,1024]{3,2,0,1:T(8,128)(2,1)S(1)} %get-tuple-element.15), channel_id=1, source_target_pairs={{8,0},{16,8},{24,16},{32,24},{40,32},{48,40},{56,48},{64,56},{72,6... | collective-permute-start | bytes 393224 | tf_op jit(solution)/shard_map/ppermute | solution.py:485
  50.6 1.4 %fusion = (bf16[2,16,1,1024]{3,2,1,0:T(2,128)(2,1)S(1)}, bf16[2,16,1,1024]{3,2,1,0:T(2,128)(2,1)S(1)}) fusion(bf16[2,16,32,1024]{3,2,1,0:T(8,128)(2,1)} %bitcast.36), kind=kLoop, calls=%fused_computation.14 | loop fusion | bytes 262144 | tf_op jit(solution)/shard_map/slice | solution.py:489
  52.0 3.0 %collective-permute-start.4 = (bf16[2,1,32,1024]{3,2,0,1:T(8,128)(2,1)S(1)}, bf16[2,1,32,1024]{3,2,0,1:T(8,128)(2,1)S(1)}, u32[]{:S(2)}, u32[]{:S(2)}) collective-permute-start(bf16[2,1,32,1024]{3,2,0,1:T(8,128)(2,1)S(1)} %get-tuple-element.16), channel_id=1, source_target_pairs={{0,8},{8,16},{16,24},{24,32},{32,40},{40,48},{48,56},{56,64},{64,7... | collective-permute-start | bytes 393224 | tf_op jit(solution)/shard_map/ppermute | solution.py:484
  55.1 0.0 collective-permute-done.5
  55.1 0.9 collective-permute-done.4
  56.1 3.0 %all-to-all-done = bf16[16,16,1024]{2,1,0:T(8,128)(2,1)S(1)} async-done(((bf16[16,16,1024]{2,1,0:T(8,128)(2,1)}), bf16[16,16,1024]{2,1,0:T(8,128)(2,1)S(1)}, u32[]{:S(2)}, u32[]{:S(2)}) %all-to-all-start) | async-done | bytes 524320 | tf_op jit(solution)/shard_map/all_to_all | solution.py:486
  59.1 0.0 copy-done.4
  59.1 0.0 copy-done.2
  59.1 1.6 %combine.1 = bf16[8,48,1024]{2,1,0:T(8,128)(2,1)} custom-call(s32[2]{0:T(128)S(1)} %pad_add_fusion.refs_0_.place_ref, bf16[8,48,256]{2,1,0:T(8,128)(2,1)S(1)} %copy-done.2, bf16[256,1024]{1,0:T(8,128)(2,1)S(1)} %bitcast.32), custom_call_target="tpu_custom_call" | custom-call | tf_op jit(solution)/shard_map/combine/pallas_call | solution.py:496
  60.8 8.4 %all-to-all-start.1 = ((bf16[8,48,1024]{2,1,0:T(8,128)(2,1)}), bf16[8,48,1024]{2,1,0:T(8,128)(2,1)S(1)}, u32[]{:S(2)}, u32[]{:S(2)}) async-start(bf16[8,48,1024]{2,1,0:T(8,128)(2,1)} %combine.1), calls=%async_computation.1 | async-start | bytes 1572864 | tf_op jit(solution)/shard_map/all_to_all | solution.py:511
  69.2 4.9 %collective-permute-start.6 = (bf16[2,18,1024]{2,1,0:T(8,128)(2,1)S(1)}, bf16[2,18,1024]{2,1,0:T(8,128)(2,1)S(1)}, u32[]{:S(2)}, u32[]{:S(2)}) collective-permute-start(bf16[2,18,1024]{2,1,0:T(8,128)(2,1)S(1)} %pad_maximum_fusion.2), channel_id=1, source_target_pairs={{0,1},{1,2},{2,3},{3,4},{4,5},{5,6},{6,7},{8,9},{9,10},{10,11},{11... | collective-permute-start | bytes 221192 | tf_op jit(solution)/shard_map/ppermute | solution.py:491
  74.1 3.6 %collective-permute-start.7 = (bf16[2,18,1024]{2,1,0:T(8,128)(2,1)S(1)}, bf16[2,18,1024]{2,1,0:T(8,128)(2,1)S(1)}, u32[]{:S(2)}, u32[]{:S(2)}) collective-permute-start(bf16[2,18,1024]{2,1,0:T(8,128)(2,1)S(1)} %pad_maximum_fusion.3), channel_id=1, source_target_pairs={{1,0},{2,1},{3,2},{4,3},{5,4},{6,5},{7,6},{9,8},{10,9},{11,10},{12... | collective-permute-start | bytes 221192 | tf_op jit(solution)/shard_map/ppermute | solution.py:492
  77.7 5.3 %collective-permute-done.6 = bf16[2,18,1024]{2,1,0:T(8,128)(2,1)S(1)} collective-permute-done((bf16[2,18,1024]{2,1,0:T(8,128)(2,1)S(1)}, bf16[2,18,1024]{2,1,0:T(8,128)(2,1)S(1)}, u32[]{:S(2)}, u32[]{:S(2)}) %collective-permute-start.6) | collective-permute-done | bytes 73760 | tf_op jit(solution)/shard_map/ppermute | solution.py:491
  83.0 2.4 %collective-permute-done.7 = bf16[2,18,1024]{2,1,0:T(8,128)(2,1)S(1)} collective-permute-done((bf16[2,18,1024]{2,1,0:T(8,128)(2,1)S(1)}, bf16[2,18,1024]{2,1,0:T(8,128)(2,1)S(1)}, u32[]{:S(2)}, u32[]{:S(2)}) %collective-permute-start.7) | collective-permute-done | bytes 73760 | tf_op jit(solution)/shard_map/ppermute | solution.py:492
  85.4 8.4 %conv.1.conv_ref = f32[2,512,256]{2,1,0:T(8,128)S(1)} custom-call(bf16[2,512,1024]{2,1,0:T(8,128)(2,1)} %copy-done.3, bf16[2,32,1024]{2,1,0:T(8,128)(2,1)S(1)} %bitcast.40, bf16[2,32,1024]{2,1,0:T(8,128)(2,1)S(1)} %bitcast.39, bf16[2,24,1024]{2,1,0:T(8,128)(2,1)S(1)} %pad.7.left_ref, bf16[2,24,1024]{2,1,0:T(8,128)(2,1)S(1)} %pad.8.right_ref, ...), custom_call_target="tpu_custom_call" | custom-call | flops 4831838208 | bytes 6815744 | tf_op jit(solution)/shard_map/conv/pallas_call | solution.py:513
  93.8 0.0 copy-start
  93.9 1.0 copy-done
  94.8 0.0 all-to-all-done.1
  94.8 0.0 copy-start.11
  94.8 0.9 copy-done.11
  95.7 10.2 %tail.1 = bf16[2,512,256]{2,1,0:T(8,128)(2,1)} custom-call(s32[2]{0:T(128)} %copy-done.4, bf16[144,384]{1,0:T(8,128)(2,1)} %constant.38.table_ref, f32[144,1]{1,0:T(8,128)} %constant.30.clone.scale_ref, bf16[384,1024]{1,0:T(8,128)(2,1)} %bitcast.43, bf16[4,1024,512]{2,1,0:T(8,128)(2,1)} %wpool_hbm.1, bf16[3,3,3072,256]{3,2,1,0:T(8,128)(2,1)} %wjoin_hbm.1, ...), custom_call_target="tpu_custom_call" | custom-call | flops 4000000000 | bytes 13631488 | tf_op jit(solution)/shard_map/tail/pallas_call | solution.py:531
  (17 shorter events, 0.4 us)
Async XLA Ops:
  0.0 14.9 %copy-start.1 = (bf16[2,16,32,1024]{3,2,1,0:T(8,128)(2,1)S(1)}, bf16[2,16,32,1024]{3,2,1,0:T(8,128)(2,1)}, u32[]{:S(2)}) copy-start(bf16[2,16,32,1024]{3,2,1,0:T(8,128)(2,1)} %param.14) | copy-start | bytes 6291460
  0.0 14.9 %copy-start.9 = (f32[1024]{0:T(1024)S(1)}, f32[1024]{0:T(1024)}, u32[]{:S(2)}) copy-start(f32[1024]{0:T(1024)} %param.15) | copy-start | bytes 12292
  1.2 6.0 %collective-permute-start.1 = (bf16[2,2,32,1024]{3,2,1,0:T(8,128)(2,1)S(1)}, bf16[2,2,32,1024]{3,2,1,0:T(8,128)(2,1)S(1)}, u32[]{:S(2)}, u32[]{:S(2)}) collective-permute-start(bf16[2,2,32,1024]{3,2,1,0:T(8,128)(2,1)S(1)} %get-tuple-element.19), channel_id=1, source_target_pairs={{8,0},{16,8},{24,16},{32,24},{40,32},{48,40},{56,48},{64,56},{72,6... | collective-permute-start | bytes 786440 | tf_op jit(solution)/shard_map/ppermute | solution.py:409
  2.5 4.8 %collective-permute-start = (bf16[2,2,32,1024]{3,2,1,0:T(8,128)(2,1)S(1)}, bf16[2,2,32,1024]{3,2,1,0:T(8,128)(2,1)S(1)}, u32[]{:S(2)}, u32[]{:S(2)}) collective-permute-start(bf16[2,2,32,1024]{3,2,1,0:T(8,128)(2,1)S(1)} %get-tuple-element.20), channel_id=1, source_target_pairs={{0,8},{8,16},{16,24},{24,32},{32,40},{40,48},{48,56},{56,64},{64,7... | collective-permute-start | bytes 786440 | tf_op jit(solution)/shard_map/ppermute | solution.py:408
  7.1 52.0 %copy-start.4 = (s32[2]{0:T(128)}, s32[2]{0:T(128)S(1)}, u32[]{:S(2)}) copy-start(s32[2]{0:T(128)S(1)} %pad_add_fusion.refs_0_.place_ref) | copy-start | bytes 28
  7.5 15.5 %collective-permute-start.2 = (bf16[2,20,2,1024]{3,1,2,0:T(8,128)(2,1)S(1)}, bf16[2,20,2,1024]{3,1,2,0:T(8,128)(2,1)S(1)}, u32[]{:S(2)}, u32[]{:S(2)}) collective-permute-start(bf16[2,20,2,1024]{3,1,2,0:T(8,128)(2,1)S(1)} %pad_maximum_fusion), channel_id=1, source_target_pairs={{1,0},{2,1},{3,2},{4,3},{5,4},{6,5},{7,6},{9,8},{10,9},{11,10},{12... | collective-permute-start | bytes 491528 | tf_op jit(solution)/shard_map/ppermute | solution.py:415
  12.7 10.5 %collective-permute-start.3 = (bf16[2,20,2,1024]{3,1,2,0:T(8,128)(2,1)S(1)}, bf16[2,20,2,1024]{3,1,2,0:T(8,128)(2,1)S(1)}, u32[]{:S(2)}, u32[]{:S(2)}) collective-permute-start(bf16[2,20,2,1024]{3,1,2,0:T(8,128)(2,1)S(1)} %pad_maximum_fusion.1), channel_id=1, source_target_pairs={{0,1},{1,2},{2,3},{3,4},{4,5},{5,6},{6,7},{8,9},{9,10},{10,11},{11... | collective-permute-start | bytes 491528 | tf_op jit(solution)/shard_map/ppermute | solution.py:414
  15.0 1.6 %copy-start.5 = (bf16[1024,1024]{1,0:T(8,128)(2,1)S(1)}, bf16[1024,1024]{1,0:T(8,128)(2,1)}, u32[]{:S(2)}) copy-start(bf16[1024,1024]{1,0:T(8,128)(2,1)} %refs_6_.1) | copy-start | bytes 6291460
  16.6 1.2 %copy-start.7 = (bf16[1024,512]{1,0:T(8,128)(2,1)S(1)}, bf16[1024,512]{1,0:T(8,128)(2,1)}, u32[]{:S(2)}) copy-start(bf16[1024,512]{1,0:T(8,128)(2,1)} %wq_ref.1) | copy-start | bytes 3145732
  17.8 5.9 %copy-start.6 = (bf16[1024,1024]{1,0:T(8,128)(2,1)S(1)}, bf16[1024,1024]{1,0:T(8,128)(2,1)}, u32[]{:S(2)}) copy-start(bf16[1024,1024]{1,0:T(8,128)(2,1)} %refs_6_.1) | copy-start | bytes 6291460
  17.8 5.9 %copy-start.8 = (bf16[512,1024]{1,0:T(8,128)(2,1)S(1)}, bf16[512,1024]{1,0:T(8,128)(2,1)}, u32[]{:S(2)}) copy-start(bf16[512,1024]{1,0:T(8,128)(2,1)} %refs_7_.1) | copy-start | bytes 3145732
  17.8 5.9 %copy-start.10 = (f32[128,8,48]{2,1,0:T(8,128)S(1)}, f32[128,8,48]{2,1,0:T(8,128)}, u32[]{:S(2)}) copy-start(f32[128,8,48]{2,1,0:T(8,128)} %constant.27.clone.refs_8_) | copy-start | bytes 589828
  34.8 1.4 %copy-start.3 = (bf16[2,512,1024]{2,1,0:T(8,128)(2,1)}, bf16[2,512,1024]{2,1,0:T(8,128)(2,1)S(1)}, u32[]{:S(2)}) copy-start(bf16[2,512,1024]{2,1,0:T(8,128)(2,1)S(1)} %get-tuple-element.12.attended_ref) | copy-start | bytes 6291460
  36.2 22.9 %copy-start.2 = (bf16[8,48,256]{2,1,0:T(8,128)(2,1)S(1)}, bf16[8,48,256]{2,1,0:T(8,128)(2,1)}, u32[]{:S(2)}) copy-start(bf16[8,48,256]{2,1,0:T(8,128)(2,1)} %constant.39.table_ref) | copy-start | bytes 589828
  36.2 22.9 %all-to-all-start = ((bf16[16,16,1024]{2,1,0:T(8,128)(2,1)}), bf16[16,16,1024]{2,1,0:T(8,128)(2,1)S(1)}, u32[]{:S(2)}, u32[]{:S(2)}) async-start(bf16[16,16,1024]{2,1,0:T(8,128)(2,1)} %get-tuple-element.11), calls=%async_computation | async-start | bytes 1048576 | tf_op jit(solution)/shard_map/all_to_all | solution.py:486
  49.3 5.8 %collective-permute-start.5 = (bf16[2,1,32,1024]{3,2,0,1:T(8,128)(2,1)S(1)}, bf16[2,1,32,1024]{3,2,0,1:T(8,128)(2,1)S(1)}, u32[]{:S(2)}, u32[]{:S(2)}) collective-permute-start(bf16[2,1,32,1024]{3,2,0,1:T(8,128)(2,1)S(1)} %get-tuple-element.15), channel_id=1, source_target_pairs={{8,0},{16,8},{24,16},{32,24},{40,32},{48,40},{56,48},{64,56},{72,6... | collective-permute-start | bytes 393224 | tf_op jit(solution)/shard_map/ppermute | solution.py:485
  52.0 4.0 %collective-permute-start.4 = (bf16[2,1,32,1024]{3,2,0,1:T(8,128)(2,1)S(1)}, bf16[2,1,32,1024]{3,2,0,1:T(8,128)(2,1)S(1)}, u32[]{:S(2)}, u32[]{:S(2)}) collective-permute-start(bf16[2,1,32,1024]{3,2,0,1:T(8,128)(2,1)S(1)} %get-tuple-element.16), channel_id=1, source_target_pairs={{0,8},{8,16},{16,24},{24,32},{32,40},{40,48},{48,56},{56,64},{64,7... | collective-permute-start | bytes 393224 | tf_op jit(solution)/shard_map/ppermute | solution.py:484
  60.8 34.1 %all-to-all-start.1 = ((bf16[8,48,1024]{2,1,0:T(8,128)(2,1)}), bf16[8,48,1024]{2,1,0:T(8,128)(2,1)S(1)}, u32[]{:S(2)}, u32[]{:S(2)}) async-start(bf16[8,48,1024]{2,1,0:T(8,128)(2,1)} %combine.1), calls=%async_computation.1 | async-start | bytes 1572864 | tf_op jit(solution)/shard_map/all_to_all | solution.py:511
  69.2 13.8 %collective-permute-start.6 = (bf16[2,18,1024]{2,1,0:T(8,128)(2,1)S(1)}, bf16[2,18,1024]{2,1,0:T(8,128)(2,1)S(1)}, u32[]{:S(2)}, u32[]{:S(2)}) collective-permute-start(bf16[2,18,1024]{2,1,0:T(8,128)(2,1)S(1)} %pad_maximum_fusion.2), channel_id=1, source_target_pairs={{0,1},{1,2},{2,3},{3,4},{4,5},{5,6},{6,7},{8,9},{9,10},{10,11},{11... | collective-permute-start | bytes 221192 | tf_op jit(solution)/shard_map/ppermute | solution.py:491
  74.1 11.3 %collective-permute-start.7 = (bf16[2,18,1024]{2,1,0:T(8,128)(2,1)S(1)}, bf16[2,18,1024]{2,1,0:T(8,128)(2,1)S(1)}, u32[]{:S(2)}, u32[]{:S(2)}) collective-permute-start(bf16[2,18,1024]{2,1,0:T(8,128)(2,1)S(1)} %pad_maximum_fusion.3), channel_id=1, source_target_pairs={{1,0},{2,1},{3,2},{4,3},{5,4},{6,5},{7,6},{9,8},{10,9},{11,10},{12... | collective-permute-start | bytes 221192 | tf_op jit(solution)/shard_map/ppermute | solution.py:492
  93.8 1.0 copy-start
  94.8 0.9 copy-start.11

commit v3 on v2

--- a/solution.py
+++ b/solution.py
@@ -15,9 +15,12 @@
 LEVELS = (1, 2, 3, 6)
 CODED = (6, 3, 2)
 UNITS = 8
-STRIP_UNITS = 24
-STRIP_AT = {6: 0, 3: 12, 2: 18}
-SLOTS = {1: 8, 2: 8, 3: 16, 6: 40}
+STRIP_ALL = 24
+STRIP_ALL_AT = {6: 0, 3: 12, 2: 18}
+STRIP_UNITS = 16
+STRIP_AT = {6: 0, 3: 6, 2: 12}
+NEAR = {1: 1, 2: 2, 3: 3, 6: 3}
+SLOTS = {1: 8, 2: 8, 3: 16, 6: 16}
 TAPS = 9
 f32 = jnp.float32
 bf16 = jnp.bfloat16
@@ -35,14 +38,26 @@
     return found
 
 
+def lower_bin(level, length, place):
+    return max((2 * place + 1) * level - length, 0) // (2 * length)
+
+
+def first_bin(level, length, first, count):
+    start = min(lower_bin(level, length, first - 1), level - NEAR[level])
+    assert min(lower_bin(level, length, first + count) + 1, level - 1) < start + NEAR[level]
+    return start
+
+
 def pool_tables(rows, row_strips, cols, col_strips):
     grid_h, grid_w = rows * row_strips, cols * col_strips
     row_masks = np.zeros((row_strips, col_strips, UNITS, rows), np.float32)
     col_masks = np.zeros((row_strips, col_strips, UNITS, cols), np.float32)
-    strip = np.zeros((col_strips, 2 * STRIP_UNITS, row_strips, 2 * UNITS), np.float32)
+    strip = np.zeros((col_strips, 2 * STRIP_ALL, row_strips, 2 * UNITS), np.float32)
+    near = np.zeros((row_strips, 2 * STRIP_UNITS, 2 * STRIP_ALL), np.float32)
     slots = 2 * sum(SLOTS.values())
-    bins = np.zeros((slots, col_strips, 2 * STRIP_UNITS), np.float32)
-    scale = np.zeros((slots, 1), np.float32)
+    bins = np.zeros((col_strips, slots, col_strips, 2 * STRIP_UNITS), np.float32)
+    row_scale = np.zeros((row_strips, 1, slots), np.float32)
+    col_scale = np.zeros((col_strips, 1, slots), np.float32)
     for c in range(col_strips):
         for r in range(row_strips):
             units = []
@@ -58,31 +73,49 @@
                         at = units.index(key)
                         width = 1 if level == 2 else 2
                         for s in range(2):
-                            target = s * STRIP_UNITS + STRIP_AT[level] + i * width + g
+                            target = s * STRIP_ALL + STRIP_ALL_AT[level] + i * width + g
                             strip[c, target, r, s * UNITS + at] = 1.0
             assert len(units) <= UNITS
+    for r in range(row_strips):
+        for level in CODED:
+            width = 1 if level == 2 else 2
+            start = first_bin(level, grid_h, r * rows, rows)
+            for k in range(NEAR[level] * width):
+                for s in range(2):
+                    source = s * STRIP_ALL + STRIP_ALL_AT[level] + start * width + k
+                    near[r, s * STRIP_UNITS + STRIP_AT[level] + k, source] = 1.0
+    for c in range(col_strips):
         base = 0
         for level in LEVELS:
             source = 2 if level == 1 else level
-            for g, (j, _) in enumerate(bins_of(source, grid_w, c * cols, cols)):
-                for i in range(source):
-                    for s in range(2):
-                        cell = 0 if level == 1 else i * level + j
-                        row = base + s * SLOTS[level] + cell
-                        width = 1 if source == 2 else 2
-                        bins[row, c, s * STRIP_UNITS + STRIP_AT[source] + i * width + g] = 1.0
+            width = 1 if source == 2 else 2
+            start = first_bin(level, grid_w, c * cols, cols)
+            for p in range(col_strips):
+                for g, (j, _) in enumerate(bins_of(source, grid_w, p * cols, cols)):
+                    j = 0 if level == 1 else j - start
+                    if not 0 <= j < NEAR[level]:
+                        continue
+                    for i in range(NEAR[source]):
+                        for s in range(2):
+                            cell = 0 if level == 1 else i * NEAR[level] + j
+                            at = base + s * SLOTS[level] + cell
+                            bins[c, at, p, s * STRIP_UNITS + STRIP_AT[source] + i * width + g] = 1.0
             base += 2 * SLOTS[level]
-    base = 0
-    for level in LEVELS:
-        row_all = bins_of(level, grid_h, 0, grid_h)
-        col_all = bins_of(level, grid_w, 0, grid_w)
-        for s in range(2):
-            for i, row_mask in row_all:
-                for j, col_mask in col_all:
-                    row = base + s * SLOTS[level] + i * level + j
-                    scale[row, 0] = 1.0 / (row_mask.sum() * col_mask.sum())
-        base += 2 * SLOTS[level]
-    return row_masks, col_masks, strip.reshape(col_strips, 2 * STRIP_UNITS, -1), bins.reshape(slots, -1), scale
+    for table, strips, size, along_rows in ((row_scale, row_strips, rows, True), (col_scale, col_strips, cols, False)):
+        for at in range(strips):
+            base = 0
+            for level in LEVELS:
+                length = size * strips
+                start = first_bin(level, length, at * size, size)
+                sizes = [mask.sum() for _, mask in bins_of(level, length, 0, length)]
+                for i in range(NEAR[level]):
+                    for j in range(NEAR[level]):
+                        for s in range(2):
+                            k = base + s * SLOTS[level] + i * NEAR[level] + j
+                            table[at, 0, k] = 1.0 / sizes[start + (i if along_rows else j)]
+                base += 2 * SLOTS[level]
+    strip = strip.reshape(col_strips, 2 * STRIP_ALL, -1)
+    return row_masks, col_masks, strip, near, bins.reshape(col_strips, slots, -1), row_scale, col_scale
 
 
 def upsample_weights(level, length, first, count):
@@ -98,30 +131,36 @@
 
 
 def upsample_tables(rows, row_strips, cols, col_strips):
-    grid_h, grid_w = rows * row_strips, cols * col_strips
     width = TAPS * sum(SLOTS.values())
-    cells = sum(LEVELS)
-    by_row = np.zeros((row_strips, rows, 64), np.float32)
-    by_col = np.zeros((col_strips, cols, 64), np.float32)
+    cells = sum(NEAR.values())
     spread = np.zeros((2, 64, width), np.float32)
+
+    def strips_of(size, strips):
+        table = np.zeros((strips, size, 64), np.float32)
+        length = size * strips
+        for strip in range(strips):
+            first = 0
+            for level in LEVELS:
+                start = first_bin(level, length, strip * size, size)
+                for a in range(3):
+                    w = upsample_weights(level, length, strip * size + a - 1, size)
+                    at = a * cells + first
+                    table[strip, :, at : at + NEAR[level]] = w[:, start : start + NEAR[level]]
+                first += NEAR[level]
+        return table
+
     base, first = 0, 0
     for level in LEVELS:
         for a in range(3):
-            for strip in range(row_strips):
-                w = upsample_weights(level, grid_h, strip * rows + a - 1, rows)
-                by_row[strip, :, a * cells + first : a * cells + first + level] = w
-            for strip in range(col_strips):
-                w = upsample_weights(level, grid_w, strip * cols + a - 1, cols)
-                by_col[strip, :, a * cells + first : a * cells + first + level] = w
             for c in range(3):
-                for i in range(level):
-                    for j in range(level):
-                        at = base + (a * 3 + c) * SLOTS[level] + i * level + j
+                for i in range(NEAR[level]):
+                    for j in range(NEAR[level]):
+                        at = base + (a * 3 + c) * SLOTS[level] + i * NEAR[level] + j
                         spread[0, a * cells + first + i, at] = 1.0
                         spread[1, c * cells + first + j, at] = 1.0
         base += TAPS * SLOTS[level]
-        first += level
-    return by_row, by_col, spread
+        first += NEAR[level]
+    return strips_of(rows, row_strips), strips_of(cols, col_strips), spread
 
 
 def layer_norm(tokens, gain):
@@ -136,14 +175,31 @@
     return jnp.dot(a, b, preferred_element_type=f32)
 
 
-def project_kernel(tokens_ref, above_ref, below_ref, gain_ref, wq_ref, wkv_ref, q_ref, kv_ref):
+def project_kernel(tokens_ref, above_ref, below_ref, gain_ref, wq_hbm, wkv_hbm, q_ref, kv_ref, wq, wkv, sems):
     rows, cols, inner = q_ref.shape
-    gain, wkv = gain_ref[...], wkv_ref[...]
+    first = pl.program_id(0) == 0
+    fetches = (
+        pltpu.make_async_copy(wq_hbm, wq, sems.at[0]),
+        pltpu.make_async_copy(wkv_hbm, wkv, sems.at[1]),
+    )
+
+    @pl.when(first)
+    def _():
+        for fetch in fetches:
+            fetch.start()
+
+    gain = gain_ref[...]
     normed = layer_norm(tokens_ref[...], gain)
-    q_ref[...] = dot(normed, wq_ref[...]).astype(bf16).astype(f32).reshape(rows, cols, inner)
-    kv_ref[HALO : rows + HALO] = dot(normed, wkv).astype(bf16).astype(f32).reshape(rows, cols, -1)
     edge = layer_norm(jnp.concatenate([above_ref[...], below_ref[...]], axis=0), gain)
-    edge = dot(edge, wkv).astype(bf16).astype(f32).reshape(2 * HALO, cols, -1)
+
+    @pl.when(first)
+    def _():
+        for fetch in fetches:
+            fetch.wait()
+
+    q_ref[...] = dot(normed, wq[...]).astype(bf16).astype(f32).reshape(rows, cols, inner)
+    kv_ref[HALO : rows + HALO] = dot(normed, wkv[...]).astype(bf16).astype(f32).reshape(rows, cols, -1)
+    edge = dot(edge, wkv[...]).astype(bf16).astype(f32).reshape(2 * HALO, cols, -1)
     kv_ref[0:HALO] = edge[:HALO]
     kv_ref[rows + HALO :] = edge[HALO:]
 
@@ -266,8 +322,9 @@
     sums_ref[...] = jnp.broadcast_to(sums[None], sums_ref.shape)
 
 
-def combine_kernel(place_ref, table_ref, parts_ref, out_ref):
-    added = dot(table_ref[...].astype(bf16), parts_ref[...]).astype(bf16)
+def combine_kernel(place_ref, near_ref, table_ref, parts_ref, out_ref):
+    table = dot(near_ref[...], table_ref[...]).astype(bf16)
+    added = dot(table, parts_ref[...]).astype(bf16)
     out_ref[...] = jnp.broadcast_to(added[None], out_ref.shape)
 
 
@@ -319,53 +376,62 @@
 
 
 def tail_kernel(
-    place_ref, table_ref, scale_ref, parts_ref, wpool_hbm, wjoin_hbm, by_row_ref, by_col_ref, spread_ref, conv_ref,
-    out_ref, taps, wpool, wjoin, sems,
+    place_ref, table_ref, row_scale_ref, col_scale_ref, parts_ref, wpool_hbm, wjoin_hbm, by_row_ref, by_col_ref,
+    spread_ref, conv_hbm, out_ref, taps, wpool, wjoin, conv, sems,
 ):
     width, ppm = wpool.shape[1], wpool.shape[2]
-    copies = []
-    for index in range(len(LEVELS)):
-        copies.append((
-            pltpu.make_async_copy(wpool_hbm.at[index], wpool.at[index], sems.at[0, index]),
-            pltpu.make_async_copy(
-                wjoin_hbm.at[:, :, width + index * ppm : width + (index + 1) * ppm, :], wjoin.at[index], sems.at[1, index]
-            ),
-        ))
-    for pair in copies:
-        for copy in pair:
-            copy.start()
-    pooled = dot(table_ref[...], parts_ref[...]) * scale_ref[...]
+    count = len(LEVELS)
+    copies = [pltpu.make_async_copy(wpool_hbm.at[k], wpool.at[k], sems.at[k]) for k in range(count)]
+    for k in range(count):
+        lines = slice(width + k * ppm, width + (k + 1) * ppm)
+        copies.append(pltpu.make_async_copy(wjoin_hbm.at[:, :, lines, :], wjoin.at[k], sems.at[count + k]))
+    copies.append(pltpu.make_async_copy(conv_hbm, conv, sems.at[2 * count]))
+    ahead = 3
+    for copy in copies[:ahead]:
+        copy.start()
+
+    def ready(k):
+        copies[k].wait()
+        if k + ahead < len(copies):
+            copies[k + ahead].start()
+
+    rows, cols = by_row_ref.shape[0], by_col_ref.shape[0]
+
+    def along(ref, axis):
+        high, low = split(ref[...])
+        return dot(high, spread_ref[axis]) + dot(low, spread_ref[axis])
+
+    grid = along(by_row_ref, 0)[:, None, :] * along(by_col_ref, 1)[None, :, :]
+    grid_high, grid_low = split(grid.reshape(rows * cols, -1))
+    scale = row_scale_ref[...] * col_scale_ref[...]
+    scale = jnp.broadcast_to(scale, (128, scale.shape[1])).T[:, :1]
+    pooled = dot(table_ref[...], parts_ref[...]) * scale
+    branches = []
     row = 0
+    for index, level in enumerate(LEVELS):
+        slots = SLOTS[level]
+        high, low = split(pooled[row : row + 2 * slots])
+        ready(index)
+        both = dot(jnp.concatenate([high, low], axis=0), wpool[index])
+        high, low = split(jnp.maximum(both[: 2 * slots] + both[2 * slots :], 0.0))
+        branches.append(jnp.concatenate([high, low], axis=0))
+        row += 2 * slots
     at = 0
     for index, level in enumerate(LEVELS):
         slots = SLOTS[level]
-        high, low = split(pooled[row : row + 2 * slots])
-        copies[index][0].wait()
-        both = dot(jnp.concatenate([high, low], axis=0), wpool[index])
-        branch = jnp.maximum(both[: 2 * slots] + both[2 * slots :], 0.0)
-        high, low = split(branch)
-        both = jnp.concatenate([high, low], axis=0)
-        copies[index][1].wait()
+        ready(count + index)
         for a in range(3):
             for c in range(3):
-                tap = dot(both, wjoin[index, a, c])
+                tap = dot(branches[index], wjoin[index, a, c])
                 tap = tap[: 2 * slots] + tap[2 * slots :]
                 start = at + (a * 3 + c) * slots
                 for s in range(2):
                     taps[s, start : start + slots, :] = tap[s * slots : (s + 1) * slots]
-        row += 2 * slots
         at += TAPS * slots
-    rows, cols = by_row_ref.shape[0], by_col_ref.shape[0]
-
-    def along(ref, axis):
-        high, low = split(ref[...])
-        return dot(high, spread_ref[axis]) + dot(low, spread_ref[axis])
-
-    grid = along(by_row_ref, 0)[:, None, :] * along(by_col_ref, 1)[None, :, :]
-    grid_high, grid_low = split(grid.reshape(rows * cols, -1))
+    ready(2 * count)
     for s in range(2):
         high, low = split(taps[s])
-        total = conv_ref[s] + dot(grid_high, high) + dot(grid_low, high) + dot(grid_high, low)
+        total = conv[s] + dot(grid_high, high) + dot(grid_low, high) + dot(grid_high, low)
         out_ref[s] = total.astype(bf16)
 
 
@@ -379,6 +445,10 @@
 
 def whole(shape):
     return pl.BlockSpec(shape, lambda *_: (0,) * len(shape))
+
+
+def in_hbm(x):
+    return pltpu.with_memory_space_constraint(x, pltpu.HBM)
 
 
 def shifts(axis):
@@ -398,7 +468,8 @@
     r, c = lax.axis_index("row"), lax.axis_index("col")
     grid_h, grid_w = rows * row_count, cols * col_count
     gain = norm_gain.reshape(1, width)
-    row_masks, col_masks, strip_table, bin_table, bin_scale = pool_tables(rows, row_count, cols, col_count)
+    tables = pool_tables(rows, row_count, cols, col_count)
+    row_masks, col_masks, strip_table, near_table, bin_table, row_scale, col_scale = tables
     by_row, by_col, spread = upsample_tables(rows, row_count, cols, col_count)
     masks = np.concatenate([row_masks, col_masks], axis=-1).reshape(row_count * col_count, UNITS, rows + cols)
 
@@ -424,17 +495,20 @@
         grid=(sheets,),
         in_specs=[
             per_sheet(area, width), per_sheet(edge, width), per_sheet(edge, width),
-            whole((1, width)), whole((width, inner)), whole((width, wide)),
+            whole((1, width)), pl.BlockSpec(memory_space=pl.ANY), pl.BlockSpec(memory_space=pl.ANY),
         ],
         out_specs=[per_sheet(rows, cols, inner), per_sheet(rows + 2 * HALO, cols, wide)],
         out_shape=[
             jax.ShapeDtypeStruct((sheets, rows, cols, inner), f32),
             jax.ShapeDtypeStruct((sheets, rows + 2 * HALO, cols, wide), f32),
         ],
+        scratch_shapes=[
+            pltpu.VMEM((width, inner), bf16), pltpu.VMEM((width, wide), bf16), pltpu.SemaphoreType.DMA((2,)),
+        ],
         compiler_params=params(28),
         cost_estimate=cost(2 * sheets * area * width * (inner + wide), 2 * (width * (inner + wide) + 5 * sheets * area * width)),
         name="project",
-    )(flat, above.reshape(sheets, edge, width), below.reshape(sheets, edge, width), gain, w_query, w_kv)
+    )(flat, above.reshape(sheets, edge, width), below.reshape(sheets, edge, width), gain, in_hbm(w_query), in_hbm(w_kv))
 
     blank = jnp.zeros((sheets, rows + 2 * HALO, BLOCK - 2 * HALO, width), bf16)
     sides = jnp.concatenate([east, blank, west], axis=2).reshape(sheets, (rows + 2 * HALO) * BLOCK, width)
@@ -499,6 +573,7 @@
             num_scalar_prefetch=1,
             grid=(1,),
             in_specs=[
+                pl.BlockSpec((None,) + near_table.shape[1:], lambda k, p: (p[0], 0, 0)),
                 pl.BlockSpec((None,) + strip_table.shape[1:], lambda k, p: (p[1], 0, 0)),
                 fixed(row_count * sheets * UNITS, width),
             ],
@@ -507,7 +582,7 @@
         out_shape=jax.ShapeDtypeStruct((col_count, strip_rows, width), bf16),
         compiler_params=params(8),
         name="combine",
-    )(at, jnp.asarray(strip_table).astype(bf16), parts)
+    )(at, near_table.astype(bf16), strip_table.astype(bf16), parts)
     strips = lax.all_to_all(strips, "col", 0, 0, tiled=True).reshape(col_count * strip_rows, width)
 
     conv = pl.pallas_call(
@@ -519,7 +594,7 @@
             pl.BlockSpec((3, None, width, out_ch), lambda k: (0, k, 0, 0)),
         ],
         out_specs=whole((sheets, area, out_ch)),
-        out_shape=jax.ShapeDtypeStruct((sheets, area, out_ch), f32),
+        out_shape=pltpu.HBM((sheets, area, out_ch), f32),
         scratch_shapes=[pltpu.VMEM((sheets, area + 2 * cols, width), bf16)],
         compiler_params=params(52),
         cost_estimate=cost(2 * sheets * area * width * 9 * out_ch, 2 * 9 * width * out_ch + 2 * sheets * area * width),
@@ -534,18 +609,22 @@
             num_scalar_prefetch=1,
             grid=(1,),
             in_specs=[
-                fixed(bin_rows, col_count * strip_rows), fixed(bin_rows, 1), fixed(col_count * strip_rows, width),
+                pl.BlockSpec((None,) + bin_table.shape[1:], lambda k, p: (p[1], 0, 0)),
+                pl.BlockSpec((None, 1, bin_rows), lambda k, p: (p[0], 0, 0)),
+                pl.BlockSpec((None, 1, bin_rows), lambda k, p: (p[1], 0, 0)),
+                fixed(col_count * strip_rows, width),
                 pl.BlockSpec(memory_space=pl.ANY), pl.BlockSpec(memory_space=pl.ANY),
                 pl.BlockSpec((None, rows, 64), lambda k, p: (p[0], 0, 0)),
                 pl.BlockSpec((None, cols, 64), lambda k, p: (p[1], 0, 0)),
-                fixed(2, 64, depth), fixed(sheets, area, out_ch),
+                fixed(2, 64, depth), pl.BlockSpec(memory_space=pl.ANY),
             ],
             out_specs=fixed(sheets, area, out_ch),
             scratch_shapes=[
                 pltpu.VMEM((sheets, depth, out_ch), f32),
                 pltpu.VMEM(w_pool.shape, bf16),
                 pltpu.VMEM((len(LEVELS), 3, 3, ppm, out_ch), bf16),
-                pltpu.SemaphoreType.DMA((2, len(LEVELS))),
+                pltpu.VMEM((sheets, area, out_ch), f32),
+                pltpu.SemaphoreType.DMA((2 * len(LEVELS) + 1,)),
             ],
         ),
         out_shape=jax.ShapeDtypeStruct((sheets, area, out_ch), bf16),
@@ -553,8 +632,8 @@
         cost_estimate=cost(4e9, 2 * (w_pool.size + 9 * 4 * ppm * out_ch)),
         name="tail",
     )(
-        at, jnp.asarray(bin_table).astype(bf16), jnp.asarray(bin_scale), strips,
-        w_pool, w_join, jnp.asarray(by_row), jnp.asarray(by_col), jnp.asarray(spread).astype(bf16), conv,
+        at, bin_table.astype(bf16), row_scale, col_scale, strips, in_hbm(w_pool), in_hbm(w_join),
+        by_row, by_col, spread.astype(bf16), in_hbm(conv),
     )
     return out.reshape(sheets, rows, cols, out_ch)
 

time: 108 us -> 102 us (0.944)
  the two profiles are of different devices: /device:TPU:2 before, /device:TPU:24 now
where the time goes in v3:
time: 102 us; the launch traced here: 101 us
  starting transfers between devices  40 us (39%)
  Pallas kernels  39.2 us (38%)
  waiting for transfers between devices  12.6 us (12%)
  local copies, waits for them, and re-layouts  7.93 us (8%)
    pallas_call x1, Pallas kernels, layer(): pl.pallas_call(lambda *refs: attend_kernel((grid_h, grid_w), *refs), grid...  11.1 us
    pallas_call x1, Pallas kernels, layer(): pl.pallas_call(tail_kernel, grid_spec=pltpu.PrefetchScalarGridSpec(num_sc...  9.71 us
    pallas_call x1, Pallas kernels, layer(): pl.pallas_call(conv_kernel, grid=(3,), in_specs=[whole((sheets, area, wid...  9.43 us
    pallas_call x1, Pallas kernels, layer(): pl.pallas_call(project_kernel, grid=(sheets,), in_specs=[per_sheet(area,...  7.27 us
    all_to_all x1, starting transfers between devices, layer(): lax.all_to_all(strips, 'col', 0, 0, tiled=True)  7.27 us
    ppermute x1, waiting for transfers between devices, layer(): att_above = lax.ppermute(att[:, rows - 1:], 'row', row_fwd)  6.43 us
    ppermute x1, waiting for transfers between devices, layer(): above = lax.ppermute(tokens[:, rows - HALO:], 'row', row_fwd)  5.85 us
    ppermute x1, starting transfers between devices, layer(): below = lax.ppermute(tokens[:, :HALO], 'row', row_bwd)  5.57 us
  transfers between devices with their start and end apart: 10, of which 3 were waited for; matrix products, arithmetic and copies ran while one was open for 4% of the time, Pallas kernels for 18%

profile of v3, /device:TPU:24, one launch (start us, length us, event | category | flops | bytes accessed | tf_op | source)
XLA Modules:
  0.0 100.9 jit_solution(7523364694332176865)
XLA Ops:
  0.0 0.0 copy-start
  0.0 0.0 copy-start.7
  0.0 1.2 %fusion.2 = (bf16[2,2,32,1024]{3,2,1,0:T(8,128)(2,1)S(1)}, bf16[2,2,32,1024]{3,2,1,0:T(8,128)(2,1)S(1)}) fusion(bf16[2,16,32,1024]{3,2,1,0:T(8,128)(2,1)} %param.16), kind=kLoop, calls=%fused_computation.16 | loop fusion | bytes 1048576 | tf_op jit(solution)/shard_map/slice | solution.py:480
  1.2 5.6 %collective-permute-start.1 = (bf16[2,2,32,1024]{3,2,1,0:T(8,128)(2,1)S(1)}, bf16[2,2,32,1024]{3,2,1,0:T(8,128)(2,1)S(1)}, u32[]{:S(2)}, u32[]{:S(2)}) collective-permute-start(bf16[2,2,32,1024]{3,2,1,0:T(8,128)(2,1)S(1)} %get-tuple-element.19), channel_id=1, source_target_pairs={{8,0},{16,8},{24,16},{32,24},{40,32},{48,40},{56,48},{64,56},{72,6... | collective-permute-start | bytes 786440 | tf_op jit(solution)/shard_map/ppermute | solution.py:480
  6.8 1.9 %collective-permute-start = (bf16[2,2,32,1024]{3,2,1,0:T(8,128)(2,1)S(1)}, bf16[2,2,32,1024]{3,2,1,0:T(8,128)(2,1)S(1)}, u32[]{:S(2)}, u32[]{:S(2)}) collective-permute-start(bf16[2,2,32,1024]{3,2,1,0:T(8,128)(2,1)S(1)} %get-tuple-element.20), channel_id=1, source_target_pairs={{0,8},{8,16},{16,24},{24,32},{32,40},{40,48},{48,56},{56,64},{64,7... | collective-permute-start | bytes 786440 | tf_op jit(solution)/shard_map/ppermute | solution.py:479
  8.7 1.4 %fusion.1 = (bf16[2,16,2,1024]{3,2,1,0:T(2,128)(2,1)S(1)}, bf16[2,16,2,1024]{3,2,1,0:T(2,128)(2,1)S(1)}) fusion(bf16[2,16,32,1024]{3,2,1,0:T(8,128)(2,1)} %param.16), kind=kLoop, calls=%fused_computation.15 | loop fusion | bytes 524288 | tf_op jit(solution)/shard_map/slice | solution.py:483
  10.1 0.1 pad_add_fusion.refs_0_.place_ref
  10.2 0.0 copy-start.4
  10.3 0.1 pad.16.clone
  10.4 0.3 collective-permute-done.1
  10.7 5.9 %collective-permute-done = bf16[2,2,32,1024]{3,2,1,0:T(8,128)(2,1)S(1)} collective-permute-done((bf16[2,2,32,1024]{3,2,1,0:T(8,128)(2,1)S(1)}, bf16[2,2,32,1024]{3,2,1,0:T(8,128)(2,1)S(1)}, u32[]{:S(2)}, u32[]{:S(2)}) %collective-permute-start) | collective-permute-done | bytes 262176 | tf_op jit(solution)/shard_map/ppermute | solution.py:479
  16.7 0.1 pad_maximum_fusion
  16.8 2.8 %collective-permute-start.2 = (bf16[2,20,2,1024]{3,1,2,0:T(8,128)(2,1)S(1)}, bf16[2,20,2,1024]{3,1,2,0:T(8,128)(2,1)S(1)}, u32[]{:S(2)}, u32[]{:S(2)}) collective-permute-start(bf16[2,20,2,1024]{3,1,2,0:T(8,128)(2,1)S(1)} %pad_maximum_fusion), channel_id=1, source_target_pairs={{1,0},{2,1},{3,2},{4,3},{5,4},{6,5},{7,6},{9,8},{10,9},{11,10},{12... | collective-permute-start | bytes 491528 | tf_op jit(solution)/shard_map/ppermute | solution.py:486
  19.6 0.1 pad_maximum_fusion.1
  19.7 5.4 %collective-permute-start.3 = (bf16[2,20,2,1024]{3,1,2,0:T(8,128)(2,1)S(1)}, bf16[2,20,2,1024]{3,1,2,0:T(8,128)(2,1)S(1)}, u32[]{:S(2)}, u32[]{:S(2)}) collective-permute-start(bf16[2,20,2,1024]{3,1,2,0:T(8,128)(2,1)S(1)} %pad_maximum_fusion.1), channel_id=1, source_target_pairs={{0,1},{1,2},{2,3},{3,4},{4,5},{5,6},{6,7},{8,9},{9,10},{10,11},{11... | collective-permute-start | bytes 491528 | tf_op jit(solution)/shard_map/ppermute | solution.py:485
  25.1 0.0 copy-done
  25.1 0.0 copy-done.7
  25.1 0.0 copy-start.5
  25.1 0.0 copy-start.6
  25.2 0.0 copy-start.8
  25.2 7.3 %project.1 = (f32[2,16,32,512]{3,2,1,0:T(8,128)S(1)}, f32[2,20,32,1024]{3,2,1,0:T(8,128)S(1)}) custom-call(bf16[2,512,1024]{2,1,0:T(8,128)(2,1)S(1)} %bitcast.33, bf16[2,64,1024]{2,1,0:T(8,128)(2,1)S(1)} %bitcast.38, bf16[2,64,1024]{2,1,0:T(8,128)(2,1)S(1)} %bitcast.37, f32[1,1024]{1,0:T(1,128)S(1)} %bitcast.41, bf16[1024,512]{1,0:T(8,128)(2,1)} %wq_hbm.1, ...), custom_call_target="tpu_custom_call" | custom-call | flops 3221225472 | bytes 13631488 | tf_op jit(solution)/shard_map/project/pallas_call | solution.py:493
  32.4 0.0 collective-permute-done.2
  32.5 0.2 copy.67
  32.6 0.0 collective-permute-done.3
  32.6 0.2 copy.68
  32.8 0.4 maximum_bitcast_fusion.refs_3_
  33.2 0.0 copy-done.5
  33.2 0.0 copy-done.6
  33.2 0.0 copy-done.8
  33.2 11.1 %attend.1 = (bf16[2,512,1024]{2,1,0:T(8,128)(2,1)S(1)}, bf16[16,16,1024]{2,1,0:T(8,128)(2,1)}) custom-call(s32[2]{0:T(128)S(1)} %pad_add_fusion.refs_0_.place_ref, f32[2,16,32,512]{3,2,1,0:T(8,128)S(1)} %get-tuple-element.9.refs_1_, f32[2,20,32,1024]{3,2,1,0:T(8,128)S(1)} %get-tuple-element.10.refs_2_, ...), custom_call_target="tpu_custom_call" | custom-call | flops 4294967296 | bytes 8388608 | tf_op jit(solution)/shard_map/attend/pallas_call | solution.py:521
  44.3 0.0 copy-start.3
  44.3 1.3 %copy-done.3 = bf16[2,512,1024]{2,1,0:T(8,128)(2,1)} copy-done((bf16[2,512,1024]{2,1,0:T(8,128)(2,1)}, bf16[2,512,1024]{2,1,0:T(8,128)(2,1)S(1)}, u32[]{:S(2)}) %copy-start.3) | copy-done | bytes 2097176
  45.7 0.0 copy-start.1
  45.7 0.0 copy-start.2
  45.7 3.6 %all-to-all-start = ((bf16[16,16,1024]{2,1,0:T(8,128)(2,1)}), bf16[16,16,1024]{2,1,0:T(8,128)(2,1)S(1)}, u32[]{:S(2)}, u32[]{:S(2)}) async-start(bf16[16,16,1024]{2,1,0:T(8,128)(2,1)} %get-tuple-element.11), calls=%async_computation | async-start | bytes 1048576 | tf_op jit(solution)/shard_map/all_to_all | solution.py:560
  49.3 1.0 slice_bitcast_fusion
  50.3 4.1 %collective-permute-start.5 = (bf16[2,1,32,1024]{3,2,0,1:T(8,128)(2,1)S(1)}, bf16[2,1,32,1024]{3,2,0,1:T(8,128)(2,1)S(1)}, u32[]{:S(2)}, u32[]{:S(2)}) collective-permute-start(bf16[2,1,32,1024]{3,2,0,1:T(8,128)(2,1)S(1)} %get-tuple-element.15), channel_id=1, source_target_pairs={{8,0},{16,8},{24,16},{32,24},{40,32},{48,40},{56,48},{64,56},{72,6... | collective-permute-start | bytes 393224 | tf_op jit(solution)/shard_map/ppermute | solution.py:559
  54.4 1.4 %fusion = (bf16[2,16,1,1024]{3,2,1,0:T(2,128)(2,1)S(1)}, bf16[2,16,1,1024]{3,2,1,0:T(2,128)(2,1)S(1)}) fusion(bf16[2,16,32,1024]{3,2,1,0:T(8,128)(2,1)} %bitcast.36), kind=kLoop, calls=%fused_computation.14 | loop fusion | bytes 262144 | tf_op jit(solution)/shard_map/slice | solution.py:563
  55.9 1.9 %collective-permute-start.4 = (bf16[2,1,32,1024]{3,2,0,1:T(8,128)(2,1)S(1)}, bf16[2,1,32,1024]{3,2,0,1:T(8,128)(2,1)S(1)}, u32[]{:S(2)}, u32[]{:S(2)}) collective-permute-start(bf16[2,1,32,1024]{3,2,0,1:T(8,128)(2,1)S(1)} %get-tuple-element.16), channel_id=1, source_target_pairs={{0,8},{8,16},{16,24},{24,32},{32,40},{40,48},{48,56},{56,64},{64,7... | collective-permute-start | bytes 393224 | tf_op jit(solution)/shard_map/ppermute | solution.py:558
  57.8 0.0 collective-permute-done.5
  57.9 6.4 %collective-permute-done.4 = bf16[2,1,32,1024]{3,2,0,1:T(8,128)(2,1)S(1)} collective-permute-done((bf16[2,1,32,1024]{3,2,0,1:T(8,128)(2,1)S(1)}, bf16[2,1,32,1024]{3,2,0,1:T(8,128)(2,1)S(1)}, u32[]{:S(2)}, u32[]{:S(2)}) %collective-permute-start.4) | collective-permute-done | bytes 131104 | tf_op jit(solution)/shard_map/ppermute | solution.py:558
  64.4 2.9 %collective-permute-start.6 = (bf16[2,18,1024]{2,1,0:T(8,128)(2,1)S(1)}, bf16[2,18,1024]{2,1,0:T(8,128)(2,1)S(1)}, u32[]{:S(2)}, u32[]{:S(2)}) collective-permute-start(bf16[2,18,1024]{2,1,0:T(8,128)(2,1)S(1)} %pad_maximum_fusion.2), channel_id=1, source_target_pairs={{0,1},{1,2},{2,3},{3,4},{4,5},{5,6},{6,7},{8,9},{9,10},{10,11},{11... | collective-permute-start | bytes 221192 | tf_op jit(solution)/shard_map/ppermute | solution.py:565
  67.3 4.5 %collective-permute-start.7 = (bf16[2,18,1024]{2,1,0:T(8,128)(2,1)S(1)}, bf16[2,18,1024]{2,1,0:T(8,128)(2,1)S(1)}, u32[]{:S(2)}, u32[]{:S(2)}) collective-permute-start(bf16[2,18,1024]{2,1,0:T(8,128)(2,1)S(1)} %pad_maximum_fusion.3), channel_id=1, source_target_pairs={{1,0},{2,1},{3,2},{4,3},{5,4},{6,5},{7,6},{9,8},{10,9},{11,10},{12... | collective-permute-start | bytes 221192 | tf_op jit(solution)/shard_map/ppermute | solution.py:566
  71.8 0.0 all-to-all-done
  71.8 0.0 copy-done.4
  71.8 0.0 copy-done.1
  71.8 0.0 copy-done.2
  71.8 1.6 %combine.1 = bf16[8,32,1024]{2,1,0:T(8,128)(2,1)} custom-call(s32[2]{0:T(128)S(1)} %pad_add_fusion.refs_0_.place_ref, bf16[16,32,48]{2,1,0:T(8,128)(2,1)S(1)} %copy-done.2, bf16[8,48,256]{2,1,0:T(8,128)(2,1)S(1)} %copy-done.1, bf16[256,1024]{1,0:T(8,128)(2,1)S(1)} %bitcast.32), custom_call_target="tpu_custom_call" | custom-call | tf_op jit(solution)/shard_map/combine/pallas_call | solution.py:570
  73.5 7.3 %all-to-all-start.1 = ((bf16[8,32,1024]{2,1,0:T(8,128)(2,1)}), bf16[8,32,1024]{2,1,0:T(8,128)(2,1)S(1)}, u32[]{:S(2)}, u32[]{:S(2)}) async-start(bf16[8,32,1024]{2,1,0:T(8,128)(2,1)} %combine.1), calls=%async_computation.1 | async-start | bytes 1048576 | tf_op jit(solution)/shard_map/all_to_all | solution.py:586
  80.8 0.0 collective-permute-done.6
  80.8 0.0 collective-permute-done.7
  80.8 9.4 %conv.1.conv_hbm = f32[2,512,256]{2,1,0:T(8,128)} custom-call(bf16[2,512,1024]{2,1,0:T(8,128)(2,1)} %copy-done.3, bf16[2,32,1024]{2,1,0:T(8,128)(2,1)S(1)} %bitcast.40, bf16[2,32,1024]{2,1,0:T(8,128)(2,1)S(1)} %bitcast.39, bf16[2,24,1024]{2,1,0:T(8,128)(2,1)S(1)} %pad.7.left_ref, bf16[2,24,1024]{2,1,0:T(8,128)(2,1)S(1)} %pad.8.right_ref, ...), custom_call_target="tpu_custom_call" | custom-call | flops 4831838208 | bytes 6815744 | tf_op jit(solution)/shard_map/conv/pallas_call | solution.py:588
  90.2 0.0 all-to-all-done.1
  90.2 0.0 copy-start.9
  90.2 0.8 copy-done.9
  91.0 9.7 %tail.1 = bf16[2,512,256]{2,1,0:T(8,128)(2,1)} custom-call(s32[2]{0:T(128)} %copy-done.4, bf16[8,96,256]{2,1,0:T(8,128)(2,1)} %constant.34.clone.table_ref, f32[16,1,96]{2,1,0:T(1,128)} %constant.35.clone.row_scale_ref, f32[8,1,96]{2,1,0:T(1,128)} %constant.36.clone.col_scale_ref, bf16[256,1024]{1,0:T(8,128)(2,1)} %bitcast.43, ...), custom_call_target="tpu_custom_call" | custom-call | flops 4000000000 | bytes 13631488 | tf_op jit(solution)/shard_map/tail/pallas_call | solution.py:606
  (17 shorter events, 0.4 us)
Async XLA Ops:
  0.0 25.1 %copy-start = (bf16[2,16,32,1024]{3,2,1,0:T(8,128)(2,1)S(1)}, bf16[2,16,32,1024]{3,2,1,0:T(8,128)(2,1)}, u32[]{:S(2)}) copy-start(bf16[2,16,32,1024]{3,2,1,0:T(8,128)(2,1)} %param.16) | copy-start | bytes 6291460
  0.0 25.1 %copy-start.7 = (f32[1024]{0:T(1024)S(1)}, f32[1024]{0:T(1024)}, u32[]{:S(2)}) copy-start(f32[1024]{0:T(1024)} %param.17) | copy-start | bytes 12292
  1.2 9.4 %collective-permute-start.1 = (bf16[2,2,32,1024]{3,2,1,0:T(8,128)(2,1)S(1)}, bf16[2,2,32,1024]{3,2,1,0:T(8,128)(2,1)S(1)}, u32[]{:S(2)}, u32[]{:S(2)}) collective-permute-start(bf16[2,2,32,1024]{3,2,1,0:T(8,128)(2,1)S(1)} %get-tuple-element.19), channel_id=1, source_target_pairs={{8,0},{16,8},{24,16},{32,24},{40,32},{48,40},{56,48},{64,56},{72,6... | collective-permute-start | bytes 786440 | tf_op jit(solution)/shard_map/ppermute | solution.py:480
  6.8 9.8 %collective-permute-start = (bf16[2,2,32,1024]{3,2,1,0:T(8,128)(2,1)S(1)}, bf16[2,2,32,1024]{3,2,1,0:T(8,128)(2,1)S(1)}, u32[]{:S(2)}, u32[]{:S(2)}) collective-permute-start(bf16[2,2,32,1024]{3,2,1,0:T(8,128)(2,1)S(1)} %get-tuple-element.20), channel_id=1, source_target_pairs={{0,8},{8,16},{16,24},{24,32},{32,40},{40,48},{48,56},{56,64},{64,7... | collective-permute-start | bytes 786440 | tf_op jit(solution)/shard_map/ppermute | solution.py:479
  10.2 61.6 %copy-start.4 = (s32[2]{0:T(128)}, s32[2]{0:T(128)S(1)}, u32[]{:S(2)}) copy-start(s32[2]{0:T(128)S(1)} %pad_add_fusion.refs_0_.place_ref) | copy-start | bytes 28
  16.8 15.7 %collective-permute-start.2 = (bf16[2,20,2,1024]{3,1,2,0:T(8,128)(2,1)S(1)}, bf16[2,20,2,1024]{3,1,2,0:T(8,128)(2,1)S(1)}, u32[]{:S(2)}, u32[]{:S(2)}) collective-permute-start(bf16[2,20,2,1024]{3,1,2,0:T(8,128)(2,1)S(1)} %pad_maximum_fusion), channel_id=1, source_target_pairs={{1,0},{2,1},{3,2},{4,3},{5,4},{6,5},{7,6},{9,8},{10,9},{11,10},{12... | collective-permute-start | bytes 491528 | tf_op jit(solution)/shard_map/ppermute | solution.py:486
  19.7 12.9 %collective-permute-start.3 = (bf16[2,20,2,1024]{3,1,2,0:T(8,128)(2,1)S(1)}, bf16[2,20,2,1024]{3,1,2,0:T(8,128)(2,1)S(1)}, u32[]{:S(2)}, u32[]{:S(2)}) collective-permute-start(bf16[2,20,2,1024]{3,1,2,0:T(8,128)(2,1)S(1)} %pad_maximum_fusion.1), channel_id=1, source_target_pairs={{0,1},{1,2},{2,3},{3,4},{4,5},{5,6},{6,7},{8,9},{9,10},{10,11},{11... | collective-permute-start | bytes 491528 | tf_op jit(solution)/shard_map/ppermute | solution.py:485
  25.1 8.1 %copy-start.5 = (bf16[1024,1024]{1,0:T(8,128)(2,1)S(1)}, bf16[1024,1024]{1,0:T(8,128)(2,1)}, u32[]{:S(2)}) copy-start(bf16[1024,1024]{1,0:T(8,128)(2,1)} %refs_6_.1) | copy-start | bytes 6291460
  25.1 8.1 %copy-start.6 = (bf16[512,1024]{1,0:T(8,128)(2,1)S(1)}, bf16[512,1024]{1,0:T(8,128)(2,1)}, u32[]{:S(2)}) copy-start(bf16[512,1024]{1,0:T(8,128)(2,1)} %refs_7_.1) | copy-start | bytes 3145732
  25.2 8.1 %copy-start.8 = (f32[128,8,48]{2,1,0:T(8,128)S(1)}, f32[128,8,48]{2,1,0:T(8,128)}, u32[]{:S(2)}) copy-start(f32[128,8,48]{2,1,0:T(8,128)} %constant.31.clone.refs_8_) | copy-start | bytes 589828
  44.3 1.3 %copy-start.3 = (bf16[2,512,1024]{2,1,0:T(8,128)(2,1)}, bf16[2,512,1024]{2,1,0:T(8,128)(2,1)S(1)}, u32[]{:S(2)}) copy-start(bf16[2,512,1024]{2,1,0:T(8,128)(2,1)S(1)} %get-tuple-element.12.attended_ref) | copy-start | bytes 6291460
  45.7 26.1 %copy-start.1 = (bf16[8,48,256]{2,1,0:T(8,128)(2,1)S(1)}, bf16[8,48,256]{2,1,0:T(8,128)(2,1)}, u32[]{:S(2)}) copy-start(bf16[8,48,256]{2,1,0:T(8,128)(2,1)} %constant.33.clone.table_ref) | copy-start | bytes 589828
  45.7 26.1 %copy-start.2 = (bf16[16,32,48]{2,1,0:T(8,128)(2,1)S(1)}, bf16[16,32,48]{2,1,0:T(8,128)(2,1)}, u32[]{:S(2)}) copy-start(bf16[16,32,48]{2,1,0:T(8,128)(2,1)} %constant.32.clone.near_ref) | copy-start | bytes 147460
  45.7 26.1 %all-to-all-start = ((bf16[16,16,1024]{2,1,0:T(8,128)(2,1)}), bf16[16,16,1024]{2,1,0:T(8,128)(2,1)S(1)}, u32[]{:S(2)}, u32[]{:S(2)}) async-start(bf16[16,16,1024]{2,1,0:T(8,128)(2,1)} %get-tuple-element.11), calls=%async_computation | async-start | bytes 1048576 | tf_op jit(solution)/shard_map/all_to_all | solution.py:560
  50.3 7.6 %collective-permute-start.5 = (bf16[2,1,32,1024]{3,2,0,1:T(8,128)(2,1)S(1)}, bf16[2,1,32,1024]{3,2,0,1:T(8,128)(2,1)S(1)}, u32[]{:S(2)}, u32[]{:S(2)}) collective-permute-start(bf16[2,1,32,1024]{3,2,0,1:T(8,128)(2,1)S(1)} %get-tuple-element.15), channel_id=1, source_target_pairs={{8,0},{16,8},{24,16},{32,24},{40,32},{48,40},{56,48},{64,56},{72,6... | collective-permute-start | bytes 393224 | tf_op jit(solution)/shard_map/ppermute | solution.py:559
  55.9 8.4 %collective-permute-start.4 = (bf16[2,1,32,1024]{3,2,0,1:T(8,128)(2,1)S(1)}, bf16[2,1,32,1024]{3,2,0,1:T(8,128)(2,1)S(1)}, u32[]{:S(2)}, u32[]{:S(2)}) collective-permute-start(bf16[2,1,32,1024]{3,2,0,1:T(8,128)(2,1)S(1)} %get-tuple-element.16), channel_id=1, source_target_pairs={{0,8},{8,16},{16,24},{24,32},{32,40},{40,48},{48,56},{56,64},{64,7... | collective-permute-start | bytes 393224 | tf_op jit(solution)/shard_map/ppermute | solution.py:558
  64.4 16.4 %collective-permute-start.6 = (bf16[2,18,1024]{2,1,0:T(8,128)(2,1)S(1)}, bf16[2,18,1024]{2,1,0:T(8,128)(2,1)S(1)}, u32[]{:S(2)}, u32[]{:S(2)}) collective-permute-start(bf16[2,18,1024]{2,1,0:T(8,128)(2,1)S(1)} %pad_maximum_fusion.2), channel_id=1, source_target_pairs={{0,1},{1,2},{2,3},{3,4},{4,5},{5,6},{6,7},{8,9},{9,10},{10,11},{11... | collective-permute-start | bytes 221192 | tf_op jit(solution)/shard_map/ppermute | solution.py:565
  67.3 13.4 %collective-permute-start.7 = (bf16[2,18,1024]{2,1,0:T(8,128)(2,1)S(1)}, bf16[2,18,1024]{2,1,0:T(8,128)(2,1)S(1)}, u32[]{:S(2)}, u32[]{:S(2)}) collective-permute-start(bf16[2,18,1024]{2,1,0:T(8,128)(2,1)S(1)} %pad_maximum_fusion.3), channel_id=1, source_target_pairs={{1,0},{2,1},{3,2},{4,3},{5,4},{6,5},{7,6},{9,8},{10,9},{11,10},{12... | collective-permute-start | bytes 221192 | tf_op jit(solution)/shard_map/ppermute | solution.py:566
  73.5 16.7 %all-to-all-start.1 = ((bf16[8,32,1024]{2,1,0:T(8,128)(2,1)}), bf16[8,32,1024]{2,1,0:T(8,128)(2,1)S(1)}, u32[]{:S(2)}, u32[]{:S(2)}) async-start(bf16[8,32,1024]{2,1,0:T(8,128)(2,1)} %combine.1), calls=%async_computation.1 | async-start | bytes 1048576 | tf_op jit(solution)/shard_map/all_to_all | solution.py:586
  90.2 0.8 copy-start.9

commit v4 on v3

--- a/solution.py
+++ b/solution.py
@@ -175,30 +175,17 @@
     return jnp.dot(a, b, preferred_element_type=f32)
 
 
-def project_kernel(tokens_ref, above_ref, below_ref, gain_ref, wq_hbm, wkv_hbm, q_ref, kv_ref, wq, wkv, sems):
+def warm_kernel(gain_ref, wq_ref, wkv_ref, out_ref):
+    out_ref[...] = gain_ref[...]
+
+
+def project_kernel(tokens_ref, above_ref, below_ref, gain_ref, wq, wkv, q_ref, kv_ref):
     rows, cols, inner = q_ref.shape
-    first = pl.program_id(0) == 0
-    fetches = (
-        pltpu.make_async_copy(wq_hbm, wq, sems.at[0]),
-        pltpu.make_async_copy(wkv_hbm, wkv, sems.at[1]),
-    )
-
-    @pl.when(first)
-    def _():
-        for fetch in fetches:
-            fetch.start()
-
     gain = gain_ref[...]
     normed = layer_norm(tokens_ref[...], gain)
-    edge = layer_norm(jnp.concatenate([above_ref[...], below_ref[...]], axis=0), gain)
-
-    @pl.when(first)
-    def _():
-        for fetch in fetches:
-            fetch.wait()
-
     q_ref[...] = dot(normed, wq[...]).astype(bf16).astype(f32).reshape(rows, cols, inner)
     kv_ref[HALO : rows + HALO] = dot(normed, wkv[...]).astype(bf16).astype(f32).reshape(rows, cols, -1)
+    edge = layer_norm(jnp.concatenate([above_ref[...], below_ref[...]], axis=0), gain)
     edge = dot(edge, wkv[...]).astype(bf16).astype(f32).reshape(2 * HALO, cols, -1)
     kv_ref[0:HALO] = edge[:HALO]
     kv_ref[rows + HALO :] = edge[HALO:]
@@ -328,46 +315,67 @@
     out_ref[...] = jnp.broadcast_to(added[None], out_ref.shape)
 
 
-def conv_kernel(attended_ref, top_ref, bottom_ref, left_ref, right_ref, w_ref, out_ref, ext):
-    sheets, area, _ = attended_ref.shape
-    cols = top_ref.shape[1]
+def conv_kernel(attended_hbm, top_hbm, bottom_hbm, left_hbm, right_hbm, w_hbm, out_hbm, ext, ends, w, out, sems):
+    sheets, area, width = attended_hbm.shape
+    cols = top_hbm.shape[1]
     rows = area // cols
-    out_ch = out_ref.shape[-1]
-    step = pl.program_id(0)
-
-    def edge(ref, s):
-        total = 0.0
-        for a in range(3):
-            total = total + dot(ref[s], w_ref[a])[a : a + rows]
-        return total.reshape(rows, 1, out_ch)
-
-    def middle(s):
-        total = dot(ext[s, 0:area], w_ref[0])
-        for a in range(1, 3):
-            total = total + dot(ext[s, a * cols : a * cols + area], w_ref[a])
-        return total.reshape(rows, cols, out_ch)
-
-    @pl.when(step == 0)
-    def _():
-        place = lax.broadcasted_iota(jnp.int32, (rows, cols, out_ch), 1)
-        for s in range(sheets):
-            ext[s, 0:cols] = top_ref[s]
-            ext[s, cols : cols + area] = attended_ref[s]
-            ext[s, cols + area :] = bottom_ref[s]
-            part = jnp.where(place == 0, edge(left_ref, s), pltpu.roll(middle(s), 1, 1))
-            out_ref[s] = part.reshape(area, out_ch)
-
-    @pl.when(step == 1)
-    def _():
-        for s in range(sheets):
-            out_ref[s] += middle(s).reshape(area, out_ch)
-
-    @pl.when(step == 2)
-    def _():
-        place = lax.broadcasted_iota(jnp.int32, (rows, cols, out_ch), 1)
-        for s in range(sheets):
-            part = jnp.where(place == cols - 1, edge(right_ref, s), pltpu.roll(middle(s), cols - 1, 1))
-            out_ref[s] += part.reshape(area, out_ch)
+    out_ch = out.shape[-1]
+
+    def tokens(s):
+        return (
+            pltpu.make_async_copy(attended_hbm.at[s], ext.at[s, cols : cols + area], sems.at[0, s]),
+            pltpu.make_async_copy(top_hbm.at[s], ext.at[s, 0:cols], sems.at[1, s]),
+            pltpu.make_async_copy(bottom_hbm.at[s], ext.at[s, cols + area :], sems.at[2, s]),
+            pltpu.make_async_copy(left_hbm.at[s], ends.at[0, s], sems.at[3, s]),
+            pltpu.make_async_copy(right_hbm.at[s], ends.at[1, s], sems.at[4, s]),
+        )
+
+    def taps(c):
+        return pltpu.make_async_copy(w_hbm.at[:, c, 0:width, :], w.at[:, c], sems.at[5, c])
+
+    def result(s):
+        return pltpu.make_async_copy(out.at[s], out_hbm.at[s], sems.at[6, s])
+
+    for copy in tokens(0):
+        copy.start()
+    for c in (1, 0, 2):
+        taps(c).start()
+    for s in range(1, sheets):
+        for copy in tokens(s):
+            copy.start()
+    place = lax.broadcasted_iota(jnp.int32, (rows, cols, out_ch), 1)
+
+    def sheet(s, carry):
+        for copy in tokens(s):
+            copy.wait()
+
+        def edge(side, c):
+            total = 0.0
+            for a in range(3):
+                total = total + dot(ends[side, s], w[a, c])[a : a + rows]
+            return total.reshape(rows, 1, out_ch)
+
+        def middle(c):
+            @pl.when(s == 0)
+            def _():
+                taps(c).wait()
+
+            total = dot(ext[s, 0:area], w[0, c])
+            for a in range(1, 3):
+                total = total + dot(ext[s, a * cols : a * cols + area], w[a, c])
+            return total.reshape(rows, cols, out_ch)
+
+        out[s] = middle(1).reshape(area, out_ch)
+        part = pltpu.roll(middle(0), 1, 1)
+        out[s] += jnp.where(place == 0, edge(0, 0), part).reshape(area, out_ch)
+        part = pltpu.roll(middle(2), cols - 1, 1)
+        out[s] += jnp.where(place == cols - 1, edge(1, 2), part).reshape(area, out_ch)
+        result(s).start()
+        return carry
+
+    lax.fori_loop(0, sheets, sheet, 0)
+    for s in range(sheets):
+        result(s).wait()
 
 
 def split(x):
@@ -376,36 +384,46 @@
 
 
 def tail_kernel(
-    place_ref, table_ref, row_scale_ref, col_scale_ref, parts_ref, wpool_hbm, wjoin_hbm, by_row_ref, by_col_ref,
-    spread_ref, conv_hbm, out_ref, taps, wpool, wjoin, conv, sems,
+    place_ref, table_hbm, row_scale_hbm, col_scale_hbm, parts_hbm, wpool_hbm, wjoin_hbm, by_row_hbm, by_col_hbm,
+    spread_hbm, conv_hbm, out_hbm,
+    table, row_scale, col_scale, parts, by_row, by_col, spread, wpool, wjoin, conv, taps, out, sems,
 ):
     width, ppm = wpool.shape[1], wpool.shape[2]
     count = len(LEVELS)
-    copies = [pltpu.make_async_copy(wpool_hbm.at[k], wpool.at[k], sems.at[k]) for k in range(count)]
+    r, c = place_ref[0], place_ref[1]
+    small = [
+        pltpu.make_async_copy(source, target, sems.at[0, k])
+        for k, (source, target) in enumerate((
+            (parts_hbm, parts), (table_hbm.at[c], table), (row_scale_hbm.at[r], row_scale),
+            (col_scale_hbm.at[c], col_scale), (by_row_hbm.at[r], by_row), (by_col_hbm.at[c], by_col), (spread_hbm, spread),
+        ))
+    ]
+    large = [pltpu.make_async_copy(wpool_hbm.at[k], wpool.at[k], sems.at[1, k]) for k in range(count)]
     for k in range(count):
         lines = slice(width + k * ppm, width + (k + 1) * ppm)
-        copies.append(pltpu.make_async_copy(wjoin_hbm.at[:, :, lines, :], wjoin.at[k], sems.at[count + k]))
-    copies.append(pltpu.make_async_copy(conv_hbm, conv, sems.at[2 * count]))
-    ahead = 3
-    for copy in copies[:ahead]:
+        large.append(pltpu.make_async_copy(wjoin_hbm.at[:, :, lines, :], wjoin.at[k], sems.at[1, count + k]))
+    large.append(pltpu.make_async_copy(conv_hbm, conv, sems.at[1, 2 * count]))
+    ahead = 5
+    for copy in small + large[:ahead]:
         copy.start()
 
     def ready(k):
-        copies[k].wait()
-        if k + ahead < len(copies):
-            copies[k + ahead].start()
-
-    rows, cols = by_row_ref.shape[0], by_col_ref.shape[0]
+        large[k].wait()
+        if k + ahead < len(large):
+            large[k + ahead].start()
+
+    for copy in small:
+        copy.wait()
 
     def along(ref, axis):
         high, low = split(ref[...])
-        return dot(high, spread_ref[axis]) + dot(low, spread_ref[axis])
-
-    grid = along(by_row_ref, 0)[:, None, :] * along(by_col_ref, 1)[None, :, :]
-    grid_high, grid_low = split(grid.reshape(rows * cols, -1))
-    scale = row_scale_ref[...] * col_scale_ref[...]
+        return dot(high, spread[axis]) + dot(low, spread[axis])
+
+    grid = along(by_row, 0)[:, None, :] * along(by_col, 1)[None, :, :]
+    grid_high, grid_low = split(grid.reshape(grid.shape[0] * grid.shape[1], -1))
+    scale = row_scale[...] * col_scale[...]
     scale = jnp.broadcast_to(scale, (128, scale.shape[1])).T[:, :1]
-    pooled = dot(table_ref[...], parts_ref[...]) * scale
+    pooled = dot(table[...], parts[...]) * scale
     branches = []
     row = 0
     for index, level in enumerate(LEVELS):
@@ -421,18 +439,22 @@
         slots = SLOTS[level]
         ready(count + index)
         for a in range(3):
-            for c in range(3):
-                tap = dot(branches[index], wjoin[index, a, c])
+            for b in range(3):
+                tap = dot(branches[index], wjoin[index, a, b])
                 tap = tap[: 2 * slots] + tap[2 * slots :]
-                start = at + (a * 3 + c) * slots
+                start = at + (a * 3 + b) * slots
                 for s in range(2):
                     taps[s, start : start + slots, :] = tap[s * slots : (s + 1) * slots]
         at += TAPS * slots
     ready(2 * count)
+    results = [pltpu.make_async_copy(out.at[s], out_hbm.at[s], sems.at[2, s]) for s in range(2)]
     for s in range(2):
         high, low = split(taps[s])
         total = conv[s] + dot(grid_high, high) + dot(grid_low, high) + dot(grid_high, low)
-        out_ref[s] = total.astype(bf16)
+        out[s] = total.astype(bf16)
+        results[s].start()
+    for copy in results:
+        copy.wait()
 
 
 def cost(flops, nbytes, transcendentals=0):
@@ -488,6 +510,16 @@
     def per_sheet(*dims):
         return pl.BlockSpec((None,) + dims, lambda s: (s,) + (0,) * len(dims))
 
+    wq_near = pltpu.with_memory_space_constraint(w_query, pltpu.VMEM)
+    wkv_near = pltpu.with_memory_space_constraint(w_kv, pltpu.VMEM)
+    gain = pl.pallas_call(
+        warm_kernel,
+        in_specs=[pl.BlockSpec(memory_space=pltpu.VMEM)] * 3,
+        out_specs=pl.BlockSpec(memory_space=pltpu.VMEM),
+        out_shape=jax.ShapeDtypeStruct((1, width), f32),
+        compiler_params=params(4),
+        name="warm",
+    )(gain, wq_near, wkv_near)
     flat = tokens.reshape(sheets, area, width)
     edge = HALO * cols
     q, kv = pl.pallas_call(
@@ -495,20 +527,17 @@
         grid=(sheets,),
         in_specs=[
             per_sheet(area, width), per_sheet(edge, width), per_sheet(edge, width),
-            whole((1, width)), pl.BlockSpec(memory_space=pl.ANY), pl.BlockSpec(memory_space=pl.ANY),
+            whole((1, width)), pl.BlockSpec(memory_space=pltpu.VMEM), pl.BlockSpec(memory_space=pltpu.VMEM),
         ],
         out_specs=[per_sheet(rows, cols, inner), per_sheet(rows + 2 * HALO, cols, wide)],
         out_shape=[
             jax.ShapeDtypeStruct((sheets, rows, cols, inner), f32),
             jax.ShapeDtypeStruct((sheets, rows + 2 * HALO, cols, wide), f32),
         ],
-        scratch_shapes=[
-            pltpu.VMEM((width, inner), bf16), pltpu.VMEM((width, wide), bf16), pltpu.SemaphoreType.DMA((2,)),
-        ],
         compiler_params=params(28),
         cost_estimate=cost(2 * sheets * area * width * (inner + wide), 2 * (width * (inner + wide) + 5 * sheets * area * width)),
         name="project",
-    )(flat, above.reshape(sheets, edge, width), below.reshape(sheets, edge, width), gain, in_hbm(w_query), in_hbm(w_kv))
+    )(flat, above.reshape(sheets, edge, width), below.reshape(sheets, edge, width), gain, wq_near, wkv_near)
 
     blank = jnp.zeros((sheets, rows + 2 * HALO, BLOCK - 2 * HALO, width), bf16)
     sides = jnp.concatenate([east, blank, west], axis=2).reshape(sheets, (rows + 2 * HALO) * BLOCK, width)
@@ -528,7 +557,7 @@
                 pl.BlockSpec((None, rows + 2 * HALO, cols, wide), lambda s, _: (s, 0, 0, 0)),
                 fixed(sheets, (rows + 2 * HALO) * BLOCK, width),
                 pl.BlockSpec((None, area, width), lambda s, _: (s, 0, 0)),
-                fixed(1, width), fixed(width, wide), fixed(inner, width),
+                fixed(1, width), pl.BlockSpec(memory_space=pltpu.VMEM), fixed(inner, width),
                 pl.BlockSpec((None, UNITS, rows + cols), lambda s, p: (p[0] * col_count + p[1], 0, 0)),
             ],
             out_specs=[
@@ -551,7 +580,7 @@
         compiler_params=params(32),
         cost_estimate=cost(2 * sheets * area * inner * width * 4, 2 * sheets * area * width * 4, sheets * blocks * keys * 1024),
         name="attend",
-    )(at, q, kv, sides, flat, gain, w_kv, w_out, jnp.asarray(masks))
+    )(at, q, kv, sides, flat, gain, wkv_near, w_out, masks)
 
     att = attended.reshape(sheets, rows, cols, width)
     strip_rows = sheets * STRIP_UNITS
@@ -587,19 +616,23 @@
 
     conv = pl.pallas_call(
         conv_kernel,
-        grid=(3,),
-        in_specs=[
-            whole((sheets, area, width)), whole((sheets, cols, width)), whole((sheets, cols, width)),
-            whole((sheets, rows + 8, width)), whole((sheets, rows + 8, width)),
-            pl.BlockSpec((3, None, width, out_ch), lambda k: (0, k, 0, 0)),
+        in_specs=[pl.BlockSpec(memory_space=pl.ANY)] * 6,
+        out_specs=pl.BlockSpec(memory_space=pl.ANY),
+        out_shape=pltpu.HBM((sheets, area, out_ch), f32),
+        scratch_shapes=[
+            pltpu.VMEM((sheets, area + 2 * cols, width), bf16),
+            pltpu.VMEM((2, sheets, rows + 8, width), bf16),
+            pltpu.VMEM((3, 3, width, out_ch), bf16),
+            pltpu.VMEM((sheets, area, out_ch), f32),
+            pltpu.SemaphoreType.DMA((7, 3)),
         ],
-        out_specs=whole((sheets, area, out_ch)),
-        out_shape=pltpu.HBM((sheets, area, out_ch), f32),
-        scratch_shapes=[pltpu.VMEM((sheets, area + 2 * cols, width), bf16)],
-        compiler_params=params(52),
+        compiler_params=params(24),
         cost_estimate=cost(2 * sheets * area * width * 9 * out_ch, 2 * 9 * width * out_ch + 2 * sheets * area * width),
         name="conv",
-    )(attended, att_above.reshape(sheets, cols, width), att_below.reshape(sheets, cols, width), att_west, att_east, w_join)
+    )(
+        attended, att_above.reshape(sheets, cols, width), att_below.reshape(sheets, cols, width),
+        att_west, att_east, in_hbm(w_join),
+    )
 
     depth = TAPS * sum(SLOTS.values())
     bin_rows = 2 * sum(SLOTS.values())
@@ -609,26 +642,27 @@
             num_scalar_prefetch=1,
             grid=(1,),
             in_specs=[
-                pl.BlockSpec((None,) + bin_table.shape[1:], lambda k, p: (p[1], 0, 0)),
-                pl.BlockSpec((None, 1, bin_rows), lambda k, p: (p[0], 0, 0)),
-                pl.BlockSpec((None, 1, bin_rows), lambda k, p: (p[1], 0, 0)),
-                fixed(col_count * strip_rows, width),
-                pl.BlockSpec(memory_space=pl.ANY), pl.BlockSpec(memory_space=pl.ANY),
-                pl.BlockSpec((None, rows, 64), lambda k, p: (p[0], 0, 0)),
-                pl.BlockSpec((None, cols, 64), lambda k, p: (p[1], 0, 0)),
-                fixed(2, 64, depth), pl.BlockSpec(memory_space=pl.ANY),
+                pl.BlockSpec(memory_space=pl.ANY) for _ in range(10)
             ],
-            out_specs=fixed(sheets, area, out_ch),
+            out_specs=pl.BlockSpec(memory_space=pl.ANY),
             scratch_shapes=[
-                pltpu.VMEM((sheets, depth, out_ch), f32),
+                pltpu.VMEM(bin_table.shape[1:], bf16),
+                pltpu.VMEM((1, bin_rows), f32),
+                pltpu.VMEM((1, bin_rows), f32),
+                pltpu.VMEM((col_count * strip_rows, width), bf16),
+                pltpu.VMEM((rows, 64), f32),
+                pltpu.VMEM((cols, 64), f32),
+                pltpu.VMEM((2, 64, depth), bf16),
                 pltpu.VMEM(w_pool.shape, bf16),
                 pltpu.VMEM((len(LEVELS), 3, 3, ppm, out_ch), bf16),
                 pltpu.VMEM((sheets, area, out_ch), f32),
-                pltpu.SemaphoreType.DMA((2 * len(LEVELS) + 1,)),
+                pltpu.VMEM((sheets, depth, out_ch), f32),
+                pltpu.VMEM((sheets, area, out_ch), bf16),
+                pltpu.SemaphoreType.DMA((3, 2 * len(LEVELS) + 1)),
             ],
         ),
         out_shape=jax.ShapeDtypeStruct((sheets, area, out_ch), bf16),
-        compiler_params=params(56),
+        compiler_params=params(40),
         cost_estimate=cost(4e9, 2 * (w_pool.size + 9 * 4 * ppm * out_ch)),
         name="tail",
     )(

time: 102 us -> 103 us (level)
  local copies, waits for them, and re-layouts: 7.93 us -> 10 us
  waiting for transfers between devices: 12.6 us -> 11.3 us
    pallas_call x1 -> x2, Pallas kernels: 9.43 us -> 12.6 us  [the longest x1 12.6 us: layer(): pl.pallas_call(conv_kernel, in_specs=[pl.BlockSpec(memory_space=pl.ANY)]...]
    pallas_call x1, Pallas kernels: 7.27 us -> 5.13 us  [layer(): pl.pallas_call(project_kernel, grid=(sheets,), in_specs=[per_sheet(area,...]
    ppermute x1, starting transfers between devices: 4.47 us -> 2.76 us  [layer(): att_east = lax.ppermute(att_edges(0), 'col', col_bwd)]
    ppermute x1, starting transfers between devices: 2.88 us -> 4.57 us  [layer(): att_west = lax.ppermute(att_edges(cols - 1), 'col', col_fwd)]
    unnamed x25 -> x43, local copies, waits for them, and re-layouts: 3.29 us -> 4.65 us
    pallas_call x1, Pallas kernels: 9.71 us -> 8.57 us  [layer(): pl.pallas_call(tail_kernel, grid_spec=pltpu.PrefetchScalarGridSpec(num_sc...]
  transfers between devices with their start and end apart: 10 -> 10, of which waited for: 3 -> 2; matrix products, arithmetic and copies ran while one was open for 4% -> 5% of each run, Pallas kernels for 18% -> 19%
where the time goes in v4:
time: 103 us
  starting transfers between devices  40.1 us (39%)
  Pallas kernels  39.2 us (38%)
  waiting for transfers between devices  11.3 us (11%)
  local copies, waits for them, and re-layouts  10 us (10%)
  other arithmetic  1.35 us (1%)
    pallas_call x1, Pallas kernels, layer(): pl.pallas_call(conv_kernel, in_specs=[pl.BlockSpec(memory_space=pl.ANY)]...  12.6 us
    pallas_call x1, Pallas kernels, layer(): pl.pallas_call(lambda *refs: attend_kernel((grid_h, grid_w), *refs), grid...  11.2 us
    pallas_call x1, Pallas kernels, layer(): pl.pallas_call(tail_kernel, grid_spec=pltpu.PrefetchScalarGridSpec(num_sc...  8.57 us
    all_to_all x1, starting transfers between devices, layer(): lax.all_to_all(strips, 'col', 0, 0, tiled=True)  7.27 us
    ppermute x1, waiting for transfers between devices, layer(): att_above = lax.ppermute(att[:, rows - 1:], 'row', row_fwd)  6.43 us
    ppermute x1, starting transfers between devices, layer(): below = lax.ppermute(tokens[:, :HALO], 'row', row_bwd)  5.55 us
    ppermute x1, starting transfers between devices, layer(): west = lax.ppermute(edges(cols - HALO), 'col', col_fwd)  5.4 us
    pallas_call x1, Pallas kernels, layer(): pl.pallas_call(project_kernel, grid=(sheets,), in_specs=[per_sheet(area,...  5.13 us
  transfers between devices with their start and end apart: 10, of which 2 were waited for; matrix products, arithmetic and copies ran while one was open for 5% of the time, Pallas kernels for 19%

profile of v4, /device:TPU:24, one launch (start us, length us, event | category | flops | bytes accessed | tf_op | source)
XLA Modules:
  0.0 102.6 jit_solution(3155072556330943823)
XLA Ops:
  0.0 0.0 copy-start
  0.0 0.0 copy-start.13
  0.0 1.9 %fusion.2 = (bf16[2,2,32,1024]{3,2,1,0:T(8,128)(2,1)}, bf16[2,2,32,1024]{3,2,1,0:T(8,128)(2,1)S(1)}) fusion(bf16[2,16,32,1024]{3,2,1,0:T(8,128)(2,1)} %param.16), kind=kLoop, calls=%fused_computation.16 | loop fusion | bytes 1048576 | tf_op jit(solution)/shard_map/slice | solution.py:502
  1.9 5.6 %collective-permute-start.1 = (bf16[2,2,32,1024]{3,2,1,0:T(8,128)(2,1)}, bf16[2,2,32,1024]{3,2,1,0:T(8,128)(2,1)S(1)}, u32[]{:S(2)}, u32[]{:S(2)}) collective-permute-start(bf16[2,2,32,1024]{3,2,1,0:T(8,128)(2,1)} %get-tuple-element.19), channel_id=1, source_target_pairs={{8,0},{16,8},{24,16},{32,24},{40,32},{48,40},{56,48},{64,56},{72,6... | collective-permute-start | bytes 786440 | tf_op jit(solution)/shard_map/ppermute | solution.py:502
  7.5 1.9 %collective-permute-start = (bf16[2,2,32,1024]{3,2,1,0:T(8,128)(2,1)S(1)}, bf16[2,2,32,1024]{3,2,1,0:T(8,128)(2,1)S(1)}, u32[]{:S(2)}, u32[]{:S(2)}) collective-permute-start(bf16[2,2,32,1024]{3,2,1,0:T(8,128)(2,1)S(1)} %get-tuple-element.20), channel_id=1, source_target_pairs={{0,8},{8,16},{16,24},{24,32},{32,40},{40,48},{48,56},{56,64},{64,7... | collective-permute-start | bytes 786440 | tf_op jit(solution)/shard_map/ppermute | solution.py:501
  9.4 1.4 %fusion.1 = (bf16[2,16,2,1024]{3,2,1,0:T(2,128)(2,1)S(1)}, bf16[2,16,2,1024]{3,2,1,0:T(2,128)(2,1)S(1)}) fusion(bf16[2,16,32,1024]{3,2,1,0:T(8,128)(2,1)} %param.16), kind=kLoop, calls=%fused_computation.15 | loop fusion | bytes 524288 | tf_op jit(solution)/shard_map/slice | solution.py:505
  10.8 0.1 pad_add_fusion.refs_0_.place_ref
  11.0 0.1 pad.16.clone
  11.1 0.0 copy-done
  11.1 0.0 copy-done.13
  11.1 1.2 %copy-done.1 = bf16[1024,512]{1,0:T(8,128)(2,1)S(1)} copy-done((bf16[1024,512]{1,0:T(8,128)(2,1)S(1)}, bf16[1024,512]{1,0:T(8,128)(2,1)}, u32[]{:S(2)}) %copy-start.1) | copy-done | bytes 1048600
  12.3 0.0 collective-permute-done.1
  12.4 4.9 %collective-permute-done = bf16[2,2,32,1024]{3,2,1,0:T(8,128)(2,1)S(1)} collective-permute-done((bf16[2,2,32,1024]{3,2,1,0:T(8,128)(2,1)S(1)}, bf16[2,2,32,1024]{3,2,1,0:T(8,128)(2,1)S(1)}, u32[]{:S(2)}, u32[]{:S(2)}) %collective-permute-start) | collective-permute-done | bytes 262176 | tf_op jit(solution)/shard_map/ppermute | solution.py:501
  17.4 0.1 pad_maximum_fusion
  17.5 2.8 %collective-permute-start.2 = (bf16[2,20,2,1024]{3,1,2,0:T(8,128)(2,1)S(1)}, bf16[2,20,2,1024]{3,1,2,0:T(8,128)(2,1)S(1)}, u32[]{:S(2)}, u32[]{:S(2)}) collective-permute-start(bf16[2,20,2,1024]{3,1,2,0:T(8,128)(2,1)S(1)} %pad_maximum_fusion), channel_id=1, source_target_pairs={{1,0},{2,1},{3,2},{4,3},{5,4},{6,5},{7,6},{9,8},{10,9},{11,10},{12... | collective-permute-start | bytes 491528 | tf_op jit(solution)/shard_map/ppermute | solution.py:508
  20.3 0.1 pad_maximum_fusion.1
  20.4 5.4 %collective-permute-start.3 = (bf16[2,20,2,1024]{3,1,2,0:T(8,128)(2,1)S(1)}, bf16[2,20,2,1024]{3,1,2,0:T(8,128)(2,1)S(1)}, u32[]{:S(2)}, u32[]{:S(2)}) collective-permute-start(bf16[2,20,2,1024]{3,1,2,0:T(8,128)(2,1)S(1)} %pad_maximum_fusion.1), channel_id=1, source_target_pairs={{0,1},{1,2},{2,3},{3,4},{4,5},{5,6},{6,7},{8,9},{9,10},{10,11},{11... | collective-permute-start | bytes 491528 | tf_op jit(solution)/shard_map/ppermute | solution.py:507
  25.8 0.0 copy-done.2
  25.8 0.0 copy-done.4
  25.8 0.0 copy-start.17
  25.8 0.0 copy-start.18
  25.9 5.1 %project.1 = (f32[2,16,32,512]{3,2,1,0:T(8,128)S(1)}, f32[2,20,32,1024]{3,2,1,0:T(8,128)S(1)}) custom-call(bf16[2,512,1024]{2,1,0:T(8,128)(2,1)S(1)} %bitcast.34, bf16[2,64,1024]{2,1,0:T(8,128)(2,1)S(1)} %bitcast.40, bf16[2,64,1024]{2,1,0:T(8,128)(2,1)S(1)} %bitcast.39, f32[1,1024]{1,0:T(1,128)S(1)} %warm.1.gain_ref.refs_5_, ...), custom_call_target="tpu_custom_call" | custom-call | flops 3221225472 | bytes 13631488 | tf_op jit(solution)/shard_map/project/pallas_call | solution.py:525
  31.0 0.0 collective-permute-done.2
  31.0 0.2 copy.67
  31.2 0.0 collective-permute-done.3
  31.2 0.2 copy.68
  31.4 0.4 maximum_bitcast_fusion.refs_3_
  31.8 0.0 copy-done.17
  31.8 0.0 copy-done.18
  31.8 11.2 %attend.1 = (bf16[2,512,1024]{2,1,0:T(8,128)(2,1)S(1)}, bf16[16,16,1024]{2,1,0:T(8,128)(2,1)}) custom-call(s32[2]{0:T(128)S(1)} %pad_add_fusion.refs_0_.place_ref, f32[2,16,32,512]{3,2,1,0:T(8,128)S(1)} %get-tuple-element.9.refs_1_, f32[2,20,32,1024]{3,2,1,0:T(8,128)S(1)} %get-tuple-element.10.refs_2_, ...), custom_call_target="tpu_custom_call" | custom-call | flops 4294967296 | bytes 8388608 | tf_op jit(solution)/shard_map/attend/pallas_call | solution.py:550
  43.0 1.4 %copy-done.10 = bf16[2,512,1024]{2,1,0:T(8,128)(2,1)} copy-done((bf16[2,512,1024]{2,1,0:T(8,128)(2,1)}, bf16[2,512,1024]{2,1,0:T(8,128)(2,1)S(1)}, u32[]{:S(2)}) %copy-start.10) | copy-done | bytes 2097176
  44.3 3.6 %all-to-all-start = ((bf16[16,16,1024]{2,1,0:T(8,128)(2,1)}), bf16[16,16,1024]{2,1,0:T(8,128)(2,1)S(1)}, u32[]{:S(2)}, u32[]{:S(2)}) async-start(bf16[16,16,1024]{2,1,0:T(8,128)(2,1)} %get-tuple-element.11), calls=%async_computation | async-start | bytes 1048576 | tf_op jit(solution)/shard_map/all_to_all | solution.py:589
  47.9 1.0 slice_bitcast_fusion
  48.9 0.0 copy-start.11
  49.0 4.3 %collective-permute-start.5 = (bf16[2,1,32,1024]{3,2,0,1:T(8,128)(2,1)S(1)}, bf16[2,1,32,1024]{3,2,0,1:T(8,128)(2,1)S(1)}, u32[]{:S(2)}, u32[]{:S(2)}) collective-permute-start(bf16[2,1,32,1024]{3,2,0,1:T(8,128)(2,1)S(1)} %get-tuple-element.15), channel_id=1, source_target_pairs={{8,0},{16,8},{24,16},{32,24},{40,32},{48,40},{56,48},{64,56},{72,6... | collective-permute-start | bytes 393224 | tf_op jit(solution)/shard_map/ppermute | solution.py:588
  53.2 1.4 %fusion = (bf16[2,16,1,1024]{3,2,1,0:T(2,128)(2,1)S(1)}, bf16[2,16,1,1024]{3,2,1,0:T(2,128)(2,1)S(1)}) fusion(bf16[2,16,32,1024]{3,2,1,0:T(8,128)(2,1)} %bitcast.37), kind=kLoop, calls=%fused_computation.14 | loop fusion | bytes 262144 | tf_op jit(solution)/shard_map/slice | solution.py:592
  54.7 1.9 %collective-permute-start.4 = (bf16[2,1,32,1024]{3,2,0,1:T(8,128)(2,1)S(1)}, bf16[2,1,32,1024]{3,2,0,1:T(8,128)(2,1)S(1)}, u32[]{:S(2)}, u32[]{:S(2)}) collective-permute-start(bf16[2,1,32,1024]{3,2,0,1:T(8,128)(2,1)S(1)} %get-tuple-element.16), channel_id=1, source_target_pairs={{0,8},{8,16},{16,24},{24,32},{32,40},{40,48},{48,56},{56,64},{64,7... | collective-permute-start | bytes 393224 | tf_op jit(solution)/shard_map/ppermute | solution.py:587
  56.6 0.0 collective-permute-done.5
  56.7 6.4 %collective-permute-done.4 = bf16[2,1,32,1024]{3,2,0,1:T(8,128)(2,1)S(1)} collective-permute-done((bf16[2,1,32,1024]{3,2,0,1:T(8,128)(2,1)S(1)}, bf16[2,1,32,1024]{3,2,0,1:T(8,128)(2,1)S(1)}, u32[]{:S(2)}, u32[]{:S(2)}) %collective-permute-start.4) | collective-permute-done | bytes 131104 | tf_op jit(solution)/shard_map/ppermute | solution.py:587
  63.2 4.6 %collective-permute-start.6 = (bf16[2,18,1024]{2,1,0:T(8,128)(2,1)S(1)}, bf16[2,18,1024]{2,1,0:T(8,128)(2,1)S(1)}, u32[]{:S(2)}, u32[]{:S(2)}) collective-permute-start(bf16[2,18,1024]{2,1,0:T(8,128)(2,1)S(1)} %pad_maximum_fusion.2), channel_id=1, source_target_pairs={{0,1},{1,2},{2,3},{3,4},{4,5},{5,6},{6,7},{8,9},{9,10},{10,11},{11... | collective-permute-start | bytes 221192 | tf_op jit(solution)/shard_map/ppermute | solution.py:594
  67.8 0.7 pad_maximum_fusion.3
  68.4 2.8 %collective-permute-start.7 = (bf16[2,18,1024]{2,1,0:T(8,128)(2,1)}, bf16[2,18,1024]{2,1,0:T(8,128)(2,1)S(1)}, u32[]{:S(2)}, u32[]{:S(2)}) collective-permute-start(bf16[2,18,1024]{2,1,0:T(8,128)(2,1)} %pad_maximum_fusion.3), channel_id=1, source_target_pairs={{1,0},{2,1},{3,2},{4,3},{5,4},{6,5},{7,6},{9,8},{10,9},{11,10},{12... | collective-permute-start | bytes 221192 | tf_op jit(solution)/shard_map/ppermute | solution.py:595
  71.2 0.0 all-to-all-done
  71.2 0.0 copy-done.5
  71.2 0.0 copy-done.9
  71.2 1.6 %combine.1 = bf16[8,32,1024]{2,1,0:T(8,128)(2,1)} custom-call(s32[2]{0:T(128)S(1)} %pad_add_fusion.refs_0_.place_ref, bf16[16,32,48]{2,1,0:T(8,128)(2,1)S(1)} %copy-done.9, bf16[8,48,256]{2,1,0:T(8,128)(2,1)S(1)} %copy-done.5, bf16[256,1024]{1,0:T(8,128)(2,1)S(1)} %bitcast.32), custom_call_target="tpu_custom_call" | custom-call | tf_op jit(solution)/shard_map/combine/pallas_call | solution.py:599
  72.9 7.3 %all-to-all-start.1 = ((bf16[8,32,1024]{2,1,0:T(8,128)(2,1)}), bf16[8,32,1024]{2,1,0:T(8,128)(2,1)S(1)}, u32[]{:S(2)}, u32[]{:S(2)}) async-start(bf16[8,32,1024]{2,1,0:T(8,128)(2,1)} %combine.1), calls=%async_computation.1 | async-start | bytes 1048576 | tf_op jit(solution)/shard_map/all_to_all | solution.py:615
  80.2 0.0 collective-permute-done.6
  80.2 0.0 collective-permute-done.7
  80.2 0.0 copy-done.15
  80.2 0.0 copy-done.11
  80.2 0.0 copy-start.16
  80.2 0.9 copy-done.16
  81.1 0.0 copy-start.12
  81.1 0.0 copy-start.14
  81.2 12.6 %conv.1.conv_hbm = f32[2,512,256]{2,1,0:T(8,128)} custom-call(bf16[2,512,1024]{2,1,0:T(8,128)(2,1)S(1)} %copy-done.11, bf16[2,32,1024]{2,1,0:T(8,128)(2,1)S(1)} %bitcast.42, bf16[2,32,1024]{2,1,0:T(8,128)(2,1)S(1)} %bitcast.41, bf16[2,24,1024]{2,1,0:T(8,128)(2,1)S(1)} %pad.7.left_hbm, bf16[2,24,1024]{2,1,0:T(8,128)(2,1)S(1)} %pad.8.right_hbm, ...), custom_call_target="tpu_custom_call" | custom-call | flops 4831838208 | bytes 6815744 | tf_op jit(solution)/shard_map/conv/pallas_call | solution.py:617
  93.8 0.0 all-to-all-done.1
  93.8 0.0 copy-done.3
  93.8 0.0 copy-done.6
  93.8 0.0 copy-done.7
  93.8 0.0 copy-done.8
  93.9 0.0 copy-done.12
  93.9 0.0 copy-done.14
  93.9 8.6 %tail.1 = bf16[2,512,256]{2,1,0:T(8,128)(2,1)} custom-call(s32[2]{0:T(128)S(1)} %pad_add_fusion.refs_0_.place_ref, bf16[8,96,256]{2,1,0:T(8,128)(2,1)S(1)} %copy-done.3, f32[16,1,96]{2,1,0:T(1,128)S(1)} %copy-done.12, f32[8,1,96]{2,1,0:T(1,128)S(1)} %copy-done.14, bf16[256,1024]{1,0:T(8,128)(2,1)S(1)} %bitcast.33, bf16[4,1024,512]{2,1,0:T(8,128)(2,1)} %wpool_hbm.1, ...), custom_call_target="tpu_custom_call" | custom-call | flops 4000000000 | bytes 13631488 | tf_op jit(solution)/shard_map/tail/pallas_call | solution.py:639
  (28 shorter events, 0.3 us)
Async XLA Ops:
  0.0 11.1 %copy-start = (bf16[1024,1024]{1,0:T(8,128)(2,1)S(1)}, bf16[1024,1024]{1,0:T(8,128)(2,1)}, u32[]{:S(2)}) copy-start(bf16[1024,1024]{1,0:T(8,128)(2,1)} %refs_6_.1) | copy-start | bytes 6291460
  0.0 11.1 %copy-start.13 = (f32[1024]{0:T(1024)S(1)}, f32[1024]{0:T(1024)}, u32[]{:S(2)}) copy-start(f32[1024]{0:T(1024)} %param.17) | copy-start | bytes 12292
  1.9 10.4 %collective-permute-start.1 = (bf16[2,2,32,1024]{3,2,1,0:T(8,128)(2,1)}, bf16[2,2,32,1024]{3,2,1,0:T(8,128)(2,1)S(1)}, u32[]{:S(2)}, u32[]{:S(2)}) collective-permute-start(bf16[2,2,32,1024]{3,2,1,0:T(8,128)(2,1)} %get-tuple-element.19), channel_id=1, source_target_pairs={{8,0},{16,8},{24,16},{32,24},{40,32},{48,40},{56,48},{64,56},{72,6... | collective-permute-start | bytes 786440 | tf_op jit(solution)/shard_map/ppermute | solution.py:502
  7.5 9.8 %collective-permute-start = (bf16[2,2,32,1024]{3,2,1,0:T(8,128)(2,1)S(1)}, bf16[2,2,32,1024]{3,2,1,0:T(8,128)(2,1)S(1)}, u32[]{:S(2)}, u32[]{:S(2)}) collective-permute-start(bf16[2,2,32,1024]{3,2,1,0:T(8,128)(2,1)S(1)} %get-tuple-element.20), channel_id=1, source_target_pairs={{0,8},{8,16},{16,24},{24,32},{32,40},{40,48},{48,56},{56,64},{64,7... | collective-permute-start | bytes 786440 | tf_op jit(solution)/shard_map/ppermute | solution.py:501
  11.1 1.2 %copy-start.1 = (bf16[1024,512]{1,0:T(8,128)(2,1)S(1)}, bf16[1024,512]{1,0:T(8,128)(2,1)}, u32[]{:S(2)}) copy-start(bf16[1024,512]{1,0:T(8,128)(2,1)} %wq.1) | copy-start | bytes 3145732
  12.3 13.5 %copy-start.2 = (bf16[1024,512]{1,0:T(8,128)(2,1)S(1)}, bf16[1024,512]{1,0:T(8,128)(2,1)}, u32[]{:S(2)}) copy-start(bf16[1024,512]{1,0:T(8,128)(2,1)} %wq.1) | copy-start | bytes 3145732
  12.3 13.5 %copy-start.4 = (bf16[2,16,32,1024]{3,2,1,0:T(8,128)(2,1)S(1)}, bf16[2,16,32,1024]{3,2,1,0:T(8,128)(2,1)}, u32[]{:S(2)}) copy-start(bf16[2,16,32,1024]{3,2,1,0:T(8,128)(2,1)} %param.16) | copy-start | bytes 6291460
  17.5 13.5 %collective-permute-start.2 = (bf16[2,20,2,1024]{3,1,2,0:T(8,128)(2,1)S(1)}, bf16[2,20,2,1024]{3,1,2,0:T(8,128)(2,1)S(1)}, u32[]{:S(2)}, u32[]{:S(2)}) collective-permute-start(bf16[2,20,2,1024]{3,1,2,0:T(8,128)(2,1)S(1)} %pad_maximum_fusion), channel_id=1, source_target_pairs={{1,0},{2,1},{3,2},{4,3},{5,4},{6,5},{7,6},{9,8},{10,9},{11,10},{12... | collective-permute-start | bytes 491528 | tf_op jit(solution)/shard_map/ppermute | solution.py:508
  20.4 10.8 %collective-permute-start.3 = (bf16[2,20,2,1024]{3,1,2,0:T(8,128)(2,1)S(1)}, bf16[2,20,2,1024]{3,1,2,0:T(8,128)(2,1)S(1)}, u32[]{:S(2)}, u32[]{:S(2)}) collective-permute-start(bf16[2,20,2,1024]{3,1,2,0:T(8,128)(2,1)S(1)} %pad_maximum_fusion.1), channel_id=1, source_target_pairs={{0,1},{1,2},{2,3},{3,4},{4,5},{5,6},{6,7},{8,9},{9,10},{10,11},{11... | collective-permute-start | bytes 491528 | tf_op jit(solution)/shard_map/ppermute | solution.py:507
  25.8 5.9 %copy-start.17 = (bf16[512,1024]{1,0:T(8,128)(2,1)S(1)}, bf16[512,1024]{1,0:T(8,128)(2,1)}, u32[]{:S(2)}) copy-start(bf16[512,1024]{1,0:T(8,128)(2,1)} %refs_7_.1) | copy-start | bytes 3145732
  25.8 5.9 %copy-start.18 = (f32[128,8,48]{2,1,0:T(8,128)S(1)}, f32[128,8,48]{2,1,0:T(8,128)}, u32[]{:S(2)}) copy-start(f32[128,8,48]{2,1,0:T(8,128)} %constant.31.clone.refs_8_) | copy-start | bytes 589828
  43.0 1.4 %copy-start.10 = (bf16[2,512,1024]{2,1,0:T(8,128)(2,1)}, bf16[2,512,1024]{2,1,0:T(8,128)(2,1)S(1)}, u32[]{:S(2)}) copy-start(bf16[2,512,1024]{2,1,0:T(8,128)(2,1)S(1)} %get-tuple-element.12.attended_hbm) | copy-start | bytes 6291460
  44.3 26.9 %copy-start.5 = (bf16[8,48,256]{2,1,0:T(8,128)(2,1)S(1)}, bf16[8,48,256]{2,1,0:T(8,128)(2,1)}, u32[]{:S(2)}) copy-start(bf16[8,48,256]{2,1,0:T(8,128)(2,1)} %constant.33.clone.table_ref) | copy-start | bytes 589828
  44.3 26.9 %copy-start.9 = (bf16[16,32,48]{2,1,0:T(8,128)(2,1)S(1)}, bf16[16,32,48]{2,1,0:T(8,128)(2,1)}, u32[]{:S(2)}) copy-start(bf16[16,32,48]{2,1,0:T(8,128)(2,1)} %constant.32.clone.near_ref) | copy-start | bytes 147460
  44.3 26.9 %all-to-all-start = ((bf16[16,16,1024]{2,1,0:T(8,128)(2,1)}), bf16[16,16,1024]{2,1,0:T(8,128)(2,1)S(1)}, u32[]{:S(2)}, u32[]{:S(2)}) async-start(bf16[16,16,1024]{2,1,0:T(8,128)(2,1)} %get-tuple-element.11), calls=%async_computation | async-start | bytes 1048576 | tf_op jit(solution)/shard_map/all_to_all | solution.py:589
  48.9 31.3 %copy-start.11 = (bf16[2,512,1024]{2,1,0:T(8,128)(2,1)S(1)}, bf16[2,512,1024]{2,1,0:T(8,128)(2,1)}, u32[]{:S(2)}) copy-start(bf16[2,512,1024]{2,1,0:T(8,128)(2,1)} %copy-done.10) | copy-start | bytes 6291460
  49.0 7.7 %collective-permute-start.5 = (bf16[2,1,32,1024]{3,2,0,1:T(8,128)(2,1)S(1)}, bf16[2,1,32,1024]{3,2,0,1:T(8,128)(2,1)S(1)}, u32[]{:S(2)}, u32[]{:S(2)}) collective-permute-start(bf16[2,1,32,1024]{3,2,0,1:T(8,128)(2,1)S(1)} %get-tuple-element.15), channel_id=1, source_target_pairs={{8,0},{16,8},{24,16},{32,24},{40,32},{48,40},{56,48},{64,56},{72,6... | collective-permute-start | bytes 393224 | tf_op jit(solution)/shard_map/ppermute | solution.py:588
  54.7 8.4 %collective-permute-start.4 = (bf16[2,1,32,1024]{3,2,0,1:T(8,128)(2,1)S(1)}, bf16[2,1,32,1024]{3,2,0,1:T(8,128)(2,1)S(1)}, u32[]{:S(2)}, u32[]{:S(2)}) collective-permute-start(bf16[2,1,32,1024]{3,2,0,1:T(8,128)(2,1)S(1)} %get-tuple-element.16), channel_id=1, source_target_pairs={{0,8},{8,16},{16,24},{24,32},{32,40},{40,48},{48,56},{56,64},{64,7... | collective-permute-start | bytes 393224 | tf_op jit(solution)/shard_map/ppermute | solution.py:587
  63.1 17.1 %copy-start.15 = (bf16[2,1,32,1024]{3,2,0,1:T(8,128)(2,1)}, bf16[2,1,32,1024]{3,2,0,1:T(8,128)(2,1)S(1)}, u32[]{:S(2)}) copy-start(bf16[2,1,32,1024]{3,2,0,1:T(8,128)(2,1)S(1)} %collective-permute-done.4) | copy-start | bytes 393220
  63.2 17.0 %collective-permute-start.6 = (bf16[2,18,1024]{2,1,0:T(8,128)(2,1)S(1)}, bf16[2,18,1024]{2,1,0:T(8,128)(2,1)S(1)}, u32[]{:S(2)}, u32[]{:S(2)}) collective-permute-start(bf16[2,18,1024]{2,1,0:T(8,128)(2,1)S(1)} %pad_maximum_fusion.2), channel_id=1, source_target_pairs={{0,1},{1,2},{2,3},{3,4},{4,5},{5,6},{6,7},{8,9},{9,10},{10,11},{11... | collective-permute-start | bytes 221192 | tf_op jit(solution)/shard_map/ppermute | solution.py:594
  68.4 11.7 %collective-permute-start.7 = (bf16[2,18,1024]{2,1,0:T(8,128)(2,1)}, bf16[2,18,1024]{2,1,0:T(8,128)(2,1)S(1)}, u32[]{:S(2)}, u32[]{:S(2)}) collective-permute-start(bf16[2,18,1024]{2,1,0:T(8,128)(2,1)} %pad_maximum_fusion.3), channel_id=1, source_target_pairs={{1,0},{2,1},{3,2},{4,3},{5,4},{6,5},{7,6},{9,8},{10,9},{11,10},{12... | collective-permute-start | bytes 221192 | tf_op jit(solution)/shard_map/ppermute | solution.py:595
  72.9 20.9 %all-to-all-start.1 = ((bf16[8,32,1024]{2,1,0:T(8,128)(2,1)}), bf16[8,32,1024]{2,1,0:T(8,128)(2,1)S(1)}, u32[]{:S(2)}, u32[]{:S(2)}) async-start(bf16[8,32,1024]{2,1,0:T(8,128)(2,1)} %combine.1), calls=%async_computation.1 | async-start | bytes 1048576 | tf_op jit(solution)/shard_map/all_to_all | solution.py:615
  80.2 0.9 copy-start.16
  81.1 12.7 %copy-start.3 = (bf16[8,96,256]{2,1,0:T(8,128)(2,1)S(1)}, bf16[8,96,256]{2,1,0:T(8,128)(2,1)}, u32[]{:S(2)}) copy-start(bf16[8,96,256]{2,1,0:T(8,128)(2,1)} %constant.34.clone.table_hbm) | copy-start | bytes 1179652
  81.1 12.7 %copy-start.6 = (bf16[2,64,432]{2,1,0:T(8,128)(2,1)S(1)}, bf16[2,64,432]{2,1,0:T(8,128)(2,1)}, u32[]{:S(2)}) copy-start(bf16[2,64,432]{2,1,0:T(8,128)(2,1)} %constant.39.clone.spread_hbm) | copy-start | bytes 331780
  81.1 12.7 %copy-start.7 = (f32[8,32,64]{2,1,0:T(8,128)S(1)}, f32[8,32,64]{2,1,0:T(8,128)}, u32[]{:S(2)}) copy-start(f32[8,32,64]{2,1,0:T(8,128)} %constant.38.clone.by_col_hbm) | copy-start | bytes 196612
  81.1 12.7 %copy-start.8 = (f32[16,16,64]{2,1,0:T(8,128)S(1)}, f32[16,16,64]{2,1,0:T(8,128)}, u32[]{:S(2)}) copy-start(f32[16,16,64]{2,1,0:T(8,128)} %constant.37.clone.by_row_hbm) | copy-start | bytes 196612
  81.1 12.7 %copy-start.12 = (f32[16,1,96]{2,1,0:T(1,128)S(1)}, f32[16,1,96]{2,1,0:T(1,128)}, u32[]{:S(2)}) copy-start(f32[16,1,96]{2,1,0:T(1,128)} %constant.35.clone.row_scale_hbm) | copy-start | bytes 18436
  81.1 12.7 %copy-start.14 = (f32[8,1,96]{2,1,0:T(1,128)S(1)}, f32[8,1,96]{2,1,0:T(1,128)}, u32[]{:S(2)}) copy-start(f32[8,1,96]{2,1,0:T(1,128)} %constant.36.clone.col_scale_hbm) | copy-start | bytes 9220

commit v5 on v4

--- a/solution.py
+++ b/solution.py
@@ -211,7 +211,7 @@
 
 def attend_kernel(
     grid_shape, place_ref, q_ref, kv_ref, sides_ref, tokens_ref, gain_ref, wkv_ref, wout_ref, masks_ref,
-    attended_ref, sums_ref, sides, context, bias, pool, scores, weights,
+    attended_ref, sums_ref, first_row_ref, last_row_ref, first_col_ref, last_col_ref, sides, context, bias, pool, scores, weights,
 ):
     rows, cols, inner = q_ref.shape
     groups = cols // BLOCK
@@ -305,6 +305,11 @@
     mixed = context[...].reshape(rows * cols, inner).astype(bf16)
     attended = (tokens_ref[...].astype(f32) + dot(mixed, wout_ref[...])).astype(bf16)
     attended_ref[...] = attended
+    first_row_ref[...] = attended[:cols]
+    last_row_ref[...] = attended[(rows - 1) * cols :]
+    by_place = attended.astype(f32).reshape(rows, cols, attended.shape[-1])
+    first_col_ref[...] = by_place[:, 0].astype(bf16)
+    last_col_ref[...] = by_place[:, cols - 1].astype(bf16)
     sums = dot(pool[...], attended).astype(bf16)
     sums_ref[...] = jnp.broadcast_to(sums[None], sums_ref.shape)
 
@@ -315,67 +320,43 @@
     out_ref[...] = jnp.broadcast_to(added[None], out_ref.shape)
 
 
-def conv_kernel(attended_hbm, top_hbm, bottom_hbm, left_hbm, right_hbm, w_hbm, out_hbm, ext, ends, w, out, sems):
-    sheets, area, width = attended_hbm.shape
-    cols = top_hbm.shape[1]
+def conv_kernel(attended_ref, top_ref, bottom_ref, left_ref, right_ref, w_ref, out_ref, ext):
+    area, _ = attended_ref.shape
+    cols = top_ref.shape[0]
     rows = area // cols
-    out_ch = out.shape[-1]
-
-    def tokens(s):
-        return (
-            pltpu.make_async_copy(attended_hbm.at[s], ext.at[s, cols : cols + area], sems.at[0, s]),
-            pltpu.make_async_copy(top_hbm.at[s], ext.at[s, 0:cols], sems.at[1, s]),
-            pltpu.make_async_copy(bottom_hbm.at[s], ext.at[s, cols + area :], sems.at[2, s]),
-            pltpu.make_async_copy(left_hbm.at[s], ends.at[0, s], sems.at[3, s]),
-            pltpu.make_async_copy(right_hbm.at[s], ends.at[1, s], sems.at[4, s]),
-        )
-
-    def taps(c):
-        return pltpu.make_async_copy(w_hbm.at[:, c, 0:width, :], w.at[:, c], sems.at[5, c])
-
-    def result(s):
-        return pltpu.make_async_copy(out.at[s], out_hbm.at[s], sems.at[6, s])
-
-    for copy in tokens(0):
-        copy.start()
-    for c in (1, 0, 2):
-        taps(c).start()
-    for s in range(1, sheets):
-        for copy in tokens(s):
-            copy.start()
-    place = lax.broadcasted_iota(jnp.int32, (rows, cols, out_ch), 1)
-
-    def sheet(s, carry):
-        for copy in tokens(s):
-            copy.wait()
-
-        def edge(side, c):
-            total = 0.0
-            for a in range(3):
-                total = total + dot(ends[side, s], w[a, c])[a : a + rows]
-            return total.reshape(rows, 1, out_ch)
-
-        def middle(c):
-            @pl.when(s == 0)
-            def _():
-                taps(c).wait()
-
-            total = dot(ext[s, 0:area], w[0, c])
-            for a in range(1, 3):
-                total = total + dot(ext[s, a * cols : a * cols + area], w[a, c])
-            return total.reshape(rows, cols, out_ch)
-
-        out[s] = middle(1).reshape(area, out_ch)
-        part = pltpu.roll(middle(0), 1, 1)
-        out[s] += jnp.where(place == 0, edge(0, 0), part).reshape(area, out_ch)
-        part = pltpu.roll(middle(2), cols - 1, 1)
-        out[s] += jnp.where(place == cols - 1, edge(1, 2), part).reshape(area, out_ch)
-        result(s).start()
-        return carry
-
-    lax.fori_loop(0, sheets, sheet, 0)
-    for s in range(sheets):
-        result(s).wait()
+    out_ch = out_ref.shape[-1]
+    s, step = pl.program_id(0), pl.program_id(1)
+
+    def edge(ref):
+        total = 0.0
+        for a in range(3):
+            total = total + dot(ref[...], w_ref[a])[a : a + rows]
+        return total.reshape(rows, 1, out_ch)
+
+    def middle():
+        total = dot(ext[0:area], w_ref[0])
+        for a in range(1, 3):
+            total = total + dot(ext[a * cols : a * cols + area], w_ref[a])
+        return total.reshape(rows, cols, out_ch)
+
+    @pl.when(step == 0)
+    def _():
+        ext[0:cols] = top_ref[...]
+        ext[cols : cols + area] = attended_ref[...]
+        ext[cols + area :] = bottom_ref[...]
+        place = lax.broadcasted_iota(jnp.int32, (rows, cols, out_ch), 1)
+        part = jnp.where(place == 0, edge(left_ref), pltpu.roll(middle(), 1, 1))
+        out_ref[s] = part.reshape(area, out_ch)
+
+    @pl.when(step == 1)
+    def _():
+        out_ref[s] += middle().reshape(area, out_ch)
+
+    @pl.when(step == 2)
+    def _():
+        place = lax.broadcasted_iota(jnp.int32, (rows, cols, out_ch), 1)
+        part = jnp.where(place == cols - 1, edge(right_ref), pltpu.roll(middle(), cols - 1, 1))
+        out_ref[s] += part.reshape(area, out_ch)
 
 
 def split(x):
@@ -385,8 +366,8 @@
 
 def tail_kernel(
     place_ref, table_hbm, row_scale_hbm, col_scale_hbm, parts_hbm, wpool_hbm, wjoin_hbm, by_row_hbm, by_col_hbm,
-    spread_hbm, conv_hbm, out_hbm,
-    table, row_scale, col_scale, parts, by_row, by_col, spread, wpool, wjoin, conv, taps, out, sems,
+    spread_hbm, conv, out_hbm,
+    table, row_scale, col_scale, parts, by_row, by_col, spread, wpool, wjoin, taps, out, sems,
 ):
     width, ppm = wpool.shape[1], wpool.shape[2]
     count = len(LEVELS)
@@ -402,7 +383,6 @@
     for k in range(count):
         lines = slice(width + k * ppm, width + (k + 1) * ppm)
         large.append(pltpu.make_async_copy(wjoin_hbm.at[:, :, lines, :], wjoin.at[k], sems.at[1, count + k]))
-    large.append(pltpu.make_async_copy(conv_hbm, conv, sems.at[1, 2 * count]))
     ahead = 5
     for copy in small + large[:ahead]:
         copy.start()
@@ -446,7 +426,6 @@
                 for s in range(2):
                     taps[s, start : start + slots, :] = tap[s * slots : (s + 1) * slots]
         at += TAPS * slots
-    ready(2 * count)
     results = [pltpu.make_async_copy(out.at[s], out_hbm.at[s], sems.at[2, s]) for s in range(2)]
     for s in range(2):
         high, low = split(taps[s])
@@ -508,7 +487,7 @@
     east = lax.ppermute(edges(0), "col", col_bwd)
 
     def per_sheet(*dims):
-        return pl.BlockSpec((None,) + dims, lambda s: (s,) + (0,) * len(dims))
+        return pl.BlockSpec((None,) + dims, lambda s, *_: (s,) + (0,) * len(dims))
 
     wq_near = pltpu.with_memory_space_constraint(w_query, pltpu.VMEM)
     wkv_near = pltpu.with_memory_space_constraint(w_kv, pltpu.VMEM)
@@ -547,7 +526,7 @@
     def fixed(*dims):
         return whole(dims)
 
-    attended, sums = pl.pallas_call(
+    attended, sums, first_row, last_row, first_col, last_col = pl.pallas_call(
         lambda *refs: attend_kernel((grid_h, grid_w), *refs),
         grid_spec=pltpu.PrefetchScalarGridSpec(
             num_scalar_prefetch=1,
@@ -563,6 +542,7 @@
             out_specs=[
                 pl.BlockSpec((None, area, width), lambda s, _: (s, 0, 0)),
                 pl.BlockSpec((row_count, UNITS, width), lambda s, _: (0, s, 0)),
+                per_sheet(cols, width), per_sheet(cols, width), per_sheet(rows, width), per_sheet(rows, width),
             ],
             scratch_shapes=[
                 pltpu.VMEM((sheets, rows + 2 * HALO, BLOCK, wide), f32),
@@ -574,25 +554,28 @@
             ],
         ),
         out_shape=[
-            jax.ShapeDtypeStruct((sheets, area, width), bf16),
+            pltpu.HBM((sheets, area, width), bf16),
             jax.ShapeDtypeStruct((row_count, sheets * UNITS, width), bf16),
+            jax.ShapeDtypeStruct((sheets, cols, width), bf16),
+            jax.ShapeDtypeStruct((sheets, cols, width), bf16),
+            jax.ShapeDtypeStruct((sheets, rows, width), bf16),
+            jax.ShapeDtypeStruct((sheets, rows, width), bf16),
         ],
         compiler_params=params(32),
         cost_estimate=cost(2 * sheets * area * inner * width * 4, 2 * sheets * area * width * 4, sheets * blocks * keys * 1024),
         name="attend",
     )(at, q, kv, sides, flat, gain, wkv_near, w_out, masks)
 
-    att = attended.reshape(sheets, rows, cols, width)
     strip_rows = sheets * STRIP_UNITS
-    att_above = lax.ppermute(att[:, rows - 1 :], "row", row_fwd)
-    att_below = lax.ppermute(att[:, :1], "row", row_bwd)
+    att_above = lax.ppermute(last_row, "row", row_fwd)
+    att_below = lax.ppermute(first_row, "row", row_bwd)
     parts = lax.all_to_all(sums, "row", 0, 0, tiled=True).reshape(row_count * sheets * UNITS, width)
 
-    def att_edges(first):
-        return jnp.concatenate([x[:, :, first] for x in (att_above, att, att_below)], axis=1)
-
-    att_west = lax.ppermute(att_edges(cols - 1), "col", col_fwd)
-    att_east = lax.ppermute(att_edges(0), "col", col_bwd)
+    def att_edges(middle, at):
+        return jnp.concatenate([att_above[:, at : at + 1], middle, att_below[:, at : at + 1]], axis=1)
+
+    att_west = lax.ppermute(att_edges(last_col, cols - 1), "col", col_fwd)
+    att_east = lax.ppermute(att_edges(first_col, 0), "col", col_bwd)
     pad = ((0, 0), (0, 6), (0, 0))
     att_west, att_east = jnp.pad(att_west, pad), jnp.pad(att_east, pad)
 
@@ -616,23 +599,20 @@
 
     conv = pl.pallas_call(
         conv_kernel,
-        in_specs=[pl.BlockSpec(memory_space=pl.ANY)] * 6,
-        out_specs=pl.BlockSpec(memory_space=pl.ANY),
-        out_shape=pltpu.HBM((sheets, area, out_ch), f32),
-        scratch_shapes=[
-            pltpu.VMEM((sheets, area + 2 * cols, width), bf16),
-            pltpu.VMEM((2, sheets, rows + 8, width), bf16),
-            pltpu.VMEM((3, 3, width, out_ch), bf16),
-            pltpu.VMEM((sheets, area, out_ch), f32),
-            pltpu.SemaphoreType.DMA((7, 3)),
+        grid=(sheets, 3),
+        in_specs=[
+            per_sheet(area, width), per_sheet(cols, width), per_sheet(cols, width),
+            per_sheet(rows + 8, width), per_sheet(rows + 8, width),
+            pl.BlockSpec((3, None, width, out_ch), lambda s, k: (0, k, 0, 0)),
         ],
-        compiler_params=params(24),
+        out_specs=pl.BlockSpec(memory_space=pltpu.VMEM),
+        out_shape=pltpu.VMEM((sheets, area, out_ch), f32),
+        scratch_shapes=[pltpu.VMEM((area + 2 * cols, width), bf16)],
+        compiler_params=params(20),
         cost_estimate=cost(2 * sheets * area * width * 9 * out_ch, 2 * 9 * width * out_ch + 2 * sheets * area * width),
         name="conv",
-    )(
-        attended, att_above.reshape(sheets, cols, width), att_below.reshape(sheets, cols, width),
-        att_west, att_east, in_hbm(w_join),
-    )
+    )(in_hbm(attended), att_above, att_below, att_west, att_east, in_hbm(w_join))
+    conv = pltpu.with_memory_space_constraint(conv, pltpu.VMEM)
 
     depth = TAPS * sum(SLOTS.values())
     bin_rows = 2 * sum(SLOTS.values())
@@ -641,9 +621,7 @@
         grid_spec=pltpu.PrefetchScalarGridSpec(
             num_scalar_prefetch=1,
             grid=(1,),
-            in_specs=[
-                pl.BlockSpec(memory_space=pl.ANY) for _ in range(10)
-            ],
+            in_specs=[pl.BlockSpec(memory_space=pl.ANY) for _ in range(9)] + [pl.BlockSpec(memory_space=pltpu.VMEM)],
             out_specs=pl.BlockSpec(memory_space=pl.ANY),
             scratch_shapes=[
                 pltpu.VMEM(bin_table.shape[1:], bf16),
@@ -655,10 +633,9 @@
                 pltpu.VMEM((2, 64, depth), bf16),
                 pltpu.VMEM(w_pool.shape, bf16),
                 pltpu.VMEM((len(LEVELS), 3, 3, ppm, out_ch), bf16),
-                pltpu.VMEM((sheets, area, out_ch), f32),
                 pltpu.VMEM((sheets, depth, out_ch), f32),
                 pltpu.VMEM((sheets, area, out_ch), bf16),
-                pltpu.SemaphoreType.DMA((3, 2 * len(LEVELS) + 1)),
+                pltpu.SemaphoreType.DMA((3, 2 * len(LEVELS))),
             ],
         ),
         out_shape=jax.ShapeDtypeStruct((sheets, area, out_ch), bf16),
@@ -667,7 +644,7 @@
         name="tail",
     )(
         at, bin_table.astype(bf16), row_scale, col_scale, strips, in_hbm(w_pool), in_hbm(w_join),
-        by_row, by_col, spread.astype(bf16), in_hbm(conv),
+        by_row, by_col, spread.astype(bf16), conv,
     )
     return out.reshape(sheets, rows, cols, out_ch)
 

time: 103 us -> 95.3 us (0.925)
  the two profiles are of different devices: /device:TPU:24 before, /device:TPU:1 now
where the time goes in v5:
time: 95.3 us; the launch traced here: 94.7 us
  starting transfers between devices  42.6 us (45%)
  Pallas kernels  36.5 us (38%)
  waiting for transfers between devices  9.67 us (10%)
  local copies, waits for them, and re-layouts  4.58 us (5%)
    pallas_call x1, Pallas kernels, layer(): pl.pallas_call(lambda *refs: attend_kernel((grid_h, grid_w), *refs), grid...  11.5 us
    pallas_call x1, Pallas kernels, layer(): pl.pallas_call(conv_kernel, grid=(sheets, 3), in_specs=[per_sheet(area, w...  9.82 us
    pallas_call x1, Pallas kernels, layer(): pl.pallas_call(tail_kernel, grid_spec=pltpu.PrefetchScalarGridSpec(num_sc...  8.38 us
    all_to_all x1, starting transfers between devices, layer(): lax.all_to_all(sums, 'row', 0, 0, tiled=True)  7.85 us
    ppermute x1, waiting for transfers between devices, layer(): att_below = lax.ppermute(first_row, 'row', row_bwd)  7.77 us
    all_to_all x1, starting transfers between devices, layer(): lax.all_to_all(strips, 'col', 0, 0, tiled=True)  7.35 us
    ppermute x1, starting transfers between devices, layer(): att_west = lax.ppermute(att_edges(last_col, cols - 1), 'col', col_fwd)  5.7 us
    ppermute x1, starting transfers between devices, layer(): west = lax.ppermute(edges(cols - HALO), 'col', col_fwd)  5.5 us
  transfers between devices with their start and end apart: 10, of which 3 were waited for; matrix products, arithmetic and copies ran while one was open for 2% of the time, Pallas kernels for 18%

profile of v5, /device:TPU:1, one launch (start us, length us, event | category | flops | bytes accessed | tf_op | source)
XLA Modules:
  0.0 94.7 jit_solution(6876060877948963115)
XLA Ops:
  0.0 0.0 copy-start
  0.0 0.0 copy-start.11
  0.0 1.2 %fusion.1 = (bf16[2,2,32,1024]{3,2,1,0:T(8,128)(2,1)S(1)}, bf16[2,2,32,1024]{3,2,1,0:T(8,128)(2,1)S(1)}) fusion(bf16[2,16,32,1024]{3,2,1,0:T(8,128)(2,1)} %param.16), kind=kLoop, calls=%fused_computation.7 | loop fusion | bytes 1048576 | tf_op jit(solution)/shard_map/slice | solution.py:481
  1.2 3.3 %collective-permute-start.1 = (bf16[2,2,32,1024]{3,2,1,0:T(8,128)(2,1)S(1)}, bf16[2,2,32,1024]{3,2,1,0:T(8,128)(2,1)S(1)}, u32[]{:S(2)}, u32[]{:S(2)}) collective-permute-start(bf16[2,2,32,1024]{3,2,1,0:T(8,128)(2,1)S(1)} %get-tuple-element.23), channel_id=1, source_target_pairs={{8,0},{16,8},{24,16},{32,24},{40,32},{48,40},{56,48},{64,56},{72,6... | collective-permute-start | bytes 786440 | tf_op jit(solution)/shard_map/ppermute | solution.py:481
  4.5 3.6 %collective-permute-start = (bf16[2,2,32,1024]{3,2,1,0:T(8,128)(2,1)S(1)}, bf16[2,2,32,1024]{3,2,1,0:T(8,128)(2,1)S(1)}, u32[]{:S(2)}, u32[]{:S(2)}) collective-permute-start(bf16[2,2,32,1024]{3,2,1,0:T(8,128)(2,1)S(1)} %get-tuple-element.24), channel_id=1, source_target_pairs={{0,8},{8,16},{16,24},{24,32},{32,40},{40,48},{48,56},{56,64},{64,7... | collective-permute-start | bytes 786440 | tf_op jit(solution)/shard_map/ppermute | solution.py:480
  8.1 1.4 %fusion = (bf16[2,16,2,1024]{3,2,1,0:T(2,128)(2,1)S(1)}, bf16[2,16,2,1024]{3,2,1,0:T(2,128)(2,1)S(1)}) fusion(bf16[2,16,32,1024]{3,2,1,0:T(8,128)(2,1)} %param.16), kind=kLoop, calls=%fused_computation.6 | loop fusion | bytes 524288 | tf_op jit(solution)/shard_map/slice | solution.py:484
  9.5 0.1 pad_add_fusion.refs_0_.place_ref
  9.7 0.1 pad.16.clone
  9.7 0.0 copy-done
  9.7 0.0 copy-done.11
  9.7 0.0 copy-start.1
  9.7 1.2 %copy-done.1 = bf16[1024,512]{1,0:T(8,128)(2,1)S(1)} copy-done((bf16[1024,512]{1,0:T(8,128)(2,1)S(1)}, bf16[1024,512]{1,0:T(8,128)(2,1)}, u32[]{:S(2)}) %copy-start.1) | copy-done | bytes 1048600
  11.0 0.0 copy-start.2
  11.0 0.0 copy-start.4
  11.0 0.0 collective-permute-done.1
  11.1 0.3 collective-permute-done
  11.5 0.1 pad_maximum_fusion
  11.5 1.4 %collective-permute-start.2 = (bf16[2,20,2,1024]{3,1,2,0:T(8,128)(2,1)S(1)}, bf16[2,20,2,1024]{3,1,2,0:T(8,128)(2,1)S(1)}, u32[]{:S(2)}, u32[]{:S(2)}) collective-permute-start(bf16[2,20,2,1024]{3,1,2,0:T(8,128)(2,1)S(1)} %pad_maximum_fusion), channel_id=1, source_target_pairs={{1,0},{2,1},{3,2},{4,3},{5,4},{6,5},{7,6},{9,8},{10,9},{11,10},{12... | collective-permute-start | bytes 491528 | tf_op jit(solution)/shard_map/ppermute | solution.py:487
  13.0 0.1 pad_maximum_fusion.1
  13.1 5.5 %collective-permute-start.3 = (bf16[2,20,2,1024]{3,1,2,0:T(8,128)(2,1)S(1)}, bf16[2,20,2,1024]{3,1,2,0:T(8,128)(2,1)S(1)}, u32[]{:S(2)}, u32[]{:S(2)}) collective-permute-start(bf16[2,20,2,1024]{3,1,2,0:T(8,128)(2,1)S(1)} %pad_maximum_fusion.1), channel_id=1, source_target_pairs={{0,1},{1,2},{2,3},{3,4},{4,5},{5,6},{6,7},{8,9},{9,10},{10,11},{11... | collective-permute-start | bytes 491528 | tf_op jit(solution)/shard_map/ppermute | solution.py:486
  18.6 0.0 copy-done.2
  18.6 0.0 copy-done.4
  18.6 0.0 copy-start.13
  18.6 0.0 copy-start.14
  18.6 5.1 %project.1 = (f32[2,16,32,512]{3,2,1,0:T(8,128)S(1)}, f32[2,20,32,1024]{3,2,1,0:T(8,128)S(1)}) custom-call(bf16[2,512,1024]{2,1,0:T(8,128)(2,1)S(1)} %bitcast.13, bf16[2,64,1024]{2,1,0:T(8,128)(2,1)S(1)} %bitcast.17, bf16[2,64,1024]{2,1,0:T(8,128)(2,1)S(1)} %bitcast.16, f32[1,1024]{1,0:T(1,128)S(1)} %warm.1.gain_ref.refs_5_, ...), custom_call_target="tpu_custom_call" | custom-call | flops 3221225472 | bytes 13631488 | tf_op jit(solution)/shard_map/project/pallas_call | solution.py:504
  23.8 0.0 collective-permute-done.2
  23.8 0.2 copy.31
  23.9 1.6 %collective-permute-done.3 = bf16[2,20,2,1024]{3,1,2,0:T(8,128)(2,1)S(1)} collective-permute-done((bf16[2,20,2,1024]{3,1,2,0:T(8,128)(2,1)S(1)}, bf16[2,20,2,1024]{3,1,2,0:T(8,128)(2,1)S(1)}, u32[]{:S(2)}, u32[]{:S(2)}) %collective-permute-start.3) | collective-permute-done | bytes 163872 | tf_op jit(solution)/shard_map/ppermute | solution.py:486
  25.5 0.2 copy.32
  25.7 0.4 maximum_bitcast_fusion.refs_3_
  26.1 0.0 copy-done.13
  26.1 0.0 copy-done.14
  26.1 0.0 copy-start.5
  26.1 0.0 copy-start.9
  26.1 11.5 %attend.1 = (bf16[2,512,1024]{2,1,0:T(8,128)(2,1)}, bf16[16,16,1024]{2,1,0:T(8,128)(2,1)}, bf16[2,32,1024]{2,1,0:T(8,128)(2,1)S(1)}, bf16[2,32,1024]{2,1,0:T(8,1...) custom-call(s32[2]{0:T(128)S(1)} %pad_add_fusion.refs_0_.place_ref, ...), custom_call_target="tpu_custom_call" | custom-call | flops 4294967296 | bytes 8388608 | tf_op jit(solution)/shard_map/attend/pallas_call | solution.py:529
  37.6 4.6 %collective-permute-start.4 = (bf16[2,32,1024]{2,1,0:T(8,128)(2,1)S(1)}, bf16[2,32,1024]{2,1,0:T(8,128)(2,1)S(1)}, u32[]{:S(2)}, u32[]{:S(2)}) collective-permute-start(bf16[2,32,1024]{2,1,0:T(8,128)(2,1)S(1)} %get-tuple-element.17), channel_id=1, source_target_pairs={{0,8},{8,16},{16,24},{24,32},{32,40},{40,48},{48,56},{56,64},{64,7... | collective-permute-start | bytes 393224 | tf_op jit(solution)/shard_map/ppermute | solution.py:570
  42.3 7.9 %all-to-all-start = ((bf16[16,16,1024]{2,1,0:T(8,128)(2,1)}), bf16[16,16,1024]{2,1,0:T(8,128)(2,1)S(1)}, u32[]{:S(2)}, u32[]{:S(2)}) async-start(bf16[16,16,1024]{2,1,0:T(8,128)(2,1)} %get-tuple-element.15), calls=%async_computation | async-start | bytes 1048576 | tf_op jit(solution)/shard_map/all_to_all | solution.py:572
  50.1 2.0 %collective-permute-start.5 = (bf16[2,32,1024]{2,1,0:T(8,128)(2,1)S(1)}, bf16[2,32,1024]{2,1,0:T(8,128)(2,1)S(1)}, u32[]{:S(2)}, u32[]{:S(2)}) collective-permute-start(bf16[2,32,1024]{2,1,0:T(8,128)(2,1)S(1)} %get-tuple-element.18), channel_id=1, source_target_pairs={{8,0},{16,8},{24,16},{32,24},{40,32},{48,40},{56,48},{64,56},{72,6... | collective-permute-start | bytes 393224 | tf_op jit(solution)/shard_map/ppermute | solution.py:571
  52.1 0.0 collective-permute-done.4.top_ref
  52.2 7.8 %collective-permute-done.5.bottom_ref = bf16[2,32,1024]{2,1,0:T(8,128)(2,1)S(1)} collective-permute-done((bf16[2,32,1024]{2,1,0:T(8,128)(2,1)S(1)}, bf16[2,32,1024]{2,1,0:T(8,128)(2,1)S(1)}, u32[]{:S(2)}, u32[]{:S(2)}) %collective-permute-start.5) | collective-permute-done | bytes 131104 | tf_op jit(solution)/shard_map/ppermute | solution.py:571
  60.0 5.7 %collective-permute-start.6 = (bf16[2,18,1024]{2,1,0:T(8,128)(2,1)S(1)}, bf16[2,18,1024]{2,1,0:T(8,128)(2,1)S(1)}, u32[]{:S(2)}, u32[]{:S(2)}) collective-permute-start(bf16[2,18,1024]{2,1,0:T(8,128)(2,1)S(1)} %pad_maximum_fusion.2), channel_id=1, source_target_pairs={{0,1},{1,2},{2,3},{3,4},{4,5},{5,6},{6,7},{8,9},{9,10},{10,11},{11... | collective-permute-start | bytes 221192 | tf_op jit(solution)/shard_map/ppermute | solution.py:577
  65.8 1.3 %collective-permute-start.7 = (bf16[2,18,1024]{2,1,0:T(8,128)(2,1)S(1)}, bf16[2,18,1024]{2,1,0:T(8,128)(2,1)S(1)}, u32[]{:S(2)}, u32[]{:S(2)}) collective-permute-start(bf16[2,18,1024]{2,1,0:T(8,128)(2,1)S(1)} %pad_maximum_fusion.3), channel_id=1, source_target_pairs={{1,0},{2,1},{3,2},{4,3},{5,4},{6,5},{7,6},{9,8},{10,9},{11,10},{12... | collective-permute-start | bytes 221192 | tf_op jit(solution)/shard_map/ppermute | solution.py:578
  67.1 0.0 all-to-all-done
  67.1 0.0 copy-done.5
  67.1 0.0 copy-done.9
  67.1 1.6 %combine.1 = bf16[8,32,1024]{2,1,0:T(8,128)(2,1)} custom-call(s32[2]{0:T(128)S(1)} %pad_add_fusion.refs_0_.place_ref, bf16[16,32,48]{2,1,0:T(8,128)(2,1)S(1)} %copy-done.9, bf16[8,48,256]{2,1,0:T(8,128)(2,1)S(1)} %copy-done.5, bf16[256,1024]{1,0:T(8,128)(2,1)S(1)} %bitcast.11), custom_call_target="tpu_custom_call" | custom-call | tf_op jit(solution)/shard_map/combine/pallas_call | solution.py:582
  68.7 7.4 %all-to-all-start.1 = ((bf16[8,32,1024]{2,1,0:T(8,128)(2,1)}), bf16[8,32,1024]{2,1,0:T(8,128)(2,1)S(1)}, u32[]{:S(2)}, u32[]{:S(2)}) async-start(bf16[8,32,1024]{2,1,0:T(8,128)(2,1)} %combine.1), calls=%async_computation.1 | async-start | bytes 1048576 | tf_op jit(solution)/shard_map/all_to_all | solution.py:598
  76.1 0.0 collective-permute-done.6
  76.1 0.0 collective-permute-done.7
  76.1 0.0 copy-start.3
  76.2 0.0 copy-start.6
  76.2 0.0 copy-start.7
  76.2 0.0 copy-start.8
  76.2 0.0 copy-start.10
  76.2 0.0 copy-start.12
  76.2 9.8 %conv.1 = f32[2,512,256]{2,1,0:T(8,128)S(1)} custom-call(bf16[2,512,1024]{2,1,0:T(8,128)(2,1)} %get-tuple-element.16.attended_ref, bf16[2,32,1024]{2,1,0:T(8,128)(2,1)S(1)} %collective-permute-done.4.top_ref, bf16[2,32,1024]{2,1,0:T(8,128)(2,1)S(1)} %collective-permute-done.5.bottom_ref, bf16[2,24,1024]{2,1,0:T(8,128)(2,1)S(1)} %pad.7.left_ref, ...), custom_call_target="tpu_custom_call" | custom-call | flops 4831838208 | bytes 6815744 | tf_op jit(solution)/shard_map/conv/pallas_call | solution.py:600
  86.0 0.0 all-to-all-done.1
  86.1 0.0 copy-done.3
  86.1 0.0 copy-done.6
  86.1 0.0 copy-done.7
  86.1 0.0 copy-done.8
  86.1 0.0 copy-done.10
  86.1 0.0 copy-done.12
  86.1 8.4 %tail.1 = bf16[2,512,256]{2,1,0:T(8,128)(2,1)} custom-call(s32[2]{0:T(128)S(1)} %pad_add_fusion.refs_0_.place_ref, bf16[8,96,256]{2,1,0:T(8,128)(2,1)S(1)} %copy-done.3, f32[16,1,96]{2,1,0:T(1,128)S(1)} %copy-done.10, f32[8,1,96]{2,1,0:T(1,128)S(1)} %copy-done.12, bf16[256,1024]{1,0:T(8,128)(2,1)S(1)} %bitcast.12, bf16[4,1024,512]{2,1,0:T(8,128)(2,1)} %wpool_hbm.1, ...), custom_call_target="tpu_custom_call" | custom-call | flops 4000000000 | bytes 13631488 | tf_op jit(solution)/shard_map/tail/pallas_call | solution.py:619
  (16 shorter events, 0.3 us)
Async XLA Ops:
  0.0 9.7 %copy-start = (bf16[1024,1024]{1,0:T(8,128)(2,1)S(1)}, bf16[1024,1024]{1,0:T(8,128)(2,1)}, u32[]{:S(2)}) copy-start(bf16[1024,1024]{1,0:T(8,128)(2,1)} %refs_6_.1) | copy-start | bytes 6291460
  0.0 9.7 %copy-start.11 = (f32[1024]{0:T(1024)S(1)}, f32[1024]{0:T(1024)}, u32[]{:S(2)}) copy-start(f32[1024]{0:T(1024)} %param.17) | copy-start | bytes 12292
  1.2 9.8 %collective-permute-start.1 = (bf16[2,2,32,1024]{3,2,1,0:T(8,128)(2,1)S(1)}, bf16[2,2,32,1024]{3,2,1,0:T(8,128)(2,1)S(1)}, u32[]{:S(2)}, u32[]{:S(2)}) collective-permute-start(bf16[2,2,32,1024]{3,2,1,0:T(8,128)(2,1)S(1)} %get-tuple-element.23), channel_id=1, source_target_pairs={{8,0},{16,8},{24,16},{32,24},{40,32},{48,40},{56,48},{64,56},{72,6... | collective-permute-start | bytes 786440 | tf_op jit(solution)/shard_map/ppermute | solution.py:481
  4.5 6.9 %collective-permute-start = (bf16[2,2,32,1024]{3,2,1,0:T(8,128)(2,1)S(1)}, bf16[2,2,32,1024]{3,2,1,0:T(8,128)(2,1)S(1)}, u32[]{:S(2)}, u32[]{:S(2)}) collective-permute-start(bf16[2,2,32,1024]{3,2,1,0:T(8,128)(2,1)S(1)} %get-tuple-element.24), channel_id=1, source_target_pairs={{0,8},{8,16},{16,24},{24,32},{32,40},{40,48},{48,56},{56,64},{64,7... | collective-permute-start | bytes 786440 | tf_op jit(solution)/shard_map/ppermute | solution.py:480
  9.7 1.2 %copy-start.1 = (bf16[1024,512]{1,0:T(8,128)(2,1)S(1)}, bf16[1024,512]{1,0:T(8,128)(2,1)}, u32[]{:S(2)}) copy-start(bf16[1024,512]{1,0:T(8,128)(2,1)} %wq.1) | copy-start | bytes 3145732
  11.0 7.6 %copy-start.2 = (bf16[1024,512]{1,0:T(8,128)(2,1)S(1)}, bf16[1024,512]{1,0:T(8,128)(2,1)}, u32[]{:S(2)}) copy-start(bf16[1024,512]{1,0:T(8,128)(2,1)} %wq.1) | copy-start | bytes 3145732
  11.0 7.6 %copy-start.4 = (bf16[2,16,32,1024]{3,2,1,0:T(8,128)(2,1)S(1)}, bf16[2,16,32,1024]{3,2,1,0:T(8,128)(2,1)}, u32[]{:S(2)}) copy-start(bf16[2,16,32,1024]{3,2,1,0:T(8,128)(2,1)} %param.16) | copy-start | bytes 6291460
  11.5 12.2 %collective-permute-start.2 = (bf16[2,20,2,1024]{3,1,2,0:T(8,128)(2,1)S(1)}, bf16[2,20,2,1024]{3,1,2,0:T(8,128)(2,1)S(1)}, u32[]{:S(2)}, u32[]{:S(2)}) collective-permute-start(bf16[2,20,2,1024]{3,1,2,0:T(8,128)(2,1)S(1)} %pad_maximum_fusion), channel_id=1, source_target_pairs={{1,0},{2,1},{3,2},{4,3},{5,4},{6,5},{7,6},{9,8},{10,9},{11,10},{12... | collective-permute-start | bytes 491528 | tf_op jit(solution)/shard_map/ppermute | solution.py:487
  13.1 12.5 %collective-permute-start.3 = (bf16[2,20,2,1024]{3,1,2,0:T(8,128)(2,1)S(1)}, bf16[2,20,2,1024]{3,1,2,0:T(8,128)(2,1)S(1)}, u32[]{:S(2)}, u32[]{:S(2)}) collective-permute-start(bf16[2,20,2,1024]{3,1,2,0:T(8,128)(2,1)S(1)} %pad_maximum_fusion.1), channel_id=1, source_target_pairs={{0,1},{1,2},{2,3},{3,4},{4,5},{5,6},{6,7},{8,9},{9,10},{10,11},{11... | collective-permute-start | bytes 491528 | tf_op jit(solution)/shard_map/ppermute | solution.py:486
  18.6 7.5 %copy-start.13 = (bf16[512,1024]{1,0:T(8,128)(2,1)S(1)}, bf16[512,1024]{1,0:T(8,128)(2,1)}, u32[]{:S(2)}) copy-start(bf16[512,1024]{1,0:T(8,128)(2,1)} %refs_7_.1) | copy-start | bytes 3145732
  18.6 7.5 %copy-start.14 = (f32[128,8,48]{2,1,0:T(8,128)S(1)}, f32[128,8,48]{2,1,0:T(8,128)}, u32[]{:S(2)}) copy-start(f32[128,8,48]{2,1,0:T(8,128)} %constant.31.clone.refs_8_) | copy-start | bytes 589828
  26.1 41.0 %copy-start.5 = (bf16[8,48,256]{2,1,0:T(8,128)(2,1)S(1)}, bf16[8,48,256]{2,1,0:T(8,128)(2,1)}, u32[]{:S(2)}) copy-start(bf16[8,48,256]{2,1,0:T(8,128)(2,1)} %constant.33.clone.table_ref) | copy-start | bytes 589828
  26.1 41.0 %copy-start.9 = (bf16[16,32,48]{2,1,0:T(8,128)(2,1)S(1)}, bf16[16,32,48]{2,1,0:T(8,128)(2,1)}, u32[]{:S(2)}) copy-start(bf16[16,32,48]{2,1,0:T(8,128)(2,1)} %constant.32.clone.near_ref) | copy-start | bytes 147460
  37.6 14.5 %collective-permute-start.4 = (bf16[2,32,1024]{2,1,0:T(8,128)(2,1)S(1)}, bf16[2,32,1024]{2,1,0:T(8,128)(2,1)S(1)}, u32[]{:S(2)}, u32[]{:S(2)}) collective-permute-start(bf16[2,32,1024]{2,1,0:T(8,128)(2,1)S(1)} %get-tuple-element.17), channel_id=1, source_target_pairs={{0,8},{8,16},{16,24},{24,32},{32,40},{40,48},{48,56},{56,64},{64,7... | collective-permute-start | bytes 393224 | tf_op jit(solution)/shard_map/ppermute | solution.py:570
  42.3 24.8 %all-to-all-start = ((bf16[16,16,1024]{2,1,0:T(8,128)(2,1)}), bf16[16,16,1024]{2,1,0:T(8,128)(2,1)S(1)}, u32[]{:S(2)}, u32[]{:S(2)}) async-start(bf16[16,16,1024]{2,1,0:T(8,128)(2,1)} %get-tuple-element.15), calls=%async_computation | async-start | bytes 1048576 | tf_op jit(solution)/shard_map/all_to_all | solution.py:572
  50.1 9.8 %collective-permute-start.5 = (bf16[2,32,1024]{2,1,0:T(8,128)(2,1)S(1)}, bf16[2,32,1024]{2,1,0:T(8,128)(2,1)S(1)}, u32[]{:S(2)}, u32[]{:S(2)}) collective-permute-start(bf16[2,32,1024]{2,1,0:T(8,128)(2,1)S(1)} %get-tuple-element.18), channel_id=1, source_target_pairs={{8,0},{16,8},{24,16},{32,24},{40,32},{48,40},{56,48},{64,56},{72,6... | collective-permute-start | bytes 393224 | tf_op jit(solution)/shard_map/ppermute | solution.py:571
  60.0 16.1 %collective-permute-start.6 = (bf16[2,18,1024]{2,1,0:T(8,128)(2,1)S(1)}, bf16[2,18,1024]{2,1,0:T(8,128)(2,1)S(1)}, u32[]{:S(2)}, u32[]{:S(2)}) collective-permute-start(bf16[2,18,1024]{2,1,0:T(8,128)(2,1)S(1)} %pad_maximum_fusion.2), channel_id=1, source_target_pairs={{0,1},{1,2},{2,3},{3,4},{4,5},{5,6},{6,7},{8,9},{9,10},{10,11},{11... | collective-permute-start | bytes 221192 | tf_op jit(solution)/shard_map/ppermute | solution.py:577
  65.8 10.4 %collective-permute-start.7 = (bf16[2,18,1024]{2,1,0:T(8,128)(2,1)S(1)}, bf16[2,18,1024]{2,1,0:T(8,128)(2,1)S(1)}, u32[]{:S(2)}, u32[]{:S(2)}) collective-permute-start(bf16[2,18,1024]{2,1,0:T(8,128)(2,1)S(1)} %pad_maximum_fusion.3), channel_id=1, source_target_pairs={{1,0},{2,1},{3,2},{4,3},{5,4},{6,5},{7,6},{9,8},{10,9},{11,10},{12... | collective-permute-start | bytes 221192 | tf_op jit(solution)/shard_map/ppermute | solution.py:578
  68.7 17.3 %all-to-all-start.1 = ((bf16[8,32,1024]{2,1,0:T(8,128)(2,1)}), bf16[8,32,1024]{2,1,0:T(8,128)(2,1)S(1)}, u32[]{:S(2)}, u32[]{:S(2)}) async-start(bf16[8,32,1024]{2,1,0:T(8,128)(2,1)} %combine.1), calls=%async_computation.1 | async-start | bytes 1048576 | tf_op jit(solution)/shard_map/all_to_all | solution.py:598
  76.1 9.9 %copy-start.3 = (bf16[8,96,256]{2,1,0:T(8,128)(2,1)S(1)}, bf16[8,96,256]{2,1,0:T(8,128)(2,1)}, u32[]{:S(2)}) copy-start(bf16[8,96,256]{2,1,0:T(8,128)(2,1)} %constant.34.clone.table_hbm) | copy-start | bytes 1179652
  76.2 9.9 %copy-start.6 = (bf16[2,64,432]{2,1,0:T(8,128)(2,1)S(1)}, bf16[2,64,432]{2,1,0:T(8,128)(2,1)}, u32[]{:S(2)}) copy-start(bf16[2,64,432]{2,1,0:T(8,128)(2,1)} %constant.39.clone.spread_hbm) | copy-start | bytes 331780
  76.2 9.9 %copy-start.7 = (f32[8,32,64]{2,1,0:T(8,128)S(1)}, f32[8,32,64]{2,1,0:T(8,128)}, u32[]{:S(2)}) copy-start(f32[8,32,64]{2,1,0:T(8,128)} %constant.38.clone.by_col_hbm) | copy-start | bytes 196612
  76.2 9.9 %copy-start.8 = (f32[16,16,64]{2,1,0:T(8,128)S(1)}, f32[16,16,64]{2,1,0:T(8,128)}, u32[]{:S(2)}) copy-start(f32[16,16,64]{2,1,0:T(8,128)} %constant.37.clone.by_row_hbm) | copy-start | bytes 196612
  76.2 9.9 %copy-start.10 = (f32[16,1,96]{2,1,0:T(1,128)S(1)}, f32[16,1,96]{2,1,0:T(1,128)}, u32[]{:S(2)}) copy-start(f32[16,1,96]{2,1,0:T(1,128)} %constant.35.clone.row_scale_hbm) | copy-start | bytes 18436
  76.2 9.9 %copy-start.12 = (f32[8,1,96]{2,1,0:T(1,128)S(1)}, f32[8,1,96]{2,1,0:T(1,128)}, u32[]{:S(2)}) copy-start(f32[8,1,96]{2,1,0:T(1,128)} %constant.36.clone.col_scale_hbm) | copy-start | bytes 9220

commit v6 on v5

--- a/solution.py
+++ b/solution.py
@@ -180,15 +180,16 @@
 
 
 def project_kernel(tokens_ref, above_ref, below_ref, gain_ref, wq, wkv, q_ref, kv_ref):
-    rows, cols, inner = q_ref.shape
+    rows, cols, inner = q_ref.shape[1:]
+    s = pl.program_id(0)
     gain = gain_ref[...]
-    normed = layer_norm(tokens_ref[...], gain)
-    q_ref[...] = dot(normed, wq[...]).astype(bf16).astype(f32).reshape(rows, cols, inner)
-    kv_ref[HALO : rows + HALO] = dot(normed, wkv[...]).astype(bf16).astype(f32).reshape(rows, cols, -1)
-    edge = layer_norm(jnp.concatenate([above_ref[...], below_ref[...]], axis=0), gain)
+    normed = layer_norm(tokens_ref[s], gain)
+    q_ref[s] = dot(normed, wq[...]).astype(bf16).astype(f32).reshape(rows, cols, inner)
+    kv_ref[s, HALO : rows + HALO] = dot(normed, wkv[...]).astype(bf16).astype(f32).reshape(rows, cols, -1)
+    edge = layer_norm(jnp.concatenate([above_ref[s], below_ref[s]], axis=0), gain)
     edge = dot(edge, wkv[...]).astype(bf16).astype(f32).reshape(2 * HALO, cols, -1)
-    kv_ref[0:HALO] = edge[:HALO]
-    kv_ref[rows + HALO :] = edge[HALO:]
+    kv_ref[s, 0:HALO] = edge[:HALO]
+    kv_ref[s, rows + HALO :] = edge[HALO:]
 
 
 def window_bias(bias, first_row, first_col, grid_h, grid_w):
@@ -213,7 +214,7 @@
     grid_shape, place_ref, q_ref, kv_ref, sides_ref, tokens_ref, gain_ref, wkv_ref, wout_ref, masks_ref,
     attended_ref, sums_ref, first_row_ref, last_row_ref, first_col_ref, last_col_ref, sides, context, bias, pool, scores, weights,
 ):
-    rows, cols, inner = q_ref.shape
+    rows, cols, inner = q_ref.shape[1:]
     groups = cols // BLOCK
     span = BLOCK + 2 * HALO
 
@@ -245,13 +246,13 @@
 
         def keys_of(b, lanes):
             mid = slice(b * BLOCK, (b + 1) * BLOCK)
-            main = kv_ref[pl.ds(at, span), mid, lanes].reshape(span * BLOCK, 128)
+            main = kv_ref[sheet, pl.ds(at, span), mid, lanes].reshape(span * BLOCK, 128)
 
             def beside(g):
                 if g < 0 or g >= groups:
                     found = sides[sheet, pl.ds(at, span), :, lanes]
                 else:
-                    found = kv_ref[pl.ds(at, span), g * BLOCK : (g + 1) * BLOCK, lanes]
+                    found = kv_ref[sheet, pl.ds(at, span), g * BLOCK : (g + 1) * BLOCK, lanes]
                 return found.reshape(span // 2, 2, BLOCK, 128)
 
             west, east = beside(b - 1), beside(b + 1)
@@ -267,7 +268,7 @@
             low = bias[a, b]
             for t in range(tiles):
                 lanes = slice(t * 128, (t + 1) * 128)
-                q = q_ref[pl.ds(at, BLOCK), mid, lanes].reshape(count, 128).astype(bf16)
+                q = q_ref[sheet, pl.ds(at, BLOCK), mid, lanes].reshape(count, 128).astype(bf16)
                 q = jnp.concatenate([q] * heads, axis=0) * own
                 found = lax.dot_general(keys_of(b, lanes), q, (((1,), (1,)), ((), ())), preferred_element_type=f32)
                 scores[slot, t] = found + jnp.concatenate([low] * (heads * count // 128), axis=1)
@@ -303,7 +304,7 @@
 
     lax.fori_loop(0, rows // BLOCK, band, 0)
     mixed = context[...].reshape(rows * cols, inner).astype(bf16)
-    attended = (tokens_ref[...].astype(f32) + dot(mixed, wout_ref[...])).astype(bf16)
+    attended = (tokens_ref[sheet].astype(f32) + dot(mixed, wout_ref[...])).astype(bf16)
     attended_ref[...] = attended
     first_row_ref[...] = attended[:cols]
     last_row_ref[...] = attended[(rows - 1) * cols :]
@@ -320,20 +321,35 @@
     out_ref[...] = jnp.broadcast_to(added[None], out_ref.shape)
 
 
-def conv_kernel(attended_ref, top_ref, bottom_ref, left_ref, right_ref, w_ref, out_ref, ext):
-    area, _ = attended_ref.shape
+def conv_kernel(attended_ref, top_ref, bottom_ref, left_ref, right_ref, taps_ref, w_hbm, out_ref, ext, w, sems):
+    area, width = attended_ref.shape
     cols = top_ref.shape[0]
     rows = area // cols
     out_ch = out_ref.shape[-1]
     s, step = pl.program_id(0), pl.program_id(1)
 
-    def edge(ref):
+    fetches = [
+        pltpu.make_async_copy(w_hbm.at[:, k, 0:width, :], w.at[k - 1], sems.at[k - 1]) for k in (1, 2)
+    ]
+
+    @pl.when((s == 0) & (step == 0))
+    def _():
+        for fetch in fetches:
+            fetch.start()
+
+    for k, fetch in enumerate(fetches):
+
+        @pl.when((s == 0) & (step == k + 1))
+        def _():
+            fetch.wait()
+
+    def edge(ref, w_ref):
         total = 0.0
         for a in range(3):
             total = total + dot(ref[...], w_ref[a])[a : a + rows]
         return total.reshape(rows, 1, out_ch)
 
-    def middle():
+    def middle(w_ref):
         total = dot(ext[0:area], w_ref[0])
         for a in range(1, 3):
             total = total + dot(ext[a * cols : a * cols + area], w_ref[a])
@@ -345,17 +361,17 @@
         ext[cols : cols + area] = attended_ref[...]
         ext[cols + area :] = bottom_ref[...]
         place = lax.broadcasted_iota(jnp.int32, (rows, cols, out_ch), 1)
-        part = jnp.where(place == 0, edge(left_ref), pltpu.roll(middle(), 1, 1))
+        part = jnp.where(place == 0, edge(left_ref, taps_ref), pltpu.roll(middle(taps_ref), 1, 1))
         out_ref[s] = part.reshape(area, out_ch)
 
     @pl.when(step == 1)
     def _():
-        out_ref[s] += middle().reshape(area, out_ch)
+        out_ref[s] += middle(w.at[0]).reshape(area, out_ch)
 
     @pl.when(step == 2)
     def _():
         place = lax.broadcasted_iota(jnp.int32, (rows, cols, out_ch), 1)
-        part = jnp.where(place == cols - 1, edge(right_ref), pltpu.roll(middle(), cols - 1, 1))
+        part = jnp.where(place == cols - 1, edge(right_ref, w.at[1]), pltpu.roll(middle(w.at[1]), cols - 1, 1))
         out_ref[s] += part.reshape(area, out_ch)
 
 
@@ -366,8 +382,8 @@
 
 def tail_kernel(
     place_ref, table_hbm, row_scale_hbm, col_scale_hbm, parts_hbm, wpool_hbm, wjoin_hbm, by_row_hbm, by_col_hbm,
-    spread_hbm, conv, out_hbm,
-    table, row_scale, col_scale, parts, by_row, by_col, spread, wpool, wjoin, taps, out, sems,
+    spread_hbm, conv_ref, out_hbm,
+    table, row_scale, col_scale, parts, by_row, by_col, spread, wpool, wjoin, conv, taps, out, sems,
 ):
     width, ppm = wpool.shape[1], wpool.shape[2]
     count = len(LEVELS)
@@ -414,9 +430,20 @@
         high, low = split(jnp.maximum(both[: 2 * slots] + both[2 * slots :], 0.0))
         branches.append(jnp.concatenate([high, low], axis=0))
         row += 2 * slots
+    results = [pltpu.make_async_copy(out.at[s], out_hbm.at[s], sems.at[2, s]) for s in range(2)]
+
+    def spread_over(s, part):
+        high, low = split(taps[s, part])
+        lines = dot(grid_high[:, part], high) + dot(grid_low[:, part], high)
+        return lines + dot(grid_high[:, part], low)
+
     at = 0
     for index, level in enumerate(LEVELS):
         slots = SLOTS[level]
+        last = index == count - 1
+        if last:
+            for s in range(2):
+                conv[s] = conv_ref[s] + spread_over(s, slice(0, at))
         ready(count + index)
         for a in range(3):
             for b in range(3):
@@ -425,13 +452,11 @@
                 start = at + (a * 3 + b) * slots
                 for s in range(2):
                     taps[s, start : start + slots, :] = tap[s * slots : (s + 1) * slots]
+        if last:
+            for s in range(2):
+                out[s] = (conv[s] + spread_over(s, slice(at, at + TAPS * slots))).astype(bf16)
+                results[s].start()
         at += TAPS * slots
-    results = [pltpu.make_async_copy(out.at[s], out_hbm.at[s], sems.at[2, s]) for s in range(2)]
-    for s in range(2):
-        high, low = split(taps[s])
-        total = conv[s] + dot(grid_high, high) + dot(grid_low, high) + dot(grid_high, low)
-        out[s] = total.astype(bf16)
-        results[s].start()
     for copy in results:
         copy.wait()
 
@@ -446,6 +471,10 @@
 
 def whole(shape):
     return pl.BlockSpec(shape, lambda *_: (0,) * len(shape))
+
+
+def in_vmem(x):
+    return pltpu.with_memory_space_constraint(x, pltpu.VMEM)
 
 
 def in_hbm(x):
@@ -489,8 +518,9 @@
     def per_sheet(*dims):
         return pl.BlockSpec((None,) + dims, lambda s, *_: (s,) + (0,) * len(dims))
 
-    wq_near = pltpu.with_memory_space_constraint(w_query, pltpu.VMEM)
-    wkv_near = pltpu.with_memory_space_constraint(w_kv, pltpu.VMEM)
+    near = pl.BlockSpec(memory_space=pltpu.VMEM)
+    far = pl.BlockSpec(memory_space=pl.ANY)
+    wq_near, wkv_near = in_vmem(w_query), in_vmem(w_kv)
     gain = pl.pallas_call(
         warm_kernel,
         in_specs=[pl.BlockSpec(memory_space=pltpu.VMEM)] * 3,
@@ -499,24 +529,23 @@
         compiler_params=params(4),
         name="warm",
     )(gain, wq_near, wkv_near)
-    flat = tokens.reshape(sheets, area, width)
+    flat = in_vmem(tokens.reshape(sheets, area, width))
     edge = HALO * cols
     q, kv = pl.pallas_call(
         project_kernel,
         grid=(sheets,),
-        in_specs=[
-            per_sheet(area, width), per_sheet(edge, width), per_sheet(edge, width),
-            whole((1, width)), pl.BlockSpec(memory_space=pltpu.VMEM), pl.BlockSpec(memory_space=pltpu.VMEM),
-        ],
-        out_specs=[per_sheet(rows, cols, inner), per_sheet(rows + 2 * HALO, cols, wide)],
+        in_specs=[near] * 6,
+        out_specs=[near] * 2,
         out_shape=[
-            jax.ShapeDtypeStruct((sheets, rows, cols, inner), f32),
-            jax.ShapeDtypeStruct((sheets, rows + 2 * HALO, cols, wide), f32),
+            pltpu.VMEM((sheets, rows, cols, inner), f32), pltpu.VMEM((sheets, rows + 2 * HALO, cols, wide), f32),
         ],
         compiler_params=params(28),
         cost_estimate=cost(2 * sheets * area * width * (inner + wide), 2 * (width * (inner + wide) + 5 * sheets * area * width)),
         name="project",
-    )(flat, above.reshape(sheets, edge, width), below.reshape(sheets, edge, width), gain, wq_near, wkv_near)
+    )(
+        flat, in_vmem(above.reshape(sheets, edge, width)), in_vmem(below.reshape(sheets, edge, width)),
+        in_vmem(gain), wq_near, wkv_near,
+    )
 
     blank = jnp.zeros((sheets, rows + 2 * HALO, BLOCK - 2 * HALO, width), bf16)
     sides = jnp.concatenate([east, blank, west], axis=2).reshape(sheets, (rows + 2 * HALO) * BLOCK, width)
@@ -532,11 +561,7 @@
             num_scalar_prefetch=1,
             grid=(sheets,),
             in_specs=[
-                pl.BlockSpec((None, rows, cols, inner), lambda s, _: (s, 0, 0, 0)),
-                pl.BlockSpec((None, rows + 2 * HALO, cols, wide), lambda s, _: (s, 0, 0, 0)),
-                fixed(sheets, (rows + 2 * HALO) * BLOCK, width),
-                pl.BlockSpec((None, area, width), lambda s, _: (s, 0, 0)),
-                fixed(1, width), pl.BlockSpec(memory_space=pltpu.VMEM), fixed(inner, width),
+                near, near, near, near, near, near, fixed(inner, width),
                 pl.BlockSpec((None, UNITS, rows + cols), lambda s, p: (p[0] * col_count + p[1], 0, 0)),
             ],
             out_specs=[
@@ -564,7 +589,9 @@
         compiler_params=params(32),
         cost_estimate=cost(2 * sheets * area * inner * width * 4, 2 * sheets * area * width * 4, sheets * blocks * keys * 1024),
         name="attend",
-    )(at, q, kv, sides, flat, gain, wkv_near, w_out, masks)
+    )(
+        at, in_vmem(q), in_vmem(kv), in_vmem(sides), flat, in_vmem(gain), wkv_near, w_out, masks,
+    )
 
     strip_rows = sheets * STRIP_UNITS
     att_above = lax.ppermute(last_row, "row", row_fwd)
@@ -603,16 +630,19 @@
         in_specs=[
             per_sheet(area, width), per_sheet(cols, width), per_sheet(cols, width),
             per_sheet(rows + 8, width), per_sheet(rows + 8, width),
-            pl.BlockSpec((3, None, width, out_ch), lambda s, k: (0, k, 0, 0)),
+            pl.BlockSpec((3, None, width, out_ch), lambda *_: (0, 0, 0, 0)), far,
         ],
         out_specs=pl.BlockSpec(memory_space=pltpu.VMEM),
         out_shape=pltpu.VMEM((sheets, area, out_ch), f32),
-        scratch_shapes=[pltpu.VMEM((area + 2 * cols, width), bf16)],
+        scratch_shapes=[
+            pltpu.VMEM((area + 2 * cols, width), bf16), pltpu.VMEM((2, 3, width, out_ch), bf16),
+            pltpu.SemaphoreType.DMA((2,)),
+        ],
         compiler_params=params(20),
         cost_estimate=cost(2 * sheets * area * width * 9 * out_ch, 2 * 9 * width * out_ch + 2 * sheets * area * width),
         name="conv",
-    )(in_hbm(attended), att_above, att_below, att_west, att_east, in_hbm(w_join))
-    conv = pltpu.with_memory_space_constraint(conv, pltpu.VMEM)
+    )(in_hbm(attended), att_above, att_below, att_west, att_east, in_hbm(w_join), in_hbm(w_join))
+    conv = in_vmem(conv)
 
     depth = TAPS * sum(SLOTS.values())
     bin_rows = 2 * sum(SLOTS.values())
@@ -633,6 +663,7 @@
                 pltpu.VMEM((2, 64, depth), bf16),
                 pltpu.VMEM(w_pool.shape, bf16),
                 pltpu.VMEM((len(LEVELS), 3, 3, ppm, out_ch), bf16),
+                pltpu.VMEM((sheets, area, out_ch), f32),
                 pltpu.VMEM((sheets, depth, out_ch), f32),
                 pltpu.VMEM((sheets, area, out_ch), bf16),
                 pltpu.SemaphoreType.DMA((3, 2 * len(LEVELS))),

time: 95.3 us -> 95 us (level)
  the two profiles are of different devices: /device:TPU:1 before, /device:TPU:32 now
where the time goes in v6:
time: 95 us; the launch traced here: 94.4 us
  starting transfers between devices  40.2 us (42%)
  Pallas kernels  36.2 us (38%)
  waiting for transfers between devices  12.1 us (13%)
  local copies, waits for them, and re-layouts  4.59 us (5%)
    pallas_call x1, Pallas kernels, layer(): pl.pallas_call(lambda *refs: attend_kernel((grid_h, grid_w), *refs), grid...  11.5 us
    all_to_all x1, starting transfers between devices, layer(): lax.all_to_all(sums, 'row', 0, 0, tiled=True)  9.46 us
    pallas_call x1, Pallas kernels, layer(): pl.pallas_call(conv_kernel, grid=(sheets, 3), in_specs=[per_sheet(area, w...  9.09 us
    pallas_call x1, Pallas kernels, layer(): pl.pallas_call(tail_kernel, grid_spec=pltpu.PrefetchScalarGridSpec(num_sc...  8.81 us
    all_to_all x1, starting transfers between devices, layer(): lax.all_to_all(strips, 'col', 0, 0, tiled=True)  7.91 us
    ppermute x1, starting transfers between devices, layer(): west = lax.ppermute(edges(cols - HALO), 'col', col_fwd)  6.06 us
    ppermute x1, starting transfers between devices, layer(): att_west = lax.ppermute(att_edges(last_col, cols - 1), 'col', col_fwd)  5.97 us
    ppermute x1, waiting for transfers between devices, layer(): att_below = lax.ppermute(first_row, 'row', row_bwd)  5.71 us
  transfers between devices with their start and end apart: 10, of which 4 were waited for; matrix products, arithmetic and copies ran while one was open for 2% of the time, Pallas kernels for 17%

profile of v6, /device:TPU:32, one launch (start us, length us, event | category | flops | bytes accessed | tf_op | source)
XLA Modules:
  0.0 94.4 jit_solution(14341980100181255695)
XLA Ops:
  0.0 0.0 copy-start
  0.0 0.0 copy-start.11
  0.0 1.2 %fusion.1 = (bf16[2,2,32,1024]{3,2,1,0:T(8,128)(2,1)S(1)}, bf16[2,2,32,1024]{3,2,1,0:T(8,128)(2,1)S(1)}) fusion(bf16[2,16,32,1024]{3,2,1,0:T(8,128)(2,1)} %param.16), kind=kLoop, calls=%fused_computation.7 | loop fusion | bytes 1048576 | tf_op jit(solution)/shard_map/slice | solution.py:510
  1.2 1.9 %collective-permute-start.1 = (bf16[2,2,32,1024]{3,2,1,0:T(8,128)(2,1)S(1)}, bf16[2,2,32,1024]{3,2,1,0:T(8,128)(2,1)S(1)}, u32[]{:S(2)}, u32[]{:S(2)}) collective-permute-start(bf16[2,2,32,1024]{3,2,1,0:T(8,128)(2,1)S(1)} %get-tuple-element.23), channel_id=1, source_target_pairs={{8,0},{16,8},{24,16},{32,24},{40,32},{48,40},{56,48},{64,56},{72,6... | collective-permute-start | bytes 786440 | tf_op jit(solution)/shard_map/ppermute | solution.py:510
  3.2 2.4 %collective-permute-start = (bf16[2,2,32,1024]{3,2,1,0:T(8,128)(2,1)S(1)}, bf16[2,2,32,1024]{3,2,1,0:T(8,128)(2,1)S(1)}, u32[]{:S(2)}, u32[]{:S(2)}) collective-permute-start(bf16[2,2,32,1024]{3,2,1,0:T(8,128)(2,1)S(1)} %get-tuple-element.24), channel_id=1, source_target_pairs={{0,8},{8,16},{16,24},{24,32},{32,40},{40,48},{48,56},{56,64},{64,7... | collective-permute-start | bytes 786440 | tf_op jit(solution)/shard_map/ppermute | solution.py:509
  5.6 1.4 %fusion = (bf16[2,16,2,1024]{3,2,1,0:T(2,128)(2,1)S(1)}, bf16[2,16,2,1024]{3,2,1,0:T(2,128)(2,1)S(1)}) fusion(bf16[2,16,32,1024]{3,2,1,0:T(8,128)(2,1)} %param.16), kind=kLoop, calls=%fused_computation.6 | loop fusion | bytes 524288 | tf_op jit(solution)/shard_map/slice | solution.py:513
  7.0 0.1 pad_add_fusion.refs_0_.place_ref
  7.2 0.1 pad.16.clone
  7.2 0.0 copy-done
  7.2 0.0 copy-done.11
  7.2 0.0 copy-start.1
  7.2 1.2 %copy-done.1 = bf16[1024,512]{1,0:T(8,128)(2,1)S(1)} copy-done((bf16[1024,512]{1,0:T(8,128)(2,1)S(1)}, bf16[1024,512]{1,0:T(8,128)(2,1)}, u32[]{:S(2)}) %copy-start.1) | copy-done | bytes 1048600
  8.5 0.0 copy-start.2
  8.5 0.0 copy-start.4
  8.5 0.0 collective-permute-done.1
  8.6 2.3 %collective-permute-done = bf16[2,2,32,1024]{3,2,1,0:T(8,128)(2,1)S(1)} collective-permute-done((bf16[2,2,32,1024]{3,2,1,0:T(8,128)(2,1)S(1)}, bf16[2,2,32,1024]{3,2,1,0:T(8,128)(2,1)S(1)}, u32[]{:S(2)}, u32[]{:S(2)}) %collective-permute-start) | collective-permute-done | bytes 262176 | tf_op jit(solution)/shard_map/ppermute | solution.py:509
  10.9 0.1 pad_maximum_fusion
  11.0 1.3 %collective-permute-start.2 = (bf16[2,20,2,1024]{3,1,2,0:T(8,128)(2,1)S(1)}, bf16[2,20,2,1024]{3,1,2,0:T(8,128)(2,1)S(1)}, u32[]{:S(2)}, u32[]{:S(2)}) collective-permute-start(bf16[2,20,2,1024]{3,1,2,0:T(8,128)(2,1)S(1)} %pad_maximum_fusion), channel_id=1, source_target_pairs={{1,0},{2,1},{3,2},{4,3},{5,4},{6,5},{7,6},{9,8},{10,9},{11,10},{12... | collective-permute-start | bytes 491528 | tf_op jit(solution)/shard_map/ppermute | solution.py:516
  12.3 0.1 pad_maximum_fusion.1
  12.4 6.1 %collective-permute-start.3 = (bf16[2,20,2,1024]{3,1,2,0:T(8,128)(2,1)S(1)}, bf16[2,20,2,1024]{3,1,2,0:T(8,128)(2,1)S(1)}, u32[]{:S(2)}, u32[]{:S(2)}) collective-permute-start(bf16[2,20,2,1024]{3,1,2,0:T(8,128)(2,1)S(1)} %pad_maximum_fusion.1), channel_id=1, source_target_pairs={{0,1},{1,2},{2,3},{3,4},{4,5},{5,6},{6,7},{8,9},{9,10},{10,11},{11... | collective-permute-start | bytes 491528 | tf_op jit(solution)/shard_map/ppermute | solution.py:515
  18.5 0.0 copy-done.2
  18.5 0.0 copy-done.4
  18.5 0.0 copy-start.13
  18.5 0.0 copy-start.14
  18.5 5.1 %project.1 = (f32[2,16,32,512]{3,2,1,0:T(8,128)S(1)}, f32[2,20,32,1024]{3,2,1,0:T(8,128)S(1)}) custom-call(bf16[2,512,1024]{2,1,0:T(8,128)(2,1)S(1)} %bitcast.13, bf16[2,64,1024]{2,1,0:T(8,128)(2,1)S(1)} %bitcast.17, bf16[2,64,1024]{2,1,0:T(8,128)(2,1)S(1)} %bitcast.16, f32[1,1024]{1,0:T(1,128)S(1)} %warm.1.gain_ref.refs_5_, ...), custom_call_target="tpu_custom_call" | custom-call | flops 3221225472 | bytes 13631488 | tf_op jit(solution)/shard_map/project/pallas_call | solution.py:534
  23.7 0.0 collective-permute-done.2
  23.7 0.2 copy.31
  23.9 1.4 %collective-permute-done.3 = bf16[2,20,2,1024]{3,1,2,0:T(8,128)(2,1)S(1)} collective-permute-done((bf16[2,20,2,1024]{3,1,2,0:T(8,128)(2,1)S(1)}, bf16[2,20,2,1024]{3,1,2,0:T(8,128)(2,1)S(1)}, u32[]{:S(2)}, u32[]{:S(2)}) %collective-permute-start.3) | collective-permute-done | bytes 163872 | tf_op jit(solution)/shard_map/ppermute | solution.py:515
  25.2 0.2 copy.32
  25.4 0.4 maximum_bitcast_fusion.refs_3_
  25.8 0.0 copy-done.13
  25.8 0.0 copy-done.14
  25.8 0.0 copy-start.5
  25.8 0.0 copy-start.9
  25.8 11.5 %attend.1 = (bf16[2,512,1024]{2,1,0:T(8,128)(2,1)}, bf16[16,16,1024]{2,1,0:T(8,128)(2,1)}, bf16[2,32,1024]{2,1,0:T(8,128)(2,1)S(1)}, bf16[2,32,1024]{2,1,0:T(8,1...) custom-call(s32[2]{0:T(128)S(1)} %pad_add_fusion.refs_0_.place_ref, ...), custom_call_target="tpu_custom_call" | custom-call | flops 4294967296 | bytes 8388608 | tf_op jit(solution)/shard_map/attend/pallas_call | solution.py:558
  37.4 1.9 %collective-permute-start.4 = (bf16[2,32,1024]{2,1,0:T(8,128)(2,1)S(1)}, bf16[2,32,1024]{2,1,0:T(8,128)(2,1)S(1)}, u32[]{:S(2)}, u32[]{:S(2)}) collective-permute-start(bf16[2,32,1024]{2,1,0:T(8,128)(2,1)S(1)} %get-tuple-element.17), channel_id=1, source_target_pairs={{0,8},{8,16},{16,24},{24,32},{32,40},{40,48},{48,56},{56,64},{64,7... | collective-permute-start | bytes 393224 | tf_op jit(solution)/shard_map/ppermute | solution.py:597
  39.3 9.5 %all-to-all-start = ((bf16[16,16,1024]{2,1,0:T(8,128)(2,1)}), bf16[16,16,1024]{2,1,0:T(8,128)(2,1)S(1)}, u32[]{:S(2)}, u32[]{:S(2)}) async-start(bf16[16,16,1024]{2,1,0:T(8,128)(2,1)} %get-tuple-element.15), calls=%async_computation | async-start | bytes 1048576 | tf_op jit(solution)/shard_map/all_to_all | solution.py:599
  48.8 2.0 %collective-permute-start.5 = (bf16[2,32,1024]{2,1,0:T(8,128)(2,1)S(1)}, bf16[2,32,1024]{2,1,0:T(8,128)(2,1)S(1)}, u32[]{:S(2)}, u32[]{:S(2)}) collective-permute-start(bf16[2,32,1024]{2,1,0:T(8,128)(2,1)S(1)} %get-tuple-element.18), channel_id=1, source_target_pairs={{8,0},{16,8},{24,16},{32,24},{40,32},{48,40},{56,48},{64,56},{72,6... | collective-permute-start | bytes 393224 | tf_op jit(solution)/shard_map/ppermute | solution.py:598
  50.8 0.0 collective-permute-done.4.top_ref
  50.8 5.7 %collective-permute-done.5.bottom_ref = bf16[2,32,1024]{2,1,0:T(8,128)(2,1)S(1)} collective-permute-done((bf16[2,32,1024]{2,1,0:T(8,128)(2,1)S(1)}, bf16[2,32,1024]{2,1,0:T(8,128)(2,1)S(1)}, u32[]{:S(2)}, u32[]{:S(2)}) %collective-permute-start.5) | collective-permute-done | bytes 131104 | tf_op jit(solution)/shard_map/ppermute | solution.py:598
  56.6 6.0 %collective-permute-start.6 = (bf16[2,18,1024]{2,1,0:T(8,128)(2,1)S(1)}, bf16[2,18,1024]{2,1,0:T(8,128)(2,1)S(1)}, u32[]{:S(2)}, u32[]{:S(2)}) collective-permute-start(bf16[2,18,1024]{2,1,0:T(8,128)(2,1)S(1)} %pad_maximum_fusion.2), channel_id=1, source_target_pairs={{0,1},{1,2},{2,3},{3,4},{4,5},{5,6},{6,7},{8,9},{9,10},{10,11},{11... | collective-permute-start | bytes 221192 | tf_op jit(solution)/shard_map/ppermute | solution.py:604
  62.6 1.3 %collective-permute-start.7 = (bf16[2,18,1024]{2,1,0:T(8,128)(2,1)S(1)}, bf16[2,18,1024]{2,1,0:T(8,128)(2,1)S(1)}, u32[]{:S(2)}, u32[]{:S(2)}) collective-permute-start(bf16[2,18,1024]{2,1,0:T(8,128)(2,1)S(1)} %pad_maximum_fusion.3), channel_id=1, source_target_pairs={{1,0},{2,1},{3,2},{4,3},{5,4},{6,5},{7,6},{9,8},{10,9},{11,10},{12... | collective-permute-start | bytes 221192 | tf_op jit(solution)/shard_map/ppermute | solution.py:605
  63.9 0.0 all-to-all-done
  63.9 0.0 copy-done.5
  63.9 0.0 copy-done.9
  64.0 1.6 %combine.1 = bf16[8,32,1024]{2,1,0:T(8,128)(2,1)} custom-call(s32[2]{0:T(128)S(1)} %pad_add_fusion.refs_0_.place_ref, bf16[16,32,48]{2,1,0:T(8,128)(2,1)S(1)} %copy-done.9, bf16[8,48,256]{2,1,0:T(8,128)(2,1)S(1)} %copy-done.5, bf16[256,1024]{1,0:T(8,128)(2,1)S(1)} %bitcast.11), custom_call_target="tpu_custom_call" | custom-call | tf_op jit(solution)/shard_map/combine/pallas_call | solution.py:609
  65.6 7.9 %all-to-all-start.1 = ((bf16[8,32,1024]{2,1,0:T(8,128)(2,1)}), bf16[8,32,1024]{2,1,0:T(8,128)(2,1)S(1)}, u32[]{:S(2)}, u32[]{:S(2)}) async-start(bf16[8,32,1024]{2,1,0:T(8,128)(2,1)} %combine.1), calls=%async_computation.1 | async-start | bytes 1048576 | tf_op jit(solution)/shard_map/all_to_all | solution.py:625
  73.5 0.0 collective-permute-done.6
  73.5 0.0 collective-permute-done.7
  73.6 0.0 copy-start.3
  73.6 0.0 copy-start.6
  73.6 0.0 copy-start.7
  73.6 0.0 copy-start.8
  73.6 0.0 copy-start.10
  73.6 0.0 copy-start.12
  73.6 9.1 %conv.1.conv_ref = f32[2,512,256]{2,1,0:T(8,128)S(1)} custom-call(bf16[2,512,1024]{2,1,0:T(8,128)(2,1)} %get-tuple-element.16.attended_ref, bf16[2,32,1024]{2,1,0:T(8,128)(2,1)S(1)} %collective-permute-done.4.top_ref, bf16[2,32,1024]{2,1,0:T(8,128)(2,1)S(1)} %collective-permute-done.5.bottom_ref, bf16[2,24,1024]{2,1,0:T(8,128)(2,1)S(1)} %pad.7.left_ref, ...), custom_call_target="tpu_custom_call" | custom-call | flops 4831838208 | bytes 6815744 | tf_op jit(solution)/shard_map/conv/pallas_call | solution.py:627
  82.7 2.7 %all-to-all-done.1 = bf16[8,32,1024]{2,1,0:T(8,128)(2,1)S(1)} async-done(((bf16[8,32,1024]{2,1,0:T(8,128)(2,1)}), bf16[8,32,1024]{2,1,0:T(8,128)(2,1)S(1)}, u32[]{:S(2)}, u32[]{:S(2)}) %all-to-all-start.1) | async-done | bytes 524320 | tf_op jit(solution)/shard_map/all_to_all | solution.py:625
  85.4 0.0 copy-done.3
  85.4 0.0 copy-done.6
  85.4 0.0 copy-done.7
  85.4 0.0 copy-done.8
  85.4 0.0 copy-done.10
  85.4 0.0 copy-done.12
  85.4 8.8 %tail.1 = bf16[2,512,256]{2,1,0:T(8,128)(2,1)} custom-call(s32[2]{0:T(128)S(1)} %pad_add_fusion.refs_0_.place_ref, bf16[8,96,256]{2,1,0:T(8,128)(2,1)S(1)} %copy-done.3, f32[16,1,96]{2,1,0:T(1,128)S(1)} %copy-done.10, f32[8,1,96]{2,1,0:T(1,128)S(1)} %copy-done.12, bf16[256,1024]{1,0:T(8,128)(2,1)S(1)} %bitcast.12, bf16[4,1024,512]{2,1,0:T(8,128)(2,1)} %wpool_hbm.1, ...), custom_call_target="tpu_custom_call" | custom-call | flops 4000000000 | bytes 13631488 | tf_op jit(solution)/shard_map/tail/pallas_call | solution.py:649
  (16 shorter events, 0.3 us)
Async XLA Ops:
  0.0 7.2 %copy-start = (bf16[1024,1024]{1,0:T(8,128)(2,1)S(1)}, bf16[1024,1024]{1,0:T(8,128)(2,1)}, u32[]{:S(2)}) copy-start(bf16[1024,1024]{1,0:T(8,128)(2,1)} %refs_6_.1) | copy-start | bytes 6291460
  0.0 7.2 %copy-start.11 = (f32[1024]{0:T(1024)S(1)}, f32[1024]{0:T(1024)}, u32[]{:S(2)}) copy-start(f32[1024]{0:T(1024)} %param.17) | copy-start | bytes 12292
  1.2 7.2 %collective-permute-start.1 = (bf16[2,2,32,1024]{3,2,1,0:T(8,128)(2,1)S(1)}, bf16[2,2,32,1024]{3,2,1,0:T(8,128)(2,1)S(1)}, u32[]{:S(2)}, u32[]{:S(2)}) collective-permute-start(bf16[2,2,32,1024]{3,2,1,0:T(8,128)(2,1)S(1)} %get-tuple-element.23), channel_id=1, source_target_pairs={{8,0},{16,8},{24,16},{32,24},{40,32},{48,40},{56,48},{64,56},{72,6... | collective-permute-start | bytes 786440 | tf_op jit(solution)/shard_map/ppermute | solution.py:510
  3.2 7.7 %collective-permute-start = (bf16[2,2,32,1024]{3,2,1,0:T(8,128)(2,1)S(1)}, bf16[2,2,32,1024]{3,2,1,0:T(8,128)(2,1)S(1)}, u32[]{:S(2)}, u32[]{:S(2)}) collective-permute-start(bf16[2,2,32,1024]{3,2,1,0:T(8,128)(2,1)S(1)} %get-tuple-element.24), channel_id=1, source_target_pairs={{0,8},{8,16},{16,24},{24,32},{32,40},{40,48},{48,56},{56,64},{64,7... | collective-permute-start | bytes 786440 | tf_op jit(solution)/shard_map/ppermute | solution.py:509
  7.2 1.2 %copy-start.1 = (bf16[1024,512]{1,0:T(8,128)(2,1)S(1)}, bf16[1024,512]{1,0:T(8,128)(2,1)}, u32[]{:S(2)}) copy-start(bf16[1024,512]{1,0:T(8,128)(2,1)} %wq.1) | copy-start | bytes 3145732
  8.5 10.0 %copy-start.2 = (bf16[1024,512]{1,0:T(8,128)(2,1)S(1)}, bf16[1024,512]{1,0:T(8,128)(2,1)}, u32[]{:S(2)}) copy-start(bf16[1024,512]{1,0:T(8,128)(2,1)} %wq.1) | copy-start | bytes 3145732
  8.5 10.0 %copy-start.4 = (bf16[2,16,32,1024]{3,2,1,0:T(8,128)(2,1)S(1)}, bf16[2,16,32,1024]{3,2,1,0:T(8,128)(2,1)}, u32[]{:S(2)}) copy-start(bf16[2,16,32,1024]{3,2,1,0:T(8,128)(2,1)} %param.16) | copy-start | bytes 6291460
  11.0 12.7 %collective-permute-start.2 = (bf16[2,20,2,1024]{3,1,2,0:T(8,128)(2,1)S(1)}, bf16[2,20,2,1024]{3,1,2,0:T(8,128)(2,1)S(1)}, u32[]{:S(2)}, u32[]{:S(2)}) collective-permute-start(bf16[2,20,2,1024]{3,1,2,0:T(8,128)(2,1)S(1)} %pad_maximum_fusion), channel_id=1, source_target_pairs={{1,0},{2,1},{3,2},{4,3},{5,4},{6,5},{7,6},{9,8},{10,9},{11,10},{12... | collective-permute-start | bytes 491528 | tf_op jit(solution)/shard_map/ppermute | solution.py:516
  12.4 12.8 %collective-permute-start.3 = (bf16[2,20,2,1024]{3,1,2,0:T(8,128)(2,1)S(1)}, bf16[2,20,2,1024]{3,1,2,0:T(8,128)(2,1)S(1)}, u32[]{:S(2)}, u32[]{:S(2)}) collective-permute-start(bf16[2,20,2,1024]{3,1,2,0:T(8,128)(2,1)S(1)} %pad_maximum_fusion.1), channel_id=1, source_target_pairs={{0,1},{1,2},{2,3},{3,4},{4,5},{5,6},{6,7},{8,9},{9,10},{10,11},{11... | collective-permute-start | bytes 491528 | tf_op jit(solution)/shard_map/ppermute | solution.py:515
  18.5 7.3 %copy-start.13 = (bf16[512,1024]{1,0:T(8,128)(2,1)S(1)}, bf16[512,1024]{1,0:T(8,128)(2,1)}, u32[]{:S(2)}) copy-start(bf16[512,1024]{1,0:T(8,128)(2,1)} %refs_7_.1) | copy-start | bytes 3145732
  18.5 7.3 %copy-start.14 = (f32[128,8,48]{2,1,0:T(8,128)S(1)}, f32[128,8,48]{2,1,0:T(8,128)}, u32[]{:S(2)}) copy-start(f32[128,8,48]{2,1,0:T(8,128)} %constant.31.clone.refs_8_) | copy-start | bytes 589828
  25.8 38.1 %copy-start.5 = (bf16[8,48,256]{2,1,0:T(8,128)(2,1)S(1)}, bf16[8,48,256]{2,1,0:T(8,128)(2,1)}, u32[]{:S(2)}) copy-start(bf16[8,48,256]{2,1,0:T(8,128)(2,1)} %constant.33.clone.table_ref) | copy-start | bytes 589828
  25.8 38.1 %copy-start.9 = (bf16[16,32,48]{2,1,0:T(8,128)(2,1)S(1)}, bf16[16,32,48]{2,1,0:T(8,128)(2,1)}, u32[]{:S(2)}) copy-start(bf16[16,32,48]{2,1,0:T(8,128)(2,1)} %constant.32.clone.near_ref) | copy-start | bytes 147460
  37.4 13.4 %collective-permute-start.4 = (bf16[2,32,1024]{2,1,0:T(8,128)(2,1)S(1)}, bf16[2,32,1024]{2,1,0:T(8,128)(2,1)S(1)}, u32[]{:S(2)}, u32[]{:S(2)}) collective-permute-start(bf16[2,32,1024]{2,1,0:T(8,128)(2,1)S(1)} %get-tuple-element.17), channel_id=1, source_target_pairs={{0,8},{8,16},{16,24},{24,32},{32,40},{40,48},{48,56},{56,64},{64,7... | collective-permute-start | bytes 393224 | tf_op jit(solution)/shard_map/ppermute | solution.py:597
  39.3 24.6 %all-to-all-start = ((bf16[16,16,1024]{2,1,0:T(8,128)(2,1)}), bf16[16,16,1024]{2,1,0:T(8,128)(2,1)S(1)}, u32[]{:S(2)}, u32[]{:S(2)}) async-start(bf16[16,16,1024]{2,1,0:T(8,128)(2,1)} %get-tuple-element.15), calls=%async_computation | async-start | bytes 1048576 | tf_op jit(solution)/shard_map/all_to_all | solution.py:599
  48.8 7.8 %collective-permute-start.5 = (bf16[2,32,1024]{2,1,0:T(8,128)(2,1)S(1)}, bf16[2,32,1024]{2,1,0:T(8,128)(2,1)S(1)}, u32[]{:S(2)}, u32[]{:S(2)}) collective-permute-start(bf16[2,32,1024]{2,1,0:T(8,128)(2,1)S(1)} %get-tuple-element.18), channel_id=1, source_target_pairs={{8,0},{16,8},{24,16},{32,24},{40,32},{48,40},{56,48},{64,56},{72,6... | collective-permute-start | bytes 393224 | tf_op jit(solution)/shard_map/ppermute | solution.py:598
  56.6 16.9 %collective-permute-start.6 = (bf16[2,18,1024]{2,1,0:T(8,128)(2,1)S(1)}, bf16[2,18,1024]{2,1,0:T(8,128)(2,1)S(1)}, u32[]{:S(2)}, u32[]{:S(2)}) collective-permute-start(bf16[2,18,1024]{2,1,0:T(8,128)(2,1)S(1)} %pad_maximum_fusion.2), channel_id=1, source_target_pairs={{0,1},{1,2},{2,3},{3,4},{4,5},{5,6},{6,7},{8,9},{9,10},{10,11},{11... | collective-permute-start | bytes 221192 | tf_op jit(solution)/shard_map/ppermute | solution.py:604
  62.6 10.9 %collective-permute-start.7 = (bf16[2,18,1024]{2,1,0:T(8,128)(2,1)S(1)}, bf16[2,18,1024]{2,1,0:T(8,128)(2,1)S(1)}, u32[]{:S(2)}, u32[]{:S(2)}) collective-permute-start(bf16[2,18,1024]{2,1,0:T(8,128)(2,1)S(1)} %pad_maximum_fusion.3), channel_id=1, source_target_pairs={{1,0},{2,1},{3,2},{4,3},{5,4},{6,5},{7,6},{9,8},{10,9},{11,10},{12... | collective-permute-start | bytes 221192 | tf_op jit(solution)/shard_map/ppermute | solution.py:605
  65.6 19.8 %all-to-all-start.1 = ((bf16[8,32,1024]{2,1,0:T(8,128)(2,1)}), bf16[8,32,1024]{2,1,0:T(8,128)(2,1)S(1)}, u32[]{:S(2)}, u32[]{:S(2)}) async-start(bf16[8,32,1024]{2,1,0:T(8,128)(2,1)} %combine.1), calls=%async_computation.1 | async-start | bytes 1048576 | tf_op jit(solution)/shard_map/all_to_all | solution.py:625
  73.6 11.8 %copy-start.3 = (bf16[8,96,256]{2,1,0:T(8,128)(2,1)S(1)}, bf16[8,96,256]{2,1,0:T(8,128)(2,1)}, u32[]{:S(2)}) copy-start(bf16[8,96,256]{2,1,0:T(8,128)(2,1)} %constant.34.clone.table_hbm) | copy-start | bytes 1179652
  73.6 11.8 %copy-start.6 = (bf16[2,64,432]{2,1,0:T(8,128)(2,1)S(1)}, bf16[2,64,432]{2,1,0:T(8,128)(2,1)}, u32[]{:S(2)}) copy-start(bf16[2,64,432]{2,1,0:T(8,128)(2,1)} %constant.39.clone.spread_hbm) | copy-start | bytes 331780
  73.6 11.8 %copy-start.7 = (f32[8,32,64]{2,1,0:T(8,128)S(1)}, f32[8,32,64]{2,1,0:T(8,128)}, u32[]{:S(2)}) copy-start(f32[8,32,64]{2,1,0:T(8,128)} %constant.38.clone.by_col_hbm) | copy-start | bytes 196612
  73.6 11.8 %copy-start.8 = (f32[16,16,64]{2,1,0:T(8,128)S(1)}, f32[16,16,64]{2,1,0:T(8,128)}, u32[]{:S(2)}) copy-start(f32[16,16,64]{2,1,0:T(8,128)} %constant.37.clone.by_row_hbm) | copy-start | bytes 196612
  73.6 11.8 %copy-start.10 = (f32[16,1,96]{2,1,0:T(1,128)S(1)}, f32[16,1,96]{2,1,0:T(1,128)}, u32[]{:S(2)}) copy-start(f32[16,1,96]{2,1,0:T(1,128)} %constant.35.clone.row_scale_hbm) | copy-start | bytes 18436
  73.6 11.8 %copy-start.12 = (f32[8,1,96]{2,1,0:T(1,128)S(1)}, f32[8,1,96]{2,1,0:T(1,128)}, u32[]{:S(2)}) copy-start(f32[8,1,96]{2,1,0:T(1,128)} %constant.36.clone.col_scale_hbm) | copy-start | bytes 9220

commit v7 on v6

--- a/solution.py
+++ b/solution.py
@@ -382,8 +382,8 @@
 
 def tail_kernel(
     place_ref, table_hbm, row_scale_hbm, col_scale_hbm, parts_hbm, wpool_hbm, wjoin_hbm, by_row_hbm, by_col_hbm,
-    spread_hbm, conv_ref, out_hbm,
-    table, row_scale, col_scale, parts, by_row, by_col, spread, wpool, wjoin, conv, taps, out, sems,
+    spread_hbm, conv, out_hbm,
+    table, row_scale, col_scale, parts, by_row, by_col, spread, wpool, wjoin, taps, out, sems,
 ):
     width, ppm = wpool.shape[1], wpool.shape[2]
     count = len(LEVELS)
@@ -432,18 +432,9 @@
         row += 2 * slots
     results = [pltpu.make_async_copy(out.at[s], out_hbm.at[s], sems.at[2, s]) for s in range(2)]
 
-    def spread_over(s, part):
-        high, low = split(taps[s, part])
-        lines = dot(grid_high[:, part], high) + dot(grid_low[:, part], high)
-        return lines + dot(grid_high[:, part], low)
-
     at = 0
     for index, level in enumerate(LEVELS):
         slots = SLOTS[level]
-        last = index == count - 1
-        if last:
-            for s in range(2):
-                conv[s] = conv_ref[s] + spread_over(s, slice(0, at))
         ready(count + index)
         for a in range(3):
             for b in range(3):
@@ -452,11 +443,12 @@
                 start = at + (a * 3 + b) * slots
                 for s in range(2):
                     taps[s, start : start + slots, :] = tap[s * slots : (s + 1) * slots]
-        if last:
-            for s in range(2):
-                out[s] = (conv[s] + spread_over(s, slice(at, at + TAPS * slots))).astype(bf16)
-                results[s].start()
         at += TAPS * slots
+    for s in range(2):
+        high, low = split(taps[s])
+        total = conv[s] + dot(grid_high, high) + dot(grid_low, high) + dot(grid_high, low)
+        out[s] = total.astype(bf16)
+        results[s].start()
     for copy in results:
         copy.wait()
 
@@ -663,7 +655,6 @@
                 pltpu.VMEM((2, 64, depth), bf16),
                 pltpu.VMEM(w_pool.shape, bf16),
                 pltpu.VMEM((len(LEVELS), 3, 3, ppm, out_ch), bf16),
-                pltpu.VMEM((sheets, area, out_ch), f32),
                 pltpu.VMEM((sheets, depth, out_ch), f32),
                 pltpu.VMEM((sheets, area, out_ch), bf16),
                 pltpu.SemaphoreType.DMA((3, 2 * len(LEVELS))),

time: 95 us -> 94.6 us (level)
  no operation moved by 1% of the time
where the time goes in v7:
time: 94.6 us; the launch traced here: 94 us
  starting transfers between devices  40.2 us (42%)
  Pallas kernels  35.8 us (38%)
  waiting for transfers between devices  12.1 us (13%)
  local copies, waits for them, and re-layouts  4.59 us (5%)
    pallas_call x1, Pallas kernels, layer(): pl.pallas_call(lambda *refs: attend_kernel((grid_h, grid_w), *refs), grid...  11.5 us
    all_to_all x1, starting transfers between devices, layer(): lax.all_to_all(sums, 'row', 0, 0, tiled=True)  9.46 us
    pallas_call x1, Pallas kernels, layer(): pl.pallas_call(conv_kernel, grid=(sheets, 3), in_specs=[per_sheet(area, w...  9.09 us
    pallas_call x1, Pallas kernels, layer(): pl.pallas_call(tail_kernel, grid_spec=pltpu.PrefetchScalarGridSpec(num_sc...  8.38 us
    all_to_all x1, starting transfers between devices, layer(): lax.all_to_all(strips, 'col', 0, 0, tiled=True)  7.91 us
    ppermute x1, starting transfers between devices, layer(): west = lax.ppermute(edges(cols - HALO), 'col', col_fwd)  6.06 us
    ppermute x1, starting transfers between devices, layer(): att_west = lax.ppermute(att_edges(last_col, cols - 1), 'col', col_fwd)  5.97 us
    ppermute x1, waiting for transfers between devices, layer(): att_below = lax.ppermute(first_row, 'row', row_bwd)  5.71 us
  transfers between devices with their start and end apart: 10, of which 4 were waited for; matrix products, arithmetic and copies ran while one was open for 2% of the time, Pallas kernels for 17%

profile of v7, /device:TPU:32, one launch (start us, length us, event | category | flops | bytes accessed | tf_op | source)
XLA Modules:
  0.0 94.0 jit_solution(4950937365224398898)
XLA Ops:
  0.0 0.0 copy-start
  0.0 0.0 copy-start.11
  0.0 1.2 %fusion.1 = (bf16[2,2,32,1024]{3,2,1,0:T(8,128)(2,1)S(1)}, bf16[2,2,32,1024]{3,2,1,0:T(8,128)(2,1)S(1)}) fusion(bf16[2,16,32,1024]{3,2,1,0:T(8,128)(2,1)} %param.16), kind=kLoop, calls=%fused_computation.7 | loop fusion | bytes 1048576 | tf_op jit(solution)/shard_map/slice | solution.py:502
  1.2 1.9 %collective-permute-start.1 = (bf16[2,2,32,1024]{3,2,1,0:T(8,128)(2,1)S(1)}, bf16[2,2,32,1024]{3,2,1,0:T(8,128)(2,1)S(1)}, u32[]{:S(2)}, u32[]{:S(2)}) collective-permute-start(bf16[2,2,32,1024]{3,2,1,0:T(8,128)(2,1)S(1)} %get-tuple-element.23), channel_id=1, source_target_pairs={{8,0},{16,8},{24,16},{32,24},{40,32},{48,40},{56,48},{64,56},{72,6... | collective-permute-start | bytes 786440 | tf_op jit(solution)/shard_map/ppermute | solution.py:502
  3.2 2.4 %collective-permute-start = (bf16[2,2,32,1024]{3,2,1,0:T(8,128)(2,1)S(1)}, bf16[2,2,32,1024]{3,2,1,0:T(8,128)(2,1)S(1)}, u32[]{:S(2)}, u32[]{:S(2)}) collective-permute-start(bf16[2,2,32,1024]{3,2,1,0:T(8,128)(2,1)S(1)} %get-tuple-element.24), channel_id=1, source_target_pairs={{0,8},{8,16},{16,24},{24,32},{32,40},{40,48},{48,56},{56,64},{64,7... | collective-permute-start | bytes 786440 | tf_op jit(solution)/shard_map/ppermute | solution.py:501
  5.6 1.4 %fusion = (bf16[2,16,2,1024]{3,2,1,0:T(2,128)(2,1)S(1)}, bf16[2,16,2,1024]{3,2,1,0:T(2,128)(2,1)S(1)}) fusion(bf16[2,16,32,1024]{3,2,1,0:T(8,128)(2,1)} %param.16), kind=kLoop, calls=%fused_computation.6 | loop fusion | bytes 524288 | tf_op jit(solution)/shard_map/slice | solution.py:505
  7.0 0.1 pad_add_fusion.refs_0_.place_ref
  7.2 0.1 pad.16.clone
  7.2 0.0 copy-done
  7.2 0.0 copy-done.11
  7.2 0.0 copy-start.1
  7.2 1.2 %copy-done.1 = bf16[1024,512]{1,0:T(8,128)(2,1)S(1)} copy-done((bf16[1024,512]{1,0:T(8,128)(2,1)S(1)}, bf16[1024,512]{1,0:T(8,128)(2,1)}, u32[]{:S(2)}) %copy-start.1) | copy-done | bytes 1048600
  8.5 0.0 copy-start.2
  8.5 0.0 copy-start.4
  8.5 0.0 collective-permute-done.1
  8.6 2.3 %collective-permute-done = bf16[2,2,32,1024]{3,2,1,0:T(8,128)(2,1)S(1)} collective-permute-done((bf16[2,2,32,1024]{3,2,1,0:T(8,128)(2,1)S(1)}, bf16[2,2,32,1024]{3,2,1,0:T(8,128)(2,1)S(1)}, u32[]{:S(2)}, u32[]{:S(2)}) %collective-permute-start) | collective-permute-done | bytes 262176 | tf_op jit(solution)/shard_map/ppermute | solution.py:501
  10.9 0.1 pad_maximum_fusion
  11.0 1.3 %collective-permute-start.2 = (bf16[2,20,2,1024]{3,1,2,0:T(8,128)(2,1)S(1)}, bf16[2,20,2,1024]{3,1,2,0:T(8,128)(2,1)S(1)}, u32[]{:S(2)}, u32[]{:S(2)}) collective-permute-start(bf16[2,20,2,1024]{3,1,2,0:T(8,128)(2,1)S(1)} %pad_maximum_fusion), channel_id=1, source_target_pairs={{1,0},{2,1},{3,2},{4,3},{5,4},{6,5},{7,6},{9,8},{10,9},{11,10},{12... | collective-permute-start | bytes 491528 | tf_op jit(solution)/shard_map/ppermute | solution.py:508
  12.3 0.1 pad_maximum_fusion.1
  12.4 6.1 %collective-permute-start.3 = (bf16[2,20,2,1024]{3,1,2,0:T(8,128)(2,1)S(1)}, bf16[2,20,2,1024]{3,1,2,0:T(8,128)(2,1)S(1)}, u32[]{:S(2)}, u32[]{:S(2)}) collective-permute-start(bf16[2,20,2,1024]{3,1,2,0:T(8,128)(2,1)S(1)} %pad_maximum_fusion.1), channel_id=1, source_target_pairs={{0,1},{1,2},{2,3},{3,4},{4,5},{5,6},{6,7},{8,9},{9,10},{10,11},{11... | collective-permute-start | bytes 491528 | tf_op jit(solution)/shard_map/ppermute | solution.py:507
  18.5 0.0 copy-done.2
  18.5 0.0 copy-done.4
  18.5 0.0 copy-start.13
  18.5 0.0 copy-start.14
  18.5 5.1 %project.1 = (f32[2,16,32,512]{3,2,1,0:T(8,128)S(1)}, f32[2,20,32,1024]{3,2,1,0:T(8,128)S(1)}) custom-call(bf16[2,512,1024]{2,1,0:T(8,128)(2,1)S(1)} %bitcast.13, bf16[2,64,1024]{2,1,0:T(8,128)(2,1)S(1)} %bitcast.17, bf16[2,64,1024]{2,1,0:T(8,128)(2,1)S(1)} %bitcast.16, f32[1,1024]{1,0:T(1,128)S(1)} %warm.1.gain_ref.refs_5_, ...), custom_call_target="tpu_custom_call" | custom-call | flops 3221225472 | bytes 13631488 | tf_op jit(solution)/shard_map/project/pallas_call | solution.py:526
  23.7 0.0 collective-permute-done.2
  23.7 0.2 copy.31
  23.9 1.4 %collective-permute-done.3 = bf16[2,20,2,1024]{3,1,2,0:T(8,128)(2,1)S(1)} collective-permute-done((bf16[2,20,2,1024]{3,1,2,0:T(8,128)(2,1)S(1)}, bf16[2,20,2,1024]{3,1,2,0:T(8,128)(2,1)S(1)}, u32[]{:S(2)}, u32[]{:S(2)}) %collective-permute-start.3) | collective-permute-done | bytes 163872 | tf_op jit(solution)/shard_map/ppermute | solution.py:507
  25.2 0.2 copy.32
  25.4 0.4 maximum_bitcast_fusion.refs_3_
  25.8 0.0 copy-done.13
  25.8 0.0 copy-done.14
  25.8 0.0 copy-start.5
  25.8 0.0 copy-start.9
  25.8 11.5 %attend.1 = (bf16[2,512,1024]{2,1,0:T(8,128)(2,1)}, bf16[16,16,1024]{2,1,0:T(8,128)(2,1)}, bf16[2,32,1024]{2,1,0:T(8,128)(2,1)S(1)}, bf16[2,32,1024]{2,1,0:T(8,1...) custom-call(s32[2]{0:T(128)S(1)} %pad_add_fusion.refs_0_.place_ref, ...), custom_call_target="tpu_custom_call" | custom-call | flops 4294967296 | bytes 8388608 | tf_op jit(solution)/shard_map/attend/pallas_call | solution.py:550
  37.4 1.9 %collective-permute-start.4 = (bf16[2,32,1024]{2,1,0:T(8,128)(2,1)S(1)}, bf16[2,32,1024]{2,1,0:T(8,128)(2,1)S(1)}, u32[]{:S(2)}, u32[]{:S(2)}) collective-permute-start(bf16[2,32,1024]{2,1,0:T(8,128)(2,1)S(1)} %get-tuple-element.17), channel_id=1, source_target_pairs={{0,8},{8,16},{16,24},{24,32},{32,40},{40,48},{48,56},{56,64},{64,7... | collective-permute-start | bytes 393224 | tf_op jit(solution)/shard_map/ppermute | solution.py:589
  39.3 9.5 %all-to-all-start = ((bf16[16,16,1024]{2,1,0:T(8,128)(2,1)}), bf16[16,16,1024]{2,1,0:T(8,128)(2,1)S(1)}, u32[]{:S(2)}, u32[]{:S(2)}) async-start(bf16[16,16,1024]{2,1,0:T(8,128)(2,1)} %get-tuple-element.15), calls=%async_computation | async-start | bytes 1048576 | tf_op jit(solution)/shard_map/all_to_all | solution.py:591
  48.8 2.0 %collective-permute-start.5 = (bf16[2,32,1024]{2,1,0:T(8,128)(2,1)S(1)}, bf16[2,32,1024]{2,1,0:T(8,128)(2,1)S(1)}, u32[]{:S(2)}, u32[]{:S(2)}) collective-permute-start(bf16[2,32,1024]{2,1,0:T(8,128)(2,1)S(1)} %get-tuple-element.18), channel_id=1, source_target_pairs={{8,0},{16,8},{24,16},{32,24},{40,32},{48,40},{56,48},{64,56},{72,6... | collective-permute-start | bytes 393224 | tf_op jit(solution)/shard_map/ppermute | solution.py:590
  50.8 0.0 collective-permute-done.4.top_ref
  50.8 5.7 %collective-permute-done.5.bottom_ref = bf16[2,32,1024]{2,1,0:T(8,128)(2,1)S(1)} collective-permute-done((bf16[2,32,1024]{2,1,0:T(8,128)(2,1)S(1)}, bf16[2,32,1024]{2,1,0:T(8,128)(2,1)S(1)}, u32[]{:S(2)}, u32[]{:S(2)}) %collective-permute-start.5) | collective-permute-done | bytes 131104 | tf_op jit(solution)/shard_map/ppermute | solution.py:590
  56.6 6.0 %collective-permute-start.6 = (bf16[2,18,1024]{2,1,0:T(8,128)(2,1)S(1)}, bf16[2,18,1024]{2,1,0:T(8,128)(2,1)S(1)}, u32[]{:S(2)}, u32[]{:S(2)}) collective-permute-start(bf16[2,18,1024]{2,1,0:T(8,128)(2,1)S(1)} %pad_maximum_fusion.2), channel_id=1, source_target_pairs={{0,1},{1,2},{2,3},{3,4},{4,5},{5,6},{6,7},{8,9},{9,10},{10,11},{11... | collective-permute-start | bytes 221192 | tf_op jit(solution)/shard_map/ppermute | solution.py:596
  62.6 1.3 %collective-permute-start.7 = (bf16[2,18,1024]{2,1,0:T(8,128)(2,1)S(1)}, bf16[2,18,1024]{2,1,0:T(8,128)(2,1)S(1)}, u32[]{:S(2)}, u32[]{:S(2)}) collective-permute-start(bf16[2,18,1024]{2,1,0:T(8,128)(2,1)S(1)} %pad_maximum_fusion.3), channel_id=1, source_target_pairs={{1,0},{2,1},{3,2},{4,3},{5,4},{6,5},{7,6},{9,8},{10,9},{11,10},{12... | collective-permute-start | bytes 221192 | tf_op jit(solution)/shard_map/ppermute | solution.py:597
  63.9 0.0 all-to-all-done
  63.9 0.0 copy-done.5
  63.9 0.0 copy-done.9
  64.0 1.6 %combine.1 = bf16[8,32,1024]{2,1,0:T(8,128)(2,1)} custom-call(s32[2]{0:T(128)S(1)} %pad_add_fusion.refs_0_.place_ref, bf16[16,32,48]{2,1,0:T(8,128)(2,1)S(1)} %copy-done.9, bf16[8,48,256]{2,1,0:T(8,128)(2,1)S(1)} %copy-done.5, bf16[256,1024]{1,0:T(8,128)(2,1)S(1)} %bitcast.11), custom_call_target="tpu_custom_call" | custom-call | tf_op jit(solution)/shard_map/combine/pallas_call | solution.py:601
  65.6 7.9 %all-to-all-start.1 = ((bf16[8,32,1024]{2,1,0:T(8,128)(2,1)}), bf16[8,32,1024]{2,1,0:T(8,128)(2,1)S(1)}, u32[]{:S(2)}, u32[]{:S(2)}) async-start(bf16[8,32,1024]{2,1,0:T(8,128)(2,1)} %combine.1), calls=%async_computation.1 | async-start | bytes 1048576 | tf_op jit(solution)/shard_map/all_to_all | solution.py:617
  73.5 0.0 collective-permute-done.6
  73.5 0.0 collective-permute-done.7
  73.6 0.0 copy-start.3
  73.6 0.0 copy-start.6
  73.6 0.0 copy-start.7
  73.6 0.0 copy-start.8
  73.6 0.0 copy-start.10
  73.6 0.0 copy-start.12
  73.6 9.1 %conv.1 = f32[2,512,256]{2,1,0:T(8,128)S(1)} custom-call(bf16[2,512,1024]{2,1,0:T(8,128)(2,1)} %get-tuple-element.16.attended_ref, bf16[2,32,1024]{2,1,0:T(8,128)(2,1)S(1)} %collective-permute-done.4.top_ref, bf16[2,32,1024]{2,1,0:T(8,128)(2,1)S(1)} %collective-permute-done.5.bottom_ref, bf16[2,24,1024]{2,1,0:T(8,128)(2,1)S(1)} %pad.7.left_ref, ...), custom_call_target="tpu_custom_call" | custom-call | flops 4831838208 | bytes 6815744 | tf_op jit(solution)/shard_map/conv/pallas_call | solution.py:619
  82.7 2.7 %all-to-all-done.1 = bf16[8,32,1024]{2,1,0:T(8,128)(2,1)S(1)} async-done(((bf16[8,32,1024]{2,1,0:T(8,128)(2,1)}), bf16[8,32,1024]{2,1,0:T(8,128)(2,1)S(1)}, u32[]{:S(2)}, u32[]{:S(2)}) %all-to-all-start.1) | async-done | bytes 524320 | tf_op jit(solution)/shard_map/all_to_all | solution.py:617
  85.4 0.0 copy-done.3
  85.4 0.0 copy-done.6
  85.4 0.0 copy-done.7
  85.4 0.0 copy-done.8
  85.4 0.0 copy-done.10
  85.4 0.0 copy-done.12
  85.4 8.4 %tail.1 = bf16[2,512,256]{2,1,0:T(8,128)(2,1)} custom-call(s32[2]{0:T(128)S(1)} %pad_add_fusion.refs_0_.place_ref, bf16[8,96,256]{2,1,0:T(8,128)(2,1)S(1)} %copy-done.3, f32[16,1,96]{2,1,0:T(1,128)S(1)} %copy-done.10, f32[8,1,96]{2,1,0:T(1,128)S(1)} %copy-done.12, bf16[256,1024]{1,0:T(8,128)(2,1)S(1)} %bitcast.12, bf16[4,1024,512]{2,1,0:T(8,128)(2,1)} %wpool_hbm.1, ...), custom_call_target="tpu_custom_call" | custom-call | flops 4000000000 | bytes 13631488 | tf_op jit(solution)/shard_map/tail/pallas_call | solution.py:641
  (16 shorter events, 0.3 us)
Async XLA Ops:
  0.0 7.2 %copy-start = (bf16[1024,1024]{1,0:T(8,128)(2,1)S(1)}, bf16[1024,1024]{1,0:T(8,128)(2,1)}, u32[]{:S(2)}) copy-start(bf16[1024,1024]{1,0:T(8,128)(2,1)} %refs_6_.1) | copy-start | bytes 6291460
  0.0 7.2 %copy-start.11 = (f32[1024]{0:T(1024)S(1)}, f32[1024]{0:T(1024)}, u32[]{:S(2)}) copy-start(f32[1024]{0:T(1024)} %param.17) | copy-start | bytes 12292
  1.2 7.2 %collective-permute-start.1 = (bf16[2,2,32,1024]{3,2,1,0:T(8,128)(2,1)S(1)}, bf16[2,2,32,1024]{3,2,1,0:T(8,128)(2,1)S(1)}, u32[]{:S(2)}, u32[]{:S(2)}) collective-permute-start(bf16[2,2,32,1024]{3,2,1,0:T(8,128)(2,1)S(1)} %get-tuple-element.23), channel_id=1, source_target_pairs={{8,0},{16,8},{24,16},{32,24},{40,32},{48,40},{56,48},{64,56},{72,6... | collective-permute-start | bytes 786440 | tf_op jit(solution)/shard_map/ppermute | solution.py:502
  3.2 7.7 %collective-permute-start = (bf16[2,2,32,1024]{3,2,1,0:T(8,128)(2,1)S(1)}, bf16[2,2,32,1024]{3,2,1,0:T(8,128)(2,1)S(1)}, u32[]{:S(2)}, u32[]{:S(2)}) collective-permute-start(bf16[2,2,32,1024]{3,2,1,0:T(8,128)(2,1)S(1)} %get-tuple-element.24), channel_id=1, source_target_pairs={{0,8},{8,16},{16,24},{24,32},{32,40},{40,48},{48,56},{56,64},{64,7... | collective-permute-start | bytes 786440 | tf_op jit(solution)/shard_map/ppermute | solution.py:501
  7.2 1.2 %copy-start.1 = (bf16[1024,512]{1,0:T(8,128)(2,1)S(1)}, bf16[1024,512]{1,0:T(8,128)(2,1)}, u32[]{:S(2)}) copy-start(bf16[1024,512]{1,0:T(8,128)(2,1)} %wq.1) | copy-start | bytes 3145732
  8.5 10.0 %copy-start.2 = (bf16[1024,512]{1,0:T(8,128)(2,1)S(1)}, bf16[1024,512]{1,0:T(8,128)(2,1)}, u32[]{:S(2)}) copy-start(bf16[1024,512]{1,0:T(8,128)(2,1)} %wq.1) | copy-start | bytes 3145732
  8.5 10.0 %copy-start.4 = (bf16[2,16,32,1024]{3,2,1,0:T(8,128)(2,1)S(1)}, bf16[2,16,32,1024]{3,2,1,0:T(8,128)(2,1)}, u32[]{:S(2)}) copy-start(bf16[2,16,32,1024]{3,2,1,0:T(8,128)(2,1)} %param.16) | copy-start | bytes 6291460
  11.0 12.7 %collective-permute-start.2 = (bf16[2,20,2,1024]{3,1,2,0:T(8,128)(2,1)S(1)}, bf16[2,20,2,1024]{3,1,2,0:T(8,128)(2,1)S(1)}, u32[]{:S(2)}, u32[]{:S(2)}) collective-permute-start(bf16[2,20,2,1024]{3,1,2,0:T(8,128)(2,1)S(1)} %pad_maximum_fusion), channel_id=1, source_target_pairs={{1,0},{2,1},{3,2},{4,3},{5,4},{6,5},{7,6},{9,8},{10,9},{11,10},{12... | collective-permute-start | bytes 491528 | tf_op jit(solution)/shard_map/ppermute | solution.py:508
  12.4 12.8 %collective-permute-start.3 = (bf16[2,20,2,1024]{3,1,2,0:T(8,128)(2,1)S(1)}, bf16[2,20,2,1024]{3,1,2,0:T(8,128)(2,1)S(1)}, u32[]{:S(2)}, u32[]{:S(2)}) collective-permute-start(bf16[2,20,2,1024]{3,1,2,0:T(8,128)(2,1)S(1)} %pad_maximum_fusion.1), channel_id=1, source_target_pairs={{0,1},{1,2},{2,3},{3,4},{4,5},{5,6},{6,7},{8,9},{9,10},{10,11},{11... | collective-permute-start | bytes 491528 | tf_op jit(solution)/shard_map/ppermute | solution.py:507
  18.5 7.3 %copy-start.13 = (bf16[512,1024]{1,0:T(8,128)(2,1)S(1)}, bf16[512,1024]{1,0:T(8,128)(2,1)}, u32[]{:S(2)}) copy-start(bf16[512,1024]{1,0:T(8,128)(2,1)} %refs_7_.1) | copy-start | bytes 3145732
  18.5 7.3 %copy-start.14 = (f32[128,8,48]{2,1,0:T(8,128)S(1)}, f32[128,8,48]{2,1,0:T(8,128)}, u32[]{:S(2)}) copy-start(f32[128,8,48]{2,1,0:T(8,128)} %constant.31.clone.refs_8_) | copy-start | bytes 589828
  25.8 38.1 %copy-start.5 = (bf16[8,48,256]{2,1,0:T(8,128)(2,1)S(1)}, bf16[8,48,256]{2,1,0:T(8,128)(2,1)}, u32[]{:S(2)}) copy-start(bf16[8,48,256]{2,1,0:T(8,128)(2,1)} %constant.33.clone.table_ref) | copy-start | bytes 589828
  25.8 38.1 %copy-start.9 = (bf16[16,32,48]{2,1,0:T(8,128)(2,1)S(1)}, bf16[16,32,48]{2,1,0:T(8,128)(2,1)}, u32[]{:S(2)}) copy-start(bf16[16,32,48]{2,1,0:T(8,128)(2,1)} %constant.32.clone.near_ref) | copy-start | bytes 147460
  37.4 13.4 %collective-permute-start.4 = (bf16[2,32,1024]{2,1,0:T(8,128)(2,1)S(1)}, bf16[2,32,1024]{2,1,0:T(8,128)(2,1)S(1)}, u32[]{:S(2)}, u32[]{:S(2)}) collective-permute-start(bf16[2,32,1024]{2,1,0:T(8,128)(2,1)S(1)} %get-tuple-element.17), channel_id=1, source_target_pairs={{0,8},{8,16},{16,24},{24,32},{32,40},{40,48},{48,56},{56,64},{64,7... | collective-permute-start | bytes 393224 | tf_op jit(solution)/shard_map/ppermute | solution.py:589
  39.3 24.6 %all-to-all-start = ((bf16[16,16,1024]{2,1,0:T(8,128)(2,1)}), bf16[16,16,1024]{2,1,0:T(8,128)(2,1)S(1)}, u32[]{:S(2)}, u32[]{:S(2)}) async-start(bf16[16,16,1024]{2,1,0:T(8,128)(2,1)} %get-tuple-element.15), calls=%async_computation | async-start | bytes 1048576 | tf_op jit(solution)/shard_map/all_to_all | solution.py:591
  48.8 7.8 %collective-permute-start.5 = (bf16[2,32,1024]{2,1,0:T(8,128)(2,1)S(1)}, bf16[2,32,1024]{2,1,0:T(8,128)(2,1)S(1)}, u32[]{:S(2)}, u32[]{:S(2)}) collective-permute-start(bf16[2,32,1024]{2,1,0:T(8,128)(2,1)S(1)} %get-tuple-element.18), channel_id=1, source_target_pairs={{8,0},{16,8},{24,16},{32,24},{40,32},{48,40},{56,48},{64,56},{72,6... | collective-permute-start | bytes 393224 | tf_op jit(solution)/shard_map/ppermute | solution.py:590
  56.6 16.9 %collective-permute-start.6 = (bf16[2,18,1024]{2,1,0:T(8,128)(2,1)S(1)}, bf16[2,18,1024]{2,1,0:T(8,128)(2,1)S(1)}, u32[]{:S(2)}, u32[]{:S(2)}) collective-permute-start(bf16[2,18,1024]{2,1,0:T(8,128)(2,1)S(1)} %pad_maximum_fusion.2), channel_id=1, source_target_pairs={{0,1},{1,2},{2,3},{3,4},{4,5},{5,6},{6,7},{8,9},{9,10},{10,11},{11... | collective-permute-start | bytes 221192 | tf_op jit(solution)/shard_map/ppermute | solution.py:596
  62.6 10.9 %collective-permute-start.7 = (bf16[2,18,1024]{2,1,0:T(8,128)(2,1)S(1)}, bf16[2,18,1024]{2,1,0:T(8,128)(2,1)S(1)}, u32[]{:S(2)}, u32[]{:S(2)}) collective-permute-start(bf16[2,18,1024]{2,1,0:T(8,128)(2,1)S(1)} %pad_maximum_fusion.3), channel_id=1, source_target_pairs={{1,0},{2,1},{3,2},{4,3},{5,4},{6,5},{7,6},{9,8},{10,9},{11,10},{12... | collective-permute-start | bytes 221192 | tf_op jit(solution)/shard_map/ppermute | solution.py:597
  65.6 19.8 %all-to-all-start.1 = ((bf16[8,32,1024]{2,1,0:T(8,128)(2,1)}), bf16[8,32,1024]{2,1,0:T(8,128)(2,1)S(1)}, u32[]{:S(2)}, u32[]{:S(2)}) async-start(bf16[8,32,1024]{2,1,0:T(8,128)(2,1)} %combine.1), calls=%async_computation.1 | async-start | bytes 1048576 | tf_op jit(solution)/shard_map/all_to_all | solution.py:617
  73.6 11.8 %copy-start.3 = (bf16[8,96,256]{2,1,0:T(8,128)(2,1)S(1)}, bf16[8,96,256]{2,1,0:T(8,128)(2,1)}, u32[]{:S(2)}) copy-start(bf16[8,96,256]{2,1,0:T(8,128)(2,1)} %constant.34.clone.table_hbm) | copy-start | bytes 1179652
  73.6 11.8 %copy-start.6 = (bf16[2,64,432]{2,1,0:T(8,128)(2,1)S(1)}, bf16[2,64,432]{2,1,0:T(8,128)(2,1)}, u32[]{:S(2)}) copy-start(bf16[2,64,432]{2,1,0:T(8,128)(2,1)} %constant.39.clone.spread_hbm) | copy-start | bytes 331780
  73.6 11.8 %copy-start.7 = (f32[8,32,64]{2,1,0:T(8,128)S(1)}, f32[8,32,64]{2,1,0:T(8,128)}, u32[]{:S(2)}) copy-start(f32[8,32,64]{2,1,0:T(8,128)} %constant.38.clone.by_col_hbm) | copy-start | bytes 196612
  73.6 11.8 %copy-start.8 = (f32[16,16,64]{2,1,0:T(8,128)S(1)}, f32[16,16,64]{2,1,0:T(8,128)}, u32[]{:S(2)}) copy-start(f32[16,16,64]{2,1,0:T(8,128)} %constant.37.clone.by_row_hbm) | copy-start | bytes 196612
  73.6 11.8 %copy-start.10 = (f32[16,1,96]{2,1,0:T(1,128)S(1)}, f32[16,1,96]{2,1,0:T(1,128)}, u32[]{:S(2)}) copy-start(f32[16,1,96]{2,1,0:T(1,128)} %constant.35.clone.row_scale_hbm) | copy-start | bytes 18436
  73.6 11.8 %copy-start.12 = (f32[8,1,96]{2,1,0:T(1,128)S(1)}, f32[8,1,96]{2,1,0:T(1,128)}, u32[]{:S(2)}) copy-start(f32[8,1,96]{2,1,0:T(1,128)} %constant.36.clone.col_scale_hbm) | copy-start | bytes 9220

commit v8 on v7

--- a/solution.py
+++ b/solution.py
@@ -179,7 +179,22 @@
     out_ref[...] = gain_ref[...]
 
 
-def project_kernel(tokens_ref, above_ref, below_ref, gain_ref, wq, wkv, q_ref, kv_ref):
+def pool_members(masks_ref, pool, cols):
+    masks = masks_ref[...].astype(bf16)
+    _, count = masks.shape
+    area = pool.shape[1]
+    rows = count - cols
+    unit = lax.broadcasted_iota(jnp.int32, (count, area), 0)
+    token = lax.broadcasted_iota(jnp.int32, (count, area), 1)
+    to_row = (unit == token // cols).astype(f32).astype(bf16)
+    to_col = (unit - rows == token % cols).astype(f32).astype(bf16)
+    pool[...] = (dot(masks, to_row) * dot(masks, to_col)).astype(bf16)
+
+
+def project_kernel(
+    grid_shape, place_ref, tokens_ref, above_ref, below_ref, gain_ref, wq, wkv, masks_ref,
+    q_ref, kv_ref, bias, pool, context, scores, weights,
+):
     rows, cols, inner = q_ref.shape[1:]
     s = pl.program_id(0)
     gain = gain_ref[...]
@@ -190,6 +205,17 @@
     edge = dot(edge, wkv[...]).astype(bf16).astype(f32).reshape(2 * HALO, cols, -1)
     kv_ref[s, 0:HALO] = edge[:HALO]
     kv_ref[s, rows + HALO :] = edge[HALO:]
+
+    @pl.when(s == 0)
+    def _():
+        window_bias(bias, place_ref[0] * rows, place_ref[1] * cols, *grid_shape)
+        pool_members(masks_ref, pool, cols)
+
+    def store(at, b, lanes, piece):
+        context[s, at : at + BLOCK, (b - 1) * BLOCK : b * BLOCK, lanes] = piece
+
+    middle = range(1, cols // BLOCK - 1)
+    attend_blocks(middle, s, q_ref, kv_ref, None, bias, scores, weights, store)
 
 
 def window_bias(bias, first_row, first_col, grid_h, grid_w):
@@ -210,28 +236,11 @@
             bias[a, b] = jnp.where(row_ok & (at >= 0) & (at < grid_w), 0.0, -1e30)
 
 
-def attend_kernel(
-    grid_shape, place_ref, q_ref, kv_ref, sides_ref, tokens_ref, gain_ref, wkv_ref, wout_ref, masks_ref,
-    attended_ref, sums_ref, first_row_ref, last_row_ref, first_col_ref, last_col_ref, sides, context, bias, pool, scores, weights,
-):
+def attend_blocks(columns, sheet, q_ref, kv_ref, sides, bias, scores, weights, store):
     rows, cols, inner = q_ref.shape[1:]
     groups = cols // BLOCK
     span = BLOCK + 2 * HALO
-
-    @pl.when(pl.program_id(0) == 0)
-    def _():
-        window_bias(bias, place_ref[0] * rows, place_ref[1] * cols, *grid_shape)
-        masks = masks_ref[...].astype(bf16)
-        unit = lax.broadcasted_iota(jnp.int32, (masks.shape[1], rows * cols), 0)
-        token = lax.broadcasted_iota(jnp.int32, (masks.shape[1], rows * cols), 1)
-        to_row = (unit == token // cols).astype(f32).astype(bf16)
-        to_col = (unit - rows == token % cols).astype(f32).astype(bf16)
-        pool[...] = (dot(masks, to_row) * dot(masks, to_col)).astype(bf16)
-        ends = layer_norm(sides_ref[...].reshape(-1, sides_ref.shape[-1]), gain_ref[...])
-        ends = dot(ends, wkv_ref[...]).astype(bf16).astype(f32)
-        sides[...] = ends.reshape(sides.shape)
-
-    sheet = pl.program_id(0)
+    tiles = inner // 128
     count = BLOCK * BLOCK
     heads = 128 // HEAD_DIM
     head_of_row = lax.broadcasted_iota(jnp.int32, (heads, count, 128), 0)
@@ -241,69 +250,81 @@
     place = lax.broadcasted_iota(jnp.int32, (span // 2, BLOCK, 128), 1)
     factor = math.log2(math.e) / math.sqrt(HEAD_DIM)
 
-    def band(a, carry):
-        at = pl.multiple_of(a * BLOCK, BLOCK)
-
-        def keys_of(b, lanes):
-            mid = slice(b * BLOCK, (b + 1) * BLOCK)
-            main = kv_ref[sheet, pl.ds(at, span), mid, lanes].reshape(span * BLOCK, 128)
-
-            def beside(g):
-                if g < 0 or g >= groups:
-                    found = sides[sheet, pl.ds(at, span), :, lanes]
-                else:
-                    found = kv_ref[sheet, pl.ds(at, span), g * BLOCK : (g + 1) * BLOCK, lanes]
-                return found.reshape(span // 2, 2, BLOCK, 128)
-
-            west, east = beside(b - 1), beside(b + 1)
-            even = jnp.where(place >= 6, west[:, 0], east[:, 0])
-            odd = pltpu.roll(jnp.where(place >= 6, west[:, 1], east[:, 1]), 4, 1)
-            extra = jnp.where((place >= 6) | (place < 2), even, odd).reshape(span * 4, 128)
-            return jnp.concatenate([main, extra], axis=0).astype(bf16)
-
-        tiles = inner // 128
-
-        def score(b, slot):
-            mid = slice(b * BLOCK, (b + 1) * BLOCK)
-            low = bias[a, b]
-            for t in range(tiles):
-                lanes = slice(t * 128, (t + 1) * 128)
-                q = q_ref[sheet, pl.ds(at, BLOCK), mid, lanes].reshape(count, 128).astype(bf16)
-                q = jnp.concatenate([q] * heads, axis=0) * own
-                found = lax.dot_general(keys_of(b, lanes), q, (((1,), (1,)), ((), ())), preferred_element_type=f32)
-                scores[slot, t] = found + jnp.concatenate([low] * (heads * count // 128), axis=1)
-
-        def soften(slot):
-            for t in range(tiles):
-                for h in range(heads * count // 128):
-                    lanes = slice(h * 128, (h + 1) * 128)
-                    found = scores[slot, t, :, lanes]
-                    top = jnp.max(found, axis=0, keepdims=True)
-                    expon = jnp.exp2((found - top) * factor)
-                    weights[slot, t, :, lanes] = (expon * (1.0 / jnp.sum(expon, axis=0, keepdims=True))).astype(bf16)
-
-        def mix(b, slot):
-            mid = slice(b * BLOCK, (b + 1) * BLOCK)
-            for t in range(tiles):
-                lanes = slice(t * 128, (t + 1) * 128)
-                values = keys_of(b, slice(inner + t * 128, inner + (t + 1) * 128))
-                mixed = lax.dot_general(weights[slot, t], values, (((0,), (0,)), ((), ())), preferred_element_type=f32)
-                mixed = mixed.reshape(heads, count, 128)
-                piece = mixed[0]
-                for k in range(1, heads):
-                    piece = jnp.where(lane >= k * HEAD_DIM, mixed[k], piece)
-                context[pl.ds(at, BLOCK), mid, lanes] = piece.reshape(BLOCK, BLOCK, 128)
-
-        score(0, 0)
-        for b in range(groups):
-            if b + 1 < groups:
-                score(b + 1, (b + 1) % 2)
-            soften(b % 2)
-            mix(b, b % 2)
-        return carry
-
-    lax.fori_loop(0, rows // BLOCK, band, 0)
-    mixed = context[...].reshape(rows * cols, inner).astype(bf16)
+    def keys_of(at, b, lanes):
+        main = kv_ref[sheet, at : at + span, b * BLOCK : (b + 1) * BLOCK, lanes].reshape(span * BLOCK, 128)
+
+        def beside(g):
+            if g < 0 or g >= groups:
+                found = sides[sheet, at : at + span, :, lanes]
+            else:
+                found = kv_ref[sheet, at : at + span, g * BLOCK : (g + 1) * BLOCK, lanes]
+            return found.reshape(span // 2, 2, BLOCK, 128)
+
+        west, east = beside(b - 1), beside(b + 1)
+        even = jnp.where(place >= 6, west[:, 0], east[:, 0])
+        odd = pltpu.roll(jnp.where(place >= 6, west[:, 1], east[:, 1]), 4, 1)
+        extra = jnp.where((place >= 6) | (place < 2), even, odd).reshape(span * 4, 128)
+        return jnp.concatenate([main, extra], axis=0).astype(bf16)
+
+    def score(at, b, slot):
+        low = bias[at // BLOCK, b]
+        for t in range(tiles):
+            lanes = slice(t * 128, (t + 1) * 128)
+            q = q_ref[sheet, at : at + BLOCK, b * BLOCK : (b + 1) * BLOCK, lanes].reshape(count, 128).astype(bf16)
+            q = jnp.concatenate([q] * heads, axis=0) * own
+            found = lax.dot_general(keys_of(at, b, lanes), q, (((1,), (1,)), ((), ())), preferred_element_type=f32)
+            scores[slot, t] = found + jnp.concatenate([low] * (heads * count // 128), axis=1)
+
+    def soften(slot):
+        for t in range(tiles):
+            for h in range(heads * count // 128):
+                lanes = slice(h * 128, (h + 1) * 128)
+                found = scores[slot, t, :, lanes]
+                top = jnp.max(found, axis=0, keepdims=True)
+                expon = jnp.exp2((found - top) * factor)
+                weights[slot, t, :, lanes] = (expon * (1.0 / jnp.sum(expon, axis=0, keepdims=True))).astype(bf16)
+
+    def mix(at, b, slot):
+        for t in range(tiles):
+            lanes = slice(t * 128, (t + 1) * 128)
+            values = keys_of(at, b, slice(inner + t * 128, inner + (t + 1) * 128))
+            mixed = lax.dot_general(weights[slot, t], values, (((0,), (0,)), ((), ())), preferred_element_type=f32)
+            mixed = mixed.reshape(heads, count, 128)
+            piece = mixed[0]
+            for k in range(1, heads):
+                piece = jnp.where(lane >= k * HEAD_DIM, mixed[k], piece)
+            store(at, b, lanes, piece.reshape(BLOCK, BLOCK, 128))
+
+    blocks = [(at, b) for at in range(0, rows, BLOCK) for b in columns]
+    score(*blocks[0], 0)
+    for k, block in enumerate(blocks):
+        if k + 1 < len(blocks):
+            score(*blocks[k + 1], (k + 1) % 2)
+        soften(k % 2)
+        mix(*block, k % 2)
+
+
+def attend_kernel(
+    q_ref, kv_ref, sides_ref, tokens_ref, gain_ref, wkv_ref, middle_ref, bias, pool, wout_ref,
+    attended_ref, sums_ref, first_row_ref, last_row_ref, first_col_ref, last_col_ref, sides, outer, scores, weights,
+):
+    rows, cols, inner = q_ref.shape[1:]
+    sheet = pl.program_id(0)
+
+    @pl.when(sheet == 0)
+    def _():
+        ends = layer_norm(sides_ref[...].reshape(-1, sides_ref.shape[-1]), gain_ref[...])
+        ends = dot(ends, wkv_ref[...]).astype(bf16).astype(f32)
+        sides[...] = ends.reshape(sides.shape)
+
+    last = cols // BLOCK - 1
+
+    def store(at, b, lanes, piece):
+        outer[b // last, at : at + BLOCK, :, lanes] = piece
+
+    attend_blocks((0, last), sheet, q_ref, kv_ref, sides, bias, scores, weights, store)
+    mixed = jnp.concatenate([outer[0], middle_ref[sheet], outer[1]], axis=1)
+    mixed = mixed.reshape(rows * cols, inner).astype(bf16)
     attended = (tokens_ref[sheet].astype(f32) + dot(mixed, wout_ref[...])).astype(bf16)
     attended_ref[...] = attended
     first_row_ref[...] = attended[:cols]
@@ -523,53 +544,51 @@
     )(gain, wq_near, wkv_near)
     flat = in_vmem(tokens.reshape(sheets, area, width))
     edge = HALO * cols
-    q, kv = pl.pallas_call(
-        project_kernel,
-        grid=(sheets,),
-        in_specs=[near] * 6,
-        out_specs=[near] * 2,
+    blocks = (rows // BLOCK) * (cols // BLOCK)
+    keys = (BLOCK + 2 * HALO) ** 2
+    stage = [pltpu.VMEM((2, inner // 128, keys, 256), f32), pltpu.VMEM((2, inner // 128, keys, 256), bf16)]
+    q, kv, bias, pool, middle = pl.pallas_call(
+        lambda *refs: project_kernel((grid_h, grid_w), *refs),
+        grid_spec=pltpu.PrefetchScalarGridSpec(
+            num_scalar_prefetch=1,
+            grid=(sheets,),
+            in_specs=[near] * 6 + [
+                pl.BlockSpec((None, UNITS, rows + cols), lambda s, p: (p[0] * col_count + p[1], 0, 0)),
+            ],
+            out_specs=[near] * 5,
+            scratch_shapes=stage,
+        ),
         out_shape=[
             pltpu.VMEM((sheets, rows, cols, inner), f32), pltpu.VMEM((sheets, rows + 2 * HALO, cols, wide), f32),
+            pltpu.VMEM((rows // BLOCK, cols // BLOCK, keys, 128), f32), pltpu.VMEM((UNITS, area), bf16),
+            pltpu.VMEM((sheets, rows, cols - 2 * BLOCK, inner), f32),
         ],
-        compiler_params=params(28),
+        compiler_params=params(16),
         cost_estimate=cost(2 * sheets * area * width * (inner + wide), 2 * (width * (inner + wide) + 5 * sheets * area * width)),
         name="project",
     )(
-        flat, in_vmem(above.reshape(sheets, edge, width)), in_vmem(below.reshape(sheets, edge, width)),
-        in_vmem(gain), wq_near, wkv_near,
+        at, flat, in_vmem(above.reshape(sheets, edge, width)), in_vmem(below.reshape(sheets, edge, width)),
+        in_vmem(gain), wq_near, wkv_near, masks,
     )
 
     blank = jnp.zeros((sheets, rows + 2 * HALO, BLOCK - 2 * HALO, width), bf16)
     sides = jnp.concatenate([east, blank, west], axis=2).reshape(sheets, (rows + 2 * HALO) * BLOCK, width)
-    blocks = (rows // BLOCK) * (cols // BLOCK)
-    keys = (BLOCK + 2 * HALO) ** 2
 
     def fixed(*dims):
         return whole(dims)
 
     attended, sums, first_row, last_row, first_col, last_col = pl.pallas_call(
-        lambda *refs: attend_kernel((grid_h, grid_w), *refs),
-        grid_spec=pltpu.PrefetchScalarGridSpec(
-            num_scalar_prefetch=1,
-            grid=(sheets,),
-            in_specs=[
-                near, near, near, near, near, near, fixed(inner, width),
-                pl.BlockSpec((None, UNITS, rows + cols), lambda s, p: (p[0] * col_count + p[1], 0, 0)),
-            ],
-            out_specs=[
-                pl.BlockSpec((None, area, width), lambda s, _: (s, 0, 0)),
-                pl.BlockSpec((row_count, UNITS, width), lambda s, _: (0, s, 0)),
-                per_sheet(cols, width), per_sheet(cols, width), per_sheet(rows, width), per_sheet(rows, width),
-            ],
-            scratch_shapes=[
-                pltpu.VMEM((sheets, rows + 2 * HALO, BLOCK, wide), f32),
-                pltpu.VMEM((rows, cols, inner), f32),
-                pltpu.VMEM((rows // BLOCK, cols // BLOCK, keys, 128), f32),
-                pltpu.VMEM((UNITS, area), bf16),
-                pltpu.VMEM((2, inner // 128, keys, 256), f32),
-                pltpu.VMEM((2, inner // 128, keys, 256), bf16),
-            ],
-        ),
+        attend_kernel,
+        grid=(sheets,),
+        in_specs=[near] * 9 + [fixed(inner, width)],
+        out_specs=[
+            per_sheet(area, width),
+            pl.BlockSpec((row_count, UNITS, width), lambda s: (0, s, 0)),
+            per_sheet(cols, width), per_sheet(cols, width), per_sheet(rows, width), per_sheet(rows, width),
+        ],
+        scratch_shapes=[
+            pltpu.VMEM((sheets, rows + 2 * HALO, BLOCK, wide), f32), pltpu.VMEM((2, rows, BLOCK, inner), f32),
+        ] + stage,
         out_shape=[
             pltpu.HBM((sheets, area, width), bf16),
             jax.ShapeDtypeStruct((row_count, sheets * UNITS, width), bf16),
@@ -578,11 +597,12 @@
             jax.ShapeDtypeStruct((sheets, rows, width), bf16),
             jax.ShapeDtypeStruct((sheets, rows, width), bf16),
         ],
-        compiler_params=params(32),
+        compiler_params=params(20),
         cost_estimate=cost(2 * sheets * area * inner * width * 4, 2 * sheets * area * width * 4, sheets * blocks * keys * 1024),
         name="attend",
     )(
-        at, in_vmem(q), in_vmem(kv), in_vmem(sides), flat, in_vmem(gain), wkv_near, w_out, masks,
+        in_vmem(q), in_vmem(kv), in_vmem(sides), flat, in_vmem(gain), wkv_near, in_vmem(middle), in_vmem(bias),
+        in_vmem(pool), w_out,
     )
 
     strip_rows = sheets * STRIP_UNITS

time: 94.6 us -> 94.4 us (level)
  waiting for transfers between devices: 12.1 us -> 10.7 us
  starting transfers between devices: 40.2 us -> 41.6 us
    ppermute x1, waiting for transfers between devices: 1.37 us -> 0.01 us  [layer(): west = lax.ppermute(edges(cols - HALO), 'col', col_fwd)]
    all_to_all x1, starting transfers between devices: 9.46 us -> 10.8 us  [layer(): lax.all_to_all(sums, 'row', 0, 0, tiled=True)]
  transfers between devices with their start and end apart: 10 -> 10, of which waited for: 4 -> 3; matrix products, arithmetic and copies ran while one was open for 2% -> 2% of each run, Pallas kernels for 17% -> 21%
where the time goes in v8:
time: 94.4 us; the launch traced here: 93.8 us
  starting transfers between devices  41.6 us (44%)
  Pallas kernels  35.6 us (38%)
  waiting for transfers between devices  10.7 us (11%)
  local copies, waits for them, and re-layouts  4.59 us (5%)
    all_to_all x1, starting transfers between devices, layer(): lax.all_to_all(sums, 'row', 0, 0, tiled=True)  10.8 us
    pallas_call x1, Pallas kernels, layer(): pl.pallas_call(lambda *refs: project_kernel((grid_h, grid_w), *refs), gri...  9.37 us
    pallas_call x1, Pallas kernels, layer(): pl.pallas_call(conv_kernel, grid=(sheets, 3), in_specs=[per_sheet(area, w...  9.09 us
    pallas_call x1, Pallas kernels, layer(): pl.pallas_call(tail_kernel, grid_spec=pltpu.PrefetchScalarGridSpec(num_sc...  8.38 us
    all_to_all x1, starting transfers between devices, layer(): lax.all_to_all(strips, 'col', 0, 0, tiled=True)  7.87 us
    pallas_call x1, Pallas kernels, layer(): pl.pallas_call(attend_kernel, grid=(sheets,), in_specs=[near] * 9 + [fixe...  7.15 us
    ppermute x1, starting transfers between devices, layer(): west = lax.ppermute(edges(cols - HALO), 'col', col_fwd)  6.06 us
    ppermute x1, starting transfers between devices, layer(): att_west = lax.ppermute(att_edges(last_col, cols - 1), 'col', col_fwd)  6 us
  transfers between devices with their start and end apart: 10, of which 3 were waited for; matrix products, arithmetic and copies ran while one was open for 2% of the time, Pallas kernels for 21%

profile of v8, /device:TPU:32, one launch (start us, length us, event | category | flops | bytes accessed | tf_op | source)
XLA Modules:
  0.0 93.8 jit_solution(11167339153659815148)
XLA Ops:
  0.0 0.0 copy-start
  0.0 0.0 copy-start.11
  0.0 1.2 %fusion.1 = (bf16[2,2,32,1024]{3,2,1,0:T(8,128)(2,1)S(1)}, bf16[2,2,32,1024]{3,2,1,0:T(8,128)(2,1)S(1)}) fusion(bf16[2,16,32,1024]{3,2,1,0:T(8,128)(2,1)} %param.16), kind=kLoop, calls=%fused_computation.7 | loop fusion | bytes 1048576 | tf_op jit(solution)/shard_map/slice | solution.py:523
  1.2 1.9 %collective-permute-start.1 = (bf16[2,2,32,1024]{3,2,1,0:T(8,128)(2,1)S(1)}, bf16[2,2,32,1024]{3,2,1,0:T(8,128)(2,1)S(1)}, u32[]{:S(2)}, u32[]{:S(2)}) collective-permute-start(bf16[2,2,32,1024]{3,2,1,0:T(8,128)(2,1)S(1)} %get-tuple-element.29), channel_id=1, source_target_pairs={{8,0},{16,8},{24,16},{32,24},{40,32},{48,40},{56,48},{64,56},{72,6... | collective-permute-start | bytes 786440 | tf_op jit(solution)/shard_map/ppermute | solution.py:523
  3.2 2.4 %collective-permute-start = (bf16[2,2,32,1024]{3,2,1,0:T(8,128)(2,1)S(1)}, bf16[2,2,32,1024]{3,2,1,0:T(8,128)(2,1)S(1)}, u32[]{:S(2)}, u32[]{:S(2)}) collective-permute-start(bf16[2,2,32,1024]{3,2,1,0:T(8,128)(2,1)S(1)} %get-tuple-element.30), channel_id=1, source_target_pairs={{0,8},{8,16},{16,24},{24,32},{32,40},{40,48},{48,56},{56,64},{64,7... | collective-permute-start | bytes 786440 | tf_op jit(solution)/shard_map/ppermute | solution.py:522
  5.6 1.4 %fusion = (bf16[2,16,2,1024]{3,2,1,0:T(2,128)(2,1)S(1)}, bf16[2,16,2,1024]{3,2,1,0:T(2,128)(2,1)S(1)}) fusion(bf16[2,16,32,1024]{3,2,1,0:T(8,128)(2,1)} %param.16), kind=kLoop, calls=%fused_computation.6 | loop fusion | bytes 524288 | tf_op jit(solution)/shard_map/slice | solution.py:526
  7.0 0.1 pad_add_fusion.refs_0_.place_ref
  7.2 0.1 pad.16.clone
  7.2 0.0 copy-done
  7.2 0.0 copy-done.11
  7.2 0.0 copy-start.1
  7.2 1.2 %copy-done.1 = bf16[1024,512]{1,0:T(8,128)(2,1)S(1)} copy-done((bf16[1024,512]{1,0:T(8,128)(2,1)S(1)}, bf16[1024,512]{1,0:T(8,128)(2,1)}, u32[]{:S(2)}) %copy-start.1) | copy-done | bytes 1048600
  8.5 0.0 copy-start.2
  8.5 0.0 copy-start.4
  8.5 0.0 copy-start.14
  8.5 0.0 collective-permute-done.1
  8.6 2.3 %collective-permute-done = bf16[2,2,32,1024]{3,2,1,0:T(8,128)(2,1)S(1)} collective-permute-done((bf16[2,2,32,1024]{3,2,1,0:T(8,128)(2,1)S(1)}, bf16[2,2,32,1024]{3,2,1,0:T(8,128)(2,1)S(1)}, u32[]{:S(2)}, u32[]{:S(2)}) %collective-permute-start) | collective-permute-done | bytes 262176 | tf_op jit(solution)/shard_map/ppermute | solution.py:522
  10.9 0.1 pad_maximum_fusion
  11.0 1.3 %collective-permute-start.2 = (bf16[2,20,2,1024]{3,1,2,0:T(8,128)(2,1)S(1)}, bf16[2,20,2,1024]{3,1,2,0:T(8,128)(2,1)S(1)}, u32[]{:S(2)}, u32[]{:S(2)}) collective-permute-start(bf16[2,20,2,1024]{3,1,2,0:T(8,128)(2,1)S(1)} %pad_maximum_fusion), channel_id=1, source_target_pairs={{1,0},{2,1},{3,2},{4,3},{5,4},{6,5},{7,6},{9,8},{10,9},{11,10},{12... | collective-permute-start | bytes 491528 | tf_op jit(solution)/shard_map/ppermute | solution.py:529
  12.3 0.1 pad_maximum_fusion.1
  12.4 6.1 %collective-permute-start.3 = (bf16[2,20,2,1024]{3,1,2,0:T(8,128)(2,1)S(1)}, bf16[2,20,2,1024]{3,1,2,0:T(8,128)(2,1)S(1)}, u32[]{:S(2)}, u32[]{:S(2)}) collective-permute-start(bf16[2,20,2,1024]{3,1,2,0:T(8,128)(2,1)S(1)} %pad_maximum_fusion.1), channel_id=1, source_target_pairs={{0,1},{1,2},{2,3},{3,4},{4,5},{5,6},{6,7},{8,9},{9,10},{10,11},{11... | collective-permute-start | bytes 491528 | tf_op jit(solution)/shard_map/ppermute | solution.py:528
  18.5 0.0 copy-done.2
  18.5 0.0 copy-done.4
  18.5 0.0 copy-done.14
  18.5 0.0 copy-start.13
  18.5 9.4 %project.1 = (f32[2,16,32,512]{3,2,1,0:T(8,128)S(1)}, f32[2,20,32,1024]{3,2,1,0:T(8,128)S(1)}, f32[2,4,144,128]{3,2,1,0:T(8,128)S(1)}, bf16[8,512]{1,0:T(8,128)(2,1)S(1)}, f32[2,16,16,512]{3,2,1,0:T(8,128)S(1)}) custom-call(s32[2]{0:T(128)S(1)} %pad_add_fusion.refs_0_.place_ref, bf16[2,512,1024]{2,1,0:T(8,128)(2,1)S(1)} %bitcast.13, ...), custom_call_target="tpu_custom_call" | custom-call | flops 3221225472 | bytes 13631488 | tf_op jit(solution)/shard_map/project/pallas_call | solution.py:550
  27.9 0.0 collective-permute-done.2
  27.9 0.2 copy.31
  28.1 0.0 collective-permute-done.3
  28.1 0.2 copy.32
  28.3 0.4 maximum_bitcast_fusion.sides_ref
  28.7 0.0 copy-done.13
  28.7 0.0 copy-start.5
  28.7 0.0 copy-start.9
  28.7 7.2 %attend.1 = (bf16[2,512,1024]{2,1,0:T(8,128)(2,1)}, bf16[16,16,1024]{2,1,0:T(8,128)(2,1)}, bf16[2,32,1024]{2,1,0:T(8,128)(2,1)S(1)}, bf16[2,32,1024]{2,1,0:T(8,1...) custom-call(f32[2,16,32,512]{3,2,1,0:T(8,128)S(1)} %get-tuple-element.16.q_ref, ...), custom_call_target="tpu_custom_call" | custom-call | flops 4294967296 | bytes 8388608 | tf_op jit(solution)/shard_map/attend/pallas_call | solution.py:580
  35.8 1.9 %collective-permute-start.4 = (bf16[2,32,1024]{2,1,0:T(8,128)(2,1)S(1)}, bf16[2,32,1024]{2,1,0:T(8,128)(2,1)S(1)}, u32[]{:S(2)}, u32[]{:S(2)}) collective-permute-start(bf16[2,32,1024]{2,1,0:T(8,128)(2,1)S(1)} %get-tuple-element.23), channel_id=1, source_target_pairs={{0,8},{8,16},{16,24},{24,32},{32,40},{40,48},{48,56},{56,64},{64,7... | collective-permute-start | bytes 393224 | tf_op jit(solution)/shard_map/ppermute | solution.py:609
  37.8 10.8 %all-to-all-start = ((bf16[16,16,1024]{2,1,0:T(8,128)(2,1)}), bf16[16,16,1024]{2,1,0:T(8,128)(2,1)S(1)}, u32[]{:S(2)}, u32[]{:S(2)}) async-start(bf16[16,16,1024]{2,1,0:T(8,128)(2,1)} %get-tuple-element.21), calls=%async_computation | async-start | bytes 1048576 | tf_op jit(solution)/shard_map/all_to_all | solution.py:611
  48.6 2.0 %collective-permute-start.5 = (bf16[2,32,1024]{2,1,0:T(8,128)(2,1)S(1)}, bf16[2,32,1024]{2,1,0:T(8,128)(2,1)S(1)}, u32[]{:S(2)}, u32[]{:S(2)}) collective-permute-start(bf16[2,32,1024]{2,1,0:T(8,128)(2,1)S(1)} %get-tuple-element.24), channel_id=1, source_target_pairs={{8,0},{16,8},{24,16},{32,24},{40,32},{48,40},{56,48},{64,56},{72,6... | collective-permute-start | bytes 393224 | tf_op jit(solution)/shard_map/ppermute | solution.py:610
  50.6 0.0 collective-permute-done.4.top_ref
  50.6 5.7 %collective-permute-done.5.bottom_ref = bf16[2,32,1024]{2,1,0:T(8,128)(2,1)S(1)} collective-permute-done((bf16[2,32,1024]{2,1,0:T(8,128)(2,1)S(1)}, bf16[2,32,1024]{2,1,0:T(8,128)(2,1)S(1)}, u32[]{:S(2)}, u32[]{:S(2)}) %collective-permute-start.5) | collective-permute-done | bytes 131104 | tf_op jit(solution)/shard_map/ppermute | solution.py:610
  56.4 6.0 %collective-permute-start.6 = (bf16[2,18,1024]{2,1,0:T(8,128)(2,1)S(1)}, bf16[2,18,1024]{2,1,0:T(8,128)(2,1)S(1)}, u32[]{:S(2)}, u32[]{:S(2)}) collective-permute-start(bf16[2,18,1024]{2,1,0:T(8,128)(2,1)S(1)} %pad_maximum_fusion.2), channel_id=1, source_target_pairs={{0,1},{1,2},{2,3},{3,4},{4,5},{5,6},{6,7},{8,9},{9,10},{10,11},{11... | collective-permute-start | bytes 221192 | tf_op jit(solution)/shard_map/ppermute | solution.py:616
  62.5 1.3 %collective-permute-start.7 = (bf16[2,18,1024]{2,1,0:T(8,128)(2,1)S(1)}, bf16[2,18,1024]{2,1,0:T(8,128)(2,1)S(1)}, u32[]{:S(2)}, u32[]{:S(2)}) collective-permute-start(bf16[2,18,1024]{2,1,0:T(8,128)(2,1)S(1)} %pad_maximum_fusion.3), channel_id=1, source_target_pairs={{1,0},{2,1},{3,2},{4,3},{5,4},{6,5},{7,6},{9,8},{10,9},{11,10},{12... | collective-permute-start | bytes 221192 | tf_op jit(solution)/shard_map/ppermute | solution.py:617
  63.8 0.0 all-to-all-done
  63.8 0.0 copy-done.5
  63.8 0.0 copy-done.9
  63.8 1.6 %combine.1 = bf16[8,32,1024]{2,1,0:T(8,128)(2,1)} custom-call(s32[2]{0:T(128)S(1)} %pad_add_fusion.refs_0_.place_ref, bf16[16,32,48]{2,1,0:T(8,128)(2,1)S(1)} %copy-done.9, bf16[8,48,256]{2,1,0:T(8,128)(2,1)S(1)} %copy-done.5, bf16[256,1024]{1,0:T(8,128)(2,1)S(1)} %bitcast.11), custom_call_target="tpu_custom_call" | custom-call | tf_op jit(solution)/shard_map/combine/pallas_call | solution.py:621
  65.5 7.9 %all-to-all-start.1 = ((bf16[8,32,1024]{2,1,0:T(8,128)(2,1)}), bf16[8,32,1024]{2,1,0:T(8,128)(2,1)S(1)}, u32[]{:S(2)}, u32[]{:S(2)}) async-start(bf16[8,32,1024]{2,1,0:T(8,128)(2,1)} %combine.1), calls=%async_computation.1 | async-start | bytes 1048576 | tf_op jit(solution)/shard_map/all_to_all | solution.py:637
  73.3 0.0 collective-permute-done.6
  73.3 0.0 collective-permute-done.7
  73.4 0.0 copy-start.3
  73.4 0.0 copy-start.6
  73.4 0.0 copy-start.7
  73.4 0.0 copy-start.8
  73.4 0.0 copy-start.10
  73.4 0.0 copy-start.12
  73.5 9.1 %conv.1 = f32[2,512,256]{2,1,0:T(8,128)S(1)} custom-call(bf16[2,512,1024]{2,1,0:T(8,128)(2,1)} %get-tuple-element.22.attended_ref, bf16[2,32,1024]{2,1,0:T(8,128)(2,1)S(1)} %collective-permute-done.4.top_ref, bf16[2,32,1024]{2,1,0:T(8,128)(2,1)S(1)} %collective-permute-done.5.bottom_ref, bf16[2,24,1024]{2,1,0:T(8,128)(2,1)S(1)} %pad.7.left_ref, ...), custom_call_target="tpu_custom_call" | custom-call | flops 4831838208 | bytes 6815744 | tf_op jit(solution)/shard_map/conv/pallas_call | solution.py:639
  82.6 2.7 %all-to-all-done.1 = bf16[8,32,1024]{2,1,0:T(8,128)(2,1)S(1)} async-done(((bf16[8,32,1024]{2,1,0:T(8,128)(2,1)}), bf16[8,32,1024]{2,1,0:T(8,128)(2,1)S(1)}, u32[]{:S(2)}, u32[]{:S(2)}) %all-to-all-start.1) | async-done | bytes 524320 | tf_op jit(solution)/shard_map/all_to_all | solution.py:637
  85.2 0.0 copy-done.3
  85.2 0.0 copy-done.6
  85.2 0.0 copy-done.7
  85.2 0.0 copy-done.8
  85.2 0.0 copy-done.10
  85.2 0.0 copy-done.12
  85.3 8.4 %tail.1 = bf16[2,512,256]{2,1,0:T(8,128)(2,1)} custom-call(s32[2]{0:T(128)S(1)} %pad_add_fusion.refs_0_.place_ref, bf16[8,96,256]{2,1,0:T(8,128)(2,1)S(1)} %copy-done.3, f32[16,1,96]{2,1,0:T(1,128)S(1)} %copy-done.10, f32[8,1,96]{2,1,0:T(1,128)S(1)} %copy-done.12, bf16[256,1024]{1,0:T(8,128)(2,1)S(1)} %bitcast.12, bf16[4,1024,512]{2,1,0:T(8,128)(2,1)} %wpool_hbm.1, ...), custom_call_target="tpu_custom_call" | custom-call | flops 4000000000 | bytes 13631488 | tf_op jit(solution)/shard_map/tail/pallas_call | solution.py:661
  (16 shorter events, 0.3 us)
Async XLA Ops:
  0.0 7.2 %copy-start = (bf16[1024,1024]{1,0:T(8,128)(2,1)S(1)}, bf16[1024,1024]{1,0:T(8,128)(2,1)}, u32[]{:S(2)}) copy-start(bf16[1024,1024]{1,0:T(8,128)(2,1)} %wkv_ref.3) | copy-start | bytes 6291460
  0.0 7.2 %copy-start.11 = (f32[1024]{0:T(1024)S(1)}, f32[1024]{0:T(1024)}, u32[]{:S(2)}) copy-start(f32[1024]{0:T(1024)} %param.17) | copy-start | bytes 12292
  1.2 7.2 %collective-permute-start.1 = (bf16[2,2,32,1024]{3,2,1,0:T(8,128)(2,1)S(1)}, bf16[2,2,32,1024]{3,2,1,0:T(8,128)(2,1)S(1)}, u32[]{:S(2)}, u32[]{:S(2)}) collective-permute-start(bf16[2,2,32,1024]{3,2,1,0:T(8,128)(2,1)S(1)} %get-tuple-element.29), channel_id=1, source_target_pairs={{8,0},{16,8},{24,16},{32,24},{40,32},{48,40},{56,48},{64,56},{72,6... | collective-permute-start | bytes 786440 | tf_op jit(solution)/shard_map/ppermute | solution.py:523
  3.2 7.7 %collective-permute-start = (bf16[2,2,32,1024]{3,2,1,0:T(8,128)(2,1)S(1)}, bf16[2,2,32,1024]{3,2,1,0:T(8,128)(2,1)S(1)}, u32[]{:S(2)}, u32[]{:S(2)}) collective-permute-start(bf16[2,2,32,1024]{3,2,1,0:T(8,128)(2,1)S(1)} %get-tuple-element.30), channel_id=1, source_target_pairs={{0,8},{8,16},{16,24},{24,32},{32,40},{40,48},{48,56},{56,64},{64,7... | collective-permute-start | bytes 786440 | tf_op jit(solution)/shard_map/ppermute | solution.py:522
  7.2 1.2 %copy-start.1 = (bf16[1024,512]{1,0:T(8,128)(2,1)S(1)}, bf16[1024,512]{1,0:T(8,128)(2,1)}, u32[]{:S(2)}) copy-start(bf16[1024,512]{1,0:T(8,128)(2,1)} %refs_5_.1) | copy-start | bytes 3145732
  8.5 10.0 %copy-start.2 = (bf16[1024,512]{1,0:T(8,128)(2,1)S(1)}, bf16[1024,512]{1,0:T(8,128)(2,1)}, u32[]{:S(2)}) copy-start(bf16[1024,512]{1,0:T(8,128)(2,1)} %refs_5_.1) | copy-start | bytes 3145732
  8.5 10.0 %copy-start.4 = (bf16[2,16,32,1024]{3,2,1,0:T(8,128)(2,1)S(1)}, bf16[2,16,32,1024]{3,2,1,0:T(8,128)(2,1)}, u32[]{:S(2)}) copy-start(bf16[2,16,32,1024]{3,2,1,0:T(8,128)(2,1)} %param.16) | copy-start | bytes 6291460
  8.5 10.0 %copy-start.14 = (f32[128,8,48]{2,1,0:T(8,128)S(1)}, f32[128,8,48]{2,1,0:T(8,128)}, u32[]{:S(2)}) copy-start(f32[128,8,48]{2,1,0:T(8,128)} %constant.31.clone.refs_7_) | copy-start | bytes 589828
  11.0 16.9 %collective-permute-start.2 = (bf16[2,20,2,1024]{3,1,2,0:T(8,128)(2,1)S(1)}, bf16[2,20,2,1024]{3,1,2,0:T(8,128)(2,1)S(1)}, u32[]{:S(2)}, u32[]{:S(2)}) collective-permute-start(bf16[2,20,2,1024]{3,1,2,0:T(8,128)(2,1)S(1)} %pad_maximum_fusion), channel_id=1, source_target_pairs={{1,0},{2,1},{3,2},{4,3},{5,4},{6,5},{7,6},{9,8},{10,9},{11,10},{12... | collective-permute-start | bytes 491528 | tf_op jit(solution)/shard_map/ppermute | solution.py:529
  12.4 15.7 %collective-permute-start.3 = (bf16[2,20,2,1024]{3,1,2,0:T(8,128)(2,1)S(1)}, bf16[2,20,2,1024]{3,1,2,0:T(8,128)(2,1)S(1)}, u32[]{:S(2)}, u32[]{:S(2)}) collective-permute-start(bf16[2,20,2,1024]{3,1,2,0:T(8,128)(2,1)S(1)} %pad_maximum_fusion.1), channel_id=1, source_target_pairs={{0,1},{1,2},{2,3},{3,4},{4,5},{5,6},{6,7},{8,9},{9,10},{10,11},{11... | collective-permute-start | bytes 491528 | tf_op jit(solution)/shard_map/ppermute | solution.py:528
  18.5 10.2 %copy-start.13 = (bf16[512,1024]{1,0:T(8,128)(2,1)S(1)}, bf16[512,1024]{1,0:T(8,128)(2,1)}, u32[]{:S(2)}) copy-start(bf16[512,1024]{1,0:T(8,128)(2,1)} %wout_ref.1) | copy-start | bytes 3145732
  28.7 35.1 %copy-start.5 = (bf16[8,48,256]{2,1,0:T(8,128)(2,1)S(1)}, bf16[8,48,256]{2,1,0:T(8,128)(2,1)}, u32[]{:S(2)}) copy-start(bf16[8,48,256]{2,1,0:T(8,128)(2,1)} %constant.33.clone.table_ref) | copy-start | bytes 589828
  28.7 35.1 %copy-start.9 = (bf16[16,32,48]{2,1,0:T(8,128)(2,1)S(1)}, bf16[16,32,48]{2,1,0:T(8,128)(2,1)}, u32[]{:S(2)}) copy-start(bf16[16,32,48]{2,1,0:T(8,128)(2,1)} %constant.32.clone.near_ref) | copy-start | bytes 147460
  35.8 14.8 %collective-permute-start.4 = (bf16[2,32,1024]{2,1,0:T(8,128)(2,1)S(1)}, bf16[2,32,1024]{2,1,0:T(8,128)(2,1)S(1)}, u32[]{:S(2)}, u32[]{:S(2)}) collective-permute-start(bf16[2,32,1024]{2,1,0:T(8,128)(2,1)S(1)} %get-tuple-element.23), channel_id=1, source_target_pairs={{0,8},{8,16},{16,24},{24,32},{32,40},{40,48},{48,56},{56,64},{64,7... | collective-permute-start | bytes 393224 | tf_op jit(solution)/shard_map/ppermute | solution.py:609
  37.8 26.0 %all-to-all-start = ((bf16[16,16,1024]{2,1,0:T(8,128)(2,1)}), bf16[16,16,1024]{2,1,0:T(8,128)(2,1)S(1)}, u32[]{:S(2)}, u32[]{:S(2)}) async-start(bf16[16,16,1024]{2,1,0:T(8,128)(2,1)} %get-tuple-element.21), calls=%async_computation | async-start | bytes 1048576 | tf_op jit(solution)/shard_map/all_to_all | solution.py:611
  48.6 7.8 %collective-permute-start.5 = (bf16[2,32,1024]{2,1,0:T(8,128)(2,1)S(1)}, bf16[2,32,1024]{2,1,0:T(8,128)(2,1)S(1)}, u32[]{:S(2)}, u32[]{:S(2)}) collective-permute-start(bf16[2,32,1024]{2,1,0:T(8,128)(2,1)S(1)} %get-tuple-element.24), channel_id=1, source_target_pairs={{8,0},{16,8},{24,16},{32,24},{40,32},{48,40},{56,48},{64,56},{72,6... | collective-permute-start | bytes 393224 | tf_op jit(solution)/shard_map/ppermute | solution.py:610
  56.4 16.9 %collective-permute-start.6 = (bf16[2,18,1024]{2,1,0:T(8,128)(2,1)S(1)}, bf16[2,18,1024]{2,1,0:T(8,128)(2,1)S(1)}, u32[]{:S(2)}, u32[]{:S(2)}) collective-permute-start(bf16[2,18,1024]{2,1,0:T(8,128)(2,1)S(1)} %pad_maximum_fusion.2), channel_id=1, source_target_pairs={{0,1},{1,2},{2,3},{3,4},{4,5},{5,6},{6,7},{8,9},{9,10},{10,11},{11... | collective-permute-start | bytes 221192 | tf_op jit(solution)/shard_map/ppermute | solution.py:616
  62.5 10.9 %collective-permute-start.7 = (bf16[2,18,1024]{2,1,0:T(8,128)(2,1)S(1)}, bf16[2,18,1024]{2,1,0:T(8,128)(2,1)S(1)}, u32[]{:S(2)}, u32[]{:S(2)}) collective-permute-start(bf16[2,18,1024]{2,1,0:T(8,128)(2,1)S(1)} %pad_maximum_fusion.3), channel_id=1, source_target_pairs={{1,0},{2,1},{3,2},{4,3},{5,4},{6,5},{7,6},{9,8},{10,9},{11,10},{12... | collective-permute-start | bytes 221192 | tf_op jit(solution)/shard_map/ppermute | solution.py:617
  65.5 19.8 %all-to-all-start.1 = ((bf16[8,32,1024]{2,1,0:T(8,128)(2,1)}), bf16[8,32,1024]{2,1,0:T(8,128)(2,1)S(1)}, u32[]{:S(2)}, u32[]{:S(2)}) async-start(bf16[8,32,1024]{2,1,0:T(8,128)(2,1)} %combine.1), calls=%async_computation.1 | async-start | bytes 1048576 | tf_op jit(solution)/shard_map/all_to_all | solution.py:637
  73.4 11.8 %copy-start.3 = (bf16[8,96,256]{2,1,0:T(8,128)(2,1)S(1)}, bf16[8,96,256]{2,1,0:T(8,128)(2,1)}, u32[]{:S(2)}) copy-start(bf16[8,96,256]{2,1,0:T(8,128)(2,1)} %constant.34.clone.table_hbm) | copy-start | bytes 1179652
  73.4 11.8 %copy-start.6 = (bf16[2,64,432]{2,1,0:T(8,128)(2,1)S(1)}, bf16[2,64,432]{2,1,0:T(8,128)(2,1)}, u32[]{:S(2)}) copy-start(bf16[2,64,432]{2,1,0:T(8,128)(2,1)} %constant.39.clone.spread_hbm) | copy-start | bytes 331780
  73.4 11.8 %copy-start.7 = (f32[8,32,64]{2,1,0:T(8,128)S(1)}, f32[8,32,64]{2,1,0:T(8,128)}, u32[]{:S(2)}) copy-start(f32[8,32,64]{2,1,0:T(8,128)} %constant.38.clone.by_col_hbm) | copy-start | bytes 196612
  73.4 11.8 %copy-start.8 = (f32[16,16,64]{2,1,0:T(8,128)S(1)}, f32[16,16,64]{2,1,0:T(8,128)}, u32[]{:S(2)}) copy-start(f32[16,16,64]{2,1,0:T(8,128)} %constant.37.clone.by_row_hbm) | copy-start | bytes 196612
  73.4 11.8 %copy-start.10 = (f32[16,1,96]{2,1,0:T(1,128)S(1)}, f32[16,1,96]{2,1,0:T(1,128)}, u32[]{:S(2)}) copy-start(f32[16,1,96]{2,1,0:T(1,128)} %constant.35.clone.row_scale_hbm) | copy-start | bytes 18436
  73.4 11.8 %copy-start.12 = (f32[8,1,96]{2,1,0:T(1,128)S(1)}, f32[8,1,96]{2,1,0:T(1,128)}, u32[]{:S(2)}) copy-start(f32[8,1,96]{2,1,0:T(1,128)} %constant.36.clone.col_scale_hbm) | copy-start | bytes 9220

commit v9 on v8

--- a/solution.py
+++ b/solution.py
@@ -175,8 +175,12 @@
     return jnp.dot(a, b, preferred_element_type=f32)
 
 
-def warm_kernel(gain_ref, wq_ref, wkv_ref, out_ref):
-    out_ref[...] = gain_ref[...]
+def project_kernel(tokens_ref, gain_ref, wq, wkv, q_ref, kv_ref):
+    rows, cols, inner = q_ref.shape[1:]
+    s = pl.program_id(0)
+    normed = layer_norm(tokens_ref[s], gain_ref[...])
+    q_ref[s] = dot(normed, wq[...]).astype(bf16).astype(f32).reshape(rows, cols, inner)
+    kv_ref[s] = dot(normed, wkv[...]).astype(bf16).astype(f32).reshape(rows, cols, -1)
 
 
 def pool_members(masks_ref, pool, cols):
@@ -191,31 +195,26 @@
     pool[...] = (dot(masks, to_row) * dot(masks, to_col)).astype(bf16)
 
 
-def project_kernel(
-    grid_shape, place_ref, tokens_ref, above_ref, below_ref, gain_ref, wq, wkv, masks_ref,
-    q_ref, kv_ref, bias, pool, context, scores, weights,
+def middle_kernel(
+    grid_shape, place_ref, q_ref, kv_ref, above_ref, below_ref, gain_ref, wkv, masks_ref,
+    halo_ref, bias, pool, context, scores, weights,
 ):
-    rows, cols, inner = q_ref.shape[1:]
+    rows, cols = q_ref.shape[1:3]
     s = pl.program_id(0)
-    gain = gain_ref[...]
-    normed = layer_norm(tokens_ref[s], gain)
-    q_ref[s] = dot(normed, wq[...]).astype(bf16).astype(f32).reshape(rows, cols, inner)
-    kv_ref[s, HALO : rows + HALO] = dot(normed, wkv[...]).astype(bf16).astype(f32).reshape(rows, cols, -1)
-    edge = layer_norm(jnp.concatenate([above_ref[s], below_ref[s]], axis=0), gain)
-    edge = dot(edge, wkv[...]).astype(bf16).astype(f32).reshape(2 * HALO, cols, -1)
-    kv_ref[s, 0:HALO] = edge[:HALO]
-    kv_ref[s, rows + HALO :] = edge[HALO:]
 
     @pl.when(s == 0)
     def _():
         window_bias(bias, place_ref[0] * rows, place_ref[1] * cols, *grid_shape)
         pool_members(masks_ref, pool, cols)
+        edge = jnp.concatenate([above_ref[...], below_ref[...]], axis=1)
+        edge = layer_norm(edge.reshape(-1, edge.shape[-1]), gain_ref[...])
+        halo_ref[...] = dot(edge, wkv[...]).astype(bf16).astype(f32).reshape(halo_ref.shape)
 
     def store(at, b, lanes, piece):
         context[s, at : at + BLOCK, (b - 1) * BLOCK : b * BLOCK, lanes] = piece
 
     middle = range(1, cols // BLOCK - 1)
-    attend_blocks(middle, s, q_ref, kv_ref, None, bias, scores, weights, store)
+    attend_blocks(middle, s, q_ref, kv_ref, halo_ref, None, bias, scores, weights, store)
 
 
 def window_bias(bias, first_row, first_col, grid_h, grid_w):
@@ -236,7 +235,7 @@
             bias[a, b] = jnp.where(row_ok & (at >= 0) & (at < grid_w), 0.0, -1e30)
 
 
-def attend_blocks(columns, sheet, q_ref, kv_ref, sides, bias, scores, weights, store):
+def attend_blocks(columns, sheet, q_ref, kv_ref, halo_ref, sides, bias, scores, weights, store):
     rows, cols, inner = q_ref.shape[1:]
     groups = cols // BLOCK
     span = BLOCK + 2 * HALO
@@ -250,14 +249,23 @@
     place = lax.broadcasted_iota(jnp.int32, (span // 2, BLOCK, 128), 1)
     factor = math.log2(math.e) / math.sqrt(HEAD_DIM)
 
+    def rows_of(at, g, lanes):
+        places = slice(g * BLOCK, (g + 1) * BLOCK)
+        parts = [kv_ref[sheet, max(at - HALO, 0) : min(at + BLOCK + HALO, rows), places, lanes]]
+        if at == 0:
+            parts = [halo_ref[sheet, 0:HALO, places, lanes]] + parts
+        if at + BLOCK == rows:
+            parts = parts + [halo_ref[sheet, HALO:, places, lanes]]
+        return jnp.concatenate(parts, axis=0)
+
     def keys_of(at, b, lanes):
-        main = kv_ref[sheet, at : at + span, b * BLOCK : (b + 1) * BLOCK, lanes].reshape(span * BLOCK, 128)
+        main = rows_of(at, b, lanes).reshape(span * BLOCK, 128)
 
         def beside(g):
             if g < 0 or g >= groups:
                 found = sides[sheet, at : at + span, :, lanes]
             else:
-                found = kv_ref[sheet, at : at + span, g * BLOCK : (g + 1) * BLOCK, lanes]
+                found = rows_of(at, g, lanes)
             return found.reshape(span // 2, 2, BLOCK, 128)
 
         west, east = beside(b - 1), beside(b + 1)
@@ -305,7 +313,7 @@
 
 
 def attend_kernel(
-    q_ref, kv_ref, sides_ref, tokens_ref, gain_ref, wkv_ref, middle_ref, bias, pool, wout_ref,
+    q_ref, kv_ref, halo_ref, sides_ref, tokens_ref, gain_ref, wkv_ref, middle_ref, bias, pool, wout_ref,
     attended_ref, sums_ref, first_row_ref, last_row_ref, first_col_ref, last_col_ref, sides, outer, scores, weights,
 ):
     rows, cols, inner = q_ref.shape[1:]
@@ -322,7 +330,7 @@
     def store(at, b, lanes, piece):
         outer[b // last, at : at + BLOCK, :, lanes] = piece
 
-    attend_blocks((0, last), sheet, q_ref, kv_ref, sides, bias, scores, weights, store)
+    attend_blocks((0, last), sheet, q_ref, kv_ref, halo_ref, sides, bias, scores, weights, store)
     mixed = jnp.concatenate([outer[0], middle_ref[sheet], outer[1]], axis=1)
     mixed = mixed.reshape(rows * cols, inner).astype(bf16)
     attended = (tokens_ref[sheet].astype(f32) + dot(mixed, wout_ref[...])).astype(bf16)
@@ -534,41 +542,45 @@
     near = pl.BlockSpec(memory_space=pltpu.VMEM)
     far = pl.BlockSpec(memory_space=pl.ANY)
     wq_near, wkv_near = in_vmem(w_query), in_vmem(w_kv)
-    gain = pl.pallas_call(
-        warm_kernel,
-        in_specs=[pl.BlockSpec(memory_space=pltpu.VMEM)] * 3,
-        out_specs=pl.BlockSpec(memory_space=pltpu.VMEM),
-        out_shape=jax.ShapeDtypeStruct((1, width), f32),
-        compiler_params=params(4),
-        name="warm",
-    )(gain, wq_near, wkv_near)
     flat = in_vmem(tokens.reshape(sheets, area, width))
     edge = HALO * cols
     blocks = (rows // BLOCK) * (cols // BLOCK)
     keys = (BLOCK + 2 * HALO) ** 2
     stage = [pltpu.VMEM((2, inner // 128, keys, 256), f32), pltpu.VMEM((2, inner // 128, keys, 256), bf16)]
-    q, kv, bias, pool, middle = pl.pallas_call(
-        lambda *refs: project_kernel((grid_h, grid_w), *refs),
+    gain = in_vmem(gain)
+    q, kv = pl.pallas_call(
+        project_kernel,
+        grid=(sheets,),
+        in_specs=[near] * 4,
+        out_specs=[near] * 2,
+        out_shape=[pltpu.VMEM((sheets, rows, cols, inner), f32), pltpu.VMEM((sheets, rows, cols, wide), f32)],
+        compiler_params=params(16),
+        cost_estimate=cost(2 * sheets * area * width * (inner + wide), 2 * (width * (inner + wide) + 5 * sheets * area * width)),
+        name="project",
+    )(flat, gain, wq_near, wkv_near)
+    q, kv = in_vmem(q), in_vmem(kv)
+    halo, bias, pool, middle = pl.pallas_call(
+        lambda *refs: middle_kernel((grid_h, grid_w), *refs),
         grid_spec=pltpu.PrefetchScalarGridSpec(
             num_scalar_prefetch=1,
             grid=(sheets,),
             in_specs=[near] * 6 + [
                 pl.BlockSpec((None, UNITS, rows + cols), lambda s, p: (p[0] * col_count + p[1], 0, 0)),
             ],
-            out_specs=[near] * 5,
+            out_specs=[near] * 4,
             scratch_shapes=stage,
         ),
         out_shape=[
-            pltpu.VMEM((sheets, rows, cols, inner), f32), pltpu.VMEM((sheets, rows + 2 * HALO, cols, wide), f32),
+            pltpu.VMEM((sheets, 2 * HALO, cols, wide), f32),
             pltpu.VMEM((rows // BLOCK, cols // BLOCK, keys, 128), f32), pltpu.VMEM((UNITS, area), bf16),
             pltpu.VMEM((sheets, rows, cols - 2 * BLOCK, inner), f32),
         ],
         compiler_params=params(16),
-        cost_estimate=cost(2 * sheets * area * width * (inner + wide), 2 * (width * (inner + wide) + 5 * sheets * area * width)),
-        name="project",
+        cost_estimate=cost(2 * sheets * area * width * wide, 8 * sheets * area * width, sheets * blocks * keys * 512),
+        name="middle",
     )(
-        at, flat, in_vmem(above.reshape(sheets, edge, width)), in_vmem(below.reshape(sheets, edge, width)),
-        in_vmem(gain), wq_near, wkv_near, masks,
+        at, q, kv, in_vmem(above.reshape(sheets, edge, width)), in_vmem(below.reshape(sheets, edge, width)),
+        gain, wkv_near, masks,
     )
 
     blank = jnp.zeros((sheets, rows + 2 * HALO, BLOCK - 2 * HALO, width), bf16)
@@ -580,7 +592,7 @@
     attended, sums, first_row, last_row, first_col, last_col = pl.pallas_call(
         attend_kernel,
         grid=(sheets,),
-        in_specs=[near] * 9 + [fixed(inner, width)],
+        in_specs=[near] * 10 + [fixed(inner, width)],
         out_specs=[
             per_sheet(area, width),
             pl.BlockSpec((row_count, UNITS, width), lambda s: (0, s, 0)),
@@ -601,7 +613,7 @@
         cost_estimate=cost(2 * sheets * area * inner * width * 4, 2 * sheets * area * width * 4, sheets * blocks * keys * 1024),
         name="attend",
     )(
-        in_vmem(q), in_vmem(kv), in_vmem(sides), flat, in_vmem(gain), wkv_near, in_vmem(middle), in_vmem(bias),
+        q, kv, in_vmem(halo), in_vmem(sides), flat, gain, wkv_near, in_vmem(middle), in_vmem(bias),
         in_vmem(pool), w_out,
     )
 

time: 94.4 us -> 93.3 us (0.988)
  starting transfers between devices: 41.6 us -> 37.2 us
  local copies, waits for them, and re-layouts: 4.59 us -> 7.1 us
    all_to_all x1, starting transfers between devices: 10.8 us -> 6.39 us  [layer(): lax.all_to_all(sums, 'row', 0, 0, tiled=True)]
    unnamed x32 -> x36, local copies, waits for them, and re-layouts: 1.36 us -> 5.22 us
    ppermute x1, waiting for transfers between devices: 0.01 us -> 2.55 us  [layer(): west = lax.ppermute(edges(cols - HALO), 'col', col_fwd)]
    ppermute x1, waiting for transfers between devices: 2.29 us -> 0.01 us  [layer(): above = lax.ppermute(tokens[:, rows - HALO:], 'row', row_fwd)]
    slice x7, local copies, waits for them, and re-layouts: 1.53 us -> 0.33 us  [edges(): x[:, :, first:first + HALO]]
  transfers between devices with their start and end apart: 10 -> 10, of which waited for: 3 -> 3; matrix products, arithmetic and copies ran while one was open for 2% -> 1% of each run, Pallas kernels for 21% -> 22%
where the time goes in v9:
time: 93.3 us; the launch traced here: 92.7 us
  starting transfers between devices  37.2 us (40%)
  Pallas kernels  36.1 us (39%)
  waiting for transfers between devices  10.9 us (12%)
  local copies, waits for them, and re-layouts  7.1 us (8%)
    pallas_call x1, Pallas kernels, layer(): pl.pallas_call(conv_kernel, grid=(sheets, 3), in_specs=[per_sheet(area, w...  9.09 us
    pallas_call x1, Pallas kernels, layer(): pl.pallas_call(tail_kernel, grid_spec=pltpu.PrefetchScalarGridSpec(num_sc...  8.38 us
    all_to_all x1, starting transfers between devices, layer(): lax.all_to_all(strips, 'col', 0, 0, tiled=True)  7.87 us
    pallas_call x1, Pallas kernels, layer(): pl.pallas_call(attend_kernel, grid=(sheets,), in_specs=[near] * 10 + [fix...  7.16 us
    all_to_all x1, starting transfers between devices, layer(): lax.all_to_all(sums, 'row', 0, 0, tiled=True)  6.39 us
    ppermute x1, starting transfers between devices, layer(): west = lax.ppermute(edges(cols - HALO), 'col', col_fwd)  6.06 us
    ppermute x1, starting transfers between devices, layer(): att_west = lax.ppermute(att_edges(last_col, cols - 1), 'col', col_fwd)  5.9 us
    ppermute x1, waiting for transfers between devices, layer(): att_below = lax.ppermute(first_row, 'row', row_bwd)  5.71 us
  transfers between devices with their start and end apart: 10, of which 3 were waited for; matrix products, arithmetic and copies ran while one was open for 1% of the time, Pallas kernels for 22%

profile of v9, /device:TPU:32, one launch (start us, length us, event | category | flops | bytes accessed | tf_op | source)
XLA Modules:
  0.0 92.7 jit_solution(13316304599228969449)
XLA Ops:
  0.0 1.1 %fusion.1 = (bf16[2,2,32,1024]{3,2,1,0:T(8,128)(2,1)S(1)}, bf16[2,2,32,1024]{3,2,1,0:T(8,128)(2,1)S(1)}) fusion(bf16[2,16,32,1024]{3,2,1,0:T(8,128)(2,1)} %param.16), kind=kLoop, calls=%fused_computation.7 | loop fusion | bytes 1048576 | tf_op jit(solution)/shard_map/slice | solution.py:531
  1.1 1.9 %collective-permute-start.1 = (bf16[2,2,32,1024]{3,2,1,0:T(8,128)(2,1)S(1)}, bf16[2,2,32,1024]{3,2,1,0:T(8,128)(2,1)S(1)}, u32[]{:S(2)}, u32[]{:S(2)}) collective-permute-start(bf16[2,2,32,1024]{3,2,1,0:T(8,128)(2,1)S(1)} %get-tuple-element.31), channel_id=1, source_target_pairs={{8,0},{16,8},{24,16},{32,24},{40,32},{48,40},{56,48},{64,56},{72,6... | collective-permute-start | bytes 786440 | tf_op jit(solution)/shard_map/ppermute | solution.py:531
  3.0 2.4 %collective-permute-start = (bf16[2,2,32,1024]{3,2,1,0:T(8,128)(2,1)S(1)}, bf16[2,2,32,1024]{3,2,1,0:T(8,128)(2,1)S(1)}, u32[]{:S(2)}, u32[]{:S(2)}) collective-permute-start(bf16[2,2,32,1024]{3,2,1,0:T(8,128)(2,1)S(1)} %get-tuple-element.32), channel_id=1, source_target_pairs={{0,8},{8,16},{16,24},{24,32},{32,40},{40,48},{48,56},{56,64},{64,7... | collective-permute-start | bytes 786440 | tf_op jit(solution)/shard_map/ppermute | solution.py:530
  5.4 0.0 copy-start
  5.4 1.6 %copy-done = bf16[1024,1024]{1,0:T(8,128)(2,1)S(1)} copy-done((bf16[1024,1024]{1,0:T(8,128)(2,1)S(1)}, bf16[1024,1024]{1,0:T(8,128)(2,1)}, u32[]{:S(2)}) %copy-start) | copy-done | bytes 2097176
  7.0 1.6 %copy-done.4 = bf16[2,16,32,1024]{3,2,1,0:T(8,128)(2,1)S(1)} copy-done((bf16[2,16,32,1024]{3,2,1,0:T(8,128)(2,1)S(1)}, bf16[2,16,32,1024]{3,2,1,0:T(8,128)(2,1)}, u32[]{:S(2)}) %copy-start.4) | copy-done | bytes 2097176
  8.6 0.7 copy-done.12
  9.3 1.2 %copy-done.15 = bf16[1024,512]{1,0:T(8,128)(2,1)S(1)} copy-done((bf16[1024,512]{1,0:T(8,128)(2,1)S(1)}, bf16[1024,512]{1,0:T(8,128)(2,1)}, u32[]{:S(2)}) %copy-start.15) | copy-done | bytes 1048600
  10.5 4.6 %project.1 = (f32[2,16,32,512]{3,2,1,0:T(8,128)S(1)}, f32[2,16,32,1024]{3,2,1,0:T(8,128)S(1)}) custom-call(bf16[2,512,1024]{2,1,0:T(8,128)(2,1)S(1)} %bitcast.15, f32[1,1024]{1,0:T(1,128)S(1)} %bitcast.17, bf16[1024,512]{1,0:T(8,128)(2,1)S(1)} %copy-done.15, bf16[1024,1024]{1,0:T(8,128)(2,1)S(1)} %copy-done), custom_call_target="tpu_custom_call" | custom-call | flops 3221225472 | bytes 13631488 | tf_op jit(solution)/shard_map/project/pallas_call | solution.py:551
  15.1 0.0 copy-start.2
  15.1 0.2 fusion
  15.3 0.1 pad_add_fusion.refs_0_.place_ref
  15.5 0.1 pad.16.clone
  15.6 0.0 collective-permute-done.1
  15.7 0.0 collective-permute-done
  15.7 0.1 pad_maximum_fusion
  15.8 1.3 %collective-permute-start.2 = (bf16[2,20,2,1024]{3,1,2,0:T(8,128)(2,1)S(1)}, bf16[2,20,2,1024]{3,1,2,0:T(8,128)(2,1)S(1)}, u32[]{:S(2)}, u32[]{:S(2)}) collective-permute-start(bf16[2,20,2,1024]{3,1,2,0:T(8,128)(2,1)S(1)} %pad_maximum_fusion), channel_id=1, source_target_pairs={{1,0},{2,1},{3,2},{4,3},{5,4},{6,5},{7,6},{9,8},{10,9},{11,10},{12... | collective-permute-start | bytes 491528 | tf_op jit(solution)/shard_map/ppermute | solution.py:537
  17.1 0.1 pad_maximum_fusion.1
  17.2 6.1 %collective-permute-start.3 = (bf16[2,20,2,1024]{3,1,2,0:T(8,128)(2,1)S(1)}, bf16[2,20,2,1024]{3,1,2,0:T(8,128)(2,1)S(1)}, u32[]{:S(2)}, u32[]{:S(2)}) collective-permute-start(bf16[2,20,2,1024]{3,1,2,0:T(8,128)(2,1)S(1)} %pad_maximum_fusion.1), channel_id=1, source_target_pairs={{0,1},{1,2},{2,3},{3,4},{4,5},{5,6},{6,7},{8,9},{9,10},{10,11},{11... | collective-permute-start | bytes 491528 | tf_op jit(solution)/shard_map/ppermute | solution.py:536
  23.3 0.0 copy-done.1
  23.3 0.0 copy-done.2
  23.3 0.0 copy-start.5
  23.3 0.0 copy-start.13
  23.3 0.0 copy-start.16
  23.3 5.2 %middle.1 = (f32[2,4,32,1024]{3,2,1,0:T(8,128)S(1)}, f32[2,4,144,128]{3,2,1,0:T(8,128)S(1)}, bf16[8,512]{1,0:T(8,128)(2,1)S(1)}, f32[2,16,16,512]{3,2,1,0:T(8,128)S(1)}) custom-call(s32[2]{0:T(128)S(1)} %pad_add_fusion.refs_0_.place_ref, f32[2,16,32,512]{3,2,1,0:T(8,128)S(1)} %get-tuple-element.17.refs_1_.q_ref, ...), custom_call_target="tpu_custom_call" | custom-call | flops 2147483648 | bytes 8388608 | tf_op jit(solution)/shard_map/middle/pallas_call | solution.py:562
  28.6 0.0 collective-permute-done.2
  28.6 0.2 copy.31
  28.8 2.5 %collective-permute-done.3 = bf16[2,20,2,1024]{3,1,2,0:T(8,128)(2,1)S(1)} collective-permute-done((bf16[2,20,2,1024]{3,1,2,0:T(8,128)(2,1)S(1)}, bf16[2,20,2,1024]{3,1,2,0:T(8,128)(2,1)S(1)}, u32[]{:S(2)}, u32[]{:S(2)}) %collective-permute-start.3) | collective-permute-done | bytes 163872 | tf_op jit(solution)/shard_map/ppermute | solution.py:536
  31.3 0.2 copy.32
  31.5 0.4 maximum_bitcast_fusion.sides_ref
  31.9 0.0 copy-done.5
  31.9 0.0 copy-done.13
  31.9 0.0 copy-done.16
  31.9 0.0 copy-start.6
  31.9 0.0 copy-start.10
  31.9 7.2 %attend.1 = (bf16[2,512,1024]{2,1,0:T(8,128)(2,1)}, bf16[16,16,1024]{2,1,0:T(8,128)(2,1)}, bf16[2,32,1024]{2,1,0:T(8,128)(2,1)S(1)}, bf16[2,32,1024]{2,1,0:T(8,1...) custom-call(f32[2,16,32,512]{3,2,1,0:T(8,128)S(1)} %get-tuple-element.17.refs_1_.q_ref, ...), custom_call_target="tpu_custom_call" | custom-call | flops 4294967296 | bytes 8388608 | tf_op jit(solution)/shard_map/attend/pallas_call | solution.py:592
  39.1 2.1 %collective-permute-start.4 = (bf16[2,32,1024]{2,1,0:T(8,128)(2,1)S(1)}, bf16[2,32,1024]{2,1,0:T(8,128)(2,1)S(1)}, u32[]{:S(2)}, u32[]{:S(2)}) collective-permute-start(bf16[2,32,1024]{2,1,0:T(8,128)(2,1)S(1)} %get-tuple-element.25), channel_id=1, source_target_pairs={{0,8},{8,16},{16,24},{24,32},{32,40},{40,48},{48,56},{56,64},{64,7... | collective-permute-start | bytes 393224 | tf_op jit(solution)/shard_map/ppermute | solution.py:621
  41.2 6.4 %all-to-all-start = ((bf16[16,16,1024]{2,1,0:T(8,128)(2,1)}), bf16[16,16,1024]{2,1,0:T(8,128)(2,1)S(1)}, u32[]{:S(2)}, u32[]{:S(2)}) async-start(bf16[16,16,1024]{2,1,0:T(8,128)(2,1)} %get-tuple-element.23), calls=%async_computation | async-start | bytes 1048576 | tf_op jit(solution)/shard_map/all_to_all | solution.py:623
  47.5 2.0 %collective-permute-start.5 = (bf16[2,32,1024]{2,1,0:T(8,128)(2,1)S(1)}, bf16[2,32,1024]{2,1,0:T(8,128)(2,1)S(1)}, u32[]{:S(2)}, u32[]{:S(2)}) collective-permute-start(bf16[2,32,1024]{2,1,0:T(8,128)(2,1)S(1)} %get-tuple-element.26), channel_id=1, source_target_pairs={{8,0},{16,8},{24,16},{32,24},{40,32},{48,40},{56,48},{64,56},{72,6... | collective-permute-start | bytes 393224 | tf_op jit(solution)/shard_map/ppermute | solution.py:622
  49.6 0.0 collective-permute-done.4.top_ref
  49.6 5.7 %collective-permute-done.5.bottom_ref = bf16[2,32,1024]{2,1,0:T(8,128)(2,1)S(1)} collective-permute-done((bf16[2,32,1024]{2,1,0:T(8,128)(2,1)S(1)}, bf16[2,32,1024]{2,1,0:T(8,128)(2,1)S(1)}, u32[]{:S(2)}, u32[]{:S(2)}) %collective-permute-start.5) | collective-permute-done | bytes 131104 | tf_op jit(solution)/shard_map/ppermute | solution.py:622
  55.4 5.9 %collective-permute-start.6 = (bf16[2,18,1024]{2,1,0:T(8,128)(2,1)S(1)}, bf16[2,18,1024]{2,1,0:T(8,128)(2,1)S(1)}, u32[]{:S(2)}, u32[]{:S(2)}) collective-permute-start(bf16[2,18,1024]{2,1,0:T(8,128)(2,1)S(1)} %pad_maximum_fusion.2), channel_id=1, source_target_pairs={{0,1},{1,2},{2,3},{3,4},{4,5},{5,6},{6,7},{8,9},{9,10},{10,11},{11... | collective-permute-start | bytes 221192 | tf_op jit(solution)/shard_map/ppermute | solution.py:628
  61.3 1.3 %collective-permute-start.7 = (bf16[2,18,1024]{2,1,0:T(8,128)(2,1)S(1)}, bf16[2,18,1024]{2,1,0:T(8,128)(2,1)S(1)}, u32[]{:S(2)}, u32[]{:S(2)}) collective-permute-start(bf16[2,18,1024]{2,1,0:T(8,128)(2,1)S(1)} %pad_maximum_fusion.3), channel_id=1, source_target_pairs={{1,0},{2,1},{3,2},{4,3},{5,4},{6,5},{7,6},{9,8},{10,9},{11,10},{12... | collective-permute-start | bytes 221192 | tf_op jit(solution)/shard_map/ppermute | solution.py:629
  62.6 0.0 all-to-all-done
  62.6 0.0 copy-done.6
  62.7 0.0 copy-done.10
  62.7 1.6 %combine.1 = bf16[8,32,1024]{2,1,0:T(8,128)(2,1)} custom-call(s32[2]{0:T(128)S(1)} %pad_add_fusion.refs_0_.place_ref, bf16[16,32,48]{2,1,0:T(8,128)(2,1)S(1)} %copy-done.10, bf16[8,48,256]{2,1,0:T(8,128)(2,1)S(1)} %copy-done.6, bf16[256,1024]{1,0:T(8,128)(2,1)S(1)} %bitcast.11), custom_call_target="tpu_custom_call" | custom-call | tf_op jit(solution)/shard_map/combine/pallas_call | solution.py:633
  64.3 7.9 %all-to-all-start.1 = ((bf16[8,32,1024]{2,1,0:T(8,128)(2,1)}), bf16[8,32,1024]{2,1,0:T(8,128)(2,1)S(1)}, u32[]{:S(2)}, u32[]{:S(2)}) async-start(bf16[8,32,1024]{2,1,0:T(8,128)(2,1)} %combine.1), calls=%async_computation.1 | async-start | bytes 1048576 | tf_op jit(solution)/shard_map/all_to_all | solution.py:649
  72.2 0.0 collective-permute-done.6
  72.2 0.0 collective-permute-done.7
  72.2 0.0 copy-start.3
  72.3 0.0 copy-start.7
  72.3 0.0 copy-start.8
  72.3 0.0 copy-start.9
  72.3 0.0 copy-start.11
  72.3 0.0 copy-start.14
  72.3 9.1 %conv.1 = f32[2,512,256]{2,1,0:T(8,128)S(1)} custom-call(bf16[2,512,1024]{2,1,0:T(8,128)(2,1)} %get-tuple-element.24.attended_ref, bf16[2,32,1024]{2,1,0:T(8,128)(2,1)S(1)} %collective-permute-done.4.top_ref, bf16[2,32,1024]{2,1,0:T(8,128)(2,1)S(1)} %collective-permute-done.5.bottom_ref, bf16[2,24,1024]{2,1,0:T(8,128)(2,1)S(1)} %pad.7.left_ref, ...), custom_call_target="tpu_custom_call" | custom-call | flops 4831838208 | bytes 6815744 | tf_op jit(solution)/shard_map/conv/pallas_call | solution.py:651
  81.4 2.7 %all-to-all-done.1 = bf16[8,32,1024]{2,1,0:T(8,128)(2,1)S(1)} async-done(((bf16[8,32,1024]{2,1,0:T(8,128)(2,1)}), bf16[8,32,1024]{2,1,0:T(8,128)(2,1)S(1)}, u32[]{:S(2)}, u32[]{:S(2)}) %all-to-all-start.1) | async-done | bytes 524320 | tf_op jit(solution)/shard_map/all_to_all | solution.py:649
  84.1 0.0 copy-done.3
  84.1 0.0 copy-done.7
  84.1 0.0 copy-done.8
  84.1 0.0 copy-done.9
  84.1 0.0 copy-done.11
  84.1 8.4 %tail.1 = bf16[2,512,256]{2,1,0:T(8,128)(2,1)} custom-call(s32[2]{0:T(128)S(1)} %pad_add_fusion.refs_0_.place_ref, bf16[8,96,256]{2,1,0:T(8,128)(2,1)S(1)} %copy-done.3, f32[16,1,96]{2,1,0:T(1,128)S(1)} %copy-done.11, f32[8,1,96]{2,1,0:T(1,128)S(1)} %copy-done.14, bf16[256,1024]{1,0:T(8,128)(2,1)S(1)} %bitcast.12, bf16[4,1024,512]{2,1,0:T(8,128)(2,1)} %wpool_hbm.1, ...), custom_call_target="tpu_custom_call" | custom-call | flops 4000000000 | bytes 13631488 | tf_op jit(solution)/shard_map/tail/pallas_call | solution.py:673
  (20 shorter events, 0.3 us)
Async XLA Ops:
  1.1 14.5 %collective-permute-start.1 = (bf16[2,2,32,1024]{3,2,1,0:T(8,128)(2,1)S(1)}, bf16[2,2,32,1024]{3,2,1,0:T(8,128)(2,1)S(1)}, u32[]{:S(2)}, u32[]{:S(2)}) collective-permute-start(bf16[2,2,32,1024]{3,2,1,0:T(8,128)(2,1)S(1)} %get-tuple-element.31), channel_id=1, source_target_pairs={{8,0},{16,8},{24,16},{32,24},{40,32},{48,40},{56,48},{64,56},{72,6... | collective-permute-start | bytes 786440 | tf_op jit(solution)/shard_map/ppermute | solution.py:531
  3.0 12.6 %collective-permute-start = (bf16[2,2,32,1024]{3,2,1,0:T(8,128)(2,1)S(1)}, bf16[2,2,32,1024]{3,2,1,0:T(8,128)(2,1)S(1)}, u32[]{:S(2)}, u32[]{:S(2)}) collective-permute-start(bf16[2,2,32,1024]{3,2,1,0:T(8,128)(2,1)S(1)} %get-tuple-element.32), channel_id=1, source_target_pairs={{0,8},{8,16},{16,24},{24,32},{32,40},{40,48},{48,56},{56,64},{64,7... | collective-permute-start | bytes 786440 | tf_op jit(solution)/shard_map/ppermute | solution.py:530
  5.4 1.6 %copy-start = (bf16[1024,1024]{1,0:T(8,128)(2,1)S(1)}, bf16[1024,1024]{1,0:T(8,128)(2,1)}, u32[]{:S(2)}) copy-start(bf16[1024,1024]{1,0:T(8,128)(2,1)} %wkv_ref.1) | copy-start | bytes 6291460
  7.0 1.6 %copy-start.4 = (bf16[2,16,32,1024]{3,2,1,0:T(8,128)(2,1)S(1)}, bf16[2,16,32,1024]{3,2,1,0:T(8,128)(2,1)}, u32[]{:S(2)}) copy-start(bf16[2,16,32,1024]{3,2,1,0:T(8,128)(2,1)} %param.16) | copy-start | bytes 6291460
  8.6 0.7 copy-start.12
  9.3 1.2 %copy-start.15 = (bf16[1024,512]{1,0:T(8,128)(2,1)S(1)}, bf16[1024,512]{1,0:T(8,128)(2,1)}, u32[]{:S(2)}) copy-start(bf16[1024,512]{1,0:T(8,128)(2,1)} %wq.1) | copy-start | bytes 3145732
  10.5 12.8 %copy-start.1 = (bf16[1024,1024]{1,0:T(8,128)(2,1)S(1)}, bf16[1024,1024]{1,0:T(8,128)(2,1)}, u32[]{:S(2)}) copy-start(bf16[1024,1024]{1,0:T(8,128)(2,1)} %wkv_ref.1) | copy-start | bytes 6291460
  15.1 8.2 %copy-start.2 = (f32[128,8,48]{2,1,0:T(8,128)S(1)}, f32[128,8,48]{2,1,0:T(8,128)}, u32[]{:S(2)}) copy-start(f32[128,8,48]{2,1,0:T(8,128)} %constant.31.clone.refs_7_) | copy-start | bytes 589828
  15.8 12.7 %collective-permute-start.2 = (bf16[2,20,2,1024]{3,1,2,0:T(8,128)(2,1)S(1)}, bf16[2,20,2,1024]{3,1,2,0:T(8,128)(2,1)S(1)}, u32[]{:S(2)}, u32[]{:S(2)}) collective-permute-start(bf16[2,20,2,1024]{3,1,2,0:T(8,128)(2,1)S(1)} %pad_maximum_fusion), channel_id=1, source_target_pairs={{1,0},{2,1},{3,2},{4,3},{5,4},{6,5},{7,6},{9,8},{10,9},{11,10},{12... | collective-permute-start | bytes 491528 | tf_op jit(solution)/shard_map/ppermute | solution.py:537
  17.2 14.1 %collective-permute-start.3 = (bf16[2,20,2,1024]{3,1,2,0:T(8,128)(2,1)S(1)}, bf16[2,20,2,1024]{3,1,2,0:T(8,128)(2,1)S(1)}, u32[]{:S(2)}, u32[]{:S(2)}) collective-permute-start(bf16[2,20,2,1024]{3,1,2,0:T(8,128)(2,1)S(1)} %pad_maximum_fusion.1), channel_id=1, source_target_pairs={{0,1},{1,2},{2,3},{3,4},{4,5},{5,6},{6,7},{8,9},{9,10},{10,11},{11... | collective-permute-start | bytes 491528 | tf_op jit(solution)/shard_map/ppermute | solution.py:536
  23.3 8.6 %copy-start.5 = (bf16[2,16,32,1024]{3,2,1,0:T(8,128)(2,1)S(1)}, bf16[2,16,32,1024]{3,2,1,0:T(8,128)(2,1)}, u32[]{:S(2)}) copy-start(bf16[2,16,32,1024]{3,2,1,0:T(8,128)(2,1)} %param.16) | copy-start | bytes 6291460
  23.3 8.6 %copy-start.13 = (f32[1024]{0:T(1024)S(1)}, f32[1024]{0:T(1024)}, u32[]{:S(2)}) copy-start(f32[1024]{0:T(1024)} %param.17) | copy-start | bytes 12292
  23.3 8.6 %copy-start.16 = (bf16[512,1024]{1,0:T(8,128)(2,1)S(1)}, bf16[512,1024]{1,0:T(8,128)(2,1)}, u32[]{:S(2)}) copy-start(bf16[512,1024]{1,0:T(8,128)(2,1)} %wout_ref.1) | copy-start | bytes 3145732
  31.9 30.8 %copy-start.6 = (bf16[8,48,256]{2,1,0:T(8,128)(2,1)S(1)}, bf16[8,48,256]{2,1,0:T(8,128)(2,1)}, u32[]{:S(2)}) copy-start(bf16[8,48,256]{2,1,0:T(8,128)(2,1)} %constant.33.clone.table_ref) | copy-start | bytes 589828
  31.9 30.8 %copy-start.10 = (bf16[16,32,48]{2,1,0:T(8,128)(2,1)S(1)}, bf16[16,32,48]{2,1,0:T(8,128)(2,1)}, u32[]{:S(2)}) copy-start(bf16[16,32,48]{2,1,0:T(8,128)(2,1)} %constant.32.clone.near_ref) | copy-start | bytes 147460
  39.1 10.5 %collective-permute-start.4 = (bf16[2,32,1024]{2,1,0:T(8,128)(2,1)S(1)}, bf16[2,32,1024]{2,1,0:T(8,128)(2,1)S(1)}, u32[]{:S(2)}, u32[]{:S(2)}) collective-permute-start(bf16[2,32,1024]{2,1,0:T(8,128)(2,1)S(1)} %get-tuple-element.25), channel_id=1, source_target_pairs={{0,8},{8,16},{16,24},{24,32},{32,40},{40,48},{48,56},{56,64},{64,7... | collective-permute-start | bytes 393224 | tf_op jit(solution)/shard_map/ppermute | solution.py:621
  41.2 21.5 %all-to-all-start = ((bf16[16,16,1024]{2,1,0:T(8,128)(2,1)}), bf16[16,16,1024]{2,1,0:T(8,128)(2,1)S(1)}, u32[]{:S(2)}, u32[]{:S(2)}) async-start(bf16[16,16,1024]{2,1,0:T(8,128)(2,1)} %get-tuple-element.23), calls=%async_computation | async-start | bytes 1048576 | tf_op jit(solution)/shard_map/all_to_all | solution.py:623
  47.5 7.8 %collective-permute-start.5 = (bf16[2,32,1024]{2,1,0:T(8,128)(2,1)S(1)}, bf16[2,32,1024]{2,1,0:T(8,128)(2,1)S(1)}, u32[]{:S(2)}, u32[]{:S(2)}) collective-permute-start(bf16[2,32,1024]{2,1,0:T(8,128)(2,1)S(1)} %get-tuple-element.26), channel_id=1, source_target_pairs={{8,0},{16,8},{24,16},{32,24},{40,32},{48,40},{56,48},{64,56},{72,6... | collective-permute-start | bytes 393224 | tf_op jit(solution)/shard_map/ppermute | solution.py:622
  55.4 16.8 %collective-permute-start.6 = (bf16[2,18,1024]{2,1,0:T(8,128)(2,1)S(1)}, bf16[2,18,1024]{2,1,0:T(8,128)(2,1)S(1)}, u32[]{:S(2)}, u32[]{:S(2)}) collective-permute-start(bf16[2,18,1024]{2,1,0:T(8,128)(2,1)S(1)} %pad_maximum_fusion.2), channel_id=1, source_target_pairs={{0,1},{1,2},{2,3},{3,4},{4,5},{5,6},{6,7},{8,9},{9,10},{10,11},{11... | collective-permute-start | bytes 221192 | tf_op jit(solution)/shard_map/ppermute | solution.py:628
  61.3 10.9 %collective-permute-start.7 = (bf16[2,18,1024]{2,1,0:T(8,128)(2,1)S(1)}, bf16[2,18,1024]{2,1,0:T(8,128)(2,1)S(1)}, u32[]{:S(2)}, u32[]{:S(2)}) collective-permute-start(bf16[2,18,1024]{2,1,0:T(8,128)(2,1)S(1)} %pad_maximum_fusion.3), channel_id=1, source_target_pairs={{1,0},{2,1},{3,2},{4,3},{5,4},{6,5},{7,6},{9,8},{10,9},{11,10},{12... | collective-permute-start | bytes 221192 | tf_op jit(solution)/shard_map/ppermute | solution.py:629
  64.3 19.8 %all-to-all-start.1 = ((bf16[8,32,1024]{2,1,0:T(8,128)(2,1)}), bf16[8,32,1024]{2,1,0:T(8,128)(2,1)S(1)}, u32[]{:S(2)}, u32[]{:S(2)}) async-start(bf16[8,32,1024]{2,1,0:T(8,128)(2,1)} %combine.1), calls=%async_computation.1 | async-start | bytes 1048576 | tf_op jit(solution)/shard_map/all_to_all | solution.py:649
  72.2 11.8 %copy-start.3 = (bf16[8,96,256]{2,1,0:T(8,128)(2,1)S(1)}, bf16[8,96,256]{2,1,0:T(8,128)(2,1)}, u32[]{:S(2)}) copy-start(bf16[8,96,256]{2,1,0:T(8,128)(2,1)} %constant.34.clone.table_hbm) | copy-start | bytes 1179652
  72.3 11.8 %copy-start.7 = (bf16[2,64,432]{2,1,0:T(8,128)(2,1)S(1)}, bf16[2,64,432]{2,1,0:T(8,128)(2,1)}, u32[]{:S(2)}) copy-start(bf16[2,64,432]{2,1,0:T(8,128)(2,1)} %constant.39.clone.spread_hbm) | copy-start | bytes 331780
  72.3 11.8 %copy-start.8 = (f32[8,32,64]{2,1,0:T(8,128)S(1)}, f32[8,32,64]{2,1,0:T(8,128)}, u32[]{:S(2)}) copy-start(f32[8,32,64]{2,1,0:T(8,128)} %constant.38.clone.by_col_hbm) | copy-start | bytes 196612
  72.3 11.8 %copy-start.9 = (f32[16,16,64]{2,1,0:T(8,128)S(1)}, f32[16,16,64]{2,1,0:T(8,128)}, u32[]{:S(2)}) copy-start(f32[16,16,64]{2,1,0:T(8,128)} %constant.37.clone.by_row_hbm) | copy-start | bytes 196612
  72.3 11.8 %copy-start.11 = (f32[16,1,96]{2,1,0:T(1,128)S(1)}, f32[16,1,96]{2,1,0:T(1,128)}, u32[]{:S(2)}) copy-start(f32[16,1,96]{2,1,0:T(1,128)} %constant.35.clone.row_scale_hbm) | copy-start | bytes 18436
  72.3 11.8 %copy-start.14 = (f32[8,1,96]{2,1,0:T(1,128)S(1)}, f32[8,1,96]{2,1,0:T(1,128)}, u32[]{:S(2)}) copy-start(f32[8,1,96]{2,1,0:T(1,128)} %constant.36.clone.col_scale_hbm) | copy-start | bytes 9220

commit v10 on v9

--- a/solution.py
+++ b/solution.py
@@ -175,12 +175,12 @@
     return jnp.dot(a, b, preferred_element_type=f32)
 
 
-def project_kernel(tokens_ref, gain_ref, wq, wkv, q_ref, kv_ref):
-    rows, cols, inner = q_ref.shape[1:]
+def project_kernel(tokens_ref, gain_ref, wkv, normed_ref, kv_ref):
+    rows, cols, wide = kv_ref.shape[1:]
     s = pl.program_id(0)
-    normed = layer_norm(tokens_ref[s], gain_ref[...])
-    q_ref[s] = dot(normed, wq[...]).astype(bf16).astype(f32).reshape(rows, cols, inner)
-    kv_ref[s] = dot(normed, wkv[...]).astype(bf16).astype(f32).reshape(rows, cols, -1)
+    normed = layer_norm(tokens_ref[...], gain_ref[...])
+    normed_ref[s] = normed
+    kv_ref[s] = dot(normed, wkv[...]).astype(bf16).astype(f32).reshape(rows, cols, wide)
 
 
 def pool_members(masks_ref, pool, cols):
@@ -196,11 +196,12 @@
 
 
 def middle_kernel(
-    grid_shape, place_ref, q_ref, kv_ref, above_ref, below_ref, gain_ref, wkv, masks_ref,
-    halo_ref, bias, pool, context, scores, weights,
+    grid_shape, place_ref, normed_ref, kv_ref, above_ref, below_ref, gain_ref, wq, wkv, masks_ref,
+    q_ref, halo_ref, bias, pool, context, scores, weights,
 ):
-    rows, cols = q_ref.shape[1:3]
+    rows, cols, inner = q_ref.shape[1:]
     s = pl.program_id(0)
+    q_ref[s] = dot(normed_ref[s], wq[...]).astype(bf16).astype(f32).reshape(rows, cols, inner)
 
     @pl.when(s == 0)
     def _():
@@ -548,30 +549,30 @@
     keys = (BLOCK + 2 * HALO) ** 2
     stage = [pltpu.VMEM((2, inner // 128, keys, 256), f32), pltpu.VMEM((2, inner // 128, keys, 256), bf16)]
     gain = in_vmem(gain)
-    q, kv = pl.pallas_call(
+    normed, kv = pl.pallas_call(
         project_kernel,
         grid=(sheets,),
-        in_specs=[near] * 4,
+        in_specs=[per_sheet(area, width), near, near],
         out_specs=[near] * 2,
-        out_shape=[pltpu.VMEM((sheets, rows, cols, inner), f32), pltpu.VMEM((sheets, rows, cols, wide), f32)],
+        out_shape=[pltpu.VMEM((sheets, area, width), bf16), pltpu.VMEM((sheets, rows, cols, wide), f32)],
         compiler_params=params(16),
-        cost_estimate=cost(2 * sheets * area * width * (inner + wide), 2 * (width * (inner + wide) + 5 * sheets * area * width)),
+        cost_estimate=cost(2 * sheets * area * width * wide, 2 * (width * (inner + wide) + 5 * sheets * area * width)),
         name="project",
-    )(flat, gain, wq_near, wkv_near)
-    q, kv = in_vmem(q), in_vmem(kv)
-    halo, bias, pool, middle = pl.pallas_call(
+    )(in_hbm(tokens.reshape(sheets, area, width)), gain, wkv_near)
+    kv = in_vmem(kv)
+    q, halo, bias, pool, middle = pl.pallas_call(
         lambda *refs: middle_kernel((grid_h, grid_w), *refs),
         grid_spec=pltpu.PrefetchScalarGridSpec(
             num_scalar_prefetch=1,
             grid=(sheets,),
-            in_specs=[near] * 6 + [
+            in_specs=[near] * 7 + [
                 pl.BlockSpec((None, UNITS, rows + cols), lambda s, p: (p[0] * col_count + p[1], 0, 0)),
             ],
-            out_specs=[near] * 4,
+            out_specs=[near] * 5,
             scratch_shapes=stage,
         ),
         out_shape=[
-            pltpu.VMEM((sheets, 2 * HALO, cols, wide), f32),
+            pltpu.VMEM((sheets, rows, cols, inner), f32), pltpu.VMEM((sheets, 2 * HALO, cols, wide), f32),
             pltpu.VMEM((rows // BLOCK, cols // BLOCK, keys, 128), f32), pltpu.VMEM((UNITS, area), bf16),
             pltpu.VMEM((sheets, rows, cols - 2 * BLOCK, inner), f32),
         ],
@@ -579,8 +580,8 @@
         cost_estimate=cost(2 * sheets * area * width * wide, 8 * sheets * area * width, sheets * blocks * keys * 512),
         name="middle",
     )(
-        at, q, kv, in_vmem(above.reshape(sheets, edge, width)), in_vmem(below.reshape(sheets, edge, width)),
-        gain, wkv_near, masks,
+        at, in_vmem(normed), kv, in_vmem(above.reshape(sheets, edge, width)),
+        in_vmem(below.reshape(sheets, edge, width)), gain, wq_near, wkv_near, masks,
     )
 
     blank = jnp.zeros((sheets, rows + 2 * HALO, BLOCK - 2 * HALO, width), bf16)
@@ -613,7 +614,7 @@
         cost_estimate=cost(2 * sheets * area * inner * width * 4, 2 * sheets * area * width * 4, sheets * blocks * keys * 1024),
         name="attend",
     )(
-        q, kv, in_vmem(halo), in_vmem(sides), flat, gain, wkv_near, in_vmem(middle), in_vmem(bias),
+        in_vmem(q), kv, in_vmem(halo), in_vmem(sides), flat, gain, wkv_near, in_vmem(middle), in_vmem(bias),
         in_vmem(pool), w_out,
     )
 

time: 93.3 us -> 92.6 us (level)
  local copies, waits for them, and re-layouts: 7.1 us -> 5.49 us
  Pallas kernels: 36.1 us -> 37.7 us
  waiting for transfers between devices: 10.9 us -> 9.58 us
    unnamed x36 -> x34, local copies, waits for them, and re-layouts: 5.22 us -> 2.41 us
    ppermute x1, waiting for transfers between devices: 2.55 us -> 1.19 us  [layer(): west = lax.ppermute(edges(cols - HALO), 'col', col_fwd)]
    pallas_call x1, Pallas kernels: 5.21 us -> 6.56 us  [layer(): pl.pallas_call(lambda *refs: middle_kernel((grid_h, grid_w), *refs), grid...]
    slice x7, local copies, waits for them, and re-layouts: 0.33 us -> 1.53 us  [edges(): x[:, :, first:first + HALO]]
  transfers between devices with their start and end apart: 10 -> 10, of which waited for: 3 -> 3; matrix products, arithmetic and copies ran while one was open for 1% -> 2% of each run, Pallas kernels for 22% -> 24%
where the time goes in v10:
time: 92.6 us; the launch traced here: 91.9 us
  starting transfers between devices  37.8 us (41%)
  Pallas kernels  37.7 us (41%)
  waiting for transfers between devices  9.58 us (10%)
  local copies, waits for them, and re-layouts  5.49 us (6%)
    pallas_call x1, Pallas kernels, layer(): pl.pallas_call(conv_kernel, grid=(sheets, 3), in_specs=[per_sheet(area, w...  9.09 us
    pallas_call x1, Pallas kernels, layer(): pl.pallas_call(tail_kernel, grid_spec=pltpu.PrefetchScalarGridSpec(num_sc...  8.38 us
    all_to_all x1, starting transfers between devices, layer(): lax.all_to_all(strips, 'col', 0, 0, tiled=True)  7.89 us
    pallas_call x1, Pallas kernels, layer(): pl.pallas_call(attend_kernel, grid=(sheets,), in_specs=[near] * 10 + [fix...  7.15 us
    all_to_all x1, starting transfers between devices, layer(): lax.all_to_all(sums, 'row', 0, 0, tiled=True)  6.92 us
    pallas_call x1, Pallas kernels, layer(): pl.pallas_call(lambda *refs: middle_kernel((grid_h, grid_w), *refs), grid...  6.56 us
    ppermute x1, starting transfers between devices, layer(): west = lax.ppermute(edges(cols - HALO), 'col', col_fwd)  6.06 us
    ppermute x1, starting transfers between devices, layer(): att_west = lax.ppermute(att_edges(last_col, cols - 1), 'col', col_fwd)  5.99 us
  transfers between devices with their start and end apart: 10, of which 3 were waited for; matrix products, arithmetic and copies ran while one was open for 2% of the time, Pallas kernels for 24%

profile of v10, /device:TPU:32, one launch (start us, length us, event | category | flops | bytes accessed | tf_op | source)
XLA Modules:
  0.0 91.9 jit_solution(13048610295040143662)
XLA Ops:
  0.0 1.1 %fusion.1 = (bf16[2,2,32,1024]{3,2,1,0:T(8,128)(2,1)S(1)}, bf16[2,2,32,1024]{3,2,1,0:T(8,128)(2,1)S(1)}) fusion(bf16[2,16,32,1024]{3,2,1,0:T(8,128)(2,1)} %param.16), kind=kLoop, calls=%fused_computation.7 | loop fusion | bytes 1048576 | tf_op jit(solution)/shard_map/slice | solution.py:532
  1.1 1.9 %collective-permute-start.1 = (bf16[2,2,32,1024]{3,2,1,0:T(8,128)(2,1)S(1)}, bf16[2,2,32,1024]{3,2,1,0:T(8,128)(2,1)S(1)}, u32[]{:S(2)}, u32[]{:S(2)}) collective-permute-start(bf16[2,2,32,1024]{3,2,1,0:T(8,128)(2,1)S(1)} %get-tuple-element.33), channel_id=1, source_target_pairs={{8,0},{16,8},{24,16},{32,24},{40,32},{48,40},{56,48},{64,56},{72,6... | collective-permute-start | bytes 786440 | tf_op jit(solution)/shard_map/ppermute | solution.py:532
  3.0 2.4 %collective-permute-start = (bf16[2,2,32,1024]{3,2,1,0:T(8,128)(2,1)S(1)}, bf16[2,2,32,1024]{3,2,1,0:T(8,128)(2,1)S(1)}, u32[]{:S(2)}, u32[]{:S(2)}) collective-permute-start(bf16[2,2,32,1024]{3,2,1,0:T(8,128)(2,1)S(1)} %get-tuple-element.34), channel_id=1, source_target_pairs={{0,8},{8,16},{16,24},{24,32},{32,40},{40,48},{48,56},{56,64},{64,7... | collective-permute-start | bytes 786440 | tf_op jit(solution)/shard_map/ppermute | solution.py:531
  5.4 1.4 %fusion = (bf16[2,16,2,1024]{3,2,1,0:T(2,128)(2,1)S(1)}, bf16[2,16,2,1024]{3,2,1,0:T(2,128)(2,1)S(1)}) fusion(bf16[2,16,32,1024]{3,2,1,0:T(8,128)(2,1)} %param.16), kind=kLoop, calls=%fused_computation.6 | loop fusion | bytes 524288 | tf_op jit(solution)/shard_map/slice | solution.py:535
  6.8 0.0 copy-start
  6.9 1.6 %copy-done = bf16[1024,1024]{1,0:T(8,128)(2,1)S(1)} copy-done((bf16[1024,1024]{1,0:T(8,128)(2,1)S(1)}, bf16[1024,1024]{1,0:T(8,128)(2,1)}, u32[]{:S(2)}) %copy-start) | copy-done | bytes 2097176
  8.4 0.7 copy-done.12
  9.1 4.8 %project.1 = (bf16[2,512,1024]{2,1,0:T(8,128)(2,1)S(1)}, f32[2,16,32,1024]{3,2,1,0:T(8,128)S(1)}) custom-call(bf16[2,512,1024]{2,1,0:T(8,128)(2,1)} %bitcast.15, f32[1,1024]{1,0:T(1,128)S(1)} %bitcast.17, bf16[1024,1024]{1,0:T(8,128)(2,1)S(1)} %copy-done), custom_call_target="tpu_custom_call" | custom-call | flops 2147483648 | bytes 13631488 | tf_op jit(solution)/shard_map/project/pallas_call | solution.py:552
  14.0 0.0 copy-start.2
  14.0 0.1 pad_add_fusion.refs_0_.place_ref
  14.1 0.1 pad.16.clone
  14.2 0.0 collective-permute-done.1
  14.3 0.0 collective-permute-done
  14.4 0.1 pad_maximum_fusion
  14.5 1.3 %collective-permute-start.2 = (bf16[2,20,2,1024]{3,1,2,0:T(8,128)(2,1)S(1)}, bf16[2,20,2,1024]{3,1,2,0:T(8,128)(2,1)S(1)}, u32[]{:S(2)}, u32[]{:S(2)}) collective-permute-start(bf16[2,20,2,1024]{3,1,2,0:T(8,128)(2,1)S(1)} %pad_maximum_fusion), channel_id=1, source_target_pairs={{1,0},{2,1},{3,2},{4,3},{5,4},{6,5},{7,6},{9,8},{10,9},{11,10},{12... | collective-permute-start | bytes 491528 | tf_op jit(solution)/shard_map/ppermute | solution.py:538
  15.8 0.1 pad_maximum_fusion.1
  15.9 6.1 %collective-permute-start.3 = (bf16[2,20,2,1024]{3,1,2,0:T(8,128)(2,1)S(1)}, bf16[2,20,2,1024]{3,1,2,0:T(8,128)(2,1)S(1)}, u32[]{:S(2)}, u32[]{:S(2)}) collective-permute-start(bf16[2,20,2,1024]{3,1,2,0:T(8,128)(2,1)S(1)} %pad_maximum_fusion.1), channel_id=1, source_target_pairs={{0,1},{1,2},{2,3},{3,4},{4,5},{5,6},{6,7},{8,9},{9,10},{10,11},{11... | collective-permute-start | bytes 491528 | tf_op jit(solution)/shard_map/ppermute | solution.py:537
  21.9 0.0 copy-done.3
  21.9 0.0 copy-done.2
  21.9 0.0 copy-start.1
  22.0 0.0 copy-start.5
  22.0 0.0 copy-start.13
  22.0 0.0 copy-start.15
  22.0 6.6 %middle.1 = (f32[2,16,32,512]{3,2,1,0:T(8,128)S(1)}, f32[2,4,32,1024]{3,2,1,0:T(8,128)S(1)}, f32[2,4,144,128]{3,2,1,0:T(8,128)S(1)}, bf16[8,512]{1,0:T(8,128)(2,1)S(1)}, f32[2,16,16,512]{3,2,1,0:T(8,128)S(1)}) custom-call(s32[2]{0:T(128)S(1)} %pad_add_fusion.refs_0_.place_ref, bf16[2,512,1024]{2,1,0:T(8,128)(2,1)S(1)} %get-tuple-element.18.refs_1_, ...), custom_call_target="tpu_custom_call" | custom-call | flops 2147483648 | bytes 8388608 | tf_op jit(solution)/shard_map/middle/pallas_call | solution.py:563
  28.6 0.0 collective-permute-done.2
  28.6 0.2 copy.31
  28.8 1.2 %collective-permute-done.3 = bf16[2,20,2,1024]{3,1,2,0:T(8,128)(2,1)S(1)} collective-permute-done((bf16[2,20,2,1024]{3,1,2,0:T(8,128)(2,1)S(1)}, bf16[2,20,2,1024]{3,1,2,0:T(8,128)(2,1)S(1)}, u32[]{:S(2)}, u32[]{:S(2)}) %collective-permute-start.3) | collective-permute-done | bytes 163872 | tf_op jit(solution)/shard_map/ppermute | solution.py:537
  29.9 0.2 copy.32
  30.1 0.4 maximum_bitcast_fusion.sides_ref
  30.5 0.0 copy-done.1
  30.5 0.0 copy-done.5
  30.5 0.0 copy-done.13
  30.5 0.0 copy-done.15
  30.5 0.0 copy-start.6
  30.6 0.0 copy-start.10
  30.6 7.1 %attend.1 = (bf16[2,512,1024]{2,1,0:T(8,128)(2,1)}, bf16[16,16,1024]{2,1,0:T(8,128)(2,1)}, bf16[2,32,1024]{2,1,0:T(8,128)(2,1)S(1)}, bf16[2,32,1024]{2,1,0:T(8,1...) custom-call(f32[2,16,32,512]{3,2,1,0:T(8,128)S(1)} %get-tuple-element.20.q_ref, ...), custom_call_target="tpu_custom_call" | custom-call | flops 4294967296 | bytes 8388608 | tf_op jit(solution)/shard_map/attend/pallas_call | solution.py:593
  37.7 2.1 %collective-permute-start.4 = (bf16[2,32,1024]{2,1,0:T(8,128)(2,1)S(1)}, bf16[2,32,1024]{2,1,0:T(8,128)(2,1)S(1)}, u32[]{:S(2)}, u32[]{:S(2)}) collective-permute-start(bf16[2,32,1024]{2,1,0:T(8,128)(2,1)S(1)} %get-tuple-element.27), channel_id=1, source_target_pairs={{0,8},{8,16},{16,24},{24,32},{32,40},{40,48},{48,56},{56,64},{64,7... | collective-permute-start | bytes 393224 | tf_op jit(solution)/shard_map/ppermute | solution.py:622
  39.8 6.9 %all-to-all-start = ((bf16[16,16,1024]{2,1,0:T(8,128)(2,1)}), bf16[16,16,1024]{2,1,0:T(8,128)(2,1)S(1)}, u32[]{:S(2)}, u32[]{:S(2)}) async-start(bf16[16,16,1024]{2,1,0:T(8,128)(2,1)} %get-tuple-element.25), calls=%async_computation | async-start | bytes 1048576 | tf_op jit(solution)/shard_map/all_to_all | solution.py:624
  46.7 2.0 %collective-permute-start.5 = (bf16[2,32,1024]{2,1,0:T(8,128)(2,1)S(1)}, bf16[2,32,1024]{2,1,0:T(8,128)(2,1)S(1)}, u32[]{:S(2)}, u32[]{:S(2)}) collective-permute-start(bf16[2,32,1024]{2,1,0:T(8,128)(2,1)S(1)} %get-tuple-element.28), channel_id=1, source_target_pairs={{8,0},{16,8},{24,16},{32,24},{40,32},{48,40},{56,48},{64,56},{72,6... | collective-permute-start | bytes 393224 | tf_op jit(solution)/shard_map/ppermute | solution.py:623
  48.7 0.0 collective-permute-done.4.top_ref
  48.8 5.7 %collective-permute-done.5.bottom_ref = bf16[2,32,1024]{2,1,0:T(8,128)(2,1)S(1)} collective-permute-done((bf16[2,32,1024]{2,1,0:T(8,128)(2,1)S(1)}, bf16[2,32,1024]{2,1,0:T(8,128)(2,1)S(1)}, u32[]{:S(2)}, u32[]{:S(2)}) %collective-permute-start.5) | collective-permute-done | bytes 131104 | tf_op jit(solution)/shard_map/ppermute | solution.py:623
  54.5 6.0 %collective-permute-start.6 = (bf16[2,18,1024]{2,1,0:T(8,128)(2,1)S(1)}, bf16[2,18,1024]{2,1,0:T(8,128)(2,1)S(1)}, u32[]{:S(2)}, u32[]{:S(2)}) collective-permute-start(bf16[2,18,1024]{2,1,0:T(8,128)(2,1)S(1)} %pad_maximum_fusion.2), channel_id=1, source_target_pairs={{0,1},{1,2},{2,3},{3,4},{4,5},{5,6},{6,7},{8,9},{9,10},{10,11},{11... | collective-permute-start | bytes 221192 | tf_op jit(solution)/shard_map/ppermute | solution.py:629
  60.6 1.3 %collective-permute-start.7 = (bf16[2,18,1024]{2,1,0:T(8,128)(2,1)S(1)}, bf16[2,18,1024]{2,1,0:T(8,128)(2,1)S(1)}, u32[]{:S(2)}, u32[]{:S(2)}) collective-permute-start(bf16[2,18,1024]{2,1,0:T(8,128)(2,1)S(1)} %pad_maximum_fusion.3), channel_id=1, source_target_pairs={{1,0},{2,1},{3,2},{4,3},{5,4},{6,5},{7,6},{9,8},{10,9},{11,10},{12... | collective-permute-start | bytes 221192 | tf_op jit(solution)/shard_map/ppermute | solution.py:630
  61.9 0.0 all-to-all-done
  61.9 0.0 copy-done.6
  61.9 0.0 copy-done.10
  61.9 1.6 %combine.1 = bf16[8,32,1024]{2,1,0:T(8,128)(2,1)} custom-call(s32[2]{0:T(128)S(1)} %pad_add_fusion.refs_0_.place_ref, bf16[16,32,48]{2,1,0:T(8,128)(2,1)S(1)} %copy-done.10, bf16[8,48,256]{2,1,0:T(8,128)(2,1)S(1)} %copy-done.6, bf16[256,1024]{1,0:T(8,128)(2,1)S(1)} %bitcast.11), custom_call_target="tpu_custom_call" | custom-call | tf_op jit(solution)/shard_map/combine/pallas_call | solution.py:634
  63.6 7.9 %all-to-all-start.1 = ((bf16[8,32,1024]{2,1,0:T(8,128)(2,1)}), bf16[8,32,1024]{2,1,0:T(8,128)(2,1)S(1)}, u32[]{:S(2)}, u32[]{:S(2)}) async-start(bf16[8,32,1024]{2,1,0:T(8,128)(2,1)} %combine.1), calls=%async_computation.1 | async-start | bytes 1048576 | tf_op jit(solution)/shard_map/all_to_all | solution.py:650
  71.5 0.0 collective-permute-done.6
  71.5 0.0 collective-permute-done.7
  71.5 0.0 copy-start.4
  71.5 0.0 copy-start.7
  71.5 0.0 copy-start.8
  71.5 0.0 copy-start.9
  71.6 0.0 copy-start.11
  71.6 0.0 copy-start.14
  71.6 9.1 %conv.1 = f32[2,512,256]{2,1,0:T(8,128)S(1)} custom-call(bf16[2,512,1024]{2,1,0:T(8,128)(2,1)} %get-tuple-element.26.attended_ref, bf16[2,32,1024]{2,1,0:T(8,128)(2,1)S(1)} %collective-permute-done.4.top_ref, bf16[2,32,1024]{2,1,0:T(8,128)(2,1)S(1)} %collective-permute-done.5.bottom_ref, bf16[2,24,1024]{2,1,0:T(8,128)(2,1)S(1)} %pad.7.left_ref, ...), custom_call_target="tpu_custom_call" | custom-call | flops 4831838208 | bytes 6815744 | tf_op jit(solution)/shard_map/conv/pallas_call | solution.py:652
  80.7 2.7 %all-to-all-done.1 = bf16[8,32,1024]{2,1,0:T(8,128)(2,1)S(1)} async-done(((bf16[8,32,1024]{2,1,0:T(8,128)(2,1)}), bf16[8,32,1024]{2,1,0:T(8,128)(2,1)S(1)}, u32[]{:S(2)}, u32[]{:S(2)}) %all-to-all-start.1) | async-done | bytes 524320 | tf_op jit(solution)/shard_map/all_to_all | solution.py:650
  83.3 0.0 copy-done.4
  83.3 0.0 copy-done.7
  83.4 0.0 copy-done.8
  83.4 0.0 copy-done.9
  83.4 0.0 copy-done.11
  83.4 8.4 %tail.1 = bf16[2,512,256]{2,1,0:T(8,128)(2,1)} custom-call(s32[2]{0:T(128)S(1)} %pad_add_fusion.refs_0_.place_ref, bf16[8,96,256]{2,1,0:T(8,128)(2,1)S(1)} %copy-done.4, f32[16,1,96]{2,1,0:T(1,128)S(1)} %copy-done.11, f32[8,1,96]{2,1,0:T(1,128)S(1)} %copy-done.14, bf16[256,1024]{1,0:T(8,128)(2,1)S(1)} %bitcast.12, bf16[4,1024,512]{2,1,0:T(8,128)(2,1)} %wpool_hbm.1, ...), custom_call_target="tpu_custom_call" | custom-call | flops 4000000000 | bytes 13631488 | tf_op jit(solution)/shard_map/tail/pallas_call | solution.py:674
  (18 shorter events, 0.3 us)
Async XLA Ops:
  1.1 13.1 %collective-permute-start.1 = (bf16[2,2,32,1024]{3,2,1,0:T(8,128)(2,1)S(1)}, bf16[2,2,32,1024]{3,2,1,0:T(8,128)(2,1)S(1)}, u32[]{:S(2)}, u32[]{:S(2)}) collective-permute-start(bf16[2,2,32,1024]{3,2,1,0:T(8,128)(2,1)S(1)} %get-tuple-element.33), channel_id=1, source_target_pairs={{8,0},{16,8},{24,16},{32,24},{40,32},{48,40},{56,48},{64,56},{72,6... | collective-permute-start | bytes 786440 | tf_op jit(solution)/shard_map/ppermute | solution.py:532
  3.0 11.3 %collective-permute-start = (bf16[2,2,32,1024]{3,2,1,0:T(8,128)(2,1)S(1)}, bf16[2,2,32,1024]{3,2,1,0:T(8,128)(2,1)S(1)}, u32[]{:S(2)}, u32[]{:S(2)}) collective-permute-start(bf16[2,2,32,1024]{3,2,1,0:T(8,128)(2,1)S(1)} %get-tuple-element.34), channel_id=1, source_target_pairs={{0,8},{8,16},{16,24},{24,32},{32,40},{40,48},{48,56},{56,64},{64,7... | collective-permute-start | bytes 786440 | tf_op jit(solution)/shard_map/ppermute | solution.py:531
  6.8 1.6 %copy-start = (bf16[1024,1024]{1,0:T(8,128)(2,1)S(1)}, bf16[1024,1024]{1,0:T(8,128)(2,1)}, u32[]{:S(2)}) copy-start(bf16[1024,1024]{1,0:T(8,128)(2,1)} %wkv_ref.1) | copy-start | bytes 6291460
  8.4 0.7 copy-start.12
  9.1 12.8 %copy-start.3 = (f32[128,8,48]{2,1,0:T(8,128)S(1)}, f32[128,8,48]{2,1,0:T(8,128)}, u32[]{:S(2)}) copy-start(f32[128,8,48]{2,1,0:T(8,128)} %constant.31.clone.refs_8_) | copy-start | bytes 589828
  14.0 8.0 %copy-start.2 = (bf16[1024,512]{1,0:T(8,128)(2,1)S(1)}, bf16[1024,512]{1,0:T(8,128)(2,1)}, u32[]{:S(2)}) copy-start(bf16[1024,512]{1,0:T(8,128)(2,1)} %refs_6_.1) | copy-start | bytes 3145732
  14.5 14.1 %collective-permute-start.2 = (bf16[2,20,2,1024]{3,1,2,0:T(8,128)(2,1)S(1)}, bf16[2,20,2,1024]{3,1,2,0:T(8,128)(2,1)S(1)}, u32[]{:S(2)}, u32[]{:S(2)}) collective-permute-start(bf16[2,20,2,1024]{3,1,2,0:T(8,128)(2,1)S(1)} %pad_maximum_fusion), channel_id=1, source_target_pairs={{1,0},{2,1},{3,2},{4,3},{5,4},{6,5},{7,6},{9,8},{10,9},{11,10},{12... | collective-permute-start | bytes 491528 | tf_op jit(solution)/shard_map/ppermute | solution.py:538
  15.9 14.1 %collective-permute-start.3 = (bf16[2,20,2,1024]{3,1,2,0:T(8,128)(2,1)S(1)}, bf16[2,20,2,1024]{3,1,2,0:T(8,128)(2,1)S(1)}, u32[]{:S(2)}, u32[]{:S(2)}) collective-permute-start(bf16[2,20,2,1024]{3,1,2,0:T(8,128)(2,1)S(1)} %pad_maximum_fusion.1), channel_id=1, source_target_pairs={{0,1},{1,2},{2,3},{3,4},{4,5},{5,6},{6,7},{8,9},{9,10},{10,11},{11... | collective-permute-start | bytes 491528 | tf_op jit(solution)/shard_map/ppermute | solution.py:537
  21.9 8.6 %copy-start.1 = (bf16[1024,1024]{1,0:T(8,128)(2,1)S(1)}, bf16[1024,1024]{1,0:T(8,128)(2,1)}, u32[]{:S(2)}) copy-start(bf16[1024,1024]{1,0:T(8,128)(2,1)} %wkv_ref.1) | copy-start | bytes 6291460
  22.0 8.6 %copy-start.5 = (bf16[2,16,32,1024]{3,2,1,0:T(8,128)(2,1)S(1)}, bf16[2,16,32,1024]{3,2,1,0:T(8,128)(2,1)}, u32[]{:S(2)}) copy-start(bf16[2,16,32,1024]{3,2,1,0:T(8,128)(2,1)} %param.16) | copy-start | bytes 6291460
  22.0 8.6 %copy-start.13 = (f32[1024]{0:T(1024)S(1)}, f32[1024]{0:T(1024)}, u32[]{:S(2)}) copy-start(f32[1024]{0:T(1024)} %param.17) | copy-start | bytes 12292
  22.0 8.5 %copy-start.15 = (bf16[512,1024]{1,0:T(8,128)(2,1)S(1)}, bf16[512,1024]{1,0:T(8,128)(2,1)}, u32[]{:S(2)}) copy-start(bf16[512,1024]{1,0:T(8,128)(2,1)} %wout_ref.1) | copy-start | bytes 3145732
  30.5 31.4 %copy-start.6 = (bf16[8,48,256]{2,1,0:T(8,128)(2,1)S(1)}, bf16[8,48,256]{2,1,0:T(8,128)(2,1)}, u32[]{:S(2)}) copy-start(bf16[8,48,256]{2,1,0:T(8,128)(2,1)} %constant.33.clone.table_ref) | copy-start | bytes 589828
  30.6 31.4 %copy-start.10 = (bf16[16,32,48]{2,1,0:T(8,128)(2,1)S(1)}, bf16[16,32,48]{2,1,0:T(8,128)(2,1)}, u32[]{:S(2)}) copy-start(bf16[16,32,48]{2,1,0:T(8,128)(2,1)} %constant.32.clone.near_ref) | copy-start | bytes 147460
  37.7 11.0 %collective-permute-start.4 = (bf16[2,32,1024]{2,1,0:T(8,128)(2,1)S(1)}, bf16[2,32,1024]{2,1,0:T(8,128)(2,1)S(1)}, u32[]{:S(2)}, u32[]{:S(2)}) collective-permute-start(bf16[2,32,1024]{2,1,0:T(8,128)(2,1)S(1)} %get-tuple-element.27), channel_id=1, source_target_pairs={{0,8},{8,16},{16,24},{24,32},{32,40},{40,48},{48,56},{56,64},{64,7... | collective-permute-start | bytes 393224 | tf_op jit(solution)/shard_map/ppermute | solution.py:622
  39.8 22.1 %all-to-all-start = ((bf16[16,16,1024]{2,1,0:T(8,128)(2,1)}), bf16[16,16,1024]{2,1,0:T(8,128)(2,1)S(1)}, u32[]{:S(2)}, u32[]{:S(2)}) async-start(bf16[16,16,1024]{2,1,0:T(8,128)(2,1)} %get-tuple-element.25), calls=%async_computation | async-start | bytes 1048576 | tf_op jit(solution)/shard_map/all_to_all | solution.py:624
  46.7 7.8 %collective-permute-start.5 = (bf16[2,32,1024]{2,1,0:T(8,128)(2,1)S(1)}, bf16[2,32,1024]{2,1,0:T(8,128)(2,1)S(1)}, u32[]{:S(2)}, u32[]{:S(2)}) collective-permute-start(bf16[2,32,1024]{2,1,0:T(8,128)(2,1)S(1)} %get-tuple-element.28), channel_id=1, source_target_pairs={{8,0},{16,8},{24,16},{32,24},{40,32},{48,40},{56,48},{64,56},{72,6... | collective-permute-start | bytes 393224 | tf_op jit(solution)/shard_map/ppermute | solution.py:623
  54.5 16.9 %collective-permute-start.6 = (bf16[2,18,1024]{2,1,0:T(8,128)(2,1)S(1)}, bf16[2,18,1024]{2,1,0:T(8,128)(2,1)S(1)}, u32[]{:S(2)}, u32[]{:S(2)}) collective-permute-start(bf16[2,18,1024]{2,1,0:T(8,128)(2,1)S(1)} %pad_maximum_fusion.2), channel_id=1, source_target_pairs={{0,1},{1,2},{2,3},{3,4},{4,5},{5,6},{6,7},{8,9},{9,10},{10,11},{11... | collective-permute-start | bytes 221192 | tf_op jit(solution)/shard_map/ppermute | solution.py:629
  60.6 10.9 %collective-permute-start.7 = (bf16[2,18,1024]{2,1,0:T(8,128)(2,1)S(1)}, bf16[2,18,1024]{2,1,0:T(8,128)(2,1)S(1)}, u32[]{:S(2)}, u32[]{:S(2)}) collective-permute-start(bf16[2,18,1024]{2,1,0:T(8,128)(2,1)S(1)} %pad_maximum_fusion.3), channel_id=1, source_target_pairs={{1,0},{2,1},{3,2},{4,3},{5,4},{6,5},{7,6},{9,8},{10,9},{11,10},{12... | collective-permute-start | bytes 221192 | tf_op jit(solution)/shard_map/ppermute | solution.py:630
  63.6 19.8 %all-to-all-start.1 = ((bf16[8,32,1024]{2,1,0:T(8,128)(2,1)}), bf16[8,32,1024]{2,1,0:T(8,128)(2,1)S(1)}, u32[]{:S(2)}, u32[]{:S(2)}) async-start(bf16[8,32,1024]{2,1,0:T(8,128)(2,1)} %combine.1), calls=%async_computation.1 | async-start | bytes 1048576 | tf_op jit(solution)/shard_map/all_to_all | solution.py:650
  71.5 11.8 %copy-start.4 = (bf16[8,96,256]{2,1,0:T(8,128)(2,1)S(1)}, bf16[8,96,256]{2,1,0:T(8,128)(2,1)}, u32[]{:S(2)}) copy-start(bf16[8,96,256]{2,1,0:T(8,128)(2,1)} %constant.34.clone.table_hbm) | copy-start | bytes 1179652
  71.5 11.8 %copy-start.7 = (bf16[2,64,432]{2,1,0:T(8,128)(2,1)S(1)}, bf16[2,64,432]{2,1,0:T(8,128)(2,1)}, u32[]{:S(2)}) copy-start(bf16[2,64,432]{2,1,0:T(8,128)(2,1)} %constant.39.clone.spread_hbm) | copy-start | bytes 331780
  71.5 11.8 %copy-start.8 = (f32[8,32,64]{2,1,0:T(8,128)S(1)}, f32[8,32,64]{2,1,0:T(8,128)}, u32[]{:S(2)}) copy-start(f32[8,32,64]{2,1,0:T(8,128)} %constant.38.clone.by_col_hbm) | copy-start | bytes 196612
  71.5 11.8 %copy-start.9 = (f32[16,16,64]{2,1,0:T(8,128)S(1)}, f32[16,16,64]{2,1,0:T(8,128)}, u32[]{:S(2)}) copy-start(f32[16,16,64]{2,1,0:T(8,128)} %constant.37.clone.by_row_hbm) | copy-start | bytes 196612
  71.6 11.8 %copy-start.11 = (f32[16,1,96]{2,1,0:T(1,128)S(1)}, f32[16,1,96]{2,1,0:T(1,128)}, u32[]{:S(2)}) copy-start(f32[16,1,96]{2,1,0:T(1,128)} %constant.35.clone.row_scale_hbm) | copy-start | bytes 18436
  71.6 11.8 %copy-start.14 = (f32[8,1,96]{2,1,0:T(1,128)S(1)}, f32[8,1,96]{2,1,0:T(1,128)}, u32[]{:S(2)}) copy-start(f32[8,1,96]{2,1,0:T(1,128)} %constant.36.clone.col_scale_hbm) | copy-start | bytes 9220

commit v11 on v10

--- a/solution.py
+++ b/solution.py
@@ -175,9 +175,13 @@
     return jnp.dot(a, b, preferred_element_type=f32)
 
 
-def project_kernel(tokens_ref, gain_ref, wkv, normed_ref, kv_ref):
+def project_kernel(tokens_ref, gain_ref, wkv, normed_ref, kv_ref, first_ref, last_ref):
     rows, cols, wide = kv_ref.shape[1:]
     s = pl.program_id(0)
+    by_place = tokens_ref[...].astype(f32).reshape(rows, cols, tokens_ref.shape[-1])
+    for k in range(HALO):
+        first_ref[s, k] = by_place[:, k].astype(bf16)
+        last_ref[s, k] = by_place[:, cols - HALO + k].astype(bf16)
     normed = layer_norm(tokens_ref[...], gain_ref[...])
     normed_ref[s] = normed
     kv_ref[s] = dot(normed, wkv[...]).astype(bf16).astype(f32).reshape(rows, cols, wide)
@@ -429,7 +433,7 @@
     for k in range(count):
         lines = slice(width + k * ppm, width + (k + 1) * ppm)
         large.append(pltpu.make_async_copy(wjoin_hbm.at[:, :, lines, :], wjoin.at[k], sems.at[1, count + k]))
-    ahead = 5
+    ahead = len(large)
     for copy in small + large[:ahead]:
         copy.start()
 
@@ -528,14 +532,11 @@
     at = jnp.stack([r, c]).astype(jnp.int32)
     row_fwd, row_bwd = shifts("row")
     col_fwd, col_bwd = shifts("col")
-    above = lax.ppermute(tokens[:, rows - HALO :], "row", row_fwd)
-    below = lax.ppermute(tokens[:, :HALO], "row", row_bwd)
-
-    def edges(first):
-        return jnp.concatenate([x[:, :, first : first + HALO] for x in (above, tokens, below)], axis=1)
-
-    west = lax.ppermute(edges(cols - HALO), "col", col_fwd)
-    east = lax.ppermute(edges(0), "col", col_bwd)
+    edge = HALO * cols
+    flat_above = lax.ppermute(tokens[:, rows - HALO :].reshape(sheets, edge, width), "row", row_fwd)
+    flat_below = lax.ppermute(tokens[:, :HALO].reshape(sheets, edge, width), "row", row_bwd)
+    above = flat_above.reshape(sheets, HALO, cols, width)
+    below = flat_below.reshape(sheets, HALO, cols, width)
 
     def per_sheet(*dims):
         return pl.BlockSpec((None,) + dims, lambda s, *_: (s,) + (0,) * len(dims))
@@ -544,22 +545,32 @@
     far = pl.BlockSpec(memory_space=pl.ANY)
     wq_near, wkv_near = in_vmem(w_query), in_vmem(w_kv)
     flat = in_vmem(tokens.reshape(sheets, area, width))
-    edge = HALO * cols
     blocks = (rows // BLOCK) * (cols // BLOCK)
     keys = (BLOCK + 2 * HALO) ** 2
     stage = [pltpu.VMEM((2, inner // 128, keys, 256), f32), pltpu.VMEM((2, inner // 128, keys, 256), bf16)]
     gain = in_vmem(gain)
-    normed, kv = pl.pallas_call(
+    normed, kv, first_cols, last_cols = pl.pallas_call(
         project_kernel,
         grid=(sheets,),
         in_specs=[per_sheet(area, width), near, near],
-        out_specs=[near] * 2,
-        out_shape=[pltpu.VMEM((sheets, area, width), bf16), pltpu.VMEM((sheets, rows, cols, wide), f32)],
+        out_specs=[near] * 4,
+        out_shape=[
+            pltpu.VMEM((sheets, area, width), bf16), pltpu.VMEM((sheets, rows, cols, wide), f32),
+            pltpu.VMEM((sheets, HALO, rows, width), bf16), pltpu.VMEM((sheets, HALO, rows, width), bf16),
+        ],
         compiler_params=params(16),
         cost_estimate=cost(2 * sheets * area * width * wide, 2 * (width * (inner + wide) + 5 * sheets * area * width)),
         name="project",
     )(in_hbm(tokens.reshape(sheets, area, width)), gain, wkv_near)
     kv = in_vmem(kv)
+
+    def edges(own, first):
+        own = jnp.swapaxes(own, 1, 2)
+        return jnp.concatenate([above[:, :, first : first + HALO], own, below[:, :, first : first + HALO]], axis=1)
+
+    west = lax.ppermute(edges(last_cols, cols - HALO), "col", col_fwd)
+    east = lax.ppermute(edges(first_cols, 0), "col", col_bwd)
+
     q, halo, bias, pool, middle = pl.pallas_call(
         lambda *refs: middle_kernel((grid_h, grid_w), *refs),
         grid_spec=pltpu.PrefetchScalarGridSpec(
@@ -580,8 +591,8 @@
         cost_estimate=cost(2 * sheets * area * width * wide, 8 * sheets * area * width, sheets * blocks * keys * 512),
         name="middle",
     )(
-        at, in_vmem(normed), kv, in_vmem(above.reshape(sheets, edge, width)),
-        in_vmem(below.reshape(sheets, edge, width)), gain, wq_near, wkv_near, masks,
+        at, in_vmem(normed), kv, in_vmem(flat_above),
+        in_vmem(flat_below), gain, wq_near, wkv_near, masks,
     )
 
     blank = jnp.zeros((sheets, rows + 2 * HALO, BLOCK - 2 * HALO, width), bf16)

time: 92.6 us -> 90.7 us (0.979)
  local copies, waits for them, and re-layouts: 5.49 us -> 4.03 us
  starting transfers between devices: 37.8 us -> 36.4 us
    slice x8 -> x3, local copies, waits for them, and re-layouts: 2.6 us -> 1.13 us  [the longest x1 1.07 us: layer(): tokens[:, :HALO].reshape(sheets, edge, width)]
    all_to_all x1, starting transfers between devices: 6.92 us -> 5.58 us  [layer(): lax.all_to_all(sums, 'row', 0, 0, tiled=True)]
    unnamed x34 -> x36, local copies, waits for them, and re-layouts: 2.41 us -> 2.42 us
  transfers between devices with their start and end apart: 10 -> 10, of which waited for: 3 -> 4; matrix products, arithmetic and copies ran while one was open for 2% -> 1% of each run, Pallas kernels for 24% -> 25%
where the time goes in v11:
time: 90.7 us; the launch traced here: 90.1 us
  Pallas kernels  37.9 us (42%)
  starting transfers between devices  36.4 us (40%)
  waiting for transfers between devices  10.5 us (12%)
  local copies, waits for them, and re-layouts  4.03 us (4%)
    pallas_call x1, Pallas kernels, layer(): pl.pallas_call(conv_kernel, grid=(sheets, 3), in_specs=[per_sheet(area, w...  9.09 us
    pallas_call x1, Pallas kernels, layer(): pl.pallas_call(tail_kernel, grid_spec=pltpu.PrefetchScalarGridSpec(num_sc...  8.18 us
    all_to_all x1, starting transfers between devices, layer(): lax.all_to_all(strips, 'col', 0, 0, tiled=True)  7.88 us
    pallas_call x1, Pallas kernels, layer(): pl.pallas_call(attend_kernel, grid=(sheets,), in_specs=[near] * 10 + [fix...  7.15 us
    pallas_call x1, Pallas kernels, layer(): pl.pallas_call(lambda *refs: middle_kernel((grid_h, grid_w), *refs), grid...  6.56 us
    ppermute x1, starting transfers between devices, layer(): att_west = lax.ppermute(att_edges(last_col, cols - 1), 'col', col_fwd)  5.75 us
    ppermute x1, waiting for transfers between devices, layer(): att_below = lax.ppermute(first_row, 'row', row_bwd)  5.71 us
    all_to_all x1, starting transfers between devices, layer(): lax.all_to_all(sums, 'row', 0, 0, tiled=True)  5.58 us
  transfers between devices with their start and end apart: 10, of which 4 were waited for; matrix products, arithmetic and copies ran while one was open for 1% of the time, Pallas kernels for 25%

profile of v11, /device:TPU:32, one launch (start us, length us, event | category | flops | bytes accessed | tf_op | source)
XLA Modules:
  0.0 90.1 jit_solution(14767383786155135780)
XLA Ops:
  0.0 1.1 %fusion = (bf16[2,2,32,1024]{3,2,1,0:T(8,128)(2,1)S(1)}, bf16[2,2,32,1024]{3,2,1,0:T(8,128)(2,1)S(1)}) fusion(bf16[2,16,32,1024]{3,2,1,0:T(8,128)(2,1)} %param.16), kind=kLoop, calls=%fused_computation.6 | loop fusion | bytes 1048576 | tf_op jit(solution)/shard_map/slice | solution.py:537
  1.1 1.9 %collective-permute-start = (bf16[2,64,1024]{2,1,0:T(8,128)(2,1)S(1)}, bf16[2,64,1024]{2,1,0:T(8,128)(2,1)S(1)}, u32[]{:S(2)}, u32[]{:S(2)}) collective-permute-start(bf16[2,64,1024]{2,1,0:T(8,128)(2,1)S(1)} %bitcast.27), channel_id=1, source_target_pairs={{0,8},{8,16},{16,24},{24,32},{32,40},{40,48},{48,56},{56,64},{64,7... | collective-permute-start | bytes 786440 | tf_op jit(solution)/shard_map/ppermute | solution.py:536
  3.0 3.6 %collective-permute-start.1 = (bf16[2,64,1024]{2,1,0:T(8,128)(2,1)S(1)}, bf16[2,64,1024]{2,1,0:T(8,128)(2,1)S(1)}, u32[]{:S(2)}, u32[]{:S(2)}) collective-permute-start(bf16[2,64,1024]{2,1,0:T(8,128)(2,1)S(1)} %bitcast.26), channel_id=1, source_target_pairs={{8,0},{16,8},{24,16},{32,24},{40,32},{48,40},{56,48},{64,56},{72,6... | collective-permute-start | bytes 786440 | tf_op jit(solution)/shard_map/ppermute | solution.py:537
  6.7 0.0 copy-start
  6.7 1.6 %copy-done = bf16[1024,1024]{1,0:T(8,128)(2,1)S(1)} copy-done((bf16[1024,1024]{1,0:T(8,128)(2,1)S(1)}, bf16[1024,1024]{1,0:T(8,128)(2,1)}, u32[]{:S(2)}) %copy-start) | copy-done | bytes 2097176
  8.3 0.0 copy-start.12
  8.3 0.7 copy-done.12
  9.0 5.3 %project.1 = (bf16[2,512,1024]{2,1,0:T(8,128)(2,1)S(1)}, f32[2,16,32,1024]{3,2,1,0:T(8,128)S(1)}, bf16[2,2,16,1024]{3,2,1,0:T(8,128)(2,1)S(1)}, bf16[2,2,16,1024]{3,2,1,0:T(8,128)(2,1)S(1)}) custom-call(bf16[2,512,1024]{2,1,0:T(8,128)(2,1)} %bitcast.19, f32[1,1024]{1,0:T(1,128)S(1)} %bitcast.23, bf16[1024,1024]{1,0:T(8,128)(2,1)S(1)} %copy-done), custom_call_target="tpu_custom_call" | custom-call | flops 2147483648 | bytes 13631488 | tf_op jit(solution)/shard_map/project/pallas_call | solution.py:552
  14.2 0.1 pad_add_fusion.refs_0_.place_ref
  14.3 0.1 pad.16.clone
  14.4 0.0 collective-permute-done.refs_3_
  14.5 0.0 collective-permute-done.1.refs_4_
  14.6 0.1 pad_maximum_fusion.1
  14.7 5.1 %collective-permute-start.3 = (bf16[2,20,2,1024]{3,1,2,0:T(8,128)(2,1)S(1)}, bf16[2,20,2,1024]{3,1,2,0:T(8,128)(2,1)S(1)}, u32[]{:S(2)}, u32[]{:S(2)}) collective-permute-start(bf16[2,20,2,1024]{3,1,2,0:T(8,128)(2,1)S(1)} %pad_maximum_fusion.1), channel_id=1, source_target_pairs={{0,1},{1,2},{2,3},{3,4},{4,5},{5,6},{6,7},{8,9},{9,10},{10,11},{11... | collective-permute-start | bytes 491528 | tf_op jit(solution)/shard_map/ppermute | solution.py:571
  19.8 0.1 pad_maximum_fusion
  19.9 1.3 %collective-permute-start.2 = (bf16[2,20,2,1024]{3,1,2,0:T(8,128)(2,1)S(1)}, bf16[2,20,2,1024]{3,1,2,0:T(8,128)(2,1)S(1)}, u32[]{:S(2)}, u32[]{:S(2)}) collective-permute-start(bf16[2,20,2,1024]{3,1,2,0:T(8,128)(2,1)S(1)} %pad_maximum_fusion), channel_id=1, source_target_pairs={{1,0},{2,1},{3,2},{4,3},{5,4},{6,5},{7,6},{9,8},{10,9},{11,10},{12... | collective-permute-start | bytes 491528 | tf_op jit(solution)/shard_map/ppermute | solution.py:572
  21.2 0.0 copy-done.2
  21.2 0.0 copy-done.3
  21.2 0.0 copy-start.1
  21.2 0.0 copy-start.10
  21.2 0.0 copy-start.13
  21.2 0.0 copy-start.15
  21.2 6.6 %middle.1 = (f32[2,16,32,512]{3,2,1,0:T(8,128)S(1)}, f32[2,4,32,1024]{3,2,1,0:T(8,128)S(1)}, f32[2,4,144,128]{3,2,1,0:T(8,128)S(1)}, bf16[8,512]{1,0:T(8,128)(2,1)S(1)}, f32[2,16,16,512]{3,2,1,0:T(8,128)S(1)}) custom-call(s32[2]{0:T(128)S(1)} %pad_add_fusion.refs_0_.place_ref, bf16[2,512,1024]{2,1,0:T(8,128)(2,1)S(1)} %get-tuple-element.20.refs_1_, ...), custom_call_target="tpu_custom_call" | custom-call | flops 2147483648 | bytes 8388608 | tf_op jit(solution)/shard_map/middle/pallas_call | solution.py:574
  27.8 0.8 collective-permute-done.3
  28.6 0.2 copy.22
  28.8 1.3 %collective-permute-done.2 = bf16[2,20,2,1024]{3,1,2,0:T(8,128)(2,1)S(1)} collective-permute-done((bf16[2,20,2,1024]{3,1,2,0:T(8,128)(2,1)S(1)}, bf16[2,20,2,1024]{3,1,2,0:T(8,128)(2,1)S(1)}, u32[]{:S(2)}, u32[]{:S(2)}) %collective-permute-start.2) | collective-permute-done | bytes 163872 | tf_op jit(solution)/shard_map/ppermute | solution.py:572
  30.1 0.2 copy.21
  30.3 0.4 maximum_bitcast_fusion.sides_ref
  30.7 0.0 copy-done.1
  30.7 0.0 copy-done.10
  30.7 0.0 copy-done.13
  30.7 0.0 copy-done.15
  30.7 0.0 copy-start.5
  30.7 0.0 copy-start.9
  30.7 7.1 %attend.1 = (bf16[2,512,1024]{2,1,0:T(8,128)(2,1)}, bf16[16,16,1024]{2,1,0:T(8,128)(2,1)}, bf16[2,32,1024]{2,1,0:T(8,128)(2,1)S(1)}, bf16[2,32,1024]{2,1,0:T(8,1...) custom-call(f32[2,16,32,512]{3,2,1,0:T(8,128)S(1)} %get-tuple-element.22.q_ref, ...), custom_call_target="tpu_custom_call" | custom-call | flops 4294967296 | bytes 8388608 | tf_op jit(solution)/shard_map/attend/pallas_call | solution.py:604
  37.9 1.9 %collective-permute-start.4 = (bf16[2,32,1024]{2,1,0:T(8,128)(2,1)S(1)}, bf16[2,32,1024]{2,1,0:T(8,128)(2,1)S(1)}, u32[]{:S(2)}, u32[]{:S(2)}) collective-permute-start(bf16[2,32,1024]{2,1,0:T(8,128)(2,1)S(1)} %get-tuple-element.31), channel_id=1, source_target_pairs={{0,8},{8,16},{16,24},{24,32},{32,40},{40,48},{48,56},{56,64},{64,7... | collective-permute-start | bytes 393224 | tf_op jit(solution)/shard_map/ppermute | solution.py:633
  39.8 5.6 %all-to-all-start = ((bf16[16,16,1024]{2,1,0:T(8,128)(2,1)}), bf16[16,16,1024]{2,1,0:T(8,128)(2,1)S(1)}, u32[]{:S(2)}, u32[]{:S(2)}) async-start(bf16[16,16,1024]{2,1,0:T(8,128)(2,1)} %get-tuple-element.29), calls=%async_computation | async-start | bytes 1048576 | tf_op jit(solution)/shard_map/all_to_all | solution.py:635
  45.4 2.0 %collective-permute-start.5 = (bf16[2,32,1024]{2,1,0:T(8,128)(2,1)S(1)}, bf16[2,32,1024]{2,1,0:T(8,128)(2,1)S(1)}, u32[]{:S(2)}, u32[]{:S(2)}) collective-permute-start(bf16[2,32,1024]{2,1,0:T(8,128)(2,1)S(1)} %get-tuple-element.32), channel_id=1, source_target_pairs={{8,0},{16,8},{24,16},{32,24},{40,32},{48,40},{56,48},{64,56},{72,6... | collective-permute-start | bytes 393224 | tf_op jit(solution)/shard_map/ppermute | solution.py:634
  47.4 0.0 collective-permute-done.4.top_ref
  47.4 5.7 %collective-permute-done.5.bottom_ref = bf16[2,32,1024]{2,1,0:T(8,128)(2,1)S(1)} collective-permute-done((bf16[2,32,1024]{2,1,0:T(8,128)(2,1)S(1)}, bf16[2,32,1024]{2,1,0:T(8,128)(2,1)S(1)}, u32[]{:S(2)}, u32[]{:S(2)}) %collective-permute-start.5) | collective-permute-done | bytes 131104 | tf_op jit(solution)/shard_map/ppermute | solution.py:634
  53.2 5.7 %collective-permute-start.6 = (bf16[2,18,1024]{2,1,0:T(8,128)(2,1)S(1)}, bf16[2,18,1024]{2,1,0:T(8,128)(2,1)S(1)}, u32[]{:S(2)}, u32[]{:S(2)}) collective-permute-start(bf16[2,18,1024]{2,1,0:T(8,128)(2,1)S(1)} %pad_maximum_fusion.2), channel_id=1, source_target_pairs={{0,1},{1,2},{2,3},{3,4},{4,5},{5,6},{6,7},{8,9},{9,10},{10,11},{11... | collective-permute-start | bytes 221192 | tf_op jit(solution)/shard_map/ppermute | solution.py:640
  59.0 1.3 %collective-permute-start.7 = (bf16[2,18,1024]{2,1,0:T(8,128)(2,1)S(1)}, bf16[2,18,1024]{2,1,0:T(8,128)(2,1)S(1)}, u32[]{:S(2)}, u32[]{:S(2)}) collective-permute-start(bf16[2,18,1024]{2,1,0:T(8,128)(2,1)S(1)} %pad_maximum_fusion.3), channel_id=1, source_target_pairs={{1,0},{2,1},{3,2},{4,3},{5,4},{6,5},{7,6},{9,8},{10,9},{11,10},{12... | collective-permute-start | bytes 221192 | tf_op jit(solution)/shard_map/ppermute | solution.py:641
  60.3 0.0 all-to-all-done
  60.3 0.0 copy-done.5
  60.3 0.0 copy-done.9
  60.3 1.6 %combine.1 = bf16[8,32,1024]{2,1,0:T(8,128)(2,1)} custom-call(s32[2]{0:T(128)S(1)} %pad_add_fusion.refs_0_.place_ref, bf16[16,32,48]{2,1,0:T(8,128)(2,1)S(1)} %copy-done.9, bf16[8,48,256]{2,1,0:T(8,128)(2,1)S(1)} %copy-done.5, bf16[256,1024]{1,0:T(8,128)(2,1)S(1)} %bitcast.15), custom_call_target="tpu_custom_call" | custom-call | tf_op jit(solution)/shard_map/combine/pallas_call | solution.py:645
  62.0 7.9 %all-to-all-start.1 = ((bf16[8,32,1024]{2,1,0:T(8,128)(2,1)}), bf16[8,32,1024]{2,1,0:T(8,128)(2,1)S(1)}, u32[]{:S(2)}, u32[]{:S(2)}) async-start(bf16[8,32,1024]{2,1,0:T(8,128)(2,1)} %combine.1), calls=%async_computation.1 | async-start | bytes 1048576 | tf_op jit(solution)/shard_map/all_to_all | solution.py:661
  69.9 0.0 collective-permute-done.6
  69.9 0.0 collective-permute-done.7
  69.9 0.0 copy-start.4
  69.9 0.0 copy-start.6
  69.9 0.0 copy-start.7
  69.9 0.0 copy-start.8
  70.0 0.0 copy-start.11
  70.0 0.0 copy-start.14
  70.0 9.1 %conv.1 = f32[2,512,256]{2,1,0:T(8,128)S(1)} custom-call(bf16[2,512,1024]{2,1,0:T(8,128)(2,1)} %get-tuple-element.30.attended_ref, bf16[2,32,1024]{2,1,0:T(8,128)(2,1)S(1)} %collective-permute-done.4.top_ref, bf16[2,32,1024]{2,1,0:T(8,128)(2,1)S(1)} %collective-permute-done.5.bottom_ref, bf16[2,24,1024]{2,1,0:T(8,128)(2,1)S(1)} %pad.7.left_ref, ...), custom_call_target="tpu_custom_call" | custom-call | flops 4831838208 | bytes 6815744 | tf_op jit(solution)/shard_map/conv/pallas_call | solution.py:663
  79.1 2.7 %all-to-all-done.1 = bf16[8,32,1024]{2,1,0:T(8,128)(2,1)S(1)} async-done(((bf16[8,32,1024]{2,1,0:T(8,128)(2,1)}), bf16[8,32,1024]{2,1,0:T(8,128)(2,1)S(1)}, u32[]{:S(2)}, u32[]{:S(2)}) %all-to-all-start.1) | async-done | bytes 524320 | tf_op jit(solution)/shard_map/all_to_all | solution.py:661
  81.7 0.0 copy-done.4
  81.7 0.0 copy-done.6
  81.7 0.0 copy-done.7
  81.8 0.0 copy-done.8
  81.8 0.0 copy-done.11
  81.8 0.0 copy-done.14
  81.8 8.2 %tail.1 = bf16[2,512,256]{2,1,0:T(8,128)(2,1)} custom-call(s32[2]{0:T(128)S(1)} %pad_add_fusion.refs_0_.place_ref, bf16[8,96,256]{2,1,0:T(8,128)(2,1)S(1)} %copy-done.4, f32[16,1,96]{2,1,0:T(1,128)S(1)} %copy-done.11, f32[8,1,96]{2,1,0:T(1,128)S(1)} %copy-done.14, bf16[256,1024]{1,0:T(8,128)(2,1)S(1)} %bitcast.16, bf16[4,1024,512]{2,1,0:T(8,128)(2,1)} %wpool_hbm.1, ...), custom_call_target="tpu_custom_call" | custom-call | flops 4000000000 | bytes 13631488 | tf_op jit(solution)/shard_map/tail/pallas_call | solution.py:685
  (15 shorter events, 0.3 us)
Async XLA Ops:
  1.1 13.3 %collective-permute-start = (bf16[2,64,1024]{2,1,0:T(8,128)(2,1)S(1)}, bf16[2,64,1024]{2,1,0:T(8,128)(2,1)S(1)}, u32[]{:S(2)}, u32[]{:S(2)}) collective-permute-start(bf16[2,64,1024]{2,1,0:T(8,128)(2,1)S(1)} %bitcast.27), channel_id=1, source_target_pairs={{0,8},{8,16},{16,24},{24,32},{32,40},{40,48},{48,56},{56,64},{64,7... | collective-permute-start | bytes 786440 | tf_op jit(solution)/shard_map/ppermute | solution.py:536
  3.0 11.5 %collective-permute-start.1 = (bf16[2,64,1024]{2,1,0:T(8,128)(2,1)S(1)}, bf16[2,64,1024]{2,1,0:T(8,128)(2,1)S(1)}, u32[]{:S(2)}, u32[]{:S(2)}) collective-permute-start(bf16[2,64,1024]{2,1,0:T(8,128)(2,1)S(1)} %bitcast.26), channel_id=1, source_target_pairs={{8,0},{16,8},{24,16},{32,24},{40,32},{48,40},{56,48},{64,56},{72,6... | collective-permute-start | bytes 786440 | tf_op jit(solution)/shard_map/ppermute | solution.py:537
  6.7 1.6 %copy-start = (bf16[1024,1024]{1,0:T(8,128)(2,1)S(1)}, bf16[1024,1024]{1,0:T(8,128)(2,1)}, u32[]{:S(2)}) copy-start(bf16[1024,1024]{1,0:T(8,128)(2,1)} %wkv_ref.1) | copy-start | bytes 6291460
  8.3 0.7 copy-start.12
  8.9 12.2 %copy-start.2 = (bf16[1024,512]{1,0:T(8,128)(2,1)S(1)}, bf16[1024,512]{1,0:T(8,128)(2,1)}, u32[]{:S(2)}) copy-start(bf16[1024,512]{1,0:T(8,128)(2,1)} %refs_6_.1) | copy-start | bytes 3145732
  8.9 12.2 %copy-start.3 = (f32[128,8,48]{2,1,0:T(8,128)S(1)}, f32[128,8,48]{2,1,0:T(8,128)}, u32[]{:S(2)}) copy-start(f32[128,8,48]{2,1,0:T(8,128)} %constant.31.clone.refs_8_) | copy-start | bytes 589828
  14.7 14.0 %collective-permute-start.3 = (bf16[2,20,2,1024]{3,1,2,0:T(8,128)(2,1)S(1)}, bf16[2,20,2,1024]{3,1,2,0:T(8,128)(2,1)S(1)}, u32[]{:S(2)}, u32[]{:S(2)}) collective-permute-start(bf16[2,20,2,1024]{3,1,2,0:T(8,128)(2,1)S(1)} %pad_maximum_fusion.1), channel_id=1, source_target_pairs={{0,1},{1,2},{2,3},{3,4},{4,5},{5,6},{6,7},{8,9},{9,10},{10,11},{11... | collective-permute-start | bytes 491528 | tf_op jit(solution)/shard_map/ppermute | solution.py:571
  19.9 10.2 %collective-permute-start.2 = (bf16[2,20,2,1024]{3,1,2,0:T(8,128)(2,1)S(1)}, bf16[2,20,2,1024]{3,1,2,0:T(8,128)(2,1)S(1)}, u32[]{:S(2)}, u32[]{:S(2)}) collective-permute-start(bf16[2,20,2,1024]{3,1,2,0:T(8,128)(2,1)S(1)} %pad_maximum_fusion), channel_id=1, source_target_pairs={{1,0},{2,1},{3,2},{4,3},{5,4},{6,5},{7,6},{9,8},{10,9},{11,10},{12... | collective-permute-start | bytes 491528 | tf_op jit(solution)/shard_map/ppermute | solution.py:572
  21.2 9.5 %copy-start.1 = (bf16[1024,1024]{1,0:T(8,128)(2,1)S(1)}, bf16[1024,1024]{1,0:T(8,128)(2,1)}, u32[]{:S(2)}) copy-start(bf16[1024,1024]{1,0:T(8,128)(2,1)} %wkv_ref.1) | copy-start | bytes 6291460
  21.2 9.5 %copy-start.10 = (bf16[2,16,32,1024]{3,2,1,0:T(8,128)(2,1)S(1)}, bf16[2,16,32,1024]{3,2,1,0:T(8,128)(2,1)}, u32[]{:S(2)}) copy-start(bf16[2,16,32,1024]{3,2,1,0:T(8,128)(2,1)} %param.16) | copy-start | bytes 6291460
  21.2 9.5 %copy-start.13 = (f32[1024]{0:T(1024)S(1)}, f32[1024]{0:T(1024)}, u32[]{:S(2)}) copy-start(f32[1024]{0:T(1024)} %param.17) | copy-start | bytes 12292
  21.2 9.5 %copy-start.15 = (bf16[512,1024]{1,0:T(8,128)(2,1)S(1)}, bf16[512,1024]{1,0:T(8,128)(2,1)}, u32[]{:S(2)}) copy-start(bf16[512,1024]{1,0:T(8,128)(2,1)} %wout_ref.1) | copy-start | bytes 3145732
  30.7 29.6 %copy-start.5 = (bf16[8,48,256]{2,1,0:T(8,128)(2,1)S(1)}, bf16[8,48,256]{2,1,0:T(8,128)(2,1)}, u32[]{:S(2)}) copy-start(bf16[8,48,256]{2,1,0:T(8,128)(2,1)} %constant.33.clone.table_ref) | copy-start | bytes 589828
  30.7 29.6 %copy-start.9 = (bf16[16,32,48]{2,1,0:T(8,128)(2,1)S(1)}, bf16[16,32,48]{2,1,0:T(8,128)(2,1)}, u32[]{:S(2)}) copy-start(bf16[16,32,48]{2,1,0:T(8,128)(2,1)} %constant.32.clone.near_ref) | copy-start | bytes 147460
  37.9 9.5 %collective-permute-start.4 = (bf16[2,32,1024]{2,1,0:T(8,128)(2,1)S(1)}, bf16[2,32,1024]{2,1,0:T(8,128)(2,1)S(1)}, u32[]{:S(2)}, u32[]{:S(2)}) collective-permute-start(bf16[2,32,1024]{2,1,0:T(8,128)(2,1)S(1)} %get-tuple-element.31), channel_id=1, source_target_pairs={{0,8},{8,16},{16,24},{24,32},{32,40},{40,48},{48,56},{56,64},{64,7... | collective-permute-start | bytes 393224 | tf_op jit(solution)/shard_map/ppermute | solution.py:633
  39.8 20.5 %all-to-all-start = ((bf16[16,16,1024]{2,1,0:T(8,128)(2,1)}), bf16[16,16,1024]{2,1,0:T(8,128)(2,1)S(1)}, u32[]{:S(2)}, u32[]{:S(2)}) async-start(bf16[16,16,1024]{2,1,0:T(8,128)(2,1)} %get-tuple-element.29), calls=%async_computation | async-start | bytes 1048576 | tf_op jit(solution)/shard_map/all_to_all | solution.py:635
  45.4 7.8 %collective-permute-start.5 = (bf16[2,32,1024]{2,1,0:T(8,128)(2,1)S(1)}, bf16[2,32,1024]{2,1,0:T(8,128)(2,1)S(1)}, u32[]{:S(2)}, u32[]{:S(2)}) collective-permute-start(bf16[2,32,1024]{2,1,0:T(8,128)(2,1)S(1)} %get-tuple-element.32), channel_id=1, source_target_pairs={{8,0},{16,8},{24,16},{32,24},{40,32},{48,40},{56,48},{64,56},{72,6... | collective-permute-start | bytes 393224 | tf_op jit(solution)/shard_map/ppermute | solution.py:634
  53.2 16.7 %collective-permute-start.6 = (bf16[2,18,1024]{2,1,0:T(8,128)(2,1)S(1)}, bf16[2,18,1024]{2,1,0:T(8,128)(2,1)S(1)}, u32[]{:S(2)}, u32[]{:S(2)}) collective-permute-start(bf16[2,18,1024]{2,1,0:T(8,128)(2,1)S(1)} %pad_maximum_fusion.2), channel_id=1, source_target_pairs={{0,1},{1,2},{2,3},{3,4},{4,5},{5,6},{6,7},{8,9},{9,10},{10,11},{11... | collective-permute-start | bytes 221192 | tf_op jit(solution)/shard_map/ppermute | solution.py:640
  59.0 10.9 %collective-permute-start.7 = (bf16[2,18,1024]{2,1,0:T(8,128)(2,1)S(1)}, bf16[2,18,1024]{2,1,0:T(8,128)(2,1)S(1)}, u32[]{:S(2)}, u32[]{:S(2)}) collective-permute-start(bf16[2,18,1024]{2,1,0:T(8,128)(2,1)S(1)} %pad_maximum_fusion.3), channel_id=1, source_target_pairs={{1,0},{2,1},{3,2},{4,3},{5,4},{6,5},{7,6},{9,8},{10,9},{11,10},{12... | collective-permute-start | bytes 221192 | tf_op jit(solution)/shard_map/ppermute | solution.py:641
  62.0 19.8 %all-to-all-start.1 = ((bf16[8,32,1024]{2,1,0:T(8,128)(2,1)}), bf16[8,32,1024]{2,1,0:T(8,128)(2,1)S(1)}, u32[]{:S(2)}, u32[]{:S(2)}) async-start(bf16[8,32,1024]{2,1,0:T(8,128)(2,1)} %combine.1), calls=%async_computation.1 | async-start | bytes 1048576 | tf_op jit(solution)/shard_map/all_to_all | solution.py:661
  69.9 11.8 %copy-start.4 = (bf16[8,96,256]{2,1,0:T(8,128)(2,1)S(1)}, bf16[8,96,256]{2,1,0:T(8,128)(2,1)}, u32[]{:S(2)}) copy-start(bf16[8,96,256]{2,1,0:T(8,128)(2,1)} %constant.34.clone.table_hbm) | copy-start | bytes 1179652
  69.9 11.8 %copy-start.6 = (bf16[2,64,432]{2,1,0:T(8,128)(2,1)S(1)}, bf16[2,64,432]{2,1,0:T(8,128)(2,1)}, u32[]{:S(2)}) copy-start(bf16[2,64,432]{2,1,0:T(8,128)(2,1)} %constant.39.clone.spread_hbm) | copy-start | bytes 331780
  69.9 11.8 %copy-start.7 = (f32[8,32,64]{2,1,0:T(8,128)S(1)}, f32[8,32,64]{2,1,0:T(8,128)}, u32[]{:S(2)}) copy-start(f32[8,32,64]{2,1,0:T(8,128)} %constant.38.clone.by_col_hbm) | copy-start | bytes 196612
  69.9 11.8 %copy-start.8 = (f32[16,16,64]{2,1,0:T(8,128)S(1)}, f32[16,16,64]{2,1,0:T(8,128)}, u32[]{:S(2)}) copy-start(f32[16,16,64]{2,1,0:T(8,128)} %constant.37.clone.by_row_hbm) | copy-start | bytes 196612
  70.0 11.8 %copy-start.11 = (f32[16,1,96]{2,1,0:T(1,128)S(1)}, f32[16,1,96]{2,1,0:T(1,128)}, u32[]{:S(2)}) copy-start(f32[16,1,96]{2,1,0:T(1,128)} %constant.35.clone.row_scale_hbm) | copy-start | bytes 18436
  70.0 11.8 %copy-start.14 = (f32[8,1,96]{2,1,0:T(1,128)S(1)}, f32[8,1,96]{2,1,0:T(1,128)}, u32[]{:S(2)}) copy-start(f32[8,1,96]{2,1,0:T(1,128)} %constant.36.clone.col_scale_hbm) | copy-start | bytes 9220

commit v12 on v11

--- a/solution.py
+++ b/solution.py
@@ -175,16 +175,43 @@
     return jnp.dot(a, b, preferred_element_type=f32)
 
 
-def project_kernel(tokens_ref, gain_ref, wkv, normed_ref, kv_ref, first_ref, last_ref):
+def project_kernel(
+    tokens_hbm, gain_hbm, wkv_hbm, normed_ref, kv_ref, first_ref, last_ref, tokens_ref, gain_ref, wkv_ref, sems,
+):
     rows, cols, wide = kv_ref.shape[1:]
     s = pl.program_id(0)
-    by_place = tokens_ref[...].astype(f32).reshape(rows, cols, tokens_ref.shape[-1])
+    sheets = tokens_ref.shape[0]
+    gain_copy = pltpu.make_async_copy(gain_hbm, gain_ref, sems.at[sheets])
+    wkv_copy = pltpu.make_async_copy(wkv_hbm, wkv_ref, sems.at[sheets + 1])
+    token_copies = [pltpu.make_async_copy(tokens_hbm.at[k], tokens_ref.at[k], sems.at[k]) for k in range(sheets)]
+
+    @pl.when(s == 0)
+    def _():
+        gain_copy.start()
+        token_copies[0].start()
+        wkv_copy.start()
+        for copy in token_copies[1:]:
+            copy.start()
+        gain_copy.wait()
+
+    for k, copy in enumerate(token_copies):
+
+        @pl.when(s == k)
+        def _():
+            copy.wait()
+
+    by_place = tokens_ref[s].astype(f32).reshape(rows, cols, tokens_ref.shape[-1])
     for k in range(HALO):
         first_ref[s, k] = by_place[:, k].astype(bf16)
         last_ref[s, k] = by_place[:, cols - HALO + k].astype(bf16)
-    normed = layer_norm(tokens_ref[...], gain_ref[...])
+    normed = layer_norm(tokens_ref[s], gain_ref[...])
     normed_ref[s] = normed
-    kv_ref[s] = dot(normed, wkv[...]).astype(bf16).astype(f32).reshape(rows, cols, wide)
+
+    @pl.when(s == 0)
+    def _():
+        wkv_copy.wait()
+
+    kv_ref[s] = dot(normed_ref[s], wkv_ref[...]).astype(bf16).astype(f32).reshape(rows, cols, wide)
 
 
 def pool_members(masks_ref, pool, cols):
@@ -543,26 +570,26 @@
 
     near = pl.BlockSpec(memory_space=pltpu.VMEM)
     far = pl.BlockSpec(memory_space=pl.ANY)
-    wq_near, wkv_near = in_vmem(w_query), in_vmem(w_kv)
-    flat = in_vmem(tokens.reshape(sheets, area, width))
+    wq_near = in_vmem(w_query)
     blocks = (rows // BLOCK) * (cols // BLOCK)
     keys = (BLOCK + 2 * HALO) ** 2
     stage = [pltpu.VMEM((2, inner // 128, keys, 256), f32), pltpu.VMEM((2, inner // 128, keys, 256), bf16)]
-    gain = in_vmem(gain)
-    normed, kv, first_cols, last_cols = pl.pallas_call(
+    normed, kv, first_cols, last_cols, flat, gain, wkv_near = pl.pallas_call(
         project_kernel,
         grid=(sheets,),
-        in_specs=[per_sheet(area, width), near, near],
-        out_specs=[near] * 4,
+        in_specs=[far] * 3,
+        out_specs=[near] * 7,
         out_shape=[
             pltpu.VMEM((sheets, area, width), bf16), pltpu.VMEM((sheets, rows, cols, wide), f32),
             pltpu.VMEM((sheets, HALO, rows, width), bf16), pltpu.VMEM((sheets, HALO, rows, width), bf16),
+            pltpu.VMEM((sheets, area, width), bf16), pltpu.VMEM((1, width), f32), pltpu.VMEM((width, wide), bf16),
         ],
+        scratch_shapes=[pltpu.SemaphoreType.DMA((sheets + 2,))],
         compiler_params=params(16),
         cost_estimate=cost(2 * sheets * area * width * wide, 2 * (width * (inner + wide) + 5 * sheets * area * width)),
         name="project",
-    )(in_hbm(tokens.reshape(sheets, area, width)), gain, wkv_near)
-    kv = in_vmem(kv)
+    )(in_hbm(tokens.reshape(sheets, area, width)), in_hbm(gain), in_hbm(w_kv))
+    kv, flat, gain, wkv_near = in_vmem(kv), in_vmem(flat), in_vmem(gain), in_vmem(wkv_near)
 
     def edges(own, first):
         own = jnp.swapaxes(own, 1, 2)

time: 90.7 us -> 88.7 us (0.978)
  local copies, waits for them, and re-layouts: 4.03 us -> 1.74 us
    unnamed x36 -> x26, local copies, waits for them, and re-layouts: 2.42 us -> 0.13 us
    ppermute x1, starting transfers between devices: 5.75 us -> 4.75 us  [layer(): att_west = lax.ppermute(att_edges(last_col, cols - 1), 'col', col_fwd)]
    all_to_all x1, starting transfers between devices: 5.58 us -> 6.5 us  [layer(): lax.all_to_all(sums, 'row', 0, 0, tiled=True)]
  transfers between devices with their start and end apart: 10 -> 10, of which waited for: 4 -> 4; matrix products, arithmetic and copies ran while one was open for 1% -> 1% of each run, Pallas kernels for 25% -> 26%
where the time goes in v12:
time: 88.7 us; the launch traced here: 88.1 us
  Pallas kernels  38.3 us (43%)
  starting transfers between devices  36.3 us (41%)
  waiting for transfers between devices  10.6 us (12%)
  local copies, waits for them, and re-layouts  1.74 us (2%)
    pallas_call x1, Pallas kernels, layer(): pl.pallas_call(conv_kernel, grid=(sheets, 3), in_specs=[per_sheet(area, w...  9.09 us
    pallas_call x1, Pallas kernels, layer(): pl.pallas_call(tail_kernel, grid_spec=pltpu.PrefetchScalarGridSpec(num_sc...  8.18 us
    all_to_all x1, starting transfers between devices, layer(): lax.all_to_all(strips, 'col', 0, 0, tiled=True)  7.85 us
    pallas_call x1, Pallas kernels, layer(): pl.pallas_call(attend_kernel, grid=(sheets,), in_specs=[near] * 10 + [fix...  7.13 us
    pallas_call x1, Pallas kernels, layer(): pl.pallas_call(lambda *refs: middle_kernel((grid_h, grid_w), *refs), grid...  6.53 us
    all_to_all x1, starting transfers between devices, layer(): lax.all_to_all(sums, 'row', 0, 0, tiled=True)  6.5 us
    ppermute x1, waiting for transfers between devices, layer(): att_below = lax.ppermute(first_row, 'row', row_bwd)  5.71 us
    pallas_call x1, Pallas kernels, layer(): pl.pallas_call(project_kernel, grid=(sheets,), in_specs=[far] * 3, out_sp...  5.7 us
  transfers between devices with their start and end apart: 10, of which 4 were waited for; matrix products, arithmetic and copies ran while one was open for 1% of the time, Pallas kernels for 26%

profile of v12, /device:TPU:32, one launch (start us, length us, event | category | flops | bytes accessed | tf_op | source)
XLA Modules:
  0.0 88.1 jit_solution(3767715368065744977)
XLA Ops:
  0.0 1.1 %fusion = (bf16[2,2,32,1024]{3,2,1,0:T(8,128)(2,1)S(1)}, bf16[2,2,32,1024]{3,2,1,0:T(8,128)(2,1)S(1)}) fusion(bf16[2,16,32,1024]{3,2,1,0:T(8,128)(2,1)} %param.16), kind=kLoop, calls=%fused_computation.6 | loop fusion | bytes 1048576 | tf_op jit(solution)/shard_map/slice | solution.py:564
  1.1 1.9 %collective-permute-start = (bf16[2,64,1024]{2,1,0:T(8,128)(2,1)S(1)}, bf16[2,64,1024]{2,1,0:T(8,128)(2,1)S(1)}, u32[]{:S(2)}, u32[]{:S(2)}) collective-permute-start(bf16[2,64,1024]{2,1,0:T(8,128)(2,1)S(1)} %bitcast.22), channel_id=1, source_target_pairs={{0,8},{8,16},{16,24},{24,32},{32,40},{40,48},{48,56},{56,64},{64,7... | collective-permute-start | bytes 786440 | tf_op jit(solution)/shard_map/ppermute | solution.py:563
  3.0 3.6 %collective-permute-start.1 = (bf16[2,64,1024]{2,1,0:T(8,128)(2,1)S(1)}, bf16[2,64,1024]{2,1,0:T(8,128)(2,1)S(1)}, u32[]{:S(2)}, u32[]{:S(2)}) collective-permute-start(bf16[2,64,1024]{2,1,0:T(8,128)(2,1)S(1)} %bitcast.21), channel_id=1, source_target_pairs={{8,0},{16,8},{24,16},{32,24},{40,32},{48,40},{56,48},{64,56},{72,6... | collective-permute-start | bytes 786440 | tf_op jit(solution)/shard_map/ppermute | solution.py:564
  6.7 0.0 copy-start
  6.7 0.0 copy-start.1
  6.7 5.7 %project.1 = (bf16[2,512,1024]{2,1,0:T(8,128)(2,1)S(1)}, f32[2,16,32,1024]{3,2,1,0:T(8,128)S(1)}, bf16[2,2,16,1024]{3,2,1,0:T(8,128)(2,1)S(1)}, bf16[2,2,16,1024...) custom-call(bf16[2,512,1024]{2,1,0:T(8,128)(2,1)} %bitcast.23, ...), custom_call_target="tpu_custom_call" | custom-call | flops 2147483648 | bytes 13631488 | tf_op jit(solution)/shard_map/project/pallas_call | solution.py:577
  12.4 0.1 pad_add_fusion.refs_0_.place_ref
  12.5 0.1 pad.16.clone
  12.6 0.0 collective-permute-done.refs_3_
  12.6 0.0 collective-permute-done.1.refs_4_
  12.7 0.1 pad_maximum_fusion.1
  12.8 5.1 %collective-permute-start.3 = (bf16[2,20,2,1024]{3,1,2,0:T(8,128)(2,1)S(1)}, bf16[2,20,2,1024]{3,1,2,0:T(8,128)(2,1)S(1)}, u32[]{:S(2)}, u32[]{:S(2)}) collective-permute-start(bf16[2,20,2,1024]{3,1,2,0:T(8,128)(2,1)S(1)} %pad_maximum_fusion.1), channel_id=1, source_target_pairs={{0,1},{1,2},{2,3},{3,4},{4,5},{5,6},{6,7},{8,9},{9,10},{10,11},{11... | collective-permute-start | bytes 491528 | tf_op jit(solution)/shard_map/ppermute | solution.py:598
  17.9 0.1 pad_maximum_fusion
  18.0 1.3 %collective-permute-start.2 = (bf16[2,20,2,1024]{3,1,2,0:T(8,128)(2,1)S(1)}, bf16[2,20,2,1024]{3,1,2,0:T(8,128)(2,1)S(1)}, u32[]{:S(2)}, u32[]{:S(2)}) collective-permute-start(bf16[2,20,2,1024]{3,1,2,0:T(8,128)(2,1)S(1)} %pad_maximum_fusion), channel_id=1, source_target_pairs={{1,0},{2,1},{3,2},{4,3},{5,4},{6,5},{7,6},{9,8},{10,9},{11,10},{12... | collective-permute-start | bytes 491528 | tf_op jit(solution)/shard_map/ppermute | solution.py:599
  19.3 0.0 copy-done
  19.3 0.0 copy-done.1
  19.3 0.0 copy-start.10
  19.4 6.5 %middle.1 = (f32[2,16,32,512]{3,2,1,0:T(8,128)S(1)}, f32[2,4,32,1024]{3,2,1,0:T(8,128)S(1)}, f32[2,4,144,128]{3,2,1,0:T(8,128)S(1)}, bf16[8,512]{1,0:T(8,128)(2,1)S(1)}, f32[2,16,16,512]{3,2,1,0:T(8,128)S(1)}) custom-call(s32[2]{0:T(128)S(1)} %pad_add_fusion.refs_0_.place_ref, bf16[2,512,1024]{2,1,0:T(8,128)(2,1)S(1)} %get-tuple-element.23.refs_1_, ...), custom_call_target="tpu_custom_call" | custom-call | flops 2147483648 | bytes 8388608 | tf_op jit(solution)/shard_map/middle/pallas_call | solution.py:601
  25.9 0.9 %collective-permute-done.3 = bf16[2,20,2,1024]{3,1,2,0:T(8,128)(2,1)S(1)} collective-permute-done((bf16[2,20,2,1024]{3,1,2,0:T(8,128)(2,1)S(1)}, bf16[2,20,2,1024]{3,1,2,0:T(8,128)(2,1)S(1)}, u32[]{:S(2)}, u32[]{:S(2)}) %collective-permute-start.3) | collective-permute-done | bytes 163872 | tf_op jit(solution)/shard_map/ppermute | solution.py:598
  26.8 0.2 copy.22
  26.9 1.3 %collective-permute-done.2 = bf16[2,20,2,1024]{3,1,2,0:T(8,128)(2,1)S(1)} collective-permute-done((bf16[2,20,2,1024]{3,1,2,0:T(8,128)(2,1)S(1)}, bf16[2,20,2,1024]{3,1,2,0:T(8,128)(2,1)S(1)}, u32[]{:S(2)}, u32[]{:S(2)}) %collective-permute-start.2) | collective-permute-done | bytes 163872 | tf_op jit(solution)/shard_map/ppermute | solution.py:599
  28.2 0.2 copy.21
  28.4 0.4 maximum_bitcast_fusion.sides_ref
  28.8 0.0 copy-done.10
  28.8 0.0 copy-start.3
  28.8 0.0 copy-start.7
  28.8 7.1 %attend.1 = (bf16[2,512,1024]{2,1,0:T(8,128)(2,1)}, bf16[16,16,1024]{2,1,0:T(8,128)(2,1)}, bf16[2,32,1024]{2,1,0:T(8,128)(2,1)S(1)}, bf16[2,32,1024]{2,1,0:T(8,1...) custom-call(f32[2,16,32,512]{3,2,1,0:T(8,128)S(1)} %get-tuple-element.27.q_ref, ...), custom_call_target="tpu_custom_call" | custom-call | flops 4294967296 | bytes 8388608 | tf_op jit(solution)/shard_map/attend/pallas_call | solution.py:631
  36.0 1.9 %collective-permute-start.4 = (bf16[2,32,1024]{2,1,0:T(8,128)(2,1)S(1)}, bf16[2,32,1024]{2,1,0:T(8,128)(2,1)S(1)}, u32[]{:S(2)}, u32[]{:S(2)}) collective-permute-start(bf16[2,32,1024]{2,1,0:T(8,128)(2,1)S(1)} %get-tuple-element.37), channel_id=1, source_target_pairs={{0,8},{8,16},{16,24},{24,32},{32,40},{40,48},{48,56},{56,64},{64,7... | collective-permute-start | bytes 393224 | tf_op jit(solution)/shard_map/ppermute | solution.py:660
  37.9 6.5 %all-to-all-start = ((bf16[16,16,1024]{2,1,0:T(8,128)(2,1)}), bf16[16,16,1024]{2,1,0:T(8,128)(2,1)S(1)}, u32[]{:S(2)}, u32[]{:S(2)}) async-start(bf16[16,16,1024]{2,1,0:T(8,128)(2,1)} %get-tuple-element.35), calls=%async_computation | async-start | bytes 1048576 | tf_op jit(solution)/shard_map/all_to_all | solution.py:662
  44.4 2.0 %collective-permute-start.5 = (bf16[2,32,1024]{2,1,0:T(8,128)(2,1)S(1)}, bf16[2,32,1024]{2,1,0:T(8,128)(2,1)S(1)}, u32[]{:S(2)}, u32[]{:S(2)}) collective-permute-start(bf16[2,32,1024]{2,1,0:T(8,128)(2,1)S(1)} %get-tuple-element.38), channel_id=1, source_target_pairs={{8,0},{16,8},{24,16},{32,24},{40,32},{48,40},{56,48},{64,56},{72,6... | collective-permute-start | bytes 393224 | tf_op jit(solution)/shard_map/ppermute | solution.py:661
  46.4 0.0 collective-permute-done.4.top_ref
  46.4 5.7 %collective-permute-done.5.bottom_ref = bf16[2,32,1024]{2,1,0:T(8,128)(2,1)S(1)} collective-permute-done((bf16[2,32,1024]{2,1,0:T(8,128)(2,1)S(1)}, bf16[2,32,1024]{2,1,0:T(8,128)(2,1)S(1)}, u32[]{:S(2)}, u32[]{:S(2)}) %collective-permute-start.5) | collective-permute-done | bytes 131104 | tf_op jit(solution)/shard_map/ppermute | solution.py:661
  52.2 4.7 %collective-permute-start.6 = (bf16[2,18,1024]{2,1,0:T(8,128)(2,1)S(1)}, bf16[2,18,1024]{2,1,0:T(8,128)(2,1)S(1)}, u32[]{:S(2)}, u32[]{:S(2)}) collective-permute-start(bf16[2,18,1024]{2,1,0:T(8,128)(2,1)S(1)} %pad_maximum_fusion.2), channel_id=1, source_target_pairs={{0,1},{1,2},{2,3},{3,4},{4,5},{5,6},{6,7},{8,9},{9,10},{10,11},{11... | collective-permute-start | bytes 221192 | tf_op jit(solution)/shard_map/ppermute | solution.py:667
  57.0 1.3 %collective-permute-start.7 = (bf16[2,18,1024]{2,1,0:T(8,128)(2,1)S(1)}, bf16[2,18,1024]{2,1,0:T(8,128)(2,1)S(1)}, u32[]{:S(2)}, u32[]{:S(2)}) collective-permute-start(bf16[2,18,1024]{2,1,0:T(8,128)(2,1)S(1)} %pad_maximum_fusion.3), channel_id=1, source_target_pairs={{1,0},{2,1},{3,2},{4,3},{5,4},{6,5},{7,6},{9,8},{10,9},{11,10},{12... | collective-permute-start | bytes 221192 | tf_op jit(solution)/shard_map/ppermute | solution.py:668
  58.3 0.0 all-to-all-done
  58.3 0.0 copy-done.3
  58.4 0.0 copy-done.7
  58.4 1.6 %combine.1 = bf16[8,32,1024]{2,1,0:T(8,128)(2,1)} custom-call(s32[2]{0:T(128)S(1)} %pad_add_fusion.refs_0_.place_ref, bf16[16,32,48]{2,1,0:T(8,128)(2,1)S(1)} %copy-done.7, bf16[8,48,256]{2,1,0:T(8,128)(2,1)S(1)} %copy-done.3, bf16[256,1024]{1,0:T(8,128)(2,1)S(1)} %bitcast.15), custom_call_target="tpu_custom_call" | custom-call | tf_op jit(solution)/shard_map/combine/pallas_call | solution.py:672
  60.0 7.9 %all-to-all-start.1 = ((bf16[8,32,1024]{2,1,0:T(8,128)(2,1)}), bf16[8,32,1024]{2,1,0:T(8,128)(2,1)S(1)}, u32[]{:S(2)}, u32[]{:S(2)}) async-start(bf16[8,32,1024]{2,1,0:T(8,128)(2,1)} %combine.1), calls=%async_computation.1 | async-start | bytes 1048576 | tf_op jit(solution)/shard_map/all_to_all | solution.py:688
  67.9 0.0 collective-permute-done.6
  67.9 0.0 collective-permute-done.7
  67.9 0.0 copy-start.2
  67.9 0.0 copy-start.4
  67.9 0.0 copy-start.5
  68.0 0.0 copy-start.6
  68.0 0.0 copy-start.8
  68.0 0.0 copy-start.9
  68.0 9.1 %conv.1 = f32[2,512,256]{2,1,0:T(8,128)S(1)} custom-call(bf16[2,512,1024]{2,1,0:T(8,128)(2,1)} %get-tuple-element.36.attended_ref, bf16[2,32,1024]{2,1,0:T(8,128)(2,1)S(1)} %collective-permute-done.4.top_ref, bf16[2,32,1024]{2,1,0:T(8,128)(2,1)S(1)} %collective-permute-done.5.bottom_ref, bf16[2,24,1024]{2,1,0:T(8,128)(2,1)S(1)} %pad.7.left_ref, ...), custom_call_target="tpu_custom_call" | custom-call | flops 4831838208 | bytes 6815744 | tf_op jit(solution)/shard_map/conv/pallas_call | solution.py:690
  77.1 2.7 %all-to-all-done.1 = bf16[8,32,1024]{2,1,0:T(8,128)(2,1)S(1)} async-done(((bf16[8,32,1024]{2,1,0:T(8,128)(2,1)}), bf16[8,32,1024]{2,1,0:T(8,128)(2,1)S(1)}, u32[]{:S(2)}, u32[]{:S(2)}) %all-to-all-start.1) | async-done | bytes 524320 | tf_op jit(solution)/shard_map/all_to_all | solution.py:688
  79.8 0.0 copy-done.2
  79.8 0.0 copy-done.4
  79.8 0.0 copy-done.5
  79.8 0.0 copy-done.6
  79.8 0.0 copy-done.8
  79.8 0.0 copy-done.9
  79.8 8.2 %tail.1 = bf16[2,512,256]{2,1,0:T(8,128)(2,1)} custom-call(s32[2]{0:T(128)S(1)} %pad_add_fusion.refs_0_.place_ref, bf16[8,96,256]{2,1,0:T(8,128)(2,1)S(1)} %copy-done.2, f32[16,1,96]{2,1,0:T(1,128)S(1)} %copy-done.8, f32[8,1,96]{2,1,0:T(1,128)S(1)} %copy-done.9, bf16[256,1024]{1,0:T(8,128)(2,1)S(1)} %bitcast.16, bf16[4,1024,512]{2,1,0:T(8,128)(2,1)} %wpool_hbm.1, ...), custom_call_target="tpu_custom_call" | custom-call | flops 4000000000 | bytes 13631488 | tf_op jit(solution)/shard_map/tail/pallas_call | solution.py:712
  (13 shorter events, 0.3 us)
Async XLA Ops:
  1.1 11.5 %collective-permute-start = (bf16[2,64,1024]{2,1,0:T(8,128)(2,1)S(1)}, bf16[2,64,1024]{2,1,0:T(8,128)(2,1)S(1)}, u32[]{:S(2)}, u32[]{:S(2)}) collective-permute-start(bf16[2,64,1024]{2,1,0:T(8,128)(2,1)S(1)} %bitcast.22), channel_id=1, source_target_pairs={{0,8},{8,16},{16,24},{24,32},{32,40},{40,48},{48,56},{56,64},{64,7... | collective-permute-start | bytes 786440 | tf_op jit(solution)/shard_map/ppermute | solution.py:563
  3.0 9.6 %collective-permute-start.1 = (bf16[2,64,1024]{2,1,0:T(8,128)(2,1)S(1)}, bf16[2,64,1024]{2,1,0:T(8,128)(2,1)S(1)}, u32[]{:S(2)}, u32[]{:S(2)}) collective-permute-start(bf16[2,64,1024]{2,1,0:T(8,128)(2,1)S(1)} %bitcast.21), channel_id=1, source_target_pairs={{8,0},{16,8},{24,16},{32,24},{40,32},{48,40},{56,48},{64,56},{72,6... | collective-permute-start | bytes 786440 | tf_op jit(solution)/shard_map/ppermute | solution.py:564
  6.7 12.7 %copy-start = (bf16[1024,512]{1,0:T(8,128)(2,1)S(1)}, bf16[1024,512]{1,0:T(8,128)(2,1)}, u32[]{:S(2)}) copy-start(bf16[1024,512]{1,0:T(8,128)(2,1)} %refs_6_.1) | copy-start | bytes 3145732
  6.7 12.7 %copy-start.1 = (f32[128,8,48]{2,1,0:T(8,128)S(1)}, f32[128,8,48]{2,1,0:T(8,128)}, u32[]{:S(2)}) copy-start(f32[128,8,48]{2,1,0:T(8,128)} %constant.31.clone.refs_8_) | copy-start | bytes 589828
  12.8 14.0 %collective-permute-start.3 = (bf16[2,20,2,1024]{3,1,2,0:T(8,128)(2,1)S(1)}, bf16[2,20,2,1024]{3,1,2,0:T(8,128)(2,1)S(1)}, u32[]{:S(2)}, u32[]{:S(2)}) collective-permute-start(bf16[2,20,2,1024]{3,1,2,0:T(8,128)(2,1)S(1)} %pad_maximum_fusion.1), channel_id=1, source_target_pairs={{0,1},{1,2},{2,3},{3,4},{4,5},{5,6},{6,7},{8,9},{9,10},{10,11},{11... | collective-permute-start | bytes 491528 | tf_op jit(solution)/shard_map/ppermute | solution.py:598
  18.0 10.2 %collective-permute-start.2 = (bf16[2,20,2,1024]{3,1,2,0:T(8,128)(2,1)S(1)}, bf16[2,20,2,1024]{3,1,2,0:T(8,128)(2,1)S(1)}, u32[]{:S(2)}, u32[]{:S(2)}) collective-permute-start(bf16[2,20,2,1024]{3,1,2,0:T(8,128)(2,1)S(1)} %pad_maximum_fusion), channel_id=1, source_target_pairs={{1,0},{2,1},{3,2},{4,3},{5,4},{6,5},{7,6},{9,8},{10,9},{11,10},{12... | collective-permute-start | bytes 491528 | tf_op jit(solution)/shard_map/ppermute | solution.py:599
  19.3 9.5 %copy-start.10 = (bf16[512,1024]{1,0:T(8,128)(2,1)S(1)}, bf16[512,1024]{1,0:T(8,128)(2,1)}, u32[]{:S(2)}) copy-start(bf16[512,1024]{1,0:T(8,128)(2,1)} %wout_ref.1) | copy-start | bytes 3145732
  28.8 29.5 %copy-start.3 = (bf16[8,48,256]{2,1,0:T(8,128)(2,1)S(1)}, bf16[8,48,256]{2,1,0:T(8,128)(2,1)}, u32[]{:S(2)}) copy-start(bf16[8,48,256]{2,1,0:T(8,128)(2,1)} %constant.33.clone.table_ref) | copy-start | bytes 589828
  28.8 29.5 %copy-start.7 = (bf16[16,32,48]{2,1,0:T(8,128)(2,1)S(1)}, bf16[16,32,48]{2,1,0:T(8,128)(2,1)}, u32[]{:S(2)}) copy-start(bf16[16,32,48]{2,1,0:T(8,128)(2,1)} %constant.32.clone.near_ref) | copy-start | bytes 147460
  36.0 10.4 %collective-permute-start.4 = (bf16[2,32,1024]{2,1,0:T(8,128)(2,1)S(1)}, bf16[2,32,1024]{2,1,0:T(8,128)(2,1)S(1)}, u32[]{:S(2)}, u32[]{:S(2)}) collective-permute-start(bf16[2,32,1024]{2,1,0:T(8,128)(2,1)S(1)} %get-tuple-element.37), channel_id=1, source_target_pairs={{0,8},{8,16},{16,24},{24,32},{32,40},{40,48},{48,56},{56,64},{64,7... | collective-permute-start | bytes 393224 | tf_op jit(solution)/shard_map/ppermute | solution.py:660
  37.9 20.4 %all-to-all-start = ((bf16[16,16,1024]{2,1,0:T(8,128)(2,1)}), bf16[16,16,1024]{2,1,0:T(8,128)(2,1)S(1)}, u32[]{:S(2)}, u32[]{:S(2)}) async-start(bf16[16,16,1024]{2,1,0:T(8,128)(2,1)} %get-tuple-element.35), calls=%async_computation | async-start | bytes 1048576 | tf_op jit(solution)/shard_map/all_to_all | solution.py:662
  44.4 7.8 %collective-permute-start.5 = (bf16[2,32,1024]{2,1,0:T(8,128)(2,1)S(1)}, bf16[2,32,1024]{2,1,0:T(8,128)(2,1)S(1)}, u32[]{:S(2)}, u32[]{:S(2)}) collective-permute-start(bf16[2,32,1024]{2,1,0:T(8,128)(2,1)S(1)} %get-tuple-element.38), channel_id=1, source_target_pairs={{8,0},{16,8},{24,16},{32,24},{40,32},{48,40},{56,48},{64,56},{72,6... | collective-permute-start | bytes 393224 | tf_op jit(solution)/shard_map/ppermute | solution.py:661
  52.2 15.6 %collective-permute-start.6 = (bf16[2,18,1024]{2,1,0:T(8,128)(2,1)S(1)}, bf16[2,18,1024]{2,1,0:T(8,128)(2,1)S(1)}, u32[]{:S(2)}, u32[]{:S(2)}) collective-permute-start(bf16[2,18,1024]{2,1,0:T(8,128)(2,1)S(1)} %pad_maximum_fusion.2), channel_id=1, source_target_pairs={{0,1},{1,2},{2,3},{3,4},{4,5},{5,6},{6,7},{8,9},{9,10},{10,11},{11... | collective-permute-start | bytes 221192 | tf_op jit(solution)/shard_map/ppermute | solution.py:667
  57.0 10.9 %collective-permute-start.7 = (bf16[2,18,1024]{2,1,0:T(8,128)(2,1)S(1)}, bf16[2,18,1024]{2,1,0:T(8,128)(2,1)S(1)}, u32[]{:S(2)}, u32[]{:S(2)}) collective-permute-start(bf16[2,18,1024]{2,1,0:T(8,128)(2,1)S(1)} %pad_maximum_fusion.3), channel_id=1, source_target_pairs={{1,0},{2,1},{3,2},{4,3},{5,4},{6,5},{7,6},{9,8},{10,9},{11,10},{12... | collective-permute-start | bytes 221192 | tf_op jit(solution)/shard_map/ppermute | solution.py:668
  60.0 19.7 %all-to-all-start.1 = ((bf16[8,32,1024]{2,1,0:T(8,128)(2,1)}), bf16[8,32,1024]{2,1,0:T(8,128)(2,1)S(1)}, u32[]{:S(2)}, u32[]{:S(2)}) async-start(bf16[8,32,1024]{2,1,0:T(8,128)(2,1)} %combine.1), calls=%async_computation.1 | async-start | bytes 1048576 | tf_op jit(solution)/shard_map/all_to_all | solution.py:688
  67.9 11.8 %copy-start.2 = (bf16[8,96,256]{2,1,0:T(8,128)(2,1)S(1)}, bf16[8,96,256]{2,1,0:T(8,128)(2,1)}, u32[]{:S(2)}) copy-start(bf16[8,96,256]{2,1,0:T(8,128)(2,1)} %constant.34.clone.table_hbm) | copy-start | bytes 1179652
  67.9 11.8 %copy-start.4 = (bf16[2,64,432]{2,1,0:T(8,128)(2,1)S(1)}, bf16[2,64,432]{2,1,0:T(8,128)(2,1)}, u32[]{:S(2)}) copy-start(bf16[2,64,432]{2,1,0:T(8,128)(2,1)} %constant.39.clone.spread_hbm) | copy-start | bytes 331780
  67.9 11.8 %copy-start.5 = (f32[8,32,64]{2,1,0:T(8,128)S(1)}, f32[8,32,64]{2,1,0:T(8,128)}, u32[]{:S(2)}) copy-start(f32[8,32,64]{2,1,0:T(8,128)} %constant.38.clone.by_col_hbm) | copy-start | bytes 196612
  68.0 11.8 %copy-start.6 = (f32[16,16,64]{2,1,0:T(8,128)S(1)}, f32[16,16,64]{2,1,0:T(8,128)}, u32[]{:S(2)}) copy-start(f32[16,16,64]{2,1,0:T(8,128)} %constant.37.clone.by_row_hbm) | copy-start | bytes 196612
  68.0 11.8 %copy-start.8 = (f32[16,1,96]{2,1,0:T(1,128)S(1)}, f32[16,1,96]{2,1,0:T(1,128)}, u32[]{:S(2)}) copy-start(f32[16,1,96]{2,1,0:T(1,128)} %constant.35.clone.row_scale_hbm) | copy-start | bytes 18436
  68.0 11.8 %copy-start.9 = (f32[8,1,96]{2,1,0:T(1,128)S(1)}, f32[8,1,96]{2,1,0:T(1,128)}, u32[]{:S(2)}) copy-start(f32[8,1,96]{2,1,0:T(1,128)} %constant.36.clone.col_scale_hbm) | copy-start | bytes 9220

commit v13 on v12

--- a/solution.py
+++ b/solution.py
@@ -404,17 +404,20 @@
         def _():
             fetch.wait()
 
-    def edge(ref, w_ref):
-        total = 0.0
-        for a in range(3):
-            total = total + dot(ref[...], w_ref[a])[a : a + rows]
-        return total.reshape(rows, 1, out_ch)
-
     def middle(w_ref):
         total = dot(ext[0:area], w_ref[0])
         for a in range(1, 3):
             total = total + dot(ext[a * cols : a * cols + area], w_ref[a])
         return total.reshape(rows, cols, out_ch)
+
+    def with_edge(w_ref, side_ref):
+        total, edge = 0.0, 0.0
+        for a in range(3):
+            lines = jnp.concatenate([ext[a * cols : a * cols + area], side_ref[...]], axis=0)
+            part = dot(lines, w_ref[a])
+            total = total + part[:area]
+            edge = edge + part[area + a : area + a + rows]
+        return total.reshape(rows, cols, out_ch), edge.reshape(rows, 1, out_ch)
 
     @pl.when(step == 0)
     def _():
@@ -422,7 +425,8 @@
         ext[cols : cols + area] = attended_ref[...]
         ext[cols + area :] = bottom_ref[...]
         place = lax.broadcasted_iota(jnp.int32, (rows, cols, out_ch), 1)
-        part = jnp.where(place == 0, edge(left_ref, taps_ref), pltpu.roll(middle(taps_ref), 1, 1))
+        total, edge = with_edge(taps_ref, left_ref)
+        part = jnp.where(place == 0, edge, pltpu.roll(total, 1, 1))
         out_ref[s] = part.reshape(area, out_ch)
 
     @pl.when(step == 1)
@@ -432,7 +436,8 @@
     @pl.when(step == 2)
     def _():
         place = lax.broadcasted_iota(jnp.int32, (rows, cols, out_ch), 1)
-        part = jnp.where(place == cols - 1, edge(right_ref, w.at[1]), pltpu.roll(middle(w.at[1]), cols - 1, 1))
+        total, edge = with_edge(w.at[1], right_ref)
+        part = jnp.where(place == cols - 1, edge, pltpu.roll(total, cols - 1, 1))
         out_ref[s] += part.reshape(area, out_ch)
 
 

time: 88.7 us -> 88.7 us (level)
  no operation moved by 1% of the time
where the time goes in v13:
time: 88.7 us; the launch traced here: 88.1 us
  Pallas kernels  37.9 us (43%)
  starting transfers between devices  36.3 us (41%)
  waiting for transfers between devices  11 us (12%)
  local copies, waits for them, and re-layouts  1.74 us (2%)
    pallas_call x1, Pallas kernels, layer(): pl.pallas_call(conv_kernel, grid=(sheets, 3), in_specs=[per_sheet(area, w...  8.68 us
    pallas_call x1, Pallas kernels, layer(): pl.pallas_call(tail_kernel, grid_spec=pltpu.PrefetchScalarGridSpec(num_sc...  8.18 us
    all_to_all x1, starting transfers between devices, layer(): lax.all_to_all(strips, 'col', 0, 0, tiled=True)  7.85 us
    pallas_call x1, Pallas kernels, layer(): pl.pallas_call(attend_kernel, grid=(sheets,), in_specs=[near] * 10 + [fix...  7.13 us
    pallas_call x1, Pallas kernels, layer(): pl.pallas_call(lambda *refs: middle_kernel((grid_h, grid_w), *refs), grid...  6.53 us
    all_to_all x1, starting transfers between devices, layer(): lax.all_to_all(sums, 'row', 0, 0, tiled=True)  6.5 us
    ppermute x1, waiting for transfers between devices, layer(): att_below = lax.ppermute(first_row, 'row', row_bwd)  5.71 us
    pallas_call x1, Pallas kernels, layer(): pl.pallas_call(project_kernel, grid=(sheets,), in_specs=[far] * 3, out_sp...  5.7 us
  transfers between devices with their start and end apart: 10, of which 4 were waited for; matrix products, arithmetic and copies ran while one was open for 1% of the time, Pallas kernels for 26%

profile of v13, /device:TPU:32, one launch (start us, length us, event | category | flops | bytes accessed | tf_op | source)
XLA Modules:
  0.0 88.1 jit_solution(6423911240622767201)
XLA Ops:
  0.0 1.1 %fusion = (bf16[2,2,32,1024]{3,2,1,0:T(8,128)(2,1)S(1)}, bf16[2,2,32,1024]{3,2,1,0:T(8,128)(2,1)S(1)}) fusion(bf16[2,16,32,1024]{3,2,1,0:T(8,128)(2,1)} %param.16), kind=kLoop, calls=%fused_computation.6 | loop fusion | bytes 1048576 | tf_op jit(solution)/shard_map/slice | solution.py:569
  1.1 1.9 %collective-permute-start = (bf16[2,64,1024]{2,1,0:T(8,128)(2,1)S(1)}, bf16[2,64,1024]{2,1,0:T(8,128)(2,1)S(1)}, u32[]{:S(2)}, u32[]{:S(2)}) collective-permute-start(bf16[2,64,1024]{2,1,0:T(8,128)(2,1)S(1)} %bitcast.22), channel_id=1, source_target_pairs={{0,8},{8,16},{16,24},{24,32},{32,40},{40,48},{48,56},{56,64},{64,7... | collective-permute-start | bytes 786440 | tf_op jit(solution)/shard_map/ppermute | solution.py:568
  3.0 3.6 %collective-permute-start.1 = (bf16[2,64,1024]{2,1,0:T(8,128)(2,1)S(1)}, bf16[2,64,1024]{2,1,0:T(8,128)(2,1)S(1)}, u32[]{:S(2)}, u32[]{:S(2)}) collective-permute-start(bf16[2,64,1024]{2,1,0:T(8,128)(2,1)S(1)} %bitcast.21), channel_id=1, source_target_pairs={{8,0},{16,8},{24,16},{32,24},{40,32},{48,40},{56,48},{64,56},{72,6... | collective-permute-start | bytes 786440 | tf_op jit(solution)/shard_map/ppermute | solution.py:569
  6.7 0.0 copy-start
  6.7 0.0 copy-start.1
  6.7 5.7 %project.1 = (bf16[2,512,1024]{2,1,0:T(8,128)(2,1)S(1)}, f32[2,16,32,1024]{3,2,1,0:T(8,128)S(1)}, bf16[2,2,16,1024]{3,2,1,0:T(8,128)(2,1)S(1)}, bf16[2,2,16,1024...) custom-call(bf16[2,512,1024]{2,1,0:T(8,128)(2,1)} %bitcast.23, ...), custom_call_target="tpu_custom_call" | custom-call | flops 2147483648 | bytes 13631488 | tf_op jit(solution)/shard_map/project/pallas_call | solution.py:582
  12.4 0.1 pad_add_fusion.refs_0_.place_ref
  12.5 0.1 pad.16.clone
  12.6 0.0 collective-permute-done.refs_3_
  12.6 0.0 collective-permute-done.1.refs_4_
  12.7 0.1 pad_maximum_fusion.1
  12.8 5.1 %collective-permute-start.3 = (bf16[2,20,2,1024]{3,1,2,0:T(8,128)(2,1)S(1)}, bf16[2,20,2,1024]{3,1,2,0:T(8,128)(2,1)S(1)}, u32[]{:S(2)}, u32[]{:S(2)}) collective-permute-start(bf16[2,20,2,1024]{3,1,2,0:T(8,128)(2,1)S(1)} %pad_maximum_fusion.1), channel_id=1, source_target_pairs={{0,1},{1,2},{2,3},{3,4},{4,5},{5,6},{6,7},{8,9},{9,10},{10,11},{11... | collective-permute-start | bytes 491528 | tf_op jit(solution)/shard_map/ppermute | solution.py:603
  17.9 0.1 pad_maximum_fusion
  18.0 1.3 %collective-permute-start.2 = (bf16[2,20,2,1024]{3,1,2,0:T(8,128)(2,1)S(1)}, bf16[2,20,2,1024]{3,1,2,0:T(8,128)(2,1)S(1)}, u32[]{:S(2)}, u32[]{:S(2)}) collective-permute-start(bf16[2,20,2,1024]{3,1,2,0:T(8,128)(2,1)S(1)} %pad_maximum_fusion), channel_id=1, source_target_pairs={{1,0},{2,1},{3,2},{4,3},{5,4},{6,5},{7,6},{9,8},{10,9},{11,10},{12... | collective-permute-start | bytes 491528 | tf_op jit(solution)/shard_map/ppermute | solution.py:604
  19.3 0.0 copy-done
  19.3 0.0 copy-done.1
  19.3 0.0 copy-start.10
  19.4 6.5 %middle.1 = (f32[2,16,32,512]{3,2,1,0:T(8,128)S(1)}, f32[2,4,32,1024]{3,2,1,0:T(8,128)S(1)}, f32[2,4,144,128]{3,2,1,0:T(8,128)S(1)}, bf16[8,512]{1,0:T(8,128)(2,1)S(1)}, f32[2,16,16,512]{3,2,1,0:T(8,128)S(1)}) custom-call(s32[2]{0:T(128)S(1)} %pad_add_fusion.refs_0_.place_ref, bf16[2,512,1024]{2,1,0:T(8,128)(2,1)S(1)} %get-tuple-element.23.refs_1_, ...), custom_call_target="tpu_custom_call" | custom-call | flops 2147483648 | bytes 8388608 | tf_op jit(solution)/shard_map/middle/pallas_call | solution.py:606
  25.9 0.9 %collective-permute-done.3 = bf16[2,20,2,1024]{3,1,2,0:T(8,128)(2,1)S(1)} collective-permute-done((bf16[2,20,2,1024]{3,1,2,0:T(8,128)(2,1)S(1)}, bf16[2,20,2,1024]{3,1,2,0:T(8,128)(2,1)S(1)}, u32[]{:S(2)}, u32[]{:S(2)}) %collective-permute-start.3) | collective-permute-done | bytes 163872 | tf_op jit(solution)/shard_map/ppermute | solution.py:603
  26.8 0.2 copy.22
  26.9 1.3 %collective-permute-done.2 = bf16[2,20,2,1024]{3,1,2,0:T(8,128)(2,1)S(1)} collective-permute-done((bf16[2,20,2,1024]{3,1,2,0:T(8,128)(2,1)S(1)}, bf16[2,20,2,1024]{3,1,2,0:T(8,128)(2,1)S(1)}, u32[]{:S(2)}, u32[]{:S(2)}) %collective-permute-start.2) | collective-permute-done | bytes 163872 | tf_op jit(solution)/shard_map/ppermute | solution.py:604
  28.2 0.2 copy.21
  28.4 0.4 maximum_bitcast_fusion.sides_ref
  28.8 0.0 copy-done.10
  28.8 0.0 copy-start.3
  28.8 0.0 copy-start.7
  28.8 7.1 %attend.1 = (bf16[2,512,1024]{2,1,0:T(8,128)(2,1)}, bf16[16,16,1024]{2,1,0:T(8,128)(2,1)}, bf16[2,32,1024]{2,1,0:T(8,128)(2,1)S(1)}, bf16[2,32,1024]{2,1,0:T(8,1...) custom-call(f32[2,16,32,512]{3,2,1,0:T(8,128)S(1)} %get-tuple-element.27.q_ref, ...), custom_call_target="tpu_custom_call" | custom-call | flops 4294967296 | bytes 8388608 | tf_op jit(solution)/shard_map/attend/pallas_call | solution.py:636
  36.0 1.9 %collective-permute-start.4 = (bf16[2,32,1024]{2,1,0:T(8,128)(2,1)S(1)}, bf16[2,32,1024]{2,1,0:T(8,128)(2,1)S(1)}, u32[]{:S(2)}, u32[]{:S(2)}) collective-permute-start(bf16[2,32,1024]{2,1,0:T(8,128)(2,1)S(1)} %get-tuple-element.37), channel_id=1, source_target_pairs={{0,8},{8,16},{16,24},{24,32},{32,40},{40,48},{48,56},{56,64},{64,7... | collective-permute-start | bytes 393224 | tf_op jit(solution)/shard_map/ppermute | solution.py:665
  37.9 6.5 %all-to-all-start = ((bf16[16,16,1024]{2,1,0:T(8,128)(2,1)}), bf16[16,16,1024]{2,1,0:T(8,128)(2,1)S(1)}, u32[]{:S(2)}, u32[]{:S(2)}) async-start(bf16[16,16,1024]{2,1,0:T(8,128)(2,1)} %get-tuple-element.35), calls=%async_computation | async-start | bytes 1048576 | tf_op jit(solution)/shard_map/all_to_all | solution.py:667
  44.4 2.0 %collective-permute-start.5 = (bf16[2,32,1024]{2,1,0:T(8,128)(2,1)S(1)}, bf16[2,32,1024]{2,1,0:T(8,128)(2,1)S(1)}, u32[]{:S(2)}, u32[]{:S(2)}) collective-permute-start(bf16[2,32,1024]{2,1,0:T(8,128)(2,1)S(1)} %get-tuple-element.38), channel_id=1, source_target_pairs={{8,0},{16,8},{24,16},{32,24},{40,32},{48,40},{56,48},{64,56},{72,6... | collective-permute-start | bytes 393224 | tf_op jit(solution)/shard_map/ppermute | solution.py:666
  46.4 0.0 collective-permute-done.4.top_ref
  46.4 5.7 %collective-permute-done.5.bottom_ref = bf16[2,32,1024]{2,1,0:T(8,128)(2,1)S(1)} collective-permute-done((bf16[2,32,1024]{2,1,0:T(8,128)(2,1)S(1)}, bf16[2,32,1024]{2,1,0:T(8,128)(2,1)S(1)}, u32[]{:S(2)}, u32[]{:S(2)}) %collective-permute-start.5) | collective-permute-done | bytes 131104 | tf_op jit(solution)/shard_map/ppermute | solution.py:666
  52.2 4.7 %collective-permute-start.6 = (bf16[2,18,1024]{2,1,0:T(8,128)(2,1)S(1)}, bf16[2,18,1024]{2,1,0:T(8,128)(2,1)S(1)}, u32[]{:S(2)}, u32[]{:S(2)}) collective-permute-start(bf16[2,18,1024]{2,1,0:T(8,128)(2,1)S(1)} %pad_maximum_fusion.2), channel_id=1, source_target_pairs={{0,1},{1,2},{2,3},{3,4},{4,5},{5,6},{6,7},{8,9},{9,10},{10,11},{11... | collective-permute-start | bytes 221192 | tf_op jit(solution)/shard_map/ppermute | solution.py:672
  57.0 1.3 %collective-permute-start.7 = (bf16[2,18,1024]{2,1,0:T(8,128)(2,1)S(1)}, bf16[2,18,1024]{2,1,0:T(8,128)(2,1)S(1)}, u32[]{:S(2)}, u32[]{:S(2)}) collective-permute-start(bf16[2,18,1024]{2,1,0:T(8,128)(2,1)S(1)} %pad_maximum_fusion.3), channel_id=1, source_target_pairs={{1,0},{2,1},{3,2},{4,3},{5,4},{6,5},{7,6},{9,8},{10,9},{11,10},{12... | collective-permute-start | bytes 221192 | tf_op jit(solution)/shard_map/ppermute | solution.py:673
  58.3 0.0 all-to-all-done
  58.3 0.0 copy-done.3
  58.4 0.0 copy-done.7
  58.4 1.6 %combine.1 = bf16[8,32,1024]{2,1,0:T(8,128)(2,1)} custom-call(s32[2]{0:T(128)S(1)} %pad_add_fusion.refs_0_.place_ref, bf16[16,32,48]{2,1,0:T(8,128)(2,1)S(1)} %copy-done.7, bf16[8,48,256]{2,1,0:T(8,128)(2,1)S(1)} %copy-done.3, bf16[256,1024]{1,0:T(8,128)(2,1)S(1)} %bitcast.15), custom_call_target="tpu_custom_call" | custom-call | tf_op jit(solution)/shard_map/combine/pallas_call | solution.py:677
  60.0 7.9 %all-to-all-start.1 = ((bf16[8,32,1024]{2,1,0:T(8,128)(2,1)}), bf16[8,32,1024]{2,1,0:T(8,128)(2,1)S(1)}, u32[]{:S(2)}, u32[]{:S(2)}) async-start(bf16[8,32,1024]{2,1,0:T(8,128)(2,1)} %combine.1), calls=%async_computation.1 | async-start | bytes 1048576 | tf_op jit(solution)/shard_map/all_to_all | solution.py:693
  67.9 0.0 collective-permute-done.6
  67.9 0.0 collective-permute-done.7
  67.9 0.0 copy-start.2
  67.9 0.0 copy-start.4
  67.9 0.0 copy-start.5
  68.0 0.0 copy-start.6
  68.0 0.0 copy-start.8
  68.0 0.0 copy-start.9
  68.0 8.7 %conv.1 = f32[2,512,256]{2,1,0:T(8,128)S(1)} custom-call(bf16[2,512,1024]{2,1,0:T(8,128)(2,1)} %get-tuple-element.36.attended_ref, bf16[2,32,1024]{2,1,0:T(8,128)(2,1)S(1)} %collective-permute-done.4.top_ref, bf16[2,32,1024]{2,1,0:T(8,128)(2,1)S(1)} %collective-permute-done.5.bottom_ref, bf16[2,24,1024]{2,1,0:T(8,128)(2,1)S(1)} %pad.7.left_ref, ...), custom_call_target="tpu_custom_call" | custom-call | flops 4831838208 | bytes 6815744 | tf_op jit(solution)/shard_map/conv/pallas_call | solution.py:695
  76.7 3.1 %all-to-all-done.1 = bf16[8,32,1024]{2,1,0:T(8,128)(2,1)S(1)} async-done(((bf16[8,32,1024]{2,1,0:T(8,128)(2,1)}), bf16[8,32,1024]{2,1,0:T(8,128)(2,1)S(1)}, u32[]{:S(2)}, u32[]{:S(2)}) %all-to-all-start.1) | async-done | bytes 524320 | tf_op jit(solution)/shard_map/all_to_all | solution.py:693
  79.8 0.0 copy-done.2
  79.8 0.0 copy-done.4
  79.8 0.0 copy-done.5
  79.8 0.0 copy-done.6
  79.8 0.0 copy-done.8
  79.8 0.0 copy-done.9
  79.8 8.2 %tail.1 = bf16[2,512,256]{2,1,0:T(8,128)(2,1)} custom-call(s32[2]{0:T(128)S(1)} %pad_add_fusion.refs_0_.place_ref, bf16[8,96,256]{2,1,0:T(8,128)(2,1)S(1)} %copy-done.2, f32[16,1,96]{2,1,0:T(1,128)S(1)} %copy-done.8, f32[8,1,96]{2,1,0:T(1,128)S(1)} %copy-done.9, bf16[256,1024]{1,0:T(8,128)(2,1)S(1)} %bitcast.16, bf16[4,1024,512]{2,1,0:T(8,128)(2,1)} %wpool_hbm.1, ...), custom_call_target="tpu_custom_call" | custom-call | flops 4000000000 | bytes 13631488 | tf_op jit(solution)/shard_map/tail/pallas_call | solution.py:717
  (13 shorter events, 0.3 us)
Async XLA Ops:
  1.1 11.5 %collective-permute-start = (bf16[2,64,1024]{2,1,0:T(8,128)(2,1)S(1)}, bf16[2,64,1024]{2,1,0:T(8,128)(2,1)S(1)}, u32[]{:S(2)}, u32[]{:S(2)}) collective-permute-start(bf16[2,64,1024]{2,1,0:T(8,128)(2,1)S(1)} %bitcast.22), channel_id=1, source_target_pairs={{0,8},{8,16},{16,24},{24,32},{32,40},{40,48},{48,56},{56,64},{64,7... | collective-permute-start | bytes 786440 | tf_op jit(solution)/shard_map/ppermute | solution.py:568
  3.0 9.6 %collective-permute-start.1 = (bf16[2,64,1024]{2,1,0:T(8,128)(2,1)S(1)}, bf16[2,64,1024]{2,1,0:T(8,128)(2,1)S(1)}, u32[]{:S(2)}, u32[]{:S(2)}) collective-permute-start(bf16[2,64,1024]{2,1,0:T(8,128)(2,1)S(1)} %bitcast.21), channel_id=1, source_target_pairs={{8,0},{16,8},{24,16},{32,24},{40,32},{48,40},{56,48},{64,56},{72,6... | collective-permute-start | bytes 786440 | tf_op jit(solution)/shard_map/ppermute | solution.py:569
  6.7 12.7 %copy-start = (bf16[1024,512]{1,0:T(8,128)(2,1)S(1)}, bf16[1024,512]{1,0:T(8,128)(2,1)}, u32[]{:S(2)}) copy-start(bf16[1024,512]{1,0:T(8,128)(2,1)} %refs_6_.1) | copy-start | bytes 3145732
  6.7 12.7 %copy-start.1 = (f32[128,8,48]{2,1,0:T(8,128)S(1)}, f32[128,8,48]{2,1,0:T(8,128)}, u32[]{:S(2)}) copy-start(f32[128,8,48]{2,1,0:T(8,128)} %constant.31.clone.refs_8_) | copy-start | bytes 589828
  12.8 14.0 %collective-permute-start.3 = (bf16[2,20,2,1024]{3,1,2,0:T(8,128)(2,1)S(1)}, bf16[2,20,2,1024]{3,1,2,0:T(8,128)(2,1)S(1)}, u32[]{:S(2)}, u32[]{:S(2)}) collective-permute-start(bf16[2,20,2,1024]{3,1,2,0:T(8,128)(2,1)S(1)} %pad_maximum_fusion.1), channel_id=1, source_target_pairs={{0,1},{1,2},{2,3},{3,4},{4,5},{5,6},{6,7},{8,9},{9,10},{10,11},{11... | collective-permute-start | bytes 491528 | tf_op jit(solution)/shard_map/ppermute | solution.py:603
  18.0 10.2 %collective-permute-start.2 = (bf16[2,20,2,1024]{3,1,2,0:T(8,128)(2,1)S(1)}, bf16[2,20,2,1024]{3,1,2,0:T(8,128)(2,1)S(1)}, u32[]{:S(2)}, u32[]{:S(2)}) collective-permute-start(bf16[2,20,2,1024]{3,1,2,0:T(8,128)(2,1)S(1)} %pad_maximum_fusion), channel_id=1, source_target_pairs={{1,0},{2,1},{3,2},{4,3},{5,4},{6,5},{7,6},{9,8},{10,9},{11,10},{12... | collective-permute-start | bytes 491528 | tf_op jit(solution)/shard_map/ppermute | solution.py:604
  19.3 9.5 %copy-start.10 = (bf16[512,1024]{1,0:T(8,128)(2,1)S(1)}, bf16[512,1024]{1,0:T(8,128)(2,1)}, u32[]{:S(2)}) copy-start(bf16[512,1024]{1,0:T(8,128)(2,1)} %wout_ref.1) | copy-start | bytes 3145732
  28.8 29.5 %copy-start.3 = (bf16[8,48,256]{2,1,0:T(8,128)(2,1)S(1)}, bf16[8,48,256]{2,1,0:T(8,128)(2,1)}, u32[]{:S(2)}) copy-start(bf16[8,48,256]{2,1,0:T(8,128)(2,1)} %constant.33.clone.table_ref) | copy-start | bytes 589828
  28.8 29.5 %copy-start.7 = (bf16[16,32,48]{2,1,0:T(8,128)(2,1)S(1)}, bf16[16,32,48]{2,1,0:T(8,128)(2,1)}, u32[]{:S(2)}) copy-start(bf16[16,32,48]{2,1,0:T(8,128)(2,1)} %constant.32.clone.near_ref) | copy-start | bytes 147460
  36.0 10.4 %collective-permute-start.4 = (bf16[2,32,1024]{2,1,0:T(8,128)(2,1)S(1)}, bf16[2,32,1024]{2,1,0:T(8,128)(2,1)S(1)}, u32[]{:S(2)}, u32[]{:S(2)}) collective-permute-start(bf16[2,32,1024]{2,1,0:T(8,128)(2,1)S(1)} %get-tuple-element.37), channel_id=1, source_target_pairs={{0,8},{8,16},{16,24},{24,32},{32,40},{40,48},{48,56},{56,64},{64,7... | collective-permute-start | bytes 393224 | tf_op jit(solution)/shard_map/ppermute | solution.py:665
  37.9 20.4 %all-to-all-start = ((bf16[16,16,1024]{2,1,0:T(8,128)(2,1)}), bf16[16,16,1024]{2,1,0:T(8,128)(2,1)S(1)}, u32[]{:S(2)}, u32[]{:S(2)}) async-start(bf16[16,16,1024]{2,1,0:T(8,128)(2,1)} %get-tuple-element.35), calls=%async_computation | async-start | bytes 1048576 | tf_op jit(solution)/shard_map/all_to_all | solution.py:667
  44.4 7.8 %collective-permute-start.5 = (bf16[2,32,1024]{2,1,0:T(8,128)(2,1)S(1)}, bf16[2,32,1024]{2,1,0:T(8,128)(2,1)S(1)}, u32[]{:S(2)}, u32[]{:S(2)}) collective-permute-start(bf16[2,32,1024]{2,1,0:T(8,128)(2,1)S(1)} %get-tuple-element.38), channel_id=1, source_target_pairs={{8,0},{16,8},{24,16},{32,24},{40,32},{48,40},{56,48},{64,56},{72,6... | collective-permute-start | bytes 393224 | tf_op jit(solution)/shard_map/ppermute | solution.py:666
  52.2 15.6 %collective-permute-start.6 = (bf16[2,18,1024]{2,1,0:T(8,128)(2,1)S(1)}, bf16[2,18,1024]{2,1,0:T(8,128)(2,1)S(1)}, u32[]{:S(2)}, u32[]{:S(2)}) collective-permute-start(bf16[2,18,1024]{2,1,0:T(8,128)(2,1)S(1)} %pad_maximum_fusion.2), channel_id=1, source_target_pairs={{0,1},{1,2},{2,3},{3,4},{4,5},{5,6},{6,7},{8,9},{9,10},{10,11},{11... | collective-permute-start | bytes 221192 | tf_op jit(solution)/shard_map/ppermute | solution.py:672
  57.0 10.9 %collective-permute-start.7 = (bf16[2,18,1024]{2,1,0:T(8,128)(2,1)S(1)}, bf16[2,18,1024]{2,1,0:T(8,128)(2,1)S(1)}, u32[]{:S(2)}, u32[]{:S(2)}) collective-permute-start(bf16[2,18,1024]{2,1,0:T(8,128)(2,1)S(1)} %pad_maximum_fusion.3), channel_id=1, source_target_pairs={{1,0},{2,1},{3,2},{4,3},{5,4},{6,5},{7,6},{9,8},{10,9},{11,10},{12... | collective-permute-start | bytes 221192 | tf_op jit(solution)/shard_map/ppermute | solution.py:673
  60.0 19.7 %all-to-all-start.1 = ((bf16[8,32,1024]{2,1,0:T(8,128)(2,1)}), bf16[8,32,1024]{2,1,0:T(8,128)(2,1)S(1)}, u32[]{:S(2)}, u32[]{:S(2)}) async-start(bf16[8,32,1024]{2,1,0:T(8,128)(2,1)} %combine.1), calls=%async_computation.1 | async-start | bytes 1048576 | tf_op jit(solution)/shard_map/all_to_all | solution.py:693
  67.9 11.8 %copy-start.2 = (bf16[8,96,256]{2,1,0:T(8,128)(2,1)S(1)}, bf16[8,96,256]{2,1,0:T(8,128)(2,1)}, u32[]{:S(2)}) copy-start(bf16[8,96,256]{2,1,0:T(8,128)(2,1)} %constant.34.clone.table_hbm) | copy-start | bytes 1179652
  67.9 11.8 %copy-start.4 = (bf16[2,64,432]{2,1,0:T(8,128)(2,1)S(1)}, bf16[2,64,432]{2,1,0:T(8,128)(2,1)}, u32[]{:S(2)}) copy-start(bf16[2,64,432]{2,1,0:T(8,128)(2,1)} %constant.39.clone.spread_hbm) | copy-start | bytes 331780
  67.9 11.8 %copy-start.5 = (f32[8,32,64]{2,1,0:T(8,128)S(1)}, f32[8,32,64]{2,1,0:T(8,128)}, u32[]{:S(2)}) copy-start(f32[8,32,64]{2,1,0:T(8,128)} %constant.38.clone.by_col_hbm) | copy-start | bytes 196612
  68.0 11.8 %copy-start.6 = (f32[16,16,64]{2,1,0:T(8,128)S(1)}, f32[16,16,64]{2,1,0:T(8,128)}, u32[]{:S(2)}) copy-start(f32[16,16,64]{2,1,0:T(8,128)} %constant.37.clone.by_row_hbm) | copy-start | bytes 196612
  68.0 11.8 %copy-start.8 = (f32[16,1,96]{2,1,0:T(1,128)S(1)}, f32[16,1,96]{2,1,0:T(1,128)}, u32[]{:S(2)}) copy-start(f32[16,1,96]{2,1,0:T(1,128)} %constant.35.clone.row_scale_hbm) | copy-start | bytes 18436
  68.0 11.8 %copy-start.9 = (f32[8,1,96]{2,1,0:T(1,128)S(1)}, f32[8,1,96]{2,1,0:T(1,128)}, u32[]{:S(2)}) copy-start(f32[8,1,96]{2,1,0:T(1,128)} %constant.36.clone.col_scale_hbm) | copy-start | bytes 9220
